TPU v7x, 256 devices: a whole 4x4x8 slice. The times are simulated.
256 devices in a mesh: pts: 4 (over y_hi, core), ctr: 64 (over x, z, y_lo).
Axes of the slice: x: 4, y: 4 (y_hi: 2, y_lo: 2; y = y_hi * 2 + y_lo), z: 8, core: 2. Of those that a mesh axis runs over, the one named last changes fastest.
Arguments:
- points: bfloat16 [4096, 512], P(('pts', 'ctr')), may hold values from -6 to 6
- point_class: int32 [4096], P(('pts', 'ctr')), may hold values from 0 to 7
- targets: float32 [4096, 128], P(('pts', 'ctr')), may hold values from -6 to 6
- class_weight: float32 [8], replicated, may hold values from 0.25 to 4
- inv_scale: float32 [512], replicated, may hold values from 0.003 to 0.3
- centers: bfloat16 [262144, 512], P('ctr'), may hold values from -6 to 6
- coefficients: bfloat16 [262144, 128], P('ctr'), may hold values from -2.5 to 2.5
- center_index: int32 [4096], replicated, may hold values from 0 to 262143, as said below
- factor: float32 [4096, 4096], P('ctr'), as said below
- panel_inverse: float32 [4096, 2048], P('ctr'), as said below
Outputs:
- gradient: float32 [262144, 128], P('ctr', 'pts')
- solved: float32 [4096, 128], P('ctr', 'pts')
Inputs may be any that keep to these rules, and one draw needn't show every extreme that they name: `center_index`: the values are distinct; window row r lies in the center shard (index of ctr, 4096 centers each) numbered order[r mod 64] for one permutation order of the shards, so each shard holds exactly 64 window rows and the 64 rows of each aligned block of the window hold at most 1 of one shard's centers, a bound that is reached. factor is lower triangular with its diagonal between 1 and 2. `panel_inverse`: the rows of panel p hold the inverse of factor's diagonal block of rows and columns p * 2048 to (p + 1) * 2048 - 1.
All inputs are finite; a program needn't handle non-finite values.
Results may differ from a plain program's by a relative error of at most 0.0055.
Values may be sent and summed in bfloat16 or wider, within the bound.
No kernel may reach another device: no remote copies, remote signals or barrier semaphores. Data moves between devices by JAX's collectives and lax.ppermute only.
A program may use at most 64 MiB of HBM per device.

v0:
```python
import jax
import jax.numpy as jnp
from jax import lax
from jax.sharding import PartitionSpec as P


def from_everyone(x, axis):
    count = lax.axis_size(axis)
    return lax.all_to_all(jnp.broadcast_to(x[None], (count, *x.shape)), axis, 0, 0, tiled=True)


def laid_out(pieces, dim):
    pieces = jnp.moveaxis(pieces, 0, dim)
    dims = pieces.shape
    return pieces.reshape(*dims[:dim], dims[dim] * dims[dim + 1], *dims[dim + 2 :])


def gathered_copies(x, axis, dim):
    pieces = from_everyone(x, axis)
    return laid_out(pieces, dim)


def split_up(x, dim, count):
    dims = x.shape
    pieces = x.reshape(*dims[:dim], count, dims[dim] // count, *dims[dim + 1 :])
    return jnp.moveaxis(pieces, dim, 0)


def sent_and_summed(x, axis, dim):
    count = lax.axis_size(axis)
    pieces = lax.all_to_all(split_up(x, dim, count), axis, 0, 0, tiled=True)
    return jnp.sum(pieces, axis=0)


def gaussian(samples, anchors):
    products = lax.dot_general(
        samples, anchors, (((1,), (1,)), ((), ())), preferred_element_type=jnp.float32
    )
    left_norm = jnp.sum(jnp.square(samples.astype(jnp.float32)), axis=1)
    right_norm = jnp.sum(jnp.square(anchors.astype(jnp.float32)), axis=1)
    exponent = products - 0.5 * left_norm[:, None] - 0.5 * right_norm[None, :]
    return jnp.exp(exponent).astype(jnp.bfloat16)


def class_lookup(labels, table):
    classes = jnp.arange(table.shape[0], dtype=jnp.int32)
    return jnp.sum(jnp.where(labels[:, None] == classes[None, :], table[None, :], 0.0), axis=1)


def window_slots(center_index, shard_rows, blocks):
    owner = (center_index // shard_rows).reshape(blocks, -1)
    block_len = owner.shape[1]
    position = jnp.arange(block_len, dtype=jnp.int32)
    earlier = (owner[:, :, None] == owner[:, None, :]) & (
        position[None, None, :] < position[None, :, None]
    )
    return (owner, jnp.sum(earlier.astype(jnp.int32), axis=2))


def body(
    points,
    point_class,
    targets,
    class_weight,
    inv_scale,
    centers,
    coefficients,
    center_index,
    factor,
    panel_inverse,
):
    own_scaled = (points.astype(jnp.float32) * inv_scale[None, :]).astype(jnp.bfloat16)
    group_rows = gathered_copies(own_scaled, "ctr", 0)
    scaled_centers = (centers.astype(jnp.float32) * inv_scale[None, :]).astype(jnp.bfloat16)
    kernel = gaussian(group_rows, scaled_centers)
    partial_value = jnp.dot(kernel, coefficients, preferred_element_type=jnp.float32)
    own_weight = class_lookup(point_class, class_weight)
    shares = sent_and_summed(partial_value, "ctr", 0)
    own_residual = (own_weight[:, None] * (shares - targets)).astype(jnp.bfloat16)
    residual = gathered_copies(own_residual, "ctr", 0)
    backward = lax.dot_general(
        kernel, residual, (((0,), (0,)), ((), ())), preferred_element_type=jnp.float32
    )
    gradient = sent_and_summed(backward, "pts", 1)
    row_count = gradient.shape[0]
    shard_index = lax.axis_index("ctr")
    relative = center_index - shard_index * row_count
    inside = (relative >= 0) & (relative < row_count)
    picked = jnp.take(gradient, jnp.clip(relative, 0, row_count - 1), axis=0)
    blocks = lax.axis_size("ctr")
    block_len = center_index.shape[0] // blocks
    slot_cap = (block_len + blocks - 1) // blocks
    owner, slot = window_slots(center_index, row_count, blocks)
    block_of = jnp.arange(blocks, dtype=jnp.int32)[:, None]
    target_slot = jnp.where(
        inside.reshape(blocks, block_len), block_of * slot_cap + slot, blocks * slot_cap
    )
    outgoing = jnp.zeros((blocks * slot_cap, picked.shape[1]), jnp.float32)
    outgoing = outgoing.at[target_slot.reshape(-1)].set(picked, mode="drop")
    incoming = lax.all_to_all(outgoing, "ctr", split_axis=0, concat_axis=0, tiled=True)
    own_owner = lax.dynamic_index_in_dim(owner, shard_index, 0, keepdims=False)
    own_slot = lax.dynamic_index_in_dim(slot, shard_index, 0, keepdims=False)
    rhs_own = jnp.take(incoming, own_owner * slot_cap + own_slot, axis=0)
    own_rows = rhs_own.shape[0]
    panel_rows = panel_inverse.shape[1]
    panel_count = factor.shape[1] // panel_rows
    own_panel = shard_index * own_rows // panel_rows
    solved_full = jnp.zeros((factor.shape[1], rhs_own.shape[1]), jnp.float32)
    solved = jnp.zeros_like(rhs_own)
    for current in range(panel_count):
        reduced = rhs_own
        if current > 0:
            reduced = rhs_own - jnp.dot(factor, solved_full, precision=lax.Precision.HIGHEST)
        gathered = gathered_copies(reduced, "ctr", 0)
        begin = current * panel_rows
        panel_part = jnp.dot(
            panel_inverse, gathered[begin : begin + panel_rows], precision=lax.Precision.HIGHEST
        )
        panel_part = jnp.where(own_panel == current, panel_part, 0.0)
        solved = solved + panel_part
        if current + 1 < panel_count:
            solved_full = gathered_copies(panel_part, "ctr", 0)
    return (gradient, solved)


def solution(mesh):
    placed = (
        P(("pts", "ctr"), None),
        P(("pts", "ctr")),
        P(("pts", "ctr"), None),
        P(),
        P(),
        P("ctr", None),
        P("ctr", None),
        P(),
        P("ctr", None),
        P("ctr", None),
    )
    return jax.shard_map(
        body,
        mesh=mesh,
        in_specs=placed,
        out_specs=(P("ctr", "pts"), P("ctr", "pts")),
        check_vma=False,
    )
```

profile of v0, /device:TPU:4, one launch (start us, length us, event | category | flops | bytes accessed | tf_op | source)
XLA Modules:
  0.0 259.4 jit_solution(5261055090876658257)
XLA Ops:
  0.6 0.8 multiply_convert_fusion.2
  1.5 1.1 broadcast_in_dim.90
  2.6 13.1 %all-to-all-start = ((bf16[64,16,512]{2,1,0:T(8,128)(2,1)}), bf16[64,16,512]{2,1,0:T(8,128)(2,1)S(1)}, u32[]{:S(2)}, u32[]{:S(2)}) async-start(bf16[64,16,512]{2,1,0:T(8,128)(2,1)} %broadcast_in_dim.90), calls=%async_computation | async-start | bytes 2097152 | tf_op jit(solution)/shard_map/all_to_all | solution.py:9
  15.7 3.4 %multiply_reduce_fusion = f32[4096]{0:T(1024)S(1)} fusion(f32[512]{0:T(512)} %param.14, bf16[4096,512]{1,0:T(8,128)(2,1)} %param.15), kind=kLoop, calls=%fused_computation.6 | loop fusion | flops 12578816 | bytes 4212736 | tf_op jit(solution)/shard_map/reduce_sum | solution.py:40
  19.1 23.7 %all-to-all-done = bf16[64,16,512]{2,1,0:T(8,128)(2,1)S(1)} async-done(((bf16[64,16,512]{2,1,0:T(8,128)(2,1)}), bf16[64,16,512]{2,1,0:T(8,128)(2,1)S(1)}, u32[]{:S(2)}, u32[]{:S(2)}) %all-to-all-start) | async-done | bytes 1048608 | tf_op jit(solution)/shard_map/all_to_all | solution.py:9
  42.8 0.3 multiply_reduce_fusion.1
  43.1 7.9 %exponential_convert_fusion = bf16[1024,4096]{1,0:T(8,128)(2,1)S(1)} fusion(f32[4096]{0:T(1024)S(1)} %broadcast_multiply_fusion.1, f32[1024]{0:T(1024)S(1)} %mul.61, bf16[1024,512]{1,0:T(8,128)(2,1)S(1)} %bitcast.56, bf16[4096,512]{1,0:T(8,128)(2,1)} %param.15, f32[512]{0:T(512)S(1)} %copy-done.4), kind=kOutput, calls=%fused_computation.3 | convolution fusion | flops 4313841664 | bytes 13654016 | tf_op jit(solution)/shard_map/dot_general | solution.py:36
  51.1 3.5 %fusion.19 = f32[1024,128]{1,0:T(8,128)} fusion(bf16[1024,4096]{1,0:T(8,128)(2,1)S(1)} %exponential_convert_fusion, bf16[4096,128]{1,0:T(8,128)(2,1)S(1)} %copy-done), kind=kOutput, calls=%fused_computation.53 | convolution fusion | flops 1073741824 | bytes 9961472 | tf_op jit(solution)/shard_map/dot_general | solution.py:76
  54.6 7.8 %all-to-all-start.1 = ((f32[64,16,128]{2,1,0:T(8,128)}), f32[64,16,128]{2,1,0:T(8,128)S(1)}, u32[]{:S(2)}, u32[]{:S(2)}) async-start(f32[64,16,128]{2,1,0:T(8,128)} %bitcast.2), calls=%async_computation.1 | async-start | bytes 1048576 | tf_op jit(solution)/shard_map/all_to_all | solution.py:31
  62.5 16.0 %all-to-all-done.1 = f32[64,16,128]{2,1,0:T(8,128)S(1)} async-done(((f32[64,16,128]{2,1,0:T(8,128)}), f32[64,16,128]{2,1,0:T(8,128)S(1)}, u32[]{:S(2)}, u32[]{:S(2)}) %all-to-all-start.1) | async-done | bytes 524320 | tf_op jit(solution)/shard_map/all_to_all | solution.py:31
  78.7 17.5 %all_to_all.47 = bf16[64,16,128]{2,1,0:T(8,128)(2,1)S(1)} all-to-all(bf16[64,16,128]{2,1,0:T(8,128)(2,1)S(1)} %broadcast_in_dim.93), channel_id=1, replica_groups=mesh['pts'=4,'ctr'=64] {'ctr'}, dimensions={0} | all-to-all | bytes 524288 | tf_op jit(solution)/shard_map/all_to_all | solution.py:9
  96.2 0.1 copy.33
  96.3 6.0 %fusion.2 = f32[4,4096,32]{1,2,0:T(8,128)} fusion(bf16[4,32,1024]{2,1,0:T(8,128)(2,1)S(1)} %bitcast.62, bf16[1024,4096]{1,0:T(8,128)(2,1)} %copy-done.8), kind=kOutput, calls=%fused_computation.8 | convolution fusion | flops 1073741824 | bytes 10747904 | tf_op jit(solution)/shard_map/dot_general | solution.py:81
  102.4 4.3 %all-to-all-start.3 = ((f32[4,4096,32]{1,2,0:T(8,128)}), f32[4,4096,32]{1,2,0:T(8,128)S(1)}, u32[]{:S(2)}, u32[]{:S(2)}) async-start(f32[4,4096,32]{1,2,0:T(8,128)} %fusion.2), calls=%async_computation.3 | async-start | bytes 4194304 | tf_op jit(solution)/shard_map/all_to_all | solution.py:31
  106.8 1.9 convert_reduce_fusion
  108.8 25.1 %all-to-all-done.3 = f32[4,4096,32]{1,2,0:T(8,128)S(1)} async-done(((f32[4,4096,32]{1,2,0:T(8,128)}), f32[4,4096,32]{1,2,0:T(8,128)S(1)}, u32[]{:S(2)}, u32[]{:S(2)}) %all-to-all-start.3) | async-done | bytes 2097184 | tf_op jit(solution)/shard_map/all_to_all | solution.py:31
  133.9 0.9 reduce_sum.58
  134.8 1.6 copy.34
  136.5 24.2 %scatter_custom_fusion = f32[64,32]{1,0:T(8,128)} fusion(s32[4096]{0:T(1024)S(1)} %get-tuple-element.9, f32[]{:T(128)} %constant.79.clone.1, pred[4096]{0:T(1024)(128)(4,1)S(1)} %compare_and_fusion, f32[]{:T(128)} %constant.66.clone.1, f32[4096,32]{1,0:T(8,128)S(1)} %copy.34, s32[4096]{0:T(1024)S(1)} %get-tuple-element.8), kind=kCustom, calls=%fused_computation.9 | custom fusion | flops 131072 | bytes 2125832 | tf_op jit(solution)/shard_map/scatter | solution.py:99
  160.6 6.6 %all-to-all-start.4 = ((f32[64,1,32]{2,1,0:T(1,128)}), f32[64,1,32]{2,1,0:T(1,128)S(1)}, u32[]{:S(2)}, u32[]{:S(2)}) async-start(f32[64,1,32]{2,1,0:T(1,128)} %bitcast.8), calls=%async_computation.4 | async-start | bytes 65536 | tf_op jit(solution)/shard_map/all_to_all | solution.py:100
  167.2 8.6 %all-to-all-done.4 = f32[64,1,32]{2,1,0:T(1,128)S(1)} async-done(((f32[64,1,32]{2,1,0:T(1,128)}), f32[64,1,32]{2,1,0:T(1,128)S(1)}, u32[]{:S(2)}, u32[]{:S(2)}) %all-to-all-start.4) | async-done | bytes 8224 | tf_op jit(solution)/shard_map/all_to_all | solution.py:100
  175.8 0.6 gather_fusion
  176.5 0.1 broadcast_bitcast_fusion.2
  176.6 1.4 reshape.166
  178.1 6.4 %all-to-all-start.5 = ((f32[64,1,2048]{2,1,0:T(1,128)}), f32[64,1,2048]{2,1,0:T(1,128)S(1)}, u32[]{:S(2)}, u32[]{:S(2)}) async-start(f32[64,1,2048]{2,1,0:T(1,128)} %reshape.166), calls=%async_computation.5 | async-start | bytes 1048576 | tf_op jit(solution)/shard_map/all_to_all | solution.py:9
  184.5 15.2 %all-to-all-done.5 = f32[64,1,2048]{2,1,0:T(1,128)S(1)} async-done(((f32[64,1,2048]{2,1,0:T(1,128)}), f32[64,1,2048]{2,1,0:T(1,128)S(1)}, u32[]{:S(2)}, u32[]{:S(2)}) %all-to-all-start.5) | async-done | bytes 524320 | tf_op jit(solution)/shard_map/all_to_all | solution.py:9
  199.7 0.5 broadcast.102
  200.2 1.9 reduce.1
  202.1 0.4 reshape.167
  202.6 0.3 copy.36
  202.9 0.2 slice.13
  203.1 0.5 fusion.10
  203.6 0.1 broadcast_bitcast_fusion.1
  203.8 0.7 reshape.168
  204.4 21.9 %all_to_all.48 = f32[64,1,2048]{2,1,0:T(1,128)S(1)} all-to-all(f32[64,1,2048]{2,1,0:T(1,128)S(1)} %reshape.168), channel_id=1, replica_groups=mesh['pts'=4,'ctr'=64] {'ctr'}, dimensions={0} | all-to-all | bytes 1048576 | tf_op jit(solution)/shard_map/all_to_all | solution.py:9
  226.3 1.9 reduce.2
  228.2 0.4 reshape.169
  228.6 0.6 copy.37
  229.3 0.4 reshape.128
  229.6 2.2 fusion.7
  231.9 1.4 reshape.170
  233.4 7.1 %all-to-all-start.7 = ((f32[64,1,2048]{2,1,0:T(1,128)}), f32[64,1,2048]{2,1,0:T(1,128)S(1)}, u32[]{:S(2)}, u32[]{:S(2)}) async-start(f32[64,1,2048]{2,1,0:T(1,128)} %reshape.170), calls=%async_computation.7 | async-start | bytes 1048576 | tf_op jit(solution)/shard_map/all_to_all | solution.py:9
  240.5 14.9 %all-to-all-done.7 = f32[64,1,2048]{2,1,0:T(1,128)S(1)} async-done(((f32[64,1,2048]{2,1,0:T(1,128)}), f32[64,1,2048]{2,1,0:T(1,128)S(1)}, u32[]{:S(2)}, u32[]{:S(2)}) %all-to-all-start.7) | async-done | bytes 524320 | tf_op jit(solution)/shard_map/all_to_all | solution.py:9
  255.4 1.9 reduce.3
  257.3 0.4 reshape.171
  257.7 0.3 copy.38
  258.0 0.2 slice.15
  258.2 1.2 fusion.9
  (40 shorter events, 0.9 us)
Async XLA Ops:
  0.6 50.4 %copy-start = (bf16[4096,128]{1,0:T(8,128)(2,1)S(1)}, bf16[4096,128]{1,0:T(8,128)(2,1)}, u32[]{:S(2)}) copy-start(bf16[4096,128]{1,0:T(8,128)(2,1)} %param.16) | copy-start | bytes 3145732
  1.5 41.7 %copy-start.4 = (f32[512]{0:T(512)S(1)}, f32[512]{0:T(512)}, u32[]{:S(2)}) copy-start(f32[512]{0:T(512)} %param.14) | copy-start | bytes 6148
  2.6 40.2 %all-to-all-start = ((bf16[64,16,512]{2,1,0:T(8,128)(2,1)}), bf16[64,16,512]{2,1,0:T(8,128)(2,1)S(1)}, u32[]{:S(2)}, u32[]{:S(2)}) async-start(bf16[64,16,512]{2,1,0:T(8,128)(2,1)} %broadcast_in_dim.90), calls=%async_computation | async-start | bytes 2097152 | tf_op jit(solution)/shard_map/all_to_all | solution.py:9
  51.0 3.6 %copy-start.8 = (bf16[1024,4096]{1,0:T(8,128)(2,1)}, bf16[1024,4096]{1,0:T(8,128)(2,1)S(1)}, u32[]{:S(2)}) copy-start(bf16[1024,4096]{1,0:T(8,128)(2,1)S(1)} %exponential_convert_fusion) | copy-start | bytes 25165828
  51.1 11.4 %copy-start.6 = (f32[8]{0:T(128)S(1)}, f32[8]{0:T(128)}, u32[]{:S(2)}) copy-start(f32[8]{0:T(128)} %param.13) | copy-start | bytes 100
  51.1 11.3 %copy-start.7 = (s32[16]{0:T(128)S(1)}, s32[16]{0:T(128)}, u32[]{:S(2)}) copy-start(s32[16]{0:T(128)} %param.11) | copy-start | bytes 196
  51.1 27.5 %copy-start.5 = (f32[16,128]{1,0:T(8,128)S(1)}, f32[16,128]{1,0:T(8,128)}, u32[]{:S(2)}) copy-start(f32[16,128]{1,0:T(8,128)} %param.12) | copy-start | bytes 24580
  54.6 23.9 %all-to-all-start.1 = ((f32[64,16,128]{2,1,0:T(8,128)}), f32[64,16,128]{2,1,0:T(8,128)S(1)}, u32[]{:S(2)}, u32[]{:S(2)}) async-start(f32[64,16,128]{2,1,0:T(8,128)} %bitcast.2), calls=%async_computation.1 | async-start | bytes 1048576 | tf_op jit(solution)/shard_map/all_to_all | solution.py:31
  102.4 4.3 %copy-start.3 = (s32[4096]{0:T(1024)S(1)}, s32[4096]{0:T(1024)}, u32[]{:S(2)}) copy-start(s32[4096]{0:T(1024)} %param.17) | copy-start | bytes 49156
  102.4 31.5 %all-to-all-start.3 = ((f32[4,4096,32]{1,2,0:T(8,128)}), f32[4,4096,32]{1,2,0:T(8,128)S(1)}, u32[]{:S(2)}, u32[]{:S(2)}) async-start(f32[4,4096,32]{1,2,0:T(8,128)} %fusion.2), calls=%async_computation.3 | async-start | bytes 4194304 | tf_op jit(solution)/shard_map/all_to_all | solution.py:31
  160.6 15.2 %all-to-all-start.4 = ((f32[64,1,32]{2,1,0:T(1,128)}), f32[64,1,32]{2,1,0:T(1,128)S(1)}, u32[]{:S(2)}, u32[]{:S(2)}) async-start(f32[64,1,32]{2,1,0:T(1,128)} %bitcast.8), calls=%async_computation.4 | async-start | bytes 65536 | tf_op jit(solution)/shard_map/all_to_all | solution.py:100
  176.6 26.5 %copy-start.1 = (f32[64,2048]{1,0:T(8,128)S(1)}, f32[64,2048]{1,0:T(8,128)}, u32[]{:S(2)}) copy-start(f32[64,2048]{1,0:T(8,128)} %param.19) | copy-start | bytes 1572868
  178.1 21.6 %all-to-all-start.5 = ((f32[64,1,2048]{2,1,0:T(1,128)}), f32[64,1,2048]{2,1,0:T(1,128)S(1)}, u32[]{:S(2)}, u32[]{:S(2)}) async-start(f32[64,1,2048]{2,1,0:T(1,128)} %reshape.166), calls=%async_computation.5 | async-start | bytes 1048576 | tf_op jit(solution)/shard_map/all_to_all | solution.py:9
  231.9 26.3 %copy-start.2 = (f32[64,2048]{1,0:T(8,128)S(1)}, f32[64,2048]{1,0:T(8,128)}, u32[]{:S(2)}) copy-start(f32[64,2048]{1,0:T(8,128)} %param.19) | copy-start | bytes 1572868
  233.4 22.0 %all-to-all-start.7 = ((f32[64,1,2048]{2,1,0:T(1,128)}), f32[64,1,2048]{2,1,0:T(1,128)S(1)}, u32[]{:S(2)}, u32[]{:S(2)}) async-start(f32[64,1,2048]{2,1,0:T(1,128)} %reshape.170), calls=%async_computation.7 | async-start | bytes 1048576 | tf_op jit(solution)/shard_map/all_to_all | solution.py:9
where the time goes:
time: 261 us; the launch traced here: 259 us
  waiting for transfers between devices  103 us (39%)
  starting transfers between devices  45.3 us (17%)
  blocking collectives  39.4 us (15%)
  other arithmetic  37.4 us (14%)
  matrix products  21.3 us (8%)
  local copies, waits for them, and re-layouts  11.5 us (4%)
    all_to_all x3, waiting for transfers between devices, from_everyone(): lax.all_to_all(jnp.broadcast_to(x[None], (count, *x.shape)), axis, 0, 0,...  53.8 us
    all_to_all x2, waiting for transfers between devices, sent_and_summed(): pieces = lax.all_to_all(split_up(x, dim, count), axis, 0, 0, tiled=True)  41.1 us
    all_to_all x2, blocking collectives, from_everyone(): lax.all_to_all(jnp.broadcast_to(x[None], (count, *x.shape)), axis, 0, 0,...  39.4 us
    all_to_all x3, starting transfers between devices, from_everyone(): lax.all_to_all(jnp.broadcast_to(x[None], (count, *x.shape)), axis, 0, 0,...  26.6 us
    scatter x1, other arithmetic, body(): outgoing = outgoing.at[target_slot.reshape(-1)].set(picked, mode='drop')  24.2 us
    all_to_all x2, starting transfers between devices, sent_and_summed(): pieces = lax.all_to_all(split_up(x, dim, count), axis, 0, 0, tiled=True)  12.1 us
    all_to_all x1, waiting for transfers between devices, body(): lax.all_to_all(outgoing, 'ctr', split_axis=0, concat_axis=0, tiled=True)  8.56 us
    dot_general x1, matrix products, gaussian(): lax.dot_general(samples, anchors, (((1,), (1,)), ((), ())), preferred_ele...  7.88 us
  transfers between devices with their start and end apart: 6, of which 6 were waited for; matrix products, arithmetic and copies ran while one was open for 2% of the time, Pallas kernels for 0%

commit v1 on v0

v1 whole, which is shorter than its diff:
```python
import jax
import jax.numpy as jnp
from jax import lax
from jax.sharding import PartitionSpec as P

BF = jnp.bfloat16
F32 = jnp.float32
HI = lax.Precision.HIGHEST
LANES = 128


def gathered(x, axis):
    count = lax.axis_size(axis)
    return lax.all_to_all(jnp.broadcast_to(x[None], (count, *x.shape)), axis, 0, 0, tiled=True)


def half_norm(rows):
    return 0.5 * jnp.sum(jnp.square(rows.astype(F32)), axis=1)


def gaussian(samples, anchors, left, right):
    products = lax.dot_general(
        samples, anchors, (((1,), (1,)), ((), ())), preferred_element_type=F32
    )
    return jnp.exp(products - left[:, None] - right[None, :]).astype(BF)


def class_lookup(labels, table):
    classes = jnp.arange(table.shape[0], dtype=jnp.int32)
    return jnp.sum(jnp.where(labels[:, None] == classes[None, :], table[None, :], 0.0), axis=1)


def side_by_side(x, count):
    rows = x.shape[0] // count
    return jnp.concatenate([x[i * rows : (i + 1) * rows] for i in range(count)], axis=1)


def diagonal_sum(x, count):
    rows, cols = x.shape[0] // count, x.shape[1] // count
    total = x[:rows, :cols]
    for i in range(1, count):
        total = total + x[i * rows : (i + 1) * rows, i * cols : (i + 1) * cols]
    return total


def body(
    points,
    point_class,
    targets,
    class_weight,
    inv_scale,
    centers,
    coefficients,
    center_index,
    factor,
    panel_inverse,
):
    groups = lax.axis_size("pts")
    shards = lax.axis_size("ctr")
    shard = lax.axis_index("ctr")
    own_points, depth = points.shape
    shard_rows = centers.shape[0]
    target_count = targets.shape[1]
    target_slice = target_count // groups
    window_rows = center_index.shape[0]
    own_rows = window_rows // shards
    panel_rows = panel_inverse.shape[1]
    panel_shards = panel_rows // own_rows
    panel = shard // panel_shards
    fold = LANES // target_slice
    strip = own_rows // fold

    own_scaled = (points.astype(F32) * inv_scale[None, :]).astype(BF)
    group_rows = gathered(own_scaled, "ctr").reshape(shards * own_points, depth)

    scaled_centers = (centers.astype(F32) * inv_scale[None, :]).astype(BF)
    center_norm = half_norm(scaled_centers)

    blocks = center_index.reshape(own_rows, shards)
    order = blocks[0] // shard_rows
    here = order == shard
    local = jnp.sum(jnp.where(here[None, :], blocks - shard * shard_rows, 0), axis=1)
    choose = (local[:, None] == jnp.arange(shard_rows, dtype=jnp.int32)[None, :]).astype(BF)
    chosen = jnp.dot(choose, scaled_centers, preferred_element_type=F32).astype(BF)
    chosen_norm = half_norm(chosen)
    place = (order[:, None] == jnp.arange(shards, dtype=jnp.int32)[None, :]).astype(F32)

    halves = panel_rows // (strip * shards)
    inverse = panel_inverse.reshape(own_rows, halves, strip, shards)
    inverse_window = jnp.einsum("rhqj,js->hrsq", inverse, place, precision=HI)
    inverse_window = inverse_window.reshape(halves, own_rows, shards * strip)
    parts = []
    for i in range(fold):
        parts.append(jnp.where(panel == i // halves, inverse_window[i % halves], 0.0))
    inverse_window = jnp.concatenate(parts, axis=0)

    def folded(matrix):
        m = matrix.reshape(own_rows, panel_shards, fold, strip)
        return m.transpose(2, 0, 1, 3).reshape(fold * own_rows, panel_shards * strip)

    factor_rows = folded(factor[:, :panel_rows])
    inverse_rows = folded(panel_inverse)

    point_norm = half_norm(group_rows)
    kernel = gaussian(group_rows, scaled_centers, point_norm, center_norm)
    chosen_kernel = gaussian(group_rows, chosen, point_norm, chosen_norm)
    partial_value = jnp.dot(kernel, coefficients, preferred_element_type=F32).astype(BF)
    own_weight = class_lookup(point_class, class_weight)
    shares = lax.all_to_all(
        partial_value.reshape(shards, own_points, target_count), "ctr", 0, 0, tiled=True
    )
    predicted = jnp.sum(shares.astype(F32), axis=0)
    own_residual = (own_weight[:, None] * (predicted - targets)).astype(BF)
    residual = gathered(own_residual, "ctr").reshape(shards * own_points, target_count)

    window = lax.dot_general(
        chosen_kernel, residual, (((0,), (0,)), ((), ())), preferred_element_type=F32
    )
    pieces = jnp.stack(
        [
            side_by_side(window[:, i * target_slice : (i + 1) * target_slice], fold)
            for i in range(groups)
        ]
    )
    pieces = lax.all_to_all(pieces, "pts", 0, 0, tiled=True)
    window = jnp.sum(pieces, axis=0).astype(BF)
    window = gathered(window, "ctr").reshape(shards * strip, LANES)

    backward = lax.dot_general(
        residual, kernel, (((0,), (0,)), ((), ())), preferred_element_type=F32
    ).astype(BF)
    backward = lax.all_to_all(
        backward.reshape(groups, target_slice, shard_rows), "pts", 0, 0, tiled=True
    )
    gradient = jnp.sum(backward.astype(F32), axis=0).T

    base = diagonal_sum(jnp.dot(inverse_window, window.astype(F32), precision=HI), fold)
    first = gathered(side_by_side(base, fold).astype(BF), "ctr")
    first = first[:panel_shards].reshape(panel_shards * strip, LANES)
    update = diagonal_sum(jnp.dot(factor_rows, first.astype(F32), precision=HI), fold)
    second = gathered(side_by_side(update, fold).astype(BF), "ctr")
    second = second[panel_shards:].reshape(panel_shards * strip, LANES)
    change = diagonal_sum(jnp.dot(inverse_rows, second.astype(F32), precision=HI), fold)
    solved = base - jnp.where(panel == 1, change, 0.0)
    return (gradient, solved)


def solution(mesh):
    placed = (
        P(("pts", "ctr"), None),
        P(("pts", "ctr")),
        P(("pts", "ctr"), None),
        P(),
        P(),
        P("ctr", None),
        P("ctr", None),
        P(),
        P("ctr", None),
        P("ctr", None),
    )
    return jax.shard_map(
        body,
        mesh=mesh,
        in_specs=placed,
        out_specs=(P("ctr", "pts"), P("ctr", "pts")),
        check_vma=False,
    )
```

time: 261 us -> 190 us (0.73)
  blocking collectives: 39.4 us -> 0 us
  other arithmetic: 37.4 us -> 7.9 us
  waiting for transfers between devices: 103 us -> 73.6 us
  starting transfers between devices: 45.3 us -> 58 us
  local copies, waits for them, and re-layouts: 11.5 us -> 21.5 us
  matrix products: 21.3 us -> 26.9 us
    all_to_all x2 -> x0, blocking collectives: 39.4 us -> none  [from_everyone(): lax.all_to_all(jnp.broadcast_to(x[None], (count, *x.shape)), axis, 0, 0,...]
    all_to_all x6 -> x8, waiting for transfers between devices: 103 us -> 73.6 us  [the longest x5 44 us: gathered(): lax.all_to_all(jnp.broadcast_to(x[None], (count, *x.shape)), axis, 0, 0,...]
    scatter x1 -> x0, other arithmetic: 24.2 us -> none  [body(): outgoing = outgoing.at[target_slot.reshape(-1)].set(picked, mode='drop')]
    all_to_all x6 -> x8, starting transfers between devices: 45.3 us -> 58 us  [the longest x5 42.5 us: gathered(): lax.all_to_all(jnp.broadcast_to(x[None], (count, *x.shape)), axis, 0, 0,...]
    all_to_all x3 -> x0, other arithmetic: 5.65 us -> none  [from_everyone(): lax.all_to_all(jnp.broadcast_to(x[None], (count, *x.shape)), axis, 0, 0,...]
    dot_general x5 -> x8, matrix products: 13.4 us -> 19 us  [the longest x1 5.79 us: body(): lax.dot_general(residual, kernel, (((0,), (0,)), ((), ())), preferred_ele...]
    select_n x0 -> x4, local copies, waits for them, and re-layouts: none -> 4.47 us  [body(): jnp.where(panel == i // halves, inverse_window[i % halves], 0.0)]
    broadcast_in_dim x2 -> x5, local copies, waits for them, and re-layouts: 1.16 us -> 4.12 us  [gathered(): jnp.broadcast_to(x[None], (count, *x.shape))]
  transfers between devices with their start and end apart: 6 -> 8, of which waited for: 6 -> 8; matrix products, arithmetic and copies ran while one was open for 2% -> 16% of each run, Pallas kernels for 0% -> 0%
where the time goes in v1:
time: 190 us; the launch traced here: 189 us
  waiting for transfers between devices  73.6 us (39%)
  starting transfers between devices  58 us (31%)
  matrix products  26.9 us (14%)
  local copies, waits for them, and re-layouts  21.5 us (11%)
  other arithmetic  7.9 us (4%)
    all_to_all x5, waiting for transfers between devices, gathered(): lax.all_to_all(jnp.broadcast_to(x[None], (count, *x.shape)), axis, 0, 0,...  44 us
    all_to_all x5, starting transfers between devices, gathered(): lax.all_to_all(jnp.broadcast_to(x[None], (count, *x.shape)), axis, 0, 0,...  42.5 us
    all_to_all x1, waiting for transfers between devices, body(): lax.all_to_all(backward.reshape(groups, target_slice, shard_rows), 'pts',...  14.1 us
    all_to_all x1, waiting for transfers between devices, body(): lax.all_to_all(partial_value.reshape(shards, own_points, target_count), '...  10.5 us
    dot_general x1, matrix products, gaussian(): lax.dot_general(samples, anchors, (((1,), (1,)), ((), ())), preferred_ele...  7.88 us
    all_to_all x1, starting transfers between devices, body(): lax.all_to_all(partial_value.reshape(shards, own_points, target_count), '...  7.8 us
    dot_general x1, matrix products, body(): lax.dot_general(residual, kernel, (((0,), (0,)), ((), ())), preferred_ele...  5.79 us
    unnamed x24, local copies, waits for them, and re-layouts  5.62 us
  transfers between devices with their start and end apart: 8, of which 8 were waited for; matrix products, arithmetic and copies ran while one was open for 16% of the time, Pallas kernels for 0%

profile of v1, /device:TPU:4, one launch (start us, length us, event | category | flops | bytes accessed | tf_op | source)
XLA Modules:
  0.0 188.8 jit_solution(8083198834845378807)
XLA Ops:
  0.7 0.8 multiply_convert_fusion.5
  1.5 1.1 broadcast_in_dim.46
  2.6 13.1 %all-to-all-start = ((bf16[64,16,512]{2,1,0:T(8,128)(2,1)}), bf16[64,16,512]{2,1,0:T(8,128)(2,1)S(1)}, u32[]{:S(2)}, u32[]{:S(2)}) async-start(bf16[64,16,512]{2,1,0:T(8,128)(2,1)} %broadcast_in_dim.46), calls=%async_computation | async-start | bytes 2097152 | tf_op jit(solution)/shard_map/all_to_all | solution.py:14
  15.7 3.4 %multiply_reduce_fusion = f32[4096]{0:T(1024)S(1)} fusion(f32[512]{0:T(512)} %param.14, bf16[4096,512]{1,0:T(8,128)(2,1)} %param.15), kind=kLoop, calls=%fused_computation.1 | loop fusion | flops 12578816 | bytes 4212736 | tf_op jit(solution)/shard_map/reduce_sum | solution.py:18
  19.1 23.7 %all-to-all-done = bf16[64,16,512]{2,1,0:T(8,128)(2,1)S(1)} async-done(((bf16[64,16,512]{2,1,0:T(8,128)(2,1)}), bf16[64,16,512]{2,1,0:T(8,128)(2,1)S(1)}, u32[]{:S(2)}, u32[]{:S(2)}) %all-to-all-start) | async-done | bytes 1048608 | tf_op jit(solution)/shard_map/all_to_all | solution.py:14
  43.1 7.9 %exponential_convert_fusion = bf16[1024,4096]{1,0:T(8,128)(2,1)S(1)} fusion(f32[4096]{0:T(1024)S(1)} %broadcast_multiply_fusion.1, f32[1024]{0:T(1024)S(1)} %mul.67, bf16[1024,512]{1,0:T(8,128)(2,1)S(1)} %bitcast.54, bf16[4096,512]{1,0:T(8,128)(2,1)} %param.15, f32[512]{0:T(512)S(1)} %copy-done.7), kind=kOutput, calls=%fused_computation | convolution fusion | flops 4313841664 | bytes 13654016 | tf_op jit(solution)/shard_map/dot_general | solution.py:22
  51.0 3.2 %copy-done.1 = bf16[1024,4096]{1,0:T(8,128)(2,1)} copy-done((bf16[1024,4096]{1,0:T(8,128)(2,1)}, bf16[1024,4096]{1,0:T(8,128)(2,1)S(1)}, u32[]{:S(2)}) %copy-start.1) | copy-done | bytes 8388632
  54.3 3.0 %convolution_convert_fusion.1 = bf16[1024,128]{1,0:T(8,128)(2,1)} fusion(bf16[1024,4096]{1,0:T(8,128)(2,1)S(1)} %exponential_convert_fusion, bf16[4096,128]{1,0:T(8,128)(2,1)S(1)} %copy-done), kind=kOutput, calls=%fused_computation.8 | convolution fusion | flops 1073872896 | bytes 9699328 | tf_op jit(solution)/shard_map/dot_general | solution.py:107
  57.3 7.8 %all-to-all-start.1 = ((bf16[64,16,128]{2,1,0:T(8,128)(2,1)}), bf16[64,16,128]{2,1,0:T(8,128)(2,1)S(1)}, u32[]{:S(2)}, u32[]{:S(2)}) async-start(bf16[64,16,128]{2,1,0:T(8,128)(2,1)} %bitcast.1), calls=%async_computation.1 | async-start | bytes 524288 | tf_op jit(solution)/shard_map/all_to_all | solution.py:109
  65.5 10.5 %all-to-all-done.1 = bf16[64,16,128]{2,1,0:T(8,128)(2,1)S(1)} async-done(((bf16[64,16,128]{2,1,0:T(8,128)(2,1)}), bf16[64,16,128]{2,1,0:T(8,128)(2,1)S(1)}, u32[]{:S(2)}, u32[]{:S(2)}) %all-to-all-start.1) | async-done | bytes 262176 | tf_op jit(solution)/shard_map/all_to_all | solution.py:109
  76.2 0.7 broadcast_in_dim.47
  76.9 6.8 %all-to-all-start.2 = ((bf16[64,16,128]{2,1,0:T(8,128)(2,1)}), bf16[64,16,128]{2,1,0:T(8,128)(2,1)S(1)}, u32[]{:S(2)}, u32[]{:S(2)}) async-start(bf16[64,16,128]{2,1,0:T(8,128)(2,1)} %broadcast_in_dim.47), calls=%async_computation.2 | async-start | bytes 524288 | tf_op jit(solution)/shard_map/all_to_all | solution.py:14
  83.7 3.3 %multiply_reduce_fusion.2 = (f32[64]{0:T(128)S(1)}, bf16[64,512]{1,0:T(8,128)(2,1)S(1)}) fusion(bf16[4096,512]{1,0:T(8,128)(2,1)} %param.15, f32[512]{0:T(512)S(1)} %copy-done.7, s32[64]{0:T(128)S(1)} %select_reduce_fusion), kind=kOutput, calls=%fused_computation.34 | convolution fusion | flops 275120064 | bytes 4262400 | tf_op jit(solution)/shard_map/dot_general | solution.py:84
  87.0 7.2 %all-to-all-done.2 = bf16[64,16,128]{2,1,0:T(8,128)(2,1)S(1)} async-done(((bf16[64,16,128]{2,1,0:T(8,128)(2,1)}), bf16[64,16,128]{2,1,0:T(8,128)(2,1)S(1)}, u32[]{:S(2)}, u32[]{:S(2)}) %all-to-all-start.2) | async-done | bytes 262176 | tf_op jit(solution)/shard_map/all_to_all | solution.py:14
  94.2 0.6 fusion.4
  95.1 0.6 pad_maximum_fusion
  95.7 4.2 %all-to-all-start.4 = ((f32[4,16,128]{2,1,0:T(8,128)}), f32[4,16,128]{2,1,0:T(8,128)S(1)}, u32[]{:S(2)}, u32[]{:S(2)}) async-start(f32[4,16,128]{2,1,0:T(8,128)} %pad_maximum_fusion), calls=%async_computation.4 | async-start | bytes 65536 | tf_op jit(solution)/shard_map/all_to_all | solution.py:125
  99.9 0.4 reshape.151
  100.3 5.0 %all-to-all-done.4 = f32[4,16,128]{2,1,0:T(8,128)S(1)} async-done(((f32[4,16,128]{2,1,0:T(8,128)}), f32[4,16,128]{2,1,0:T(8,128)S(1)}, u32[]{:S(2)}, u32[]{:S(2)}) %all-to-all-start.4) | async-done | bytes 32800 | tf_op jit(solution)/shard_map/all_to_all | solution.py:125
  105.3 0.8 broadcast_in_dim.51
  106.1 6.8 %all-to-all-start.5 = ((bf16[64,16,128]{2,1,0:T(8,128)(2,1)}), bf16[64,16,128]{2,1,0:T(8,128)(2,1)}, u32[]{:S(2)}, u32[]{:S(2)}) async-start(bf16[64,16,128]{2,1,0:T(8,128)(2,1)} %broadcast_in_dim.51), calls=%async_computation.5 | async-start | bytes 524288 | tf_op jit(solution)/shard_map/all_to_all | solution.py:14
  112.9 2.0 %convolution_bitcast_fusion = f32[2,64,64,16]{1,2,3,0:T(8,128)S(1)} fusion(f32[64,2,16,64]{3,2,1,0:T(8,128)S(1)} %reshape.151, s32[64]{0:T(128)S(1)} %get-tuple-element.5), kind=kOutput, calls=%fused_computation.7 | convolution fusion | flops 100667392 | bytes 1048832 | tf_op jit(solution)/shard_map/rhqj,js->hrsq/dot_general | solution.py:90
  115.2 1.1 copy.47
  116.3 1.1 copy.46
  117.4 1.1 copy.45
  118.6 1.1 copy.44
  120.0 0.4 copy.53
  120.5 1.4 reshape.155
  121.9 2.3 %all-to-all-done.5 = bf16[64,16,128]{2,1,0:T(8,128)(2,1)} async-done(((bf16[64,16,128]{2,1,0:T(8,128)(2,1)}), bf16[64,16,128]{2,1,0:T(8,128)(2,1)}, u32[]{:S(2)}, u32[]{:S(2)}) %all-to-all-start.5) | async-done | bytes 262176 | tf_op jit(solution)/shard_map/all_to_all | solution.py:14
  124.2 2.5 %fusion.6 = f32[256,128]{0,1:T(8,128)S(1)} fusion(bf16[1024,128]{1,0:T(8,128)(2,1)} %bitcast.16, f32[64,1024]{0,1:T(8,128)} %bitcast.60, f32[64,1024]{0,1:T(8,128)} %bitcast.61, f32[64,1024]{0,1:T(8,128)} %bitcast.62, f32[64,1024]{0,1:T(8,128)} %bitcast.63), kind=kOutput, calls=%fused_computation.17 | convolution fusion | flops 403439616 | bytes 1441792 | tf_op jit(solution)/shard_map/dot_general | solution.py:137
  127.3 0.8 broadcast_in_dim.52
  128.0 9.0 %all-to-all-start.6 = ((bf16[64,16,128]{2,1,0:T(8,128)(2,1)}), bf16[64,16,128]{2,1,0:T(8,128)(2,1)S(1)}, u32[]{:S(2)}, u32[]{:S(2)}) async-start(bf16[64,16,128]{2,1,0:T(8,128)(2,1)} %broadcast_in_dim.52), calls=%async_computation.6 | async-start | bytes 524288 | tf_op jit(solution)/shard_map/all_to_all | solution.py:14
  137.1 5.8 %convolution_convert_fusion = bf16[128,4096]{1,0:T(8,128)(2,1)} fusion(bf16[1024,128]{1,0:T(8,128)(2,1)S(1)} %bitcast.59, bf16[1024,4096]{1,0:T(8,128)(2,1)} %copy-done.1), kind=kOutput, calls=%fused_computation.3 | convolution fusion | flops 1074266112 | bytes 9699328 | tf_op jit(solution)/shard_map/dot_general | solution.py:129
  142.9 5.0 %all-to-all-done.6 = bf16[64,16,128]{2,1,0:T(8,128)(2,1)S(1)} async-done(((bf16[64,16,128]{2,1,0:T(8,128)(2,1)}), bf16[64,16,128]{2,1,0:T(8,128)(2,1)S(1)}, u32[]{:S(2)}, u32[]{:S(2)}) %all-to-all-start.6) | async-done | bytes 262176 | tf_op jit(solution)/shard_map/all_to_all | solution.py:14
  147.9 0.7 copy-done.5
  148.6 3.5 %all-to-all-start.3 = ((bf16[4,32,4096]{2,1,0:T(8,128)(2,1)}), bf16[4,32,4096]{2,1,0:T(8,128)(2,1)S(1)}, u32[]{:S(2)}, u32[]{:S(2)}) async-start(bf16[4,32,4096]{2,1,0:T(8,128)(2,1)} %bitcast.3), calls=%async_computation.3 | async-start | bytes 2097152 | tf_op jit(solution)/shard_map/all_to_all | solution.py:132
  152.1 0.9 slice.227
  153.0 0.3 convolution_bitcast_fusion.2
  154.0 14.1 %all-to-all-done.3 = bf16[4,32,4096]{2,1,0:T(8,128)(2,1)S(1)} async-done(((bf16[4,32,4096]{2,1,0:T(8,128)(2,1)}), bf16[4,32,4096]{2,1,0:T(8,128)(2,1)S(1)}, u32[]{:S(2)}, u32[]{:S(2)}) %all-to-all-start.3) | async-done | bytes 1048608 | tf_op jit(solution)/shard_map/all_to_all | solution.py:132
  168.0 0.8 broadcast_in_dim.53
  168.8 6.8 %all-to-all-start.7 = ((bf16[64,16,128]{2,1,0:T(8,128)(2,1)}), bf16[64,16,128]{2,1,0:T(8,128)(2,1)S(1)}, u32[]{:S(2)}, u32[]{:S(2)}) async-start(bf16[64,16,128]{2,1,0:T(8,128)(2,1)} %broadcast_in_dim.53), calls=%async_computation.7 | async-start | bytes 524288 | tf_op jit(solution)/shard_map/all_to_all | solution.py:14
  175.6 1.3 copy.58
  176.9 1.6 copy.59
  178.6 1.4 reshape.158
  180.0 0.9 convert_reduce_fusion
  180.9 5.8 %all-to-all-done.7 = bf16[64,16,128]{2,1,0:T(8,128)(2,1)S(1)} async-done(((bf16[64,16,128]{2,1,0:T(8,128)(2,1)}), bf16[64,16,128]{2,1,0:T(8,128)(2,1)S(1)}, u32[]{:S(2)}, u32[]{:S(2)}) %all-to-all-start.7) | async-done | bytes 262176 | tf_op jit(solution)/shard_map/all_to_all | solution.py:14
  186.7 1.4 convolution_bitcast_fusion.1
  188.1 0.7 fusion.21
  (55 shorter events, 2.9 us)
Async XLA Ops:
  0.6 53.6 %copy-start = (bf16[4096,128]{1,0:T(8,128)(2,1)S(1)}, bf16[4096,128]{1,0:T(8,128)(2,1)}, u32[]{:S(2)}) copy-start(bf16[4096,128]{1,0:T(8,128)(2,1)} %param.16) | copy-start | bytes 3145732
  0.6 42.5 %copy-start.7 = (f32[512]{0:T(512)S(1)}, f32[512]{0:T(512)}, u32[]{:S(2)}) copy-start(f32[512]{0:T(512)} %param.14) | copy-start | bytes 6148
  2.6 40.2 %all-to-all-start = ((bf16[64,16,512]{2,1,0:T(8,128)(2,1)}), bf16[64,16,512]{2,1,0:T(8,128)(2,1)S(1)}, u32[]{:S(2)}, u32[]{:S(2)}) async-start(bf16[64,16,512]{2,1,0:T(8,128)(2,1)} %broadcast_in_dim.46), calls=%async_computation | async-start | bytes 2097152 | tf_op jit(solution)/shard_map/all_to_all | solution.py:14
  51.0 3.2 %copy-start.1 = (bf16[1024,4096]{1,0:T(8,128)(2,1)}, bf16[1024,4096]{1,0:T(8,128)(2,1)S(1)}, u32[]{:S(2)}) copy-start(bf16[1024,4096]{1,0:T(8,128)(2,1)S(1)} %exponential_convert_fusion) | copy-start | bytes 25165828
  54.3 10.9 %copy-start.6 = (s32[4096]{0:T(1024)S(1)}, s32[4096]{0:T(1024)}, u32[]{:S(2)}) copy-start(s32[4096]{0:T(1024)} %param.17) | copy-start | bytes 49156
  54.3 11.1 %copy-start.9 = (f32[8]{0:T(128)S(1)}, f32[8]{0:T(128)}, u32[]{:S(2)}) copy-start(f32[8]{0:T(128)} %param.13) | copy-start | bytes 100
  54.3 11.1 %copy-start.10 = (s32[16]{0:T(128)S(1)}, s32[16]{0:T(128)}, u32[]{:S(2)}) copy-start(s32[16]{0:T(128)} %param.11) | copy-start | bytes 196
  54.3 21.8 %copy-start.8 = (f32[16,128]{1,0:T(8,128)S(1)}, f32[16,128]{1,0:T(8,128)}, u32[]{:S(2)}) copy-start(f32[16,128]{1,0:T(8,128)} %param.12) | copy-start | bytes 24580
  54.3 45.6 %copy-start.2 = (f32[64,2048]{1,0:T(8,128)S(1)}, f32[64,2048]{1,0:T(8,128)}, u32[]{:S(2)}) copy-start(f32[64,2048]{1,0:T(8,128)} %param.19) | copy-start | bytes 1572868
  57.3 18.7 %all-to-all-start.1 = ((bf16[64,16,128]{2,1,0:T(8,128)(2,1)}), bf16[64,16,128]{2,1,0:T(8,128)(2,1)S(1)}, u32[]{:S(2)}, u32[]{:S(2)}) async-start(bf16[64,16,128]{2,1,0:T(8,128)(2,1)} %bitcast.1), calls=%async_computation.1 | async-start | bytes 524288 | tf_op jit(solution)/shard_map/all_to_all | solution.py:109
  76.9 17.3 %all-to-all-start.2 = ((bf16[64,16,128]{2,1,0:T(8,128)(2,1)}), bf16[64,16,128]{2,1,0:T(8,128)(2,1)S(1)}, u32[]{:S(2)}, u32[]{:S(2)}) async-start(bf16[64,16,128]{2,1,0:T(8,128)(2,1)} %broadcast_in_dim.47), calls=%async_computation.2 | async-start | bytes 524288 | tf_op jit(solution)/shard_map/all_to_all | solution.py:14
  87.0 32.7 %slice-start = ((f32[64,4096]{1,0:T(8,128)}), f32[64,2048]{1,0:T(8,128)S(1)}, s32[]{:S(2)}) async-start(f32[64,4096]{1,0:T(8,128)} %param.18), calls=%async_computation.8 | async-start | bytes 1048576 | tf_op jit(solution)/shard_map/slice | solution.py:101
  95.7 9.6 %all-to-all-start.4 = ((f32[4,16,128]{2,1,0:T(8,128)}), f32[4,16,128]{2,1,0:T(8,128)S(1)}, u32[]{:S(2)}, u32[]{:S(2)}) async-start(f32[4,16,128]{2,1,0:T(8,128)} %pad_maximum_fusion), calls=%async_computation.4 | async-start | bytes 65536 | tf_op jit(solution)/shard_map/all_to_all | solution.py:125
  106.1 18.1 %all-to-all-start.5 = ((bf16[64,16,128]{2,1,0:T(8,128)(2,1)}), bf16[64,16,128]{2,1,0:T(8,128)(2,1)}, u32[]{:S(2)}, u32[]{:S(2)}) async-start(bf16[64,16,128]{2,1,0:T(8,128)(2,1)} %broadcast_in_dim.51), calls=%async_computation.5 | async-start | bytes 524288 | tf_op jit(solution)/shard_map/all_to_all | solution.py:14
  128.0 25.0 %copy-start.4 = (f32[256,512]{0,1:T(8,128)S(1)}, f32[256,512]{0,1:T(8,128)}, u32[]{:S(2)}) copy-start(f32[256,512]{0,1:T(8,128)} %reshape.155) | copy-start | bytes 1572868
  128.0 19.9 %all-to-all-start.6 = ((bf16[64,16,128]{2,1,0:T(8,128)(2,1)}), bf16[64,16,128]{2,1,0:T(8,128)(2,1)S(1)}, u32[]{:S(2)}, u32[]{:S(2)}) async-start(bf16[64,16,128]{2,1,0:T(8,128)(2,1)} %broadcast_in_dim.52), calls=%async_computation.6 | async-start | bytes 524288 | tf_op jit(solution)/shard_map/all_to_all | solution.py:14
  137.1 38.5 %copy-start.3 = (f32[64,2048]{1,0:T(8,128)S(1)}, f32[64,2048]{1,0:T(8,128)}, u32[]{:S(2)}) copy-start(f32[64,2048]{1,0:T(8,128)} %param.19) | copy-start | bytes 1572868
  147.9 0.7 copy-start.5
  148.6 19.5 %all-to-all-start.3 = ((bf16[4,32,4096]{2,1,0:T(8,128)(2,1)}), bf16[4,32,4096]{2,1,0:T(8,128)(2,1)S(1)}, u32[]{:S(2)}, u32[]{:S(2)}) async-start(bf16[4,32,4096]{2,1,0:T(8,128)(2,1)} %bitcast.3), calls=%async_computation.3 | async-start | bytes 2097152 | tf_op jit(solution)/shard_map/all_to_all | solution.py:132
  168.8 17.9 %all-to-all-start.7 = ((bf16[64,16,128]{2,1,0:T(8,128)(2,1)}), bf16[64,16,128]{2,1,0:T(8,128)(2,1)S(1)}, u32[]{:S(2)}, u32[]{:S(2)}) async-start(bf16[64,16,128]{2,1,0:T(8,128)(2,1)} %broadcast_in_dim.53), calls=%async_computation.7 | async-start | bytes 524288 | tf_op jit(solution)/shard_map/all_to_all | solution.py:14

commit v2 on v1

--- a/solution.py
+++ b/solution.py
@@ -1,6 +1,8 @@
 import jax
 import jax.numpy as jnp
 from jax import lax
+from jax.experimental import pallas as pl
+from jax.experimental.pallas import tpu as pltpu
 from jax.sharding import PartitionSpec as P
 
 BF = jnp.bfloat16
@@ -9,9 +11,68 @@
 LANES = 128
 
 
+PLANES = 4
+TILE = 512
+
+
 def gathered(x, axis):
     count = lax.axis_size(axis)
     return lax.all_to_all(jnp.broadcast_to(x[None], (count, *x.shape)), axis, 0, 0, tiled=True)
+
+
+def plane_groups(axis):
+    size = lax.axis_size(axis) // PLANES
+    return [[plane * size + i for i in range(size)] for plane in range(PLANES)]
+
+
+def plane_exchange(pieces, axis):
+    groups = plane_groups(axis)
+    return lax.all_to_all(pieces, axis, 0, 0, tiled=True, axis_index_groups=groups)
+
+
+def plane_gathered(x, axis):
+    size = lax.axis_size(axis) // PLANES
+    return plane_exchange(jnp.broadcast_to(x[None], (size, *x.shape)), axis)
+
+
+def swapped(x, axis, bits):
+    return lax.ppermute(x, axis, [(i, i ^ bits) for i in range(lax.axis_size(axis))])
+
+
+def kernel_block(points_ref, centers_ref, norm_ref, coef_ref, kernel_ref, value_ref):
+    samples = points_ref[...]
+    wide = samples.astype(F32)
+    left = 0.5 * jnp.sum(wide * wide, axis=1, keepdims=True)
+    total = jnp.zeros(value_ref.shape, F32)
+    for i in range(centers_ref.shape[0] // TILE):
+        rows = pl.ds(i * TILE, TILE)
+        products = lax.dot_general(
+            samples, centers_ref[rows, :], (((1,), (1,)), ((), ())), preferred_element_type=F32
+        )
+        block = jnp.exp(products - left - norm_ref[:, rows]).astype(BF)
+        kernel_ref[:, rows] = block
+        total += jnp.dot(block, coef_ref[rows, :], preferred_element_type=F32)
+    value_ref[...] = total.astype(value_ref.dtype)
+
+
+def kernel_and_value(samples, anchors, norms, coefficients):
+    count, depth = samples.shape
+    total, cols = coefficients.shape
+    return pl.pallas_call(
+        kernel_block,
+        out_shape=(
+            jax.ShapeDtypeStruct((count, total), BF),
+            jax.ShapeDtypeStruct((count, cols), BF),
+        ),
+        in_specs=[pl.BlockSpec(memory_space=pltpu.VMEM)] * 4,
+        out_specs=[pl.BlockSpec(memory_space=pltpu.VMEM)] * 2,
+        compiler_params=pltpu.CompilerParams(vmem_limit_bytes=16 * 1024 * 1024),
+        cost_estimate=pl.CostEstimate(
+            flops=2 * count * total * (depth + cols),
+            bytes_accessed=2 * (count * depth + total * depth + total * cols + count * total),
+            transcendentals=count * total,
+        ),
+    )(samples, anchors, norms, coefficients)
 
 
 def half_norm(rows):
@@ -70,8 +131,18 @@
     fold = LANES // target_slice
     strip = own_rows // fold
 
+    plane_bits = [shards // PLANES * k for k in range(PLANES)]
+    plane_points = shards // PLANES * own_points
+
     own_scaled = (points.astype(F32) * inv_scale[None, :]).astype(BF)
-    group_rows = gathered(own_scaled, "ctr").reshape(shards * own_points, depth)
+    plane_rows = plane_gathered(own_scaled, "ctr").reshape(plane_points, depth)
+    far = swapped(plane_rows, "ctr", plane_bits[2])
+    chunks = [
+        plane_rows,
+        swapped(plane_rows, "ctr", plane_bits[1]),
+        far,
+        swapped(plane_rows, "ctr", plane_bits[3]),
+    ]
 
     scaled_centers = (centers.astype(F32) * inv_scale[None, :]).astype(BF)
     center_norm = half_norm(scaled_centers)
@@ -101,21 +172,33 @@
     factor_rows = folded(factor[:, :panel_rows])
     inverse_rows = folded(panel_inverse)
 
-    point_norm = half_norm(group_rows)
-    kernel = gaussian(group_rows, scaled_centers, point_norm, center_norm)
-    chosen_kernel = gaussian(group_rows, chosen, point_norm, chosen_norm)
-    partial_value = jnp.dot(kernel, coefficients, preferred_element_type=F32).astype(BF)
+    kernels = [None] * PLANES
+    arrived = None
+    for k in (0, 1, 3, 2):
+        kernels[k], value = kernel_and_value(
+            chunks[k], scaled_centers, center_norm[None, :], coefficients
+        )
+        value = value if k == 0 else swapped(value, "ctr", plane_bits[k])
+        value = value.astype(F32)
+        arrived = value if arrived is None else arrived + value
     own_weight = class_lookup(point_class, class_weight)
-    shares = lax.all_to_all(
-        partial_value.reshape(shards, own_points, target_count), "ctr", 0, 0, tiled=True
+    shares = plane_exchange(
+        arrived.astype(BF).reshape(shards // PLANES, own_points, target_count), "ctr"
     )
     predicted = jnp.sum(shares.astype(F32), axis=0)
     own_residual = (own_weight[:, None] * (predicted - targets)).astype(BF)
-    residual = gathered(own_residual, "ctr").reshape(shards * own_points, target_count)
-
-    window = lax.dot_general(
-        chosen_kernel, residual, (((0,), (0,)), ((), ())), preferred_element_type=F32
-    )
+    plane_residual = plane_gathered(own_residual, "ctr").reshape(plane_points, target_count)
+    residuals = [plane_residual] + [
+        swapped(plane_residual, "ctr", plane_bits[k]) for k in range(1, PLANES)
+    ]
+
+    window = None
+    for k in range(PLANES):
+        chosen_kernel = gaussian(chunks[k], chosen, half_norm(chunks[k]), chosen_norm)
+        part = lax.dot_general(
+            chosen_kernel, residuals[k], (((0,), (0,)), ((), ())), preferred_element_type=F32
+        )
+        window = part if window is None else window + part
     pieces = jnp.stack(
         [
             side_by_side(window[:, i * target_slice : (i + 1) * target_slice], fold)
@@ -126,13 +209,20 @@
     window = jnp.sum(pieces, axis=0).astype(BF)
     window = gathered(window, "ctr").reshape(shards * strip, LANES)
 
-    backward = lax.dot_general(
-        residual, kernel, (((0,), (0,)), ((), ())), preferred_element_type=F32
-    ).astype(BF)
-    backward = lax.all_to_all(
-        backward.reshape(groups, target_slice, shard_rows), "pts", 0, 0, tiled=True
-    )
-    gradient = jnp.sum(backward.astype(F32), axis=0).T
+    backward = None
+    for k in range(PLANES):
+        part = lax.dot_general(
+            residuals[k], kernels[k], (((0,), (0,)), ((), ())), preferred_element_type=F32
+        )
+        backward = part if backward is None else backward + part
+    backward = backward.reshape(groups, target_slice, shard_rows)
+    group = lax.axis_index("pts")
+    gradient = lax.dynamic_index_in_dim(backward, group, 0, keepdims=False)
+    backward = backward.astype(BF)
+    for k in range(1, groups):
+        piece = lax.dynamic_index_in_dim(backward, group ^ k, 0, keepdims=False)
+        gradient = gradient + swapped(piece, "pts", k).astype(F32)
+    gradient = gradient.T
 
     base = diagonal_sum(jnp.dot(inverse_window, window.astype(F32), precision=HI), fold)
     first = gathered(side_by_side(base, fold).astype(BF), "ctr")

time: 190 us -> 184 us (0.968)
  waiting for transfers between devices: 73.6 us -> 45.4 us
  local copies, waits for them, and re-layouts: 21.5 us -> 31.9 us
  Pallas kernels: 0 us -> 10.3 us
  matrix products: 26.9 us -> 19.5 us
  other arithmetic: 7.9 us -> 12.9 us
  starting transfers between devices: 58 us -> 61.9 us
    all_to_all x5 -> x3, waiting for transfers between devices: 44 us -> 18.8 us  [gathered(): lax.all_to_all(jnp.broadcast_to(x[None], (count, *x.shape)), axis, 0, 0,...]
    all_to_all x5 -> x3, starting transfers between devices: 42.5 us -> 20.6 us  [gathered(): lax.all_to_all(jnp.broadcast_to(x[None], (count, *x.shape)), axis, 0, 0,...]
    ppermute x0 -> x12, starting transfers between devices: none -> 16 us  [swapped(): lax.ppermute(x, axis, [(i, i ^ bits) for i in range(lax.axis_size(axis))])]
    pallas_call x0 -> x4, Pallas kernels: none -> 10.3 us  [kernel_and_value(): pl.pallas_call(kernel_block, out_shape=(jax.ShapeDtypeStruct((count, tota...]
    all_to_all x2 -> x3, starting transfers between devices: 11.3 us -> 21.2 us  [plane_exchange(): lax.all_to_all(pieces, axis, 0, 0, tiled=True, axis_index_groups=groups)]
    unnamed x24 -> x44, local copies, waits for them, and re-layouts: 5.62 us -> 12.7 us
    ppermute x0 -> x12, waiting for transfers between devices: none -> 6.69 us  [swapped(): lax.ppermute(x, axis, [(i, i ^ bits) for i in range(lax.axis_size(axis))])]
    all_to_all x2 -> x3, waiting for transfers between devices: 24.6 us -> 18 us  [plane_exchange(): lax.all_to_all(pieces, axis, 0, 0, tiled=True, axis_index_groups=groups)]
  transfers between devices with their start and end apart: 8 -> 19, of which waited for: 8 -> 9; matrix products, arithmetic and copies ran while one was open for 16% -> 23% of each run, Pallas kernels for 0% -> 6%
where the time goes in v2:
time: 184 us; the launch traced here: 183 us
  starting transfers between devices  61.9 us (34%)
  waiting for transfers between devices  45.4 us (25%)
  local copies, waits for them, and re-layouts  31.9 us (17%)
  matrix products  19.5 us (11%)
  other arithmetic  12.9 us (7%)
  Pallas kernels  10.3 us (6%)
    all_to_all x3, starting transfers between devices, plane_exchange(): lax.all_to_all(pieces, axis, 0, 0, tiled=True, axis_index_groups=groups)  21.2 us
    all_to_all x3, starting transfers between devices, gathered(): lax.all_to_all(jnp.broadcast_to(x[None], (count, *x.shape)), axis, 0, 0,...  20.6 us
    all_to_all x3, waiting for transfers between devices, gathered(): lax.all_to_all(jnp.broadcast_to(x[None], (count, *x.shape)), axis, 0, 0,...  18.8 us
    all_to_all x3, waiting for transfers between devices, plane_exchange(): lax.all_to_all(pieces, axis, 0, 0, tiled=True, axis_index_groups=groups)  18 us
    ppermute x12, starting transfers between devices, swapped(): lax.ppermute(x, axis, [(i, i ^ bits) for i in range(lax.axis_size(axis))])  16 us
    unnamed x44, local copies, waits for them, and re-layouts  12.7 us
    pallas_call x4, Pallas kernels, kernel_and_value(): pl.pallas_call(kernel_block, out_shape=(jax.ShapeDtypeStruct((count, tota...  10.3 us
    dot_general x4, matrix products, body(): lax.dot_general(residuals[k], kernels[k], (((0,), (0,)), ((), ())), prefe...  10 us
  transfers between devices with their start and end apart: 19, of which 9 were waited for; matrix products, arithmetic and copies ran while one was open for 23% of the time, Pallas kernels for 6%

profile of v2, /device:TPU:4, one launch (start us, length us, event | category | flops | bytes accessed | tf_op | source)
XLA Modules:
  0.0 183.0 jit_solution(1677012275075909723)
XLA Ops:
  2.1 9.6 %all-to-all-start = ((bf16[16,16,512]{2,1,0:T(8,128)(2,1)}), bf16[16,16,512]{2,1,0:T(8,128)(2,1)S(1)}, u32[]{:S(2)}, u32[]{:S(2)}) async-start(bf16[16,16,512]{2,1,0:T(8,128)(2,1)} %broadcast_in_dim.46), calls=%async_computation | async-start | bytes 524288 | tf_op jit(solution)/shard_map/all_to_all | solution.py:30
  11.7 5.4 %multiply_reduce_fusion = (f32[4096]{0:T(1024)S(1)}, bf16[4096,512]{1,0:T(8,128)(2,1)}) fusion(f32[512]{0:T(512)} %param.14, bf16[4096,512]{1,0:T(8,128)(2,1)} %param.15), kind=kLoop, calls=%fused_computation | loop fusion | flops 12578816 | bytes 8407040 | tf_op jit(solution)/shard_map/reduce_sum | solution.py:79
  17.8 3.2 %multiply_reduce_fusion.5 = (f32[64]{0:T(128)S(1)}, bf16[64,512]{1,0:T(8,128)(2,1)S(1)}) fusion(bf16[4096,512]{1,0:T(8,128)(2,1)} %get-tuple-element.23.centers_ref, s32[64]{0:T(128)S(1)} %select_reduce_fusion), kind=kOutput, calls=%fused_computation.56 | convolution fusion | flops 268828608 | bytes 4260352 | tf_op jit(solution)/shard_map/dot_general | solution.py:155
  21.0 2.0 %convolution_bitcast_fusion = f32[2,64,64,16]{1,2,3,0:T(8,128)S(1)} fusion(f32[64,2,16,64]{3,2,1,0:T(8,128)S(1)} %reshape.166, s32[64]{0:T(128)S(1)} %get-tuple-element.21), kind=kOutput, calls=%fused_computation.5 | convolution fusion | flops 100667392 | bytes 1048832 | tf_op jit(solution)/shard_map/rhqj,js->hrsq/dot_general | solution.py:161
  24.8 2.1 %copy.44 = f32[1,64,64,16]{1,3,2,0:T(8,128)} copy(f32[1,64,64,16]{1,2,3,0:T(8,128)} %get-tuple-element.24) | data formatting | bytes 524288 | tf_op jit(solution)/shard_map/jit(_where)/select_n | solution.py:165
  26.9 2.2 %copy.45 = f32[1,64,64,16]{1,3,2,0:T(8,128)} copy(f32[1,64,64,16]{1,2,3,0:T(8,128)} %get-tuple-element.27) | data formatting | bytes 524288 | tf_op jit(solution)/shard_map/jit(_where)/select_n | solution.py:165
  31.7 1.5 copy.53
  33.1 2.6 %reshape.170 = f32[256,512]{0,1:T(8,128)} reshape(f32[4,64,32,16]{1,0,3,2:T(4,128)} %copy.53) | data formatting | bytes 1048576 | tf_op jit(solution)/shard_map/reshape | solution.py:170
  35.8 1.5 copy.59
  37.2 1.8 %reshape.173 = f32[256,512]{0,1:T(8,128)S(1)} reshape(f32[4,64,32,16]{1,0,3,2:T(4,128)} %copy.59) | data formatting | bytes 1048576 | tf_op jit(solution)/shard_map/reshape | solution.py:170
  39.1 1.3 collective-permute-start
  40.4 2.9 %collective-permute-start.4 = (bf16[256,512]{1,0:T(8,128)(2,1)S(1)}, bf16[256,512]{1,0:T(8,128)(2,1)S(1)}, u32[]{:S(2)}, u32[]{:S(2)}) collective-permute-start(bf16[256,512]{1,0:T(8,128)(2,1)S(1)} %bitcast.85), channel_id=1, source_target_pairs={{0,32},{1,33},{2,34},{3,35},{4,36},{5,37},{6,38},{7,39},{8,40},{9,... | collective-permute-start | bytes 786440 | tf_op jit(solution)/shard_map/ppermute | solution.py:39
  43.5 2.2 %copy-done = bf16[4096,512]{1,0:T(8,128)(2,1)S(1)} copy-done((bf16[4096,512]{1,0:T(8,128)(2,1)S(1)}, bf16[4096,512]{1,0:T(8,128)(2,1)}, u32[]{:S(2)}) %copy-start) | copy-done | bytes 4194328
  45.7 2.6 %shard_map.113 = (bf16[256,4096]{1,0:T(8,128)(2,1)S(1)}, bf16[256,128]{1,0:T(8,128)(2,1)S(1)}) custom-call(bf16[256,512]{1,0:T(8,128)(2,1)S(1)} %bitcast.86, bf16[4096,512]{1,0:T(8,128)(2,1)S(1)} %copy-done, f32[1,4096]{1,0:T(1,128)S(1)} %bitcast.88, bf16[4096,128]{1,0:T(8,128)(2,1)S(1)} %copy-done.2), custom_call_target="tpu_custom_call" | custom-call | flops 1342177280 | bytes 7602176 | tf_op jit(solution)/shard_map/pallas_call | solution.py:61
  48.3 1.4 copy-done.7
  49.7 2.2 %copy-done.1 = bf16[4096,512]{1,0:T(8,128)(2,1)S(1)} copy-done((bf16[4096,512]{1,0:T(8,128)(2,1)S(1)}, bf16[4096,512]{1,0:T(8,128)(2,1)}, u32[]{:S(2)}) %copy-start.1) | copy-done | bytes 4194328
  51.9 2.6 %shard_map.114 = (bf16[256,4096]{1,0:T(8,128)(2,1)S(1)}, bf16[256,128]{1,0:T(8,128)(2,1)S(1)}) custom-call(bf16[256,512]{1,0:T(8,128)(2,1)S(1)} %collective-permute-done.points_ref, bf16[4096,512]{1,0:T(8,128)(2,1)S(1)} %copy-done.1, f32[1,4096]{1,0:T(1,128)S(1)} %bitcast.89, bf16[4096,128]{1,0:T(8,128)(2,1)S(1)} %copy-done.2), custom_call_target="tpu_custom_call" | custom-call | flops 1342177280 | bytes 7602176 | tf_op jit(solution)/shard_map/pallas_call | solution.py:61
  54.5 1.3 copy-done.3
  57.0 2.6 %shard_map.115 = (bf16[256,4096]{1,0:T(8,128)(2,1)S(1)}, bf16[256,128]{1,0:T(8,128)(2,1)S(1)}) custom-call(bf16[256,512]{1,0:T(8,128)(2,1)S(1)} %collective-permute-done.2.points_ref, bf16[4096,512]{1,0:T(8,128)(2,1)S(1)} %copy-done.1, f32[1,4096]{1,0:T(1,128)S(1)} %bitcast.90, bf16[4096,128]{1,0:T(8,128)(2,1)S(1)} %copy-done.2), custom_call_target="tpu_custom_call" | custom-call | flops 1342177280 | bytes 7602176 | tf_op jit(solution)/shard_map/pallas_call | solution.py:61
  59.6 1.4 copy-done.5
  61.0 2.6 %shard_map.116 = (bf16[256,4096]{1,0:T(8,128)(2,1)S(1)}, bf16[256,128]{1,0:T(8,128)(2,1)S(1)}) custom-call(bf16[256,512]{1,0:T(8,128)(2,1)S(1)} %collective-permute-done.4.points_ref, bf16[4096,512]{1,0:T(8,128)(2,1)S(1)} %copy-done.1, f32[1,4096]{1,0:T(1,128)S(1)} %bitcast.91, bf16[4096,128]{1,0:T(8,128)(2,1)S(1)} %copy-done.2), custom_call_target="tpu_custom_call" | custom-call | flops 1342177280 | bytes 7602176 | tf_op jit(solution)/shard_map/pallas_call | solution.py:61
  63.6 1.3 copy-done.8
  65.0 2.9 %collective-permute-start.5 = (bf16[256,128]{1,0:T(8,128)(2,1)S(1)}, bf16[256,128]{1,0:T(8,128)(2,1)S(1)}, u32[]{:S(2)}, u32[]{:S(2)}) collective-permute-start(bf16[256,128]{1,0:T(8,128)(2,1)S(1)} %get-tuple-element.13), channel_id=1, source_target_pairs={{0,32},{1,33},{2,34},{3,35},{4,36},{5,37},{6,38},{7,39},{8,40},{9,... | collective-permute-start | bytes 196616 | tf_op jit(solution)/shard_map/ppermute | solution.py:39
  68.1 2.6 %collective-permute-done.5 = bf16[256,128]{1,0:T(8,128)(2,1)S(1)} collective-permute-done((bf16[256,128]{1,0:T(8,128)(2,1)S(1)}, bf16[256,128]{1,0:T(8,128)(2,1)S(1)}, u32[]{:S(2)}, u32[]{:S(2)}) %collective-permute-start.5) | collective-permute-done | bytes 65568 | tf_op jit(solution)/shard_map/ppermute | solution.py:39
  71.4 8.1 %all-to-all-start.1 = ((bf16[16,16,128]{2,1,0:T(8,128)(2,1)}), bf16[16,16,128]{2,1,0:T(8,128)(2,1)S(1)}, u32[]{:S(2)}, u32[]{:S(2)}) async-start(bf16[16,16,128]{2,1,0:T(8,128)(2,1)} %bitcast.2), calls=%async_computation.1 | async-start | bytes 131072 | tf_op jit(solution)/shard_map/all_to_all | solution.py:30
  79.6 8.9 %all-to-all-done.1 = bf16[16,16,128]{2,1,0:T(8,128)(2,1)S(1)} async-done(((bf16[16,16,128]{2,1,0:T(8,128)(2,1)}), bf16[16,16,128]{2,1,0:T(8,128)(2,1)S(1)}, u32[]{:S(2)}, u32[]{:S(2)}) %all-to-all-start.1) | async-done | bytes 65568 | tf_op jit(solution)/shard_map/all_to_all | solution.py:30
  89.3 3.5 %all-to-all-start.2 = ((bf16[16,16,128]{2,1,0:T(8,128)(2,1)}), bf16[16,16,128]{2,1,0:T(8,128)(2,1)S(1)}, u32[]{:S(2)}, u32[]{:S(2)}) async-start(bf16[16,16,128]{2,1,0:T(8,128)(2,1)} %broadcast_in_dim.47), calls=%async_computation.2 | async-start | bytes 131072 | tf_op jit(solution)/shard_map/all_to_all | solution.py:30
  92.8 9.0 %all-to-all-done.2 = bf16[16,16,128]{2,1,0:T(8,128)(2,1)S(1)} async-done(((bf16[16,16,128]{2,1,0:T(8,128)(2,1)}), bf16[16,16,128]{2,1,0:T(8,128)(2,1)S(1)}, u32[]{:S(2)}, u32[]{:S(2)}) %all-to-all-start.2) | async-done | bytes 65568 | tf_op jit(solution)/shard_map/all_to_all | solution.py:30
  101.9 1.9 %collective-permute-start.6 = (bf16[256,128]{1,0:T(8,128)(2,1)S(1)}, bf16[256,128]{1,0:T(8,128)(2,1)S(1)}, u32[]{:S(2)}, u32[]{:S(2)}) collective-permute-start(bf16[256,128]{1,0:T(8,128)(2,1)S(1)} %bitcast.101), channel_id=1, source_target_pairs={{0,16},{1,17},{2,18},{3,19},{4,20},{5,21},{6,22},{7,23},{8,24},{9,... | collective-permute-start | bytes 196616 | tf_op jit(solution)/shard_map/ppermute | solution.py:39
  103.8 1.5 collective-permute-start.8
  106.7 1.4 collective-permute-done.8
  108.4 2.7 %collective-permute-done.7 = bf16[256,128]{1,0:T(8,128)(2,1)S(1)} collective-permute-done((bf16[256,128]{1,0:T(8,128)(2,1)S(1)}, bf16[256,128]{1,0:T(8,128)(2,1)S(1)}, u32[]{:S(2)}, u32[]{:S(2)}) %collective-permute-start.7) | collective-permute-done | bytes 65568 | tf_op jit(solution)/shard_map/ppermute | solution.py:39
  112.3 4.2 %all-to-all-start.3 = ((f32[4,16,128]{2,1,0:T(8,128)}), f32[4,16,128]{2,1,0:T(8,128)S(1)}, u32[]{:S(2)}, u32[]{:S(2)}) async-start(f32[4,16,128]{2,1,0:T(8,128)} %pad_maximum_fusion), calls=%async_computation.3 | async-start | bytes 65536 | tf_op jit(solution)/shard_map/all_to_all | solution.py:208
  116.5 3.6 %fusion.48 = f32[128,4096]{1,0:T(8,128)} fusion(bf16[256,128]{1,0:T(8,128)(2,1)S(1)} %bitcast.105, bf16[256,4096]{1,0:T(8,128)(2,1)} %copy-done.7), kind=kOutput, calls=%fused_computation.111 | convolution fusion | flops 268435456 | bytes 4259840 | tf_op jit(solution)/shard_map/dot_general | solution.py:214
  120.1 1.9 %all-to-all-done.3 = f32[4,16,128]{2,1,0:T(8,128)S(1)} async-done(((f32[4,16,128]{2,1,0:T(8,128)}), f32[4,16,128]{2,1,0:T(8,128)S(1)}, u32[]{:S(2)}, u32[]{:S(2)}) %all-to-all-start.3) | async-done | bytes 32800 | tf_op jit(solution)/shard_map/all_to_all | solution.py:208
  122.7 5.5 %all-to-all-start.4 = ((bf16[64,16,128]{2,1,0:T(8,128)(2,1)}), bf16[64,16,128]{2,1,0:T(8,128)(2,1)S(1)}, u32[]{:S(2)}, u32[]{:S(2)}) async-start(bf16[64,16,128]{2,1,0:T(8,128)(2,1)} %broadcast_in_dim.51), calls=%async_computation.4 | async-start | bytes 524288 | tf_op jit(solution)/shard_map/all_to_all | solution.py:20
  128.3 1.8 %fusion.49 = f32[128,4096]{1,0:T(8,128)} fusion(bf16[256,128]{1,0:T(8,128)(2,1)S(1)} %collective-permute-done.8, bf16[256,4096]{1,0:T(8,128)(2,1)S(1)} %copy-done.6), kind=kOutput, calls=%fused_computation.112 | convolution fusion | flops 268435456 | bytes 4259840 | tf_op jit(solution)/shard_map/dot_general | solution.py:214
  131.2 1.8 convolution_add_fusion.1
  133.0 6.3 %all-to-all-done.4 = bf16[64,16,128]{2,1,0:T(8,128)(2,1)S(1)} async-done(((bf16[64,16,128]{2,1,0:T(8,128)(2,1)}), bf16[64,16,128]{2,1,0:T(8,128)(2,1)S(1)}, u32[]{:S(2)}, u32[]{:S(2)}) %all-to-all-start.4) | async-done | bytes 262176 | tf_op jit(solution)/shard_map/all_to_all | solution.py:20
  139.4 2.3 %fusion.16 = f32[256,128]{0,1:T(8,128)S(1)} fusion(bf16[1024,128]{1,0:T(8,128)(2,1)S(1)} %bitcast.100, f32[64,1024]{0,1:T(8,128)} %bitcast.99, f32[64,1024]{0,1:T(8,128)} %bitcast.98, f32[64,1024]{0,1:T(8,128)} %bitcast.97, f32[64,1024]{0,1:T(8,128)S(1)} %bitcast.96), kind=kOutput, calls=%fused_computation.30 | convolution fusion | flops 403439616 | bytes 1441792 | tf_op jit(solution)/shard_map/dot_general | solution.py:227
  143.0 6.8 %all-to-all-start.5 = ((bf16[64,16,128]{2,1,0:T(8,128)(2,1)}), bf16[64,16,128]{2,1,0:T(8,128)(2,1)S(1)}, u32[]{:S(2)}, u32[]{:S(2)}) async-start(bf16[64,16,128]{2,1,0:T(8,128)(2,1)} %broadcast_in_dim.52), calls=%async_computation.5 | async-start | bytes 524288 | tf_op jit(solution)/shard_map/all_to_all | solution.py:20
  149.8 2.7 %fusion = f32[128,4096]{1,0:T(8,128)S(1)} fusion(f32[128,4096]{1,0:T(8,128)} %fusion.49, f32[128,4096]{1,0:T(8,128)} %convolution_add_fusion.1, bf16[256,128]{1,0:T(8,128)(2,1)S(1)} %collective-permute-done.7, bf16[256,4096]{1,0:T(8,128)(2,1)S(1)} %copy-done.9), kind=kOutput, calls=%fused_computation.3 | convolution fusion | flops 269484032 | bytes 8454144 | tf_op jit(solution)/shard_map/dot_general | solution.py:214
  153.9 2.1 %collective-permute-start.10 = (bf16[32,4096]{1,0:T(8,128)(2,1)S(1)}, bf16[32,4096]{1,0:T(8,128)(2,1)S(1)}, u32[]{:S(2)}, u32[]{:S(2)}) collective-permute-start(bf16[32,4096]{1,0:T(8,128)(2,1)S(1)} %get-tuple-element.30), channel_id=1, source_target_pairs={{0,128},{64,192},{128,0},{192,64},{1,129},{65,193},{129,1},{193,65... | collective-permute-start | bytes 786440 | tf_op jit(solution)/shard_map/ppermute | solution.py:39
  156.0 1.6 collective-permute-start.9
  157.5 3.0 %all-to-all-done.5 = bf16[64,16,128]{2,1,0:T(8,128)(2,1)S(1)} async-done(((bf16[64,16,128]{2,1,0:T(8,128)(2,1)}), bf16[64,16,128]{2,1,0:T(8,128)(2,1)S(1)}, u32[]{:S(2)}, u32[]{:S(2)}) %all-to-all-start.5) | async-done | bytes 262176 | tf_op jit(solution)/shard_map/all_to_all | solution.py:20
  162.3 8.2 %all-to-all-start.6 = ((bf16[64,16,128]{2,1,0:T(8,128)(2,1)}), bf16[64,16,128]{2,1,0:T(8,128)(2,1)S(1)}, u32[]{:S(2)}, u32[]{:S(2)}) async-start(bf16[64,16,128]{2,1,0:T(8,128)(2,1)} %broadcast_in_dim.53), calls=%async_computation.6 | async-start | bytes 524288 | tf_op jit(solution)/shard_map/all_to_all | solution.py:20
  170.5 1.9 %fusion.27 = f32[4096,32]{0,1:T(8,128)} fusion(bf16[32,4096]{1,0:T(8,128)(2,1)S(1)} %collective-permute-done.11, bf16[32,4096]{1,0:T(8,128)(2,1)S(1)} %collective-permute-done.10, bf16[32,4096]{1,0:T(8,128)(2,1)S(1)} %collective-permute-done.9, f32[4,32,4096]{2,1,0:T(8,128)} %bitcast.93, s32[]{:T(128)S(6)} %select_n.75), kind=kLoop, calls=%fused_computation.43 | loop fusion | flops 786432 | bytes 1835012 | tf_op jit(solution)/shard_map/transpose | solution.py:225
  172.5 9.5 %all-to-all-done.6 = bf16[64,16,128]{2,1,0:T(8,128)(2,1)S(1)} async-done(((bf16[64,16,128]{2,1,0:T(8,128)(2,1)}), bf16[64,16,128]{2,1,0:T(8,128)(2,1)S(1)}, u32[]{:S(2)}, u32[]{:S(2)}) %all-to-all-start.6) | async-done | bytes 262176 | tf_op jit(solution)/shard_map/all_to_all | solution.py:20
  (114 shorter events, 19.8 us)
Async XLA Ops:
  2.1 37.0 %all-to-all-start = ((bf16[16,16,512]{2,1,0:T(8,128)(2,1)}), bf16[16,16,512]{2,1,0:T(8,128)(2,1)S(1)}, u32[]{:S(2)}, u32[]{:S(2)}) async-start(bf16[16,16,512]{2,1,0:T(8,128)(2,1)} %broadcast_in_dim.46), calls=%async_computation | async-start | bytes 524288 | tf_op jit(solution)/shard_map/all_to_all | solution.py:30
  11.7 5.5 %copy-start.17 = (s32[4096]{0:T(1024)S(1)}, s32[4096]{0:T(1024)}, u32[]{:S(2)}) copy-start(s32[4096]{0:T(1024)} %param.17) | copy-start | bytes 49156
  11.7 5.6 %copy-start.12 = (f32[64,2048]{1,0:T(8,128)S(1)}, f32[64,2048]{1,0:T(8,128)}, u32[]{:S(2)}) copy-start(f32[64,2048]{1,0:T(8,128)} %param.19) | copy-start | bytes 1572868
  23.0 1.3 copy-start.19
  23.0 1.3 copy-start.20
  26.9 4.4 %slice-start = ((f32[64,4096]{1,0:T(8,128)}), f32[64,2048]{1,0:T(8,128)S(1)}, s32[]{:S(2)}) async-start(f32[64,4096]{1,0:T(8,128)} %param.18), calls=%async_computation.7 | async-start | bytes 1048576 | tf_op jit(solution)/shard_map/slice | solution.py:172
  35.8 7.7 %copy-start.2 = (bf16[4096,128]{1,0:T(8,128)(2,1)S(1)}, bf16[4096,128]{1,0:T(8,128)(2,1)}, u32[]{:S(2)}) copy-start(bf16[4096,128]{1,0:T(8,128)(2,1)} %coef_ref.7) | copy-start | bytes 3145732
  39.1 10.6 %collective-permute-start = (bf16[256,512]{1,0:T(8,128)(2,1)S(1)}, bf16[256,512]{1,0:T(8,128)(2,1)S(1)}, u32[]{:S(2)}, u32[]{:S(2)}) collective-permute-start(bf16[256,512]{1,0:T(8,128)(2,1)S(1)} %bitcast.83), channel_id=1, source_target_pairs={{0,16},{1,17},{2,18},{3,19},{4,20},{5,21},{6,22},{7,23},{8,24},{9,... | collective-permute-start | bytes 786440 | tf_op jit(solution)/shard_map/ppermute | solution.py:39
  40.4 16.6 %collective-permute-start.2 = (bf16[256,512]{1,0:T(8,128)(2,1)S(1)}, bf16[256,512]{1,0:T(8,128)(2,1)S(1)}, u32[]{:S(2)}, u32[]{:S(2)}) collective-permute-start(bf16[256,512]{1,0:T(8,128)(2,1)S(1)} %bitcast.84), channel_id=1, source_target_pairs={{0,48},{1,49},{2,50},{3,51},{4,52},{5,53},{6,54},{7,55},{8,56},{9,... | collective-permute-start | bytes 786440 | tf_op jit(solution)/shard_map/ppermute | solution.py:39
  40.4 20.6 %collective-permute-start.4 = (bf16[256,512]{1,0:T(8,128)(2,1)S(1)}, bf16[256,512]{1,0:T(8,128)(2,1)S(1)}, u32[]{:S(2)}, u32[]{:S(2)}) collective-permute-start(bf16[256,512]{1,0:T(8,128)(2,1)S(1)} %bitcast.85), channel_id=1, source_target_pairs={{0,32},{1,33},{2,34},{3,35},{4,36},{5,37},{6,38},{7,39},{8,40},{9,... | collective-permute-start | bytes 786440 | tf_op jit(solution)/shard_map/ppermute | solution.py:39
  43.5 2.2 %copy-start = (bf16[4096,512]{1,0:T(8,128)(2,1)S(1)}, bf16[4096,512]{1,0:T(8,128)(2,1)}, u32[]{:S(2)}) copy-start(bf16[4096,512]{1,0:T(8,128)(2,1)} %get-tuple-element.23.centers_ref) | copy-start | bytes 12582916
  48.2 1.4 copy-start.7
  49.7 2.2 %copy-start.1 = (bf16[4096,512]{1,0:T(8,128)(2,1)S(1)}, bf16[4096,512]{1,0:T(8,128)(2,1)}, u32[]{:S(2)}) copy-start(bf16[4096,512]{1,0:T(8,128)(2,1)} %get-tuple-element.23.centers_ref) | copy-start | bytes 12582916
  54.5 1.3 copy-start.3
  55.8 12.3 %collective-permute-start.1 = (bf16[256,128]{1,0:T(8,128)(2,1)S(1)}, bf16[256,128]{1,0:T(8,128)(2,1)S(1)}, u32[]{:S(2)}, u32[]{:S(2)}) collective-permute-start(bf16[256,128]{1,0:T(8,128)(2,1)S(1)} %get-tuple-element.11), channel_id=1, source_target_pairs={{0,16},{1,17},{2,18},{3,19},{4,20},{5,21},{6,22},{7,23},{8,24},{9,... | collective-permute-start | bytes 196616 | tf_op jit(solution)/shard_map/ppermute | solution.py:39
  59.6 1.4 copy-start.5
  61.0 27.6 %copy-start.18 = (f32[16,128]{1,0:T(8,128)S(1)}, f32[16,128]{1,0:T(8,128)}, u32[]{:S(2)}) copy-start(f32[16,128]{1,0:T(8,128)} %param.12) | copy-start | bytes 24580
  61.0 7.1 %collective-permute-start.3 = (bf16[256,128]{1,0:T(8,128)(2,1)S(1)}, bf16[256,128]{1,0:T(8,128)(2,1)S(1)}, u32[]{:S(2)}, u32[]{:S(2)}) collective-permute-start(bf16[256,128]{1,0:T(8,128)(2,1)S(1)} %get-tuple-element.12), channel_id=1, source_target_pairs={{0,48},{1,49},{2,50},{3,51},{4,52},{5,53},{6,54},{7,55},{8,56},{9,... | collective-permute-start | bytes 196616 | tf_op jit(solution)/shard_map/ppermute | solution.py:39
  63.6 1.4 copy-start.8
  65.0 5.8 %collective-permute-start.5 = (bf16[256,128]{1,0:T(8,128)(2,1)S(1)}, bf16[256,128]{1,0:T(8,128)(2,1)S(1)}, u32[]{:S(2)}, u32[]{:S(2)}) collective-permute-start(bf16[256,128]{1,0:T(8,128)(2,1)S(1)} %get-tuple-element.13), channel_id=1, source_target_pairs={{0,32},{1,33},{2,34},{3,35},{4,36},{5,37},{6,38},{7,39},{8,40},{9,... | collective-permute-start | bytes 196616 | tf_op jit(solution)/shard_map/ppermute | solution.py:39
  71.4 17.2 %all-to-all-start.1 = ((bf16[16,16,128]{2,1,0:T(8,128)(2,1)}), bf16[16,16,128]{2,1,0:T(8,128)(2,1)S(1)}, u32[]{:S(2)}, u32[]{:S(2)}) async-start(bf16[16,16,128]{2,1,0:T(8,128)(2,1)} %bitcast.2), calls=%async_computation.1 | async-start | bytes 131072 | tf_op jit(solution)/shard_map/all_to_all | solution.py:30
  89.3 12.6 %all-to-all-start.2 = ((bf16[16,16,128]{2,1,0:T(8,128)(2,1)}), bf16[16,16,128]{2,1,0:T(8,128)(2,1)S(1)}, u32[]{:S(2)}, u32[]{:S(2)}) async-start(bf16[16,16,128]{2,1,0:T(8,128)(2,1)} %broadcast_in_dim.47), calls=%async_computation.2 | async-start | bytes 131072 | tf_op jit(solution)/shard_map/all_to_all | solution.py:30
  101.9 4.4 %collective-permute-start.6 = (bf16[256,128]{1,0:T(8,128)(2,1)S(1)}, bf16[256,128]{1,0:T(8,128)(2,1)S(1)}, u32[]{:S(2)}, u32[]{:S(2)}) collective-permute-start(bf16[256,128]{1,0:T(8,128)(2,1)S(1)} %bitcast.101), channel_id=1, source_target_pairs={{0,16},{1,17},{2,18},{3,19},{4,20},{5,21},{6,22},{7,23},{8,24},{9,... | collective-permute-start | bytes 196616 | tf_op jit(solution)/shard_map/ppermute | solution.py:39
  103.8 4.3 %collective-permute-start.8 = (bf16[256,128]{1,0:T(8,128)(2,1)S(1)}, bf16[256,128]{1,0:T(8,128)(2,1)S(1)}, u32[]{:S(2)}, u32[]{:S(2)}) collective-permute-start(bf16[256,128]{1,0:T(8,128)(2,1)S(1)} %bitcast.102), channel_id=1, source_target_pairs={{0,48},{1,49},{2,50},{3,51},{4,52},{5,53},{6,54},{7,55},{8,56},{9,... | collective-permute-start | bytes 196616 | tf_op jit(solution)/shard_map/ppermute | solution.py:39
  105.3 5.8 %collective-permute-start.7 = (bf16[256,128]{1,0:T(8,128)(2,1)S(1)}, bf16[256,128]{1,0:T(8,128)(2,1)S(1)}, u32[]{:S(2)}, u32[]{:S(2)}) collective-permute-start(bf16[256,128]{1,0:T(8,128)(2,1)S(1)} %bitcast.103), channel_id=1, source_target_pairs={{0,32},{1,33},{2,34},{3,35},{4,36},{5,37},{6,38},{7,39},{8,40},{9,... | collective-permute-start | bytes 196616 | tf_op jit(solution)/shard_map/ppermute | solution.py:39
  106.3 13.8 %copy-start.15 = (bf16[256,128]{1,0:T(8,128)(2,1)}, bf16[256,128]{1,0:T(8,128)(2,1)S(1)}, u32[]{:S(2)}) copy-start(bf16[256,128]{1,0:T(8,128)(2,1)S(1)} %collective-permute-done.6) | copy-start | bytes 196612
  112.3 9.6 %all-to-all-start.3 = ((f32[4,16,128]{2,1,0:T(8,128)}), f32[4,16,128]{2,1,0:T(8,128)S(1)}, u32[]{:S(2)}, u32[]{:S(2)}) async-start(f32[4,16,128]{2,1,0:T(8,128)} %pad_maximum_fusion), calls=%async_computation.3 | async-start | bytes 65536 | tf_op jit(solution)/shard_map/all_to_all | solution.py:208
  116.5 11.7 %copy-start.6 = (bf16[256,4096]{1,0:T(8,128)(2,1)S(1)}, bf16[256,4096]{1,0:T(8,128)(2,1)}, u32[]{:S(2)}) copy-start(bf16[256,4096]{1,0:T(8,128)(2,1)} %copy-done.5) | copy-start | bytes 6291460
  122.7 16.7 %all-to-all-start.4 = ((bf16[64,16,128]{2,1,0:T(8,128)(2,1)}), bf16[64,16,128]{2,1,0:T(8,128)(2,1)S(1)}, u32[]{:S(2)}, u32[]{:S(2)}) async-start(bf16[64,16,128]{2,1,0:T(8,128)(2,1)} %broadcast_in_dim.51), calls=%async_computation.4 | async-start | bytes 524288 | tf_op jit(solution)/shard_map/all_to_all | solution.py:20
  128.2 1.9 %copy-start.4 = (bf16[256,4096]{1,0:T(8,128)(2,1)S(1)}, bf16[256,4096]{1,0:T(8,128)(2,1)}, u32[]{:S(2)}) copy-start(bf16[256,4096]{1,0:T(8,128)(2,1)} %copy-done.3) | copy-start | bytes 6291460
  128.2 3.0 %copy-start.11 = (f32[128,4096]{1,0:T(8,128)S(1)}, f32[128,4096]{1,0:T(8,128)}, u32[]{:S(2)}) copy-start(f32[128,4096]{1,0:T(8,128)} %fusion.48) | copy-start | bytes 6291460
  128.2 3.0 %copy-start.16 = (bf16[256,128]{1,0:T(8,128)(2,1)S(1)}, bf16[256,128]{1,0:T(8,128)(2,1)}, u32[]{:S(2)}) copy-start(bf16[256,128]{1,0:T(8,128)(2,1)} %copy-done.15) | copy-start | bytes 196612
  131.2 8.2 %copy-start.14 = (f32[1,64,64,16]{1,3,2,0:T(8,128)S(1)}, f32[1,64,64,16]{1,3,2,0:T(8,128)}, u32[]{:S(2)}) copy-start(f32[1,64,64,16]{1,3,2,0:T(8,128)} %copy.44) | copy-start | bytes 786436
  133.0 16.7 %copy-start.9 = (bf16[256,4096]{1,0:T(8,128)(2,1)S(1)}, bf16[256,4096]{1,0:T(8,128)(2,1)}, u32[]{:S(2)}) copy-start(bf16[256,4096]{1,0:T(8,128)(2,1)} %copy-done.8) | copy-start | bytes 6291460
  143.0 17.6 %all-to-all-start.5 = ((bf16[64,16,128]{2,1,0:T(8,128)(2,1)}), bf16[64,16,128]{2,1,0:T(8,128)(2,1)S(1)}, u32[]{:S(2)}, u32[]{:S(2)}) async-start(bf16[64,16,128]{2,1,0:T(8,128)(2,1)} %broadcast_in_dim.52), calls=%async_computation.5 | async-start | bytes 524288 | tf_op jit(solution)/shard_map/all_to_all | solution.py:20
  152.5 1.4 copy-start.10
  152.5 8.0 %copy-start.13 = (f32[256,512]{0,1:T(8,128)S(1)}, f32[256,512]{0,1:T(8,128)}, u32[]{:S(2)}) copy-start(f32[256,512]{0,1:T(8,128)} %reshape.170) | copy-start | bytes 1572868
  153.9 16.6 %collective-permute-start.10 = (bf16[32,4096]{1,0:T(8,128)(2,1)S(1)}, bf16[32,4096]{1,0:T(8,128)(2,1)S(1)}, u32[]{:S(2)}, u32[]{:S(2)}) collective-permute-start(bf16[32,4096]{1,0:T(8,128)(2,1)S(1)} %get-tuple-element.30), channel_id=1, source_target_pairs={{0,128},{64,192},{128,0},{192,64},{1,129},{65,193},{129,1},{193,65... | collective-permute-start | bytes 786440 | tf_op jit(solution)/shard_map/ppermute | solution.py:39
  156.0 14.5 %collective-permute-start.11 = (bf16[32,4096]{1,0:T(8,128)(2,1)S(1)}, bf16[32,4096]{1,0:T(8,128)(2,1)S(1)}, u32[]{:S(2)}, u32[]{:S(2)}) collective-permute-start(bf16[32,4096]{1,0:T(8,128)(2,1)S(1)} %get-tuple-element.29), channel_id=1, source_target_pairs={{0,192},{64,128},{128,64},{192,0},{1,193},{65,129},{129,65},{193,1... | collective-permute-start | bytes 786440 | tf_op jit(solution)/shard_map/ppermute | solution.py:39
  156.0 14.5 %collective-permute-start.9 = (bf16[32,4096]{1,0:T(8,128)(2,1)S(1)}, bf16[32,4096]{1,0:T(8,128)(2,1)S(1)}, u32[]{:S(2)}, u32[]{:S(2)}) collective-permute-start(bf16[32,4096]{1,0:T(8,128)(2,1)S(1)} %get-tuple-element.28), channel_id=1, source_target_pairs={{0,64},{64,0},{128,192},{192,128},{1,65},{65,1},{129,193},{193,129... | collective-permute-start | bytes 786440 | tf_op jit(solution)/shard_map/ppermute | solution.py:39
  162.3 19.7 %all-to-all-start.6 = ((bf16[64,16,128]{2,1,0:T(8,128)(2,1)}), bf16[64,16,128]{2,1,0:T(8,128)(2,1)S(1)}, u32[]{:S(2)}, u32[]{:S(2)}) async-start(bf16[64,16,128]{2,1,0:T(8,128)(2,1)} %broadcast_in_dim.53), calls=%async_computation.6 | async-start | bytes 524288 | tf_op jit(solution)/shard_map/all_to_all | solution.py:20

commit v3 on v2

--- a/solution.py
+++ b/solution.py
@@ -39,40 +39,76 @@
     return lax.ppermute(x, axis, [(i, i ^ bits) for i in range(lax.axis_size(axis))])
 
 
-def kernel_block(points_ref, centers_ref, norm_ref, coef_ref, kernel_ref, value_ref):
+def kernel_block(
+    points_ref, centers_ref, norm_ref, coef_ref, kernel_ref, value_ref, slots, total, sems
+):
+    step = pl.program_id(0)
     samples = points_ref[...]
     wide = samples.astype(F32)
     left = 0.5 * jnp.sum(wide * wide, axis=1, keepdims=True)
-    total = jnp.zeros(value_ref.shape, F32)
-    for i in range(centers_ref.shape[0] // TILE):
-        rows = pl.ds(i * TILE, TILE)
-        products = lax.dot_general(
-            samples, centers_ref[rows, :], (((1,), (1,)), ((), ())), preferred_element_type=F32
-        )
-        block = jnp.exp(products - left - norm_ref[:, rows]).astype(BF)
-        kernel_ref[:, rows] = block
-        total += jnp.dot(block, coef_ref[rows, :], preferred_element_type=F32)
-    value_ref[...] = total.astype(value_ref.dtype)
+    products = lax.dot_general(
+        samples, centers_ref[...], (((1,), (1,)), ((), ())), preferred_element_type=F32
+    )
+    block = jnp.exp(products - left - norm_ref[...]).astype(BF)
+    slots[step] = block
+    columns = pl.ds(pl.multiple_of(step * TILE, TILE), TILE)
+    pltpu.make_async_copy(slots.at[step], kernel_ref.at[:, columns], sems.at[step]).start()
+    part = jnp.dot(block, coef_ref[...], preferred_element_type=F32)
+
+    @pl.when(step == 0)
+    def _():
+        total[...] = part
+
+    @pl.when(step > 0)
+    def _():
+        total[...] += part
+
+    @pl.when(step == pl.num_programs(0) - 1)
+    def _():
+        value_ref[...] = total[...].astype(value_ref.dtype)
+        for i in range(slots.shape[0]):
+            rows = pl.ds(i * TILE, TILE)
+            pltpu.make_async_copy(slots.at[i], kernel_ref.at[:, rows], sems.at[i]).wait()
 
 
 def kernel_and_value(samples, anchors, norms, coefficients):
     count, depth = samples.shape
     total, cols = coefficients.shape
+    steps = total // TILE
     return pl.pallas_call(
         kernel_block,
+        grid=(steps,),
         out_shape=(
-            jax.ShapeDtypeStruct((count, total), BF),
+            pltpu.HBM((count, total), BF),
             jax.ShapeDtypeStruct((count, cols), BF),
         ),
-        in_specs=[pl.BlockSpec(memory_space=pltpu.VMEM)] * 4,
-        out_specs=[pl.BlockSpec(memory_space=pltpu.VMEM)] * 2,
+        in_specs=[
+            pl.BlockSpec((count, depth), lambda i: (0, 0)),
+            pl.BlockSpec((TILE, depth), lambda i: (i, 0)),
+            pl.BlockSpec((1, TILE), lambda i: (0, i)),
+            pl.BlockSpec((TILE, cols), lambda i: (i, 0)),
+        ],
+        out_specs=[
+            pl.BlockSpec(memory_space=pltpu.HBM),
+            pl.BlockSpec((count, cols), lambda i: (0, 0)),
+        ],
+        scratch_shapes=[
+            pltpu.VMEM((steps, count, TILE), BF),
+            pltpu.VMEM((count, cols), F32),
+            pltpu.SemaphoreType.DMA((steps,)),
+        ],
         compiler_params=pltpu.CompilerParams(vmem_limit_bytes=16 * 1024 * 1024),
         cost_estimate=pl.CostEstimate(
             flops=2 * count * total * (depth + cols),
             bytes_accessed=2 * (count * depth + total * depth + total * cols + count * total),
             transcendentals=count * total,
         ),
-    )(samples, anchors, norms, coefficients)
+    )(
+        samples,
+        pltpu.with_memory_space_constraint(anchors, pltpu.HBM),
+        norms,
+        pltpu.with_memory_space_constraint(coefficients, pltpu.HBM),
+    )
 
 
 def half_norm(rows):
@@ -147,31 +183,6 @@
     scaled_centers = (centers.astype(F32) * inv_scale[None, :]).astype(BF)
     center_norm = half_norm(scaled_centers)
 
-    blocks = center_index.reshape(own_rows, shards)
-    order = blocks[0] // shard_rows
-    here = order == shard
-    local = jnp.sum(jnp.where(here[None, :], blocks - shard * shard_rows, 0), axis=1)
-    choose = (local[:, None] == jnp.arange(shard_rows, dtype=jnp.int32)[None, :]).astype(BF)
-    chosen = jnp.dot(choose, scaled_centers, preferred_element_type=F32).astype(BF)
-    chosen_norm = half_norm(chosen)
-    place = (order[:, None] == jnp.arange(shards, dtype=jnp.int32)[None, :]).astype(F32)
-
-    halves = panel_rows // (strip * shards)
-    inverse = panel_inverse.reshape(own_rows, halves, strip, shards)
-    inverse_window = jnp.einsum("rhqj,js->hrsq", inverse, place, precision=HI)
-    inverse_window = inverse_window.reshape(halves, own_rows, shards * strip)
-    parts = []
-    for i in range(fold):
-        parts.append(jnp.where(panel == i // halves, inverse_window[i % halves], 0.0))
-    inverse_window = jnp.concatenate(parts, axis=0)
-
-    def folded(matrix):
-        m = matrix.reshape(own_rows, panel_shards, fold, strip)
-        return m.transpose(2, 0, 1, 3).reshape(fold * own_rows, panel_shards * strip)
-
-    factor_rows = folded(factor[:, :panel_rows])
-    inverse_rows = folded(panel_inverse)
-
     kernels = [None] * PLANES
     arrived = None
     for k in (0, 1, 3, 2):
@@ -181,12 +192,39 @@
         value = value if k == 0 else swapped(value, "ctr", plane_bits[k])
         value = value.astype(F32)
         arrived = value if arrived is None else arrived + value
+    arrived, panel_inverse, center_index, scaled_centers = lax.optimization_barrier(
+        (arrived, panel_inverse, center_index, scaled_centers)
+    )
+    blocks = center_index.reshape(own_rows, shards)
+    order = blocks[0] // shard_rows
+    here = order == shard
+    local = jnp.sum(jnp.where(here[None, :], blocks - shard * shard_rows, 0), axis=1)
+    choose = (local[:, None] == jnp.arange(shard_rows, dtype=jnp.int32)[None, :]).astype(BF)
+    chosen = jnp.dot(choose, scaled_centers, preferred_element_type=F32).astype(BF)
+    chosen_norm = half_norm(chosen)
+    place = (order[:, None] == jnp.arange(shards, dtype=jnp.int32)[None, :]).astype(F32)
+
+    halves = panel_rows // (strip * shards)
+    inverse = panel_inverse.reshape(own_rows, halves, strip, shards)
+    inverse_window = jnp.einsum("rhqj,js->hrsq", inverse, place, precision=HI)
+    inverse_window = inverse_window.reshape(halves, own_rows, shards * strip)
+    parts = []
+    for i in range(fold):
+        parts.append(jnp.where(panel == i // halves, inverse_window[i % halves], 0.0))
+    inverse_window = jnp.concatenate(parts, axis=0)
+
     own_weight = class_lookup(point_class, class_weight)
     shares = plane_exchange(
         arrived.astype(BF).reshape(shards // PLANES, own_points, target_count), "ctr"
     )
     predicted = jnp.sum(shares.astype(F32), axis=0)
     own_residual = (own_weight[:, None] * (predicted - targets)).astype(BF)
+    own_residual, factor = lax.optimization_barrier((own_residual, factor[:, :panel_rows]))
+    def folded(matrix):
+        m = matrix.reshape(own_rows, panel_shards, fold, strip)
+        return m.transpose(2, 0, 1, 3).reshape(fold * own_rows, panel_shards * strip)
+
+    factor_rows = folded(factor)
     plane_residual = plane_gathered(own_residual, "ctr").reshape(plane_points, target_count)
     residuals = [plane_residual] + [
         swapped(plane_residual, "ctr", plane_bits[k]) for k in range(1, PLANES)
@@ -207,6 +245,8 @@
     )
     pieces = lax.all_to_all(pieces, "pts", 0, 0, tiled=True)
     window = jnp.sum(pieces, axis=0).astype(BF)
+    window, panel_inverse = lax.optimization_barrier((window, panel_inverse))
+    inverse_rows = folded(panel_inverse)
     window = gathered(window, "ctr").reshape(shards * strip, LANES)
 
     backward = None

time: 184 us -> 189 us (1.027)
  Pallas kernels: 10.3 us -> 30.8 us
  local copies, waits for them, and re-layouts: 31.9 us -> 18.4 us
  waiting for transfers between devices: 45.4 us -> 37.3 us
  starting transfers between devices: 61.9 us -> 66.3 us
    pallas_call x4, Pallas kernels: 10.3 us -> 30.8 us  [kernel_and_value(): pl.pallas_call(kernel_block, grid=(steps,), out_shape=(pltpu.HBM((count,...]
    unnamed x44 -> x18, local copies, waits for them, and re-layouts: 12.7 us -> 0.35 us
    all_to_all x3, waiting for transfers between devices: 18 us -> 13 us  [plane_exchange(): lax.all_to_all(pieces, axis, 0, 0, tiled=True, axis_index_groups=groups)]
    all_to_all x3, waiting for transfers between devices: 18.8 us -> 14.9 us  [gathered(): lax.all_to_all(jnp.broadcast_to(x[None], (count, *x.shape)), axis, 0, 0,...]
    all_to_all x3, starting transfers between devices: 20.6 us -> 23.6 us  [gathered(): lax.all_to_all(jnp.broadcast_to(x[None], (count, *x.shape)), axis, 0, 0,...]
    select_n x4, local copies, waits for them, and re-layouts: 6.57 us -> 4.43 us  [body(): jnp.where(panel == i // halves, inverse_window[i % halves], 0.0)]
  transfers between devices with their start and end apart: 19 -> 19, of which waited for: 9 -> 7; matrix products, arithmetic and copies ran while one was open for 23% -> 22% of each run, Pallas kernels for 6% -> 16%
where the time goes in v3:
time: 189 us; the launch traced here: 187 us
  starting transfers between devices  66.3 us (35%)
  waiting for transfers between devices  37.3 us (20%)
  Pallas kernels  30.8 us (16%)
  matrix products  21.2 us (11%)
  local copies, waits for them, and re-layouts  18.4 us (10%)
  other arithmetic  11.9 us (6%)
    pallas_call x4, Pallas kernels, kernel_and_value(): pl.pallas_call(kernel_block, grid=(steps,), out_shape=(pltpu.HBM((count,...  30.8 us
    all_to_all x3, starting transfers between devices, gathered(): lax.all_to_all(jnp.broadcast_to(x[None], (count, *x.shape)), axis, 0, 0,...  23.6 us
    all_to_all x3, starting transfers between devices, plane_exchange(): lax.all_to_all(pieces, axis, 0, 0, tiled=True, axis_index_groups=groups)  21.1 us
    ppermute x12, starting transfers between devices, swapped(): lax.ppermute(x, axis, [(i, i ^ bits) for i in range(lax.axis_size(axis))])  17.4 us
    all_to_all x3, waiting for transfers between devices, gathered(): lax.all_to_all(jnp.broadcast_to(x[None], (count, *x.shape)), axis, 0, 0,...  14.9 us
    all_to_all x3, waiting for transfers between devices, plane_exchange(): lax.all_to_all(pieces, axis, 0, 0, tiled=True, axis_index_groups=groups)  13 us
    dot_general x4, matrix products, body(): lax.dot_general(residuals[k], kernels[k], (((0,), (0,)), ((), ())), prefe...  10.8 us
    ppermute x12, waiting for transfers between devices, swapped(): lax.ppermute(x, axis, [(i, i ^ bits) for i in range(lax.axis_size(axis))])  6.04 us
  transfers between devices with their start and end apart: 19, of which 7 were waited for; matrix products, arithmetic and copies ran while one was open for 22% of the time, Pallas kernels for 16%

profile of v3, /device:TPU:4, one launch (start us, length us, event | category | flops | bytes accessed | tf_op | source)
XLA Modules:
  0.0 187.0 jit_solution(7709727825120721506)
XLA Ops:
  1.4 0.7 broadcast_in_dim.46
  2.1 9.6 %all-to-all-start = ((bf16[16,16,512]{2,1,0:T(8,128)(2,1)}), bf16[16,16,512]{2,1,0:T(8,128)(2,1)S(1)}, u32[]{:S(2)}, u32[]{:S(2)}) async-start(bf16[16,16,512]{2,1,0:T(8,128)(2,1)} %broadcast_in_dim.46), calls=%async_computation | async-start | bytes 524288 | tf_op jit(solution)/shard_map/all_to_all | solution.py:30
  11.7 5.4 %multiply_reduce_fusion = (f32[4096]{0:T(1024)S(1)}, bf16[4096,512]{1,0:T(8,128)(2,1)}) fusion(f32[512]{0:T(512)} %param.14, bf16[4096,512]{1,0:T(8,128)(2,1)} %param.15), kind=kLoop, calls=%fused_computation | loop fusion | flops 12578816 | bytes 8407040 | tf_op jit(solution)/shard_map/reduce_sum | solution.py:115
  17.9 5.8 %all-to-all-done = bf16[16,16,512]{2,1,0:T(8,128)(2,1)S(1)} async-done(((bf16[16,16,512]{2,1,0:T(8,128)(2,1)}), bf16[16,16,512]{2,1,0:T(8,128)(2,1)S(1)}, u32[]{:S(2)}, u32[]{:S(2)}) %all-to-all-start) | async-done | bytes 262176 | tf_op jit(solution)/shard_map/all_to_all | solution.py:30
  24.2 2.2 %collective-permute-start.2 = (bf16[256,512]{1,0:T(8,128)(2,1)S(1)}, bf16[256,512]{1,0:T(8,128)(2,1)S(1)}, u32[]{:S(2)}, u32[]{:S(2)}) collective-permute-start(bf16[256,512]{1,0:T(8,128)(2,1)S(1)} %bitcast.80), channel_id=1, source_target_pairs={{0,48},{1,49},{2,50},{3,51},{4,52},{5,53},{6,54},{7,55},{8,56},{9,... | collective-permute-start | bytes 786440 | tf_op jit(solution)/shard_map/ppermute | solution.py:39
  26.4 2.0 %collective-permute-start = (bf16[256,512]{1,0:T(8,128)(2,1)S(1)}, bf16[256,512]{1,0:T(8,128)(2,1)S(1)}, u32[]{:S(2)}, u32[]{:S(2)}) collective-permute-start(bf16[256,512]{1,0:T(8,128)(2,1)S(1)} %bitcast.81), channel_id=1, source_target_pairs={{0,16},{1,17},{2,18},{3,19},{4,20},{5,21},{6,22},{7,23},{8,24},{9,... | collective-permute-start | bytes 786440 | tf_op jit(solution)/shard_map/ppermute | solution.py:39
  28.6 7.7 %shard_map.113 = (bf16[256,4096]{1,0:T(8,128)(2,1)}, bf16[256,128]{1,0:T(8,128)(2,1)S(1)}) custom-call(bf16[256,512]{1,0:T(8,128)(2,1)S(1)} %bitcast.82, bf16[4096,512]{1,0:T(8,128)(2,1)} %get-tuple-element.30.centers_ref, f32[1,4096]{1,0:T(1,128)S(1)} %bitcast.84, bf16[4096,128]{1,0:T(8,128)(2,1)} %coef_ref.7), custom_call_target="tpu_custom_call" | custom-call | flops 1342177280 | bytes 7602176 | tf_op jit(solution)/shard_map/pallas_call | solution.py:78
  36.3 7.7 %shard_map.116 = (bf16[256,4096]{1,0:T(8,128)(2,1)}, bf16[256,128]{1,0:T(8,128)(2,1)S(1)}) custom-call(bf16[256,512]{1,0:T(8,128)(2,1)S(1)} %collective-permute-done.4.points_ref, bf16[4096,512]{1,0:T(8,128)(2,1)} %get-tuple-element.30.centers_ref, f32[1,4096]{1,0:T(1,128)S(1)} %bitcast.85, bf16[4096,128]{1,0:T(8,128)(2,1)} %coef_ref.7), custom_call_target="tpu_custom_call" | custom-call | flops 1342177280 | bytes 7602176 | tf_op jit(solution)/shard_map/pallas_call | solution.py:78
  44.3 7.7 %shard_map.115 = (bf16[256,4096]{1,0:T(8,128)(2,1)}, bf16[256,128]{1,0:T(8,128)(2,1)S(1)}) custom-call(bf16[256,512]{1,0:T(8,128)(2,1)S(1)} %collective-permute-done.2.points_ref, bf16[4096,512]{1,0:T(8,128)(2,1)} %get-tuple-element.30.centers_ref, f32[1,4096]{1,0:T(1,128)S(1)} %bitcast.86, bf16[4096,128]{1,0:T(8,128)(2,1)} %coef_ref.7), custom_call_target="tpu_custom_call" | custom-call | flops 1342177280 | bytes 7602176 | tf_op jit(solution)/shard_map/pallas_call | solution.py:78
  52.0 1.5 collective-permute-start.3
  53.7 7.7 %shard_map.114 = (bf16[256,4096]{1,0:T(8,128)(2,1)}, bf16[256,128]{1,0:T(8,128)(2,1)S(1)}) custom-call(bf16[256,512]{1,0:T(8,128)(2,1)S(1)} %collective-permute-done.points_ref, bf16[4096,512]{1,0:T(8,128)(2,1)} %get-tuple-element.30.centers_ref, f32[1,4096]{1,0:T(1,128)S(1)} %bitcast.87, bf16[4096,128]{1,0:T(8,128)(2,1)} %coef_ref.7), custom_call_target="tpu_custom_call" | custom-call | flops 1342177280 | bytes 7602176 | tf_op jit(solution)/shard_map/pallas_call | solution.py:78
  61.4 3.3 %collective-permute-start.1 = (bf16[256,128]{1,0:T(8,128)(2,1)S(1)}, bf16[256,128]{1,0:T(8,128)(2,1)S(1)}, u32[]{:S(2)}, u32[]{:S(2)}) collective-permute-start(bf16[256,128]{1,0:T(8,128)(2,1)S(1)} %get-tuple-element.19), channel_id=1, source_target_pairs={{0,16},{1,17},{2,18},{3,19},{4,20},{5,21},{6,22},{7,23},{8,24},{9,... | collective-permute-start | bytes 196616 | tf_op jit(solution)/shard_map/ppermute | solution.py:39
  64.9 2.1 %collective-permute-done.1 = bf16[256,128]{1,0:T(8,128)(2,1)S(1)} collective-permute-done((bf16[256,128]{1,0:T(8,128)(2,1)S(1)}, bf16[256,128]{1,0:T(8,128)(2,1)S(1)}, u32[]{:S(2)}, u32[]{:S(2)}) %collective-permute-start.1) | collective-permute-done | bytes 65568 | tf_op jit(solution)/shard_map/ppermute | solution.py:39
  67.7 3.5 %all-to-all-start.1 = ((bf16[16,16,128]{2,1,0:T(8,128)(2,1)}), bf16[16,16,128]{2,1,0:T(8,128)(2,1)S(1)}, u32[]{:S(2)}, u32[]{:S(2)}) async-start(bf16[16,16,128]{2,1,0:T(8,128)(2,1)} %bitcast.2), calls=%async_computation.1 | async-start | bytes 131072 | tf_op jit(solution)/shard_map/all_to_all | solution.py:30
  71.3 1.5 reshape.164
  72.8 3.2 %multiply_reduce_fusion.5 = (f32[64]{0:T(128)S(1)}, bf16[64,512]{1,0:T(8,128)(2,1)S(1)}) fusion(bf16[4096,512]{1,0:T(8,128)(2,1)} %get-tuple-element.30.centers_ref, s32[64]{0:T(128)S(1)} %select_reduce_fusion), kind=kOutput, calls=%fused_computation.54 | convolution fusion | flops 268828608 | bytes 4260352 | tf_op jit(solution)/shard_map/dot_general | solution.py:203
  76.0 2.0 %convolution_bitcast_fusion = f32[2,64,64,16]{1,2,3,0:T(8,128)S(1)} fusion(f32[64,2,16,64]{3,2,1,0:T(8,128)S(1)} %reshape.164, s32[64]{0:T(128)S(1)} %get-tuple-element.37), kind=kOutput, calls=%fused_computation.5 | convolution fusion | flops 100667392 | bytes 1048832 | tf_op jit(solution)/shard_map/rhqj,js->hrsq/dot_general | solution.py:209
  78.4 1.1 copy.45
  79.5 1.1 copy.47
  80.6 1.1 copy.48
  81.7 1.1 copy.46
  83.5 8.0 %all-to-all-start.2 = ((bf16[16,16,128]{2,1,0:T(8,128)(2,1)}), bf16[16,16,128]{2,1,0:T(8,128)(2,1)S(1)}, u32[]{:S(2)}, u32[]{:S(2)}) async-start(bf16[16,16,128]{2,1,0:T(8,128)(2,1)} %broadcast_in_dim.47), calls=%async_computation.2 | async-start | bytes 131072 | tf_op jit(solution)/shard_map/all_to_all | solution.py:30
  92.0 1.5 reshape.169
  93.5 7.1 %all-to-all-done.2 = bf16[16,16,128]{2,1,0:T(8,128)(2,1)S(1)} async-done(((bf16[16,16,128]{2,1,0:T(8,128)(2,1)}), bf16[16,16,128]{2,1,0:T(8,128)(2,1)S(1)}, u32[]{:S(2)}, u32[]{:S(2)}) %all-to-all-start.2) | async-done | bytes 65568 | tf_op jit(solution)/shard_map/all_to_all | solution.py:30
  101.2 3.5 %collective-permute-start.7 = (bf16[256,128]{1,0:T(8,128)(2,1)S(1)}, bf16[256,128]{1,0:T(8,128)(2,1)S(1)}, u32[]{:S(2)}, u32[]{:S(2)}) collective-permute-start(bf16[256,128]{1,0:T(8,128)(2,1)S(1)} %bitcast.98), channel_id=1, source_target_pairs={{0,32},{1,33},{2,34},{3,35},{4,36},{5,37},{6,38},{7,39},{8,40},{9,... | collective-permute-start | bytes 196616 | tf_op jit(solution)/shard_map/ppermute | solution.py:39
  105.1 3.9 %collective-permute-done.6 = bf16[256,128]{1,0:T(8,128)(2,1)S(1)} collective-permute-done((bf16[256,128]{1,0:T(8,128)(2,1)S(1)}, bf16[256,128]{1,0:T(8,128)(2,1)S(1)}, u32[]{:S(2)}, u32[]{:S(2)}) %collective-permute-start.6) | collective-permute-done | bytes 65568 | tf_op jit(solution)/shard_map/ppermute | solution.py:39
  110.9 4.2 %all-to-all-start.3 = ((f32[4,16,128]{2,1,0:T(8,128)}), f32[4,16,128]{2,1,0:T(8,128)S(1)}, u32[]{:S(2)}, u32[]{:S(2)}) async-start(f32[4,16,128]{2,1,0:T(8,128)} %pad_maximum_fusion), calls=%async_computation.3 | async-start | bytes 65536 | tf_op jit(solution)/shard_map/all_to_all | solution.py:246
  115.1 2.1 %fusion.48 = f32[128,4096]{1,0:T(8,128)S(1)} fusion(bf16[256,128]{1,0:T(8,128)(2,1)S(1)} %bitcast.101, bf16[256,4096]{1,0:T(8,128)(2,1)} %get-tuple-element.24), kind=kOutput, calls=%fused_computation.109 | convolution fusion | flops 268435456 | bytes 4259840 | tf_op jit(solution)/shard_map/dot_general | solution.py:254
  117.1 3.4 %all-to-all-done.3 = f32[4,16,128]{2,1,0:T(8,128)S(1)} async-done(((f32[4,16,128]{2,1,0:T(8,128)}), f32[4,16,128]{2,1,0:T(8,128)S(1)}, u32[]{:S(2)}, u32[]{:S(2)}) %all-to-all-start.3) | async-done | bytes 32800 | tf_op jit(solution)/shard_map/all_to_all | solution.py:246
  120.5 0.8 broadcast_in_dim.51
  121.3 5.6 %all-to-all-start.4 = ((bf16[64,16,128]{2,1,0:T(8,128)(2,1)}), bf16[64,16,128]{2,1,0:T(8,128)(2,1)S(1)}, u32[]{:S(2)}, u32[]{:S(2)}) async-start(bf16[64,16,128]{2,1,0:T(8,128)(2,1)} %broadcast_in_dim.51), calls=%async_computation.4 | async-start | bytes 524288 | tf_op jit(solution)/shard_map/all_to_all | solution.py:20
  126.9 3.5 %fusion.49 = f32[128,4096]{1,0:T(8,128)} fusion(bf16[256,128]{1,0:T(8,128)(2,1)S(1)} %collective-permute-done.8, bf16[256,4096]{1,0:T(8,128)(2,1)} %get-tuple-element.27), kind=kOutput, calls=%fused_computation.110 | convolution fusion | flops 268435456 | bytes 4259840 | tf_op jit(solution)/shard_map/dot_general | solution.py:254
  130.4 1.8 convolution_add_fusion.1
  132.3 5.8 %all-to-all-done.4 = bf16[64,16,128]{2,1,0:T(8,128)(2,1)S(1)} async-done(((bf16[64,16,128]{2,1,0:T(8,128)(2,1)}), bf16[64,16,128]{2,1,0:T(8,128)(2,1)S(1)}, u32[]{:S(2)}, u32[]{:S(2)}) %all-to-all-start.4) | async-done | bytes 262176 | tf_op jit(solution)/shard_map/all_to_all | solution.py:20
  138.0 2.1 %fusion.16 = f32[256,128]{0,1:T(8,128)S(1)} fusion(bf16[1024,128]{1,0:T(8,128)(2,1)S(1)} %bitcast.96, f32[64,1024]{0,1:T(8,128)} %bitcast.94, f32[64,1024]{0,1:T(8,128)S(1)} %bitcast.93, f32[64,1024]{0,1:T(8,128)} %bitcast.95, f32[64,1024]{0,1:T(8,128)S(1)} %bitcast.92), kind=kOutput, calls=%fused_computation.28 | convolution fusion | flops 403439616 | bytes 1441792 | tf_op jit(solution)/shard_map/dot_general | solution.py:267
  140.7 0.8 broadcast_in_dim.52
  141.5 6.8 %all-to-all-start.5 = ((bf16[64,16,128]{2,1,0:T(8,128)(2,1)}), bf16[64,16,128]{2,1,0:T(8,128)(2,1)S(1)}, u32[]{:S(2)}, u32[]{:S(2)}) async-start(bf16[64,16,128]{2,1,0:T(8,128)(2,1)} %broadcast_in_dim.52), calls=%async_computation.5 | async-start | bytes 524288 | tf_op jit(solution)/shard_map/all_to_all | solution.py:20
  148.3 3.4 %fusion = f32[128,4096]{1,0:T(8,128)S(1)} fusion(f32[128,4096]{1,0:T(8,128)} %fusion.49, f32[128,4096]{1,0:T(8,128)} %convolution_add_fusion.1, bf16[256,128]{1,0:T(8,128)(2,1)S(1)} %collective-permute-done.7, bf16[256,4096]{1,0:T(8,128)(2,1)} %get-tuple-element.26), kind=kOutput, calls=%fused_computation.3 | convolution fusion | flops 269484032 | bytes 8454144 | tf_op jit(solution)/shard_map/dot_general | solution.py:254
  151.8 0.9 dynamic-slice_bitcast_fusion.2
  153.4 3.0 %collective-permute-start.10 = (bf16[32,4096]{1,0:T(8,128)(2,1)}, bf16[32,4096]{1,0:T(8,128)(2,1)}, u32[]{:S(2)}, u32[]{:S(2)}) collective-permute-start(bf16[32,4096]{1,0:T(8,128)(2,1)} %get-tuple-element.46), channel_id=1, source_target_pairs={{0,128},{64,192},{128,0},{192,64},{1,129},{65,193},{129,1},{193,65... | collective-permute-start | bytes 786440 | tf_op jit(solution)/shard_map/ppermute | solution.py:39
  156.4 1.3 copy.49
  157.7 1.6 copy.50
  159.4 1.4 reshape.167
  160.8 1.4 fusion.50
  162.8 0.7 broadcast_in_dim.53
  163.6 11.2 %all-to-all-start.6 = ((bf16[64,16,128]{2,1,0:T(8,128)(2,1)}), bf16[64,16,128]{2,1,0:T(8,128)(2,1)S(1)}, u32[]{:S(2)}, u32[]{:S(2)}) async-start(bf16[64,16,128]{2,1,0:T(8,128)(2,1)} %broadcast_in_dim.53), calls=%async_computation.6 | async-start | bytes 524288 | tf_op jit(solution)/shard_map/all_to_all | solution.py:20
  174.9 2.0 %fusion.27 = f32[4096,32]{0,1:T(8,128)} fusion(bf16[32,4096]{1,0:T(8,128)(2,1)} %collective-permute-done.11, bf16[32,4096]{1,0:T(8,128)(2,1)} %collective-permute-done.10, bf16[32,4096]{1,0:T(8,128)(2,1)} %collective-permute-done.9, f32[4,32,4096]{2,1,0:T(8,128)S(1)} %bitcast.89, s32[]{:T(128)S(6)} %select_n.75), kind=kLoop, calls=%fused_computation.41 | loop fusion | flops 786432 | bytes 1835012 | tf_op jit(solution)/shard_map/transpose | solution.py:265
  176.9 9.1 %all-to-all-done.6 = bf16[64,16,128]{2,1,0:T(8,128)(2,1)S(1)} async-done(((bf16[64,16,128]{2,1,0:T(8,128)(2,1)}), bf16[64,16,128]{2,1,0:T(8,128)(2,1)S(1)}, u32[]{:S(2)}, u32[]{:S(2)}) %all-to-all-start.6) | async-done | bytes 262176 | tf_op jit(solution)/shard_map/all_to_all | solution.py:20
  (90 shorter events, 10.8 us)
Async XLA Ops:
  2.1 21.6 %all-to-all-start = ((bf16[16,16,512]{2,1,0:T(8,128)(2,1)}), bf16[16,16,512]{2,1,0:T(8,128)(2,1)S(1)}, u32[]{:S(2)}, u32[]{:S(2)}) async-start(bf16[16,16,512]{2,1,0:T(8,128)(2,1)} %broadcast_in_dim.46), calls=%async_computation | async-start | bytes 524288 | tf_op jit(solution)/shard_map/all_to_all | solution.py:30
  11.7 5.4 %slice-start = ((f32[64,4096]{1,0:T(8,128)}), f32[64,2048]{1,0:T(8,128)S(1)}, s32[]{:S(2)}) async-start(f32[64,4096]{1,0:T(8,128)} %param.18), calls=%async_computation.7 | async-start | bytes 1048576 | tf_op jit(solution)/shard_map/slice | solution.py:222
  17.1 0.7 copy-start.7
  17.1 0.7 copy-start.8
  23.7 12.6 %collective-permute-start.4 = (bf16[256,512]{1,0:T(8,128)(2,1)S(1)}, bf16[256,512]{1,0:T(8,128)(2,1)S(1)}, u32[]{:S(2)}, u32[]{:S(2)}) collective-permute-start(bf16[256,512]{1,0:T(8,128)(2,1)S(1)} %bitcast.79), channel_id=1, source_target_pairs={{0,32},{1,33},{2,34},{3,35},{4,36},{5,37},{6,38},{7,39},{8,40},{9,... | collective-permute-start | bytes 786440 | tf_op jit(solution)/shard_map/ppermute | solution.py:39
  24.2 20.1 %collective-permute-start.2 = (bf16[256,512]{1,0:T(8,128)(2,1)S(1)}, bf16[256,512]{1,0:T(8,128)(2,1)S(1)}, u32[]{:S(2)}, u32[]{:S(2)}) collective-permute-start(bf16[256,512]{1,0:T(8,128)(2,1)S(1)} %bitcast.80), channel_id=1, source_target_pairs={{0,48},{1,49},{2,50},{3,51},{4,52},{5,53},{6,54},{7,55},{8,56},{9,... | collective-permute-start | bytes 786440 | tf_op jit(solution)/shard_map/ppermute | solution.py:39
  26.4 27.3 %collective-permute-start = (bf16[256,512]{1,0:T(8,128)(2,1)S(1)}, bf16[256,512]{1,0:T(8,128)(2,1)S(1)}, u32[]{:S(2)}, u32[]{:S(2)}) collective-permute-start(bf16[256,512]{1,0:T(8,128)(2,1)S(1)} %bitcast.81), channel_id=1, source_target_pairs={{0,16},{1,17},{2,18},{3,19},{4,20},{5,21},{6,22},{7,23},{8,24},{9,... | collective-permute-start | bytes 786440 | tf_op jit(solution)/shard_map/ppermute | solution.py:39
  44.1 20.8 %collective-permute-start.5 = (bf16[256,128]{1,0:T(8,128)(2,1)S(1)}, bf16[256,128]{1,0:T(8,128)(2,1)S(1)}, u32[]{:S(2)}, u32[]{:S(2)}) collective-permute-start(bf16[256,128]{1,0:T(8,128)(2,1)S(1)} %get-tuple-element.21), channel_id=1, source_target_pairs={{0,32},{1,33},{2,34},{3,35},{4,36},{5,37},{6,38},{7,39},{8,40},{9,... | collective-permute-start | bytes 196616 | tf_op jit(solution)/shard_map/ppermute | solution.py:39
  52.0 12.9 %collective-permute-start.3 = (bf16[256,128]{1,0:T(8,128)(2,1)S(1)}, bf16[256,128]{1,0:T(8,128)(2,1)S(1)}, u32[]{:S(2)}, u32[]{:S(2)}) collective-permute-start(bf16[256,128]{1,0:T(8,128)(2,1)S(1)} %get-tuple-element.20), channel_id=1, source_target_pairs={{0,48},{1,49},{2,50},{3,51},{4,52},{5,53},{6,54},{7,55},{8,56},{9,... | collective-permute-start | bytes 196616 | tf_op jit(solution)/shard_map/ppermute | solution.py:39
  53.7 14.0 %copy-start.5 = (s32[4096]{0:T(1024)S(1)}, s32[4096]{0:T(1024)}, u32[]{:S(2)}) copy-start(s32[4096]{0:T(1024)} %param.17) | copy-start | bytes 49156
  61.4 5.6 %collective-permute-start.1 = (bf16[256,128]{1,0:T(8,128)(2,1)S(1)}, bf16[256,128]{1,0:T(8,128)(2,1)S(1)}, u32[]{:S(2)}, u32[]{:S(2)}) collective-permute-start(bf16[256,128]{1,0:T(8,128)(2,1)S(1)} %get-tuple-element.19), channel_id=1, source_target_pairs={{0,16},{1,17},{2,18},{3,19},{4,20},{5,21},{6,22},{7,23},{8,24},{9,... | collective-permute-start | bytes 196616 | tf_op jit(solution)/shard_map/ppermute | solution.py:39
  67.7 15.1 %all-to-all-start.1 = ((bf16[16,16,128]{2,1,0:T(8,128)(2,1)}), bf16[16,16,128]{2,1,0:T(8,128)(2,1)S(1)}, u32[]{:S(2)}, u32[]{:S(2)}) async-start(bf16[16,16,128]{2,1,0:T(8,128)(2,1)} %bitcast.2), calls=%async_computation.1 | async-start | bytes 131072 | tf_op jit(solution)/shard_map/all_to_all | solution.py:30
  78.3 4.5 %copy-start.6 = (f32[16,128]{1,0:T(8,128)S(1)}, f32[16,128]{1,0:T(8,128)}, u32[]{:S(2)}) copy-start(f32[16,128]{1,0:T(8,128)} %param.12) | copy-start | bytes 24580
  83.5 17.1 %all-to-all-start.2 = ((bf16[16,16,128]{2,1,0:T(8,128)(2,1)}), bf16[16,16,128]{2,1,0:T(8,128)(2,1)S(1)}, u32[]{:S(2)}, u32[]{:S(2)}) async-start(bf16[16,16,128]{2,1,0:T(8,128)(2,1)} %broadcast_in_dim.47), calls=%async_computation.2 | async-start | bytes 131072 | tf_op jit(solution)/shard_map/all_to_all | solution.py:30
  100.6 8.7 %collective-permute-start.8 = (bf16[256,128]{1,0:T(8,128)(2,1)S(1)}, bf16[256,128]{1,0:T(8,128)(2,1)S(1)}, u32[]{:S(2)}, u32[]{:S(2)}) collective-permute-start(bf16[256,128]{1,0:T(8,128)(2,1)S(1)} %bitcast.97), channel_id=1, source_target_pairs={{0,48},{1,49},{2,50},{3,51},{4,52},{5,53},{6,54},{7,55},{8,56},{9,... | collective-permute-start | bytes 196616 | tf_op jit(solution)/shard_map/ppermute | solution.py:39
  101.2 8.5 %collective-permute-start.7 = (bf16[256,128]{1,0:T(8,128)(2,1)S(1)}, bf16[256,128]{1,0:T(8,128)(2,1)S(1)}, u32[]{:S(2)}, u32[]{:S(2)}) collective-permute-start(bf16[256,128]{1,0:T(8,128)(2,1)S(1)} %bitcast.98), channel_id=1, source_target_pairs={{0,32},{1,33},{2,34},{3,35},{4,36},{5,37},{6,38},{7,39},{8,40},{9,... | collective-permute-start | bytes 196616 | tf_op jit(solution)/shard_map/ppermute | solution.py:39
  104.7 4.3 %collective-permute-start.6 = (bf16[256,128]{1,0:T(8,128)(2,1)S(1)}, bf16[256,128]{1,0:T(8,128)(2,1)S(1)}, u32[]{:S(2)}, u32[]{:S(2)}) collective-permute-start(bf16[256,128]{1,0:T(8,128)(2,1)S(1)} %bitcast.99), channel_id=1, source_target_pairs={{0,16},{1,17},{2,18},{3,19},{4,20},{5,21},{6,22},{7,23},{8,24},{9,... | collective-permute-start | bytes 196616 | tf_op jit(solution)/shard_map/ppermute | solution.py:39
  110.9 9.6 %all-to-all-start.3 = ((f32[4,16,128]{2,1,0:T(8,128)}), f32[4,16,128]{2,1,0:T(8,128)S(1)}, u32[]{:S(2)}, u32[]{:S(2)}) async-start(f32[4,16,128]{2,1,0:T(8,128)} %pad_maximum_fusion), calls=%async_computation.3 | async-start | bytes 65536 | tf_op jit(solution)/shard_map/all_to_all | solution.py:246
  121.3 16.8 %all-to-all-start.4 = ((bf16[64,16,128]{2,1,0:T(8,128)(2,1)}), bf16[64,16,128]{2,1,0:T(8,128)(2,1)S(1)}, u32[]{:S(2)}, u32[]{:S(2)}) async-start(bf16[64,16,128]{2,1,0:T(8,128)(2,1)} %broadcast_in_dim.51), calls=%async_computation.4 | async-start | bytes 524288 | tf_op jit(solution)/shard_map/all_to_all | solution.py:20
  126.9 3.6 %copy-start = (bf16[256,4096]{1,0:T(8,128)(2,1)S(1)}, bf16[256,4096]{1,0:T(8,128)(2,1)}, u32[]{:S(2)}) copy-start(bf16[256,4096]{1,0:T(8,128)(2,1)} %get-tuple-element.25) | copy-start | bytes 6291460
  130.4 7.6 %copy-start.2 = (f32[1,64,64,16]{1,3,2,0:T(8,128)S(1)}, f32[1,64,64,16]{1,3,2,0:T(8,128)}, u32[]{:S(2)}) copy-start(f32[1,64,64,16]{1,3,2,0:T(8,128)} %copy.45) | copy-start | bytes 786436
  130.4 7.6 %copy-start.3 = (f32[1,64,64,16]{1,3,2,0:T(8,128)S(1)}, f32[1,64,64,16]{1,3,2,0:T(8,128)}, u32[]{:S(2)}) copy-start(f32[1,64,64,16]{1,3,2,0:T(8,128)} %copy.47) | copy-start | bytes 786436
  141.5 19.3 %all-to-all-start.5 = ((bf16[64,16,128]{2,1,0:T(8,128)(2,1)}), bf16[64,16,128]{2,1,0:T(8,128)(2,1)S(1)}, u32[]{:S(2)}, u32[]{:S(2)}) async-start(bf16[64,16,128]{2,1,0:T(8,128)(2,1)} %broadcast_in_dim.52), calls=%async_computation.5 | async-start | bytes 524288 | tf_op jit(solution)/shard_map/all_to_all | solution.py:20
  151.7 4.7 %copy-start.1 = (f32[64,2048]{1,0:T(8,128)S(1)}, f32[64,2048]{1,0:T(8,128)}, u32[]{:S(2)}) copy-start(f32[64,2048]{1,0:T(8,128)} %param.19) | copy-start | bytes 1572868
  152.7 22.1 %collective-permute-start.9 = (bf16[32,4096]{1,0:T(8,128)(2,1)}, bf16[32,4096]{1,0:T(8,128)(2,1)}, u32[]{:S(2)}, u32[]{:S(2)}) collective-permute-start(bf16[32,4096]{1,0:T(8,128)(2,1)} %get-tuple-element.44), channel_id=1, source_target_pairs={{0,64},{64,0},{128,192},{192,128},{1,65},{65,1},{129,193},{193,129... | collective-permute-start | bytes 786440 | tf_op jit(solution)/shard_map/ppermute | solution.py:39
  152.7 22.1 %collective-permute-start.11 = (bf16[32,4096]{1,0:T(8,128)(2,1)}, bf16[32,4096]{1,0:T(8,128)(2,1)}, u32[]{:S(2)}, u32[]{:S(2)}) collective-permute-start(bf16[32,4096]{1,0:T(8,128)(2,1)} %get-tuple-element.45), channel_id=1, source_target_pairs={{0,192},{64,128},{128,64},{192,0},{1,193},{65,129},{129,65},{193,1... | collective-permute-start | bytes 786440 | tf_op jit(solution)/shard_map/ppermute | solution.py:39
  153.4 21.4 %collective-permute-start.10 = (bf16[32,4096]{1,0:T(8,128)(2,1)}, bf16[32,4096]{1,0:T(8,128)(2,1)}, u32[]{:S(2)}, u32[]{:S(2)}) collective-permute-start(bf16[32,4096]{1,0:T(8,128)(2,1)} %get-tuple-element.46), channel_id=1, source_target_pairs={{0,128},{64,192},{128,0},{192,64},{1,129},{65,193},{129,1},{193,65... | collective-permute-start | bytes 786440 | tf_op jit(solution)/shard_map/ppermute | solution.py:39
  160.8 25.2 %copy-start.4 = (f32[256,512]{0,1:T(8,128)S(1)}, f32[256,512]{0,1:T(8,128)}, u32[]{:S(2)}) copy-start(f32[256,512]{0,1:T(8,128)} %reshape.167) | copy-start | bytes 1572868
  163.6 22.4 %all-to-all-start.6 = ((bf16[64,16,128]{2,1,0:T(8,128)(2,1)}), bf16[64,16,128]{2,1,0:T(8,128)(2,1)S(1)}, u32[]{:S(2)}, u32[]{:S(2)}) async-start(bf16[64,16,128]{2,1,0:T(8,128)(2,1)} %broadcast_in_dim.53), calls=%async_computation.6 | async-start | bytes 524288 | tf_op jit(solution)/shard_map/all_to_all | solution.py:20

commit v4 on v1

v4 whole, which is shorter than its diff:
```python
import jax
import jax.numpy as jnp
from jax import lax
from jax.experimental import pallas as pl
from jax.experimental.pallas import tpu as pltpu
from jax.sharding import PartitionSpec as P

BF = jnp.bfloat16
F32 = jnp.float32
LANES = 128
PLANES = 4
HALVES = 2
TILE = 512
VMEM = pl.BlockSpec(memory_space=pltpu.VMEM)


def exchanged(pieces, axis, parts=1):
    size = lax.axis_size(axis) // parts
    groups = [[part * size + i for i in range(size)] for part in range(parts)]
    return lax.all_to_all(
        pieces, axis, 0, 0, tiled=True, axis_index_groups=groups if parts > 1 else None
    )


def copies(x, count):
    return jnp.broadcast_to(x[None], (count, *x.shape))


def swapped(x, axis, bits):
    return lax.ppermute(x, axis, [(i, i ^ bits) for i in range(lax.axis_size(axis))])


def pick(x, index):
    return lax.dynamic_index_in_dim(x, index, 0, keepdims=False)


def kernel_block(points_ref, centers_ref, norm_ref, coef_ref, kernel_ref, value_ref, slots, sems):
    samples = points_ref[...]
    wide = samples.astype(F32)
    left = 0.5 * jnp.sum(wide * wide, axis=1, keepdims=True)
    total = jnp.zeros(value_ref.shape, F32)
    saves = []
    for i in range(centers_ref.shape[0] // TILE):
        rows = pl.ds(i * TILE, TILE)
        products = lax.dot_general(
            samples, centers_ref[rows, :], (((1,), (1,)), ((), ())), preferred_element_type=F32
        )
        block = jnp.exp(products - left - norm_ref[:, rows]).astype(BF)
        slots[i] = block
        saves.append(pltpu.make_async_copy(slots.at[i], kernel_ref.at[:, rows], sems.at[i]))
        saves[-1].start()
        total += jnp.dot(block, coef_ref[rows, :], preferred_element_type=F32)
    value_ref[...] = total.astype(value_ref.dtype)
    for save in saves:
        save.wait()


def kernel_and_value(samples, anchors, norms, coefficients):
    count, depth = samples.shape
    total, cols = coefficients.shape
    steps = total // TILE
    return pl.pallas_call(
        kernel_block,
        out_shape=(pltpu.HBM((count, total), BF), jax.ShapeDtypeStruct((count, cols), BF)),
        in_specs=[VMEM] * 4,
        out_specs=[pl.BlockSpec(memory_space=pltpu.HBM), VMEM],
        scratch_shapes=[pltpu.VMEM((steps, count, TILE), BF), pltpu.SemaphoreType.DMA((steps,))],
        compiler_params=pltpu.CompilerParams(vmem_limit_bytes=24 * 1024 * 1024),
        cost_estimate=pl.CostEstimate(
            flops=2 * count * total * (depth + cols),
            bytes_accessed=2 * count * total,
            transcendentals=count * total,
        ),
    )(samples, pltpu.with_memory_space_constraint(anchors, pltpu.VMEM), norms, coefficients)


def lane_block(shape, width, index):
    lane = lax.broadcasted_iota(jnp.int32, shape, len(shape) - 1)
    return (lane >= index * width) & (lane < (index + 1) * width)


def turned(x, lanes):
    lanes = lanes % LANES
    return pltpu.roll(x, lanes, 1) if lanes else x


def folded_sum(product, fold, strip, blocks):
    width = LANES // fold
    out = None
    for f in range(fold):
        total = None
        for r in blocks:
            row = (r * fold + f) * strip
            part = turned(product[row : row + strip, :], (f - r) * width)
            total = part if total is None else total + part
        out = total if out is None else jnp.where(lane_block(total.shape, width, f), total, out)
    return out


def first_step(matrix_ref, window_ref, sent_ref, low_ref, high_ref):
    strip = sent_ref.shape[1]
    fold = int(round((matrix_ref.shape[0] // strip) ** 0.5))
    product = jnp.dot(matrix_ref[...], window_ref[...], preferred_element_type=F32)
    low = folded_sum(product, fold, strip, range(fold // HALVES))
    high = folded_sum(product, fold, strip, range(fold // HALVES, fold))
    low_ref[...] = low
    high_ref[...] = high
    sent_ref[...] = jnp.broadcast_to(low.astype(BF)[None], sent_ref.shape)


def middle_step(matrix_ref, solved_ref, sent_ref):
    strip = sent_ref.shape[1]
    fold = int(round((matrix_ref.shape[0] // strip) ** 0.5))
    product = jnp.dot(matrix_ref[...], solved_ref[...], preferred_element_type=F32)
    total = folded_sum(product, fold, strip, range(fold))
    sent_ref[...] = jnp.broadcast_to(total.astype(BF)[None], sent_ref.shape)


def last_step(matrix_ref, update_ref, high_ref, out_ref):
    strip = out_ref.shape[0]
    fold = int(round((matrix_ref.shape[0] // strip) ** 0.5))
    product = jnp.dot(matrix_ref[...], update_ref[...], preferred_element_type=F32)
    out_ref[...] = high_ref[...] - folded_sum(product, fold, strip, range(fold))


def window_step(chosen_ref, residual_ref, pieces_ref):
    window = lax.dot_general(
        chosen_ref[...], residual_ref[...], (((0,), (0,)), ((), ())), preferred_element_type=F32
    )
    groups, strip, _ = pieces_ref.shape
    width = LANES // groups
    for p in range(groups):
        out = None
        for r in range(window.shape[0] // strip):
            part = turned(window[r * strip : (r + 1) * strip, :], (r - p) * width)
            out = part if out is None else jnp.where(lane_block(part.shape, width, r), part, out)
        pieces_ref[p] = out


def whole(body, shapes, *args):
    return pl.pallas_call(
        body,
        out_shape=shapes,
        in_specs=[VMEM] * len(args),
        out_specs=jax.tree.map(lambda _: VMEM, shapes),
        compiler_params=pltpu.CompilerParams(vmem_limit_bytes=16 * 1024 * 1024),
    )(*args)


def half_norm(rows):
    return 0.5 * jnp.sum(jnp.square(rows.astype(F32)), axis=-1)


def class_lookup(labels, table):
    classes = jnp.arange(table.shape[0], dtype=jnp.int32)
    return jnp.sum(jnp.where(labels[:, None] == classes[None, :], table[None, :], 0.0), axis=1)


def body(
    points,
    point_class,
    targets,
    class_weight,
    inv_scale,
    centers,
    coefficients,
    center_index,
    factor,
    panel_inverse,
):
    groups = lax.axis_size("pts")
    shards = lax.axis_size("ctr")
    shard = lax.axis_index("ctr")
    group = lax.axis_index("pts")
    own_points, depth = points.shape
    shard_rows = centers.shape[0]
    target_count = targets.shape[1]
    target_slice = target_count // groups
    own_rows = center_index.shape[0] // shards
    panel_rows = panel_inverse.shape[1]
    panel_shards = panel_rows // own_rows
    panel = shard // panel_shards
    fold = LANES // target_slice
    strip = own_rows // fold
    plane_size = shards // PLANES
    plane = shard // plane_size
    plane_points = plane_size * own_points

    own_scaled = (points.astype(F32) * inv_scale[None, :]).astype(BF)
    plane_rows = exchanged(copies(own_scaled, plane_size), "ctr", PLANES)
    plane_rows = plane_rows.reshape(plane_points, depth)
    chunks = [plane_rows] + [None] * (PLANES - 1)
    for k in (2, 1, 3):
        chunks[k] = swapped(plane_rows, "ctr", k * plane_size)

    scaled_centers = (centers.astype(F32) * inv_scale[None, :]).astype(BF)
    center_norm = half_norm(scaled_centers)

    blocks = center_index.reshape(own_rows, shards)
    order = blocks[0] // shard_rows
    here = order == shard
    local = jnp.sum(jnp.where(here[None, :], blocks - shard * shard_rows, 0), axis=1)
    choose = (local[:, None] == jnp.arange(shard_rows, dtype=jnp.int32)[None, :]).astype(BF)
    chosen = jnp.dot(choose, scaled_centers, preferred_element_type=F32).astype(BF)
    chosen_norm = half_norm(chosen)
    place = (order[:, None] == jnp.arange(shards, dtype=jnp.int32)[None, :]).astype(BF)

    inverse = panel_inverse.astype(BF)
    count = panel_rows // (strip * shards)
    turned_inverse = jnp.einsum(
        "rhqj,js->hrsq", inverse.reshape(own_rows, count, strip, shards), place
    ).reshape(count * own_rows, shards * strip)
    other_inverse = swapped(turned_inverse, "ctr", panel_shards)

    kernels = [None] * PLANES
    arrived = None
    for k in (0, 1, 3, 2):
        kernels[k], value = kernel_and_value(
            chunks[k], scaled_centers, center_norm[None, :], coefficients
        )
        value = value if k == 0 else swapped(value, "ctr", k * plane_size)
        value = value.astype(F32)
        arrived = value if arrived is None else arrived + value
    arrived, inverse, factor, chosen = lax.optimization_barrier(
        (arrived, inverse, factor[:, :panel_rows].astype(BF), chosen)
    )

    def folded(matrix):
        m = matrix.reshape(own_rows, panel_shards, fold, strip)
        return m.transpose(2, 0, 1, 3).reshape(fold * own_rows, panel_shards * strip)

    factor_rows = folded(factor)
    inverse_rows = folded(inverse)
    solve_rows = jnp.concatenate(
        [
            jnp.where(panel == 0, turned_inverse, other_inverse),
            jnp.where(panel == 0, other_inverse, turned_inverse),
        ],
        axis=0,
    )
    near = jnp.stack(chunks)
    products = lax.dot_general(
        near, chosen, (((2,), (1,)), ((), ())), preferred_element_type=F32
    )
    chosen_kernel = jnp.exp(products - half_norm(near)[:, :, None] - chosen_norm).astype(BF)
    chosen_kernel = jnp.concatenate([pick(chosen_kernel, plane ^ k) for k in range(PLANES)], axis=0)

    own_weight = class_lookup(point_class, class_weight)
    shares = exchanged(
        arrived.astype(BF).reshape(plane_size, own_points, target_count), "ctr", PLANES
    )
    predicted = jnp.sum(shares.astype(F32), axis=0)
    own_residual = (own_weight[:, None] * (predicted - targets)).astype(BF)
    residual = exchanged(copies(own_residual, shards), "ctr")
    residual = residual.reshape(shards * own_points, target_count)

    pieces = whole(
        window_step, jax.ShapeDtypeStruct((groups, strip, LANES), F32), chosen_kernel, residual
    )
    pieces = exchanged(pieces, "pts")
    window = jnp.sum(pieces, axis=0).astype(BF)
    window = exchanged(copies(window, shards), "ctr").reshape(shards * strip, LANES)

    planes = residual.reshape(PLANES, plane_points, target_count)
    backward = None
    for k in range(PLANES):
        part = lax.dot_general(
            pick(planes, plane ^ k), kernels[k], (((0,), (0,)), ((), ())), preferred_element_type=F32
        )
        backward = part if backward is None else backward + part
    backward = backward.reshape(groups, target_slice, shard_rows)
    near_pair = jnp.stack([pick(backward, group), pick(backward, group ^ 2)])
    far_pair = jnp.stack([pick(backward, group ^ 1), pick(backward, group ^ 3)]).astype(BF)
    near_pair = near_pair + swapped(far_pair, "pts", 1).astype(F32)
    gradient = near_pair[0] + swapped(near_pair[1].astype(BF), "pts", 2).astype(F32)
    gradient = gradient.T

    half = shards // HALVES
    sent = jax.ShapeDtypeStruct((half, strip, LANES), BF)
    packed = jax.ShapeDtypeStruct((strip, LANES), F32)
    first, low, high = whole(first_step, (sent, packed, packed), solve_rows, window)
    first = exchanged(first, "ctr", HALVES).reshape(half * strip, LANES)
    update = whole(middle_step, sent, factor_rows, first)
    update = exchanged(update, "ctr", HALVES).reshape(half * strip, LANES)
    changed = whole(last_step, packed, inverse_rows, update, high)
    solved = jnp.where(panel == 0, low, changed)
    solved = solved.reshape(strip, fold, target_slice).transpose(1, 0, 2)
    return (gradient, solved.reshape(own_rows, target_slice))


def solution(mesh):
    placed = (
        P(("pts", "ctr"), None),
        P(("pts", "ctr")),
        P(("pts", "ctr"), None),
        P(),
        P(),
        P("ctr", None),
        P("ctr", None),
        P(),
        P("ctr", None),
        P("ctr", None),
    )
    return jax.shard_map(
        body,
        mesh=mesh,
        in_specs=placed,
        out_specs=(P("ctr", "pts"), P("ctr", "pts")),
        check_vma=False,
    )
```

time: 190 us -> 158 us (0.83)
  waiting for transfers between devices: 73.6 us -> 50.2 us
  matrix products: 26.9 us -> 7.76 us
  Pallas kernels: 0 us -> 16.1 us
  local copies, waits for them, and re-layouts: 21.5 us -> 15.3 us
  other arithmetic: 7.9 us -> 14 us
  starting transfers between devices: 58 us -> 52.5 us
    all_to_all x8 -> x7, waiting for transfers between devices: 73.6 us -> 45.4 us  [exchanged(): lax.all_to_all(pieces, axis, 0, 0, tiled=True, axis_index_groups=groups i...]
    dot_general x8 -> x6, matrix products: 23.5 us -> 4.49 us  [the longest x4 3.76 us: body(): lax.dot_general(pick(planes, plane ^ k), kernels[k], (((0,), (0,)), ((),...]
    pallas_call x0 -> x8, Pallas kernels: none -> 16.1 us  [the longest x4 13 us: kernel_and_value(): pl.pallas_call(kernel_block, out_shape=(pltpu.HBM((count, total), BF), ja...]
    all_to_all x8 -> x7, starting transfers between devices: 58 us -> 44 us  [exchanged(): lax.all_to_all(pieces, axis, 0, 0, tiled=True, axis_index_groups=groups i...]
    ppermute x0 -> x9, starting transfers between devices: none -> 8.55 us  [swapped(): lax.ppermute(x, axis, [(i, i ^ bits) for i in range(lax.axis_size(axis))])]
    ppermute x0 -> x9, waiting for transfers between devices: none -> 4.76 us  [swapped(): lax.ppermute(x, axis, [(i, i ^ bits) for i in range(lax.axis_size(axis))])]
    select_n x4 -> x0, local copies, waits for them, and re-layouts: 4.47 us -> none  [body(): jnp.where(panel == i // halves, inverse_window[i % halves], 0.0)]
    add x0 -> x2, other arithmetic: none -> 2 us  [the longest x1 1.33 us: body(): near_pair = near_pair + swapped(far_pair, 'pts', 1).astype(F32)]
  transfers between devices with their start and end apart: 8 -> 16, of which waited for: 8 -> 8; matrix products, arithmetic and copies ran while one was open for 16% -> 16% of each run, Pallas kernels for 0% -> 10%
where the time goes in v4:
time: 158 us; the launch traced here: 157 us
  starting transfers between devices  52.5 us (33%)
  waiting for transfers between devices  50.2 us (32%)
  Pallas kernels  16.1 us (10%)
  local copies, waits for them, and re-layouts  15.3 us (10%)
  other arithmetic  14 us (9%)
  matrix products  7.76 us (5%)
    all_to_all x7, waiting for transfers between devices, exchanged(): lax.all_to_all(pieces, axis, 0, 0, tiled=True, axis_index_groups=groups i...  45.4 us
    all_to_all x7, starting transfers between devices, exchanged(): lax.all_to_all(pieces, axis, 0, 0, tiled=True, axis_index_groups=groups i...  44 us
    pallas_call x4, Pallas kernels, kernel_and_value(): pl.pallas_call(kernel_block, out_shape=(pltpu.HBM((count, total), BF), ja...  13 us
    ppermute x9, starting transfers between devices, swapped(): lax.ppermute(x, axis, [(i, i ^ bits) for i in range(lax.axis_size(axis))])  8.55 us
    unnamed x24, local copies, waits for them, and re-layouts  6.39 us
    reduce_sum x2, other arithmetic, half_norm(): return 0.5 * jnp.sum(jnp.square(rows.astype(F32)), axis=-1)  5.63 us
    ppermute x9, waiting for transfers between devices, swapped(): lax.ppermute(x, axis, [(i, i ^ bits) for i in range(lax.axis_size(axis))])  4.76 us
    dot_general x4, matrix products, body(): lax.dot_general(pick(planes, plane ^ k), kernels[k], (((0,), (0,)), ((),...  3.76 us
  transfers between devices with their start and end apart: 16, of which 8 were waited for; matrix products, arithmetic and copies ran while one was open for 16% of the time, Pallas kernels for 10%

profile of v4, /device:TPU:4, one launch (start us, length us, event | category | flops | bytes accessed | tf_op | source)
XLA Modules:
  0.0 157.0 jit_solution(7243248769200730163)
XLA Ops:
  0.6 0.7 multiply_convert_fusion.1
  1.4 0.7 broadcast_in_dim.28
  2.1 9.6 %all-to-all-start = ((bf16[16,16,512]{2,1,0:T(8,128)(2,1)}), bf16[16,16,512]{2,1,0:T(8,128)(2,1)S(1)}, u32[]{:S(2)}, u32[]{:S(2)}) async-start(bf16[16,16,512]{2,1,0:T(8,128)(2,1)} %broadcast_in_dim.28), calls=%async_computation | async-start | bytes 524288 | tf_op jit(solution)/shard_map/all_to_all | solution.py:20
  11.7 1.3 copy.55
  13.0 0.7 broadcast_compare_fusion
  15.6 5.4 %multiply_reduce_fusion = (f32[4096]{0:T(1024)S(1)}, bf16[4096,512]{1,0:T(8,128)(2,1)}) fusion(f32[512]{0:T(512)S(1)} %copy-done.7, bf16[4096,512]{1,0:T(8,128)(2,1)} %param.15), kind=kLoop, calls=%fused_computation | loop fusion | flops 12578816 | bytes 8407040 | tf_op jit(solution)/shard_map/reduce_sum | solution.py:151
  21.2 3.3 %multiply_reduce_fusion.2 = (f32[64]{0:T(128)S(1)}, bf16[64,512]{1,0:T(8,128)(2,1)S(1)}) fusion(bf16[4096,512]{1,0:T(8,128)(2,1)} %get-tuple-element.41.centers_ref, s32[64]{0:T(128)S(1)} %select_reduce_fusion), kind=kOutput, calls=%fused_computation.29 | convolution fusion | flops 268828608 | bytes 4260352 | tf_op jit(solution)/shard_map/dot_general | solution.py:204
  24.4 2.2 %collective-permute-start = (bf16[256,512]{1,0:T(8,128)(2,1)S(1)}, bf16[256,512]{1,0:T(8,128)(2,1)S(1)}, u32[]{:S(2)}, u32[]{:S(2)}) collective-permute-start(bf16[256,512]{1,0:T(8,128)(2,1)S(1)} %bitcast.76), channel_id=1, source_target_pairs={{0,16},{1,17},{2,18},{3,19},{4,20},{5,21},{6,22},{7,23},{8,24},{9,... | collective-permute-start | bytes 786440 | tf_op jit(solution)/shard_map/ppermute | solution.py:30
  26.6 1.5 collective-permute-start.4
  28.3 1.8 %slice.32 = bf16[64,2048]{1,0:T(8,128)(2,1)} slice(f32[64,4096]{1,0:T(8,128)} %param.18), slice={[0:64], [0:2048]} | slice | bytes 524288 | tf_op jit(solution)/shard_map/slice | solution.py:225
  30.1 3.8 %collective-permute-done.points_ref = bf16[256,512]{1,0:T(8,128)(2,1)S(1)} collective-permute-done((bf16[256,512]{1,0:T(8,128)(2,1)S(1)}, bf16[256,512]{1,0:T(8,128)(2,1)S(1)}, u32[]{:S(2)}, u32[]{:S(2)}) %collective-permute-start) | collective-permute-done | bytes 262176 | tf_op jit(solution)/shard_map/ppermute | solution.py:30
  33.8 2.2 %copy-done = bf16[4096,512]{1,0:T(8,128)(2,1)S(1)} copy-done((bf16[4096,512]{1,0:T(8,128)(2,1)S(1)}, bf16[4096,512]{1,0:T(8,128)(2,1)}, u32[]{:S(2)}) %copy-start) | copy-done | bytes 4194328
  36.0 3.3 %shard_map.114 = (bf16[256,4096]{1,0:T(8,128)(2,1)}, bf16[256,128]{1,0:T(8,128)(2,1)S(1)}) custom-call(bf16[256,512]{1,0:T(8,128)(2,1)S(1)} %collective-permute-done.points_ref, bf16[4096,512]{1,0:T(8,128)(2,1)S(1)} %copy-done, f32[1,4096]{1,0:T(1,128)S(1)} %bitcast.91, bf16[4096,128]{1,0:T(8,128)(2,1)S(1)} %copy-done.1), custom_call_target="tpu_custom_call" | custom-call | flops 1342177280 | bytes 2097152 | tf_op jit(solution)/shard_map/pallas_call | solution.py:62
  39.3 2.1 %collective-permute-start.1 = (bf16[256,128]{1,0:T(8,128)(2,1)S(1)}, bf16[256,128]{1,0:T(8,128)(2,1)S(1)}, u32[]{:S(2)}, u32[]{:S(2)}) collective-permute-start(bf16[256,128]{1,0:T(8,128)(2,1)S(1)} %get-tuple-element.18), channel_id=1, source_target_pairs={{0,16},{1,17},{2,18},{3,19},{4,20},{5,21},{6,22},{7,23},{8,24},{9,... | collective-permute-start | bytes 196616 | tf_op jit(solution)/shard_map/ppermute | solution.py:30
  41.4 3.3 %shard_map.116 = (bf16[256,4096]{1,0:T(8,128)(2,1)}, bf16[256,128]{1,0:T(8,128)(2,1)S(1)}) custom-call(bf16[256,512]{1,0:T(8,128)(2,1)S(1)} %collective-permute-done.4.points_ref, bf16[4096,512]{1,0:T(8,128)(2,1)S(1)} %copy-done, f32[1,4096]{1,0:T(1,128)S(1)} %bitcast.92, bf16[4096,128]{1,0:T(8,128)(2,1)S(1)} %copy-done.1), custom_call_target="tpu_custom_call" | custom-call | flops 1342177280 | bytes 2097152 | tf_op jit(solution)/shard_map/pallas_call | solution.py:62
  44.7 1.8 %collective-permute-start.5 = (bf16[256,128]{1,0:T(8,128)(2,1)S(1)}, bf16[256,128]{1,0:T(8,128)(2,1)S(1)}, u32[]{:S(2)}, u32[]{:S(2)}) collective-permute-start(bf16[256,128]{1,0:T(8,128)(2,1)S(1)} %get-tuple-element.20), channel_id=1, source_target_pairs={{0,32},{1,33},{2,34},{3,35},{4,36},{5,37},{6,38},{7,39},{8,40},{9,... | collective-permute-start | bytes 196616 | tf_op jit(solution)/shard_map/ppermute | solution.py:30
  46.5 3.3 %shard_map.115 = (bf16[256,4096]{1,0:T(8,128)(2,1)}, bf16[256,128]{1,0:T(8,128)(2,1)S(1)}) custom-call(bf16[256,512]{1,0:T(8,128)(2,1)S(1)} %collective-permute-done.2.points_ref, bf16[4096,512]{1,0:T(8,128)(2,1)S(1)} %copy-done, f32[1,4096]{1,0:T(1,128)S(1)} %bitcast.93, bf16[4096,128]{1,0:T(8,128)(2,1)S(1)} %copy-done.1), custom_call_target="tpu_custom_call" | custom-call | flops 1342177280 | bytes 2097152 | tf_op jit(solution)/shard_map/pallas_call | solution.py:62
  49.8 3.2 %shard_map.113 = (bf16[256,4096]{1,0:T(8,128)(2,1)}, bf16[256,128]{1,0:T(8,128)(2,1)S(1)}) custom-call(bf16[256,512]{1,0:T(8,128)(2,1)S(1)} %bitcast.79, bf16[4096,512]{1,0:T(8,128)(2,1)S(1)} %copy-done, f32[1,4096]{1,0:T(1,128)S(1)} %bitcast.94, bf16[4096,128]{1,0:T(8,128)(2,1)S(1)} %copy-done.1), custom_call_target="tpu_custom_call" | custom-call | flops 1342177280 | bytes 2097152 | tf_op jit(solution)/shard_map/pallas_call | solution.py:62
  53.1 1.0 collective-permute-done.3
  54.1 0.7 convert_add_fusion
  54.8 8.1 %all-to-all-start.1 = ((bf16[16,16,128]{2,1,0:T(8,128)(2,1)}), bf16[16,16,128]{2,1,0:T(8,128)(2,1)S(1)}, u32[]{:S(2)}, u32[]{:S(2)}) async-start(bf16[16,16,128]{2,1,0:T(8,128)(2,1)} %bitcast.2), calls=%async_computation.1 | async-start | bytes 131072 | tf_op jit(solution)/shard_map/all_to_all | solution.py:20
  62.9 0.9 broadcast_select_fusion.1
  64.1 7.9 %all-to-all-done.1 = bf16[16,16,128]{2,1,0:T(8,128)(2,1)S(1)} async-done(((bf16[16,16,128]{2,1,0:T(8,128)(2,1)}), bf16[16,16,128]{2,1,0:T(8,128)(2,1)S(1)}, u32[]{:S(2)}, u32[]{:S(2)}) %all-to-all-start.1) | async-done | bytes 65568 | tf_op jit(solution)/shard_map/all_to_all | solution.py:20
  72.0 0.7 broadcast_in_dim.31
  72.8 7.5 %all-to-all-start.2 = ((bf16[64,16,128]{2,1,0:T(8,128)(2,1)}), bf16[64,16,128]{2,1,0:T(8,128)(2,1)S(1)}, u32[]{:S(2)}, u32[]{:S(2)}) async-start(bf16[64,16,128]{2,1,0:T(8,128)(2,1)} %broadcast_in_dim.31), calls=%async_computation.2 | async-start | bytes 524288 | tf_op jit(solution)/shard_map/all_to_all | solution.py:20
  81.3 8.9 %all-to-all-done.2 = bf16[64,16,128]{2,1,0:T(8,128)(2,1)S(1)} async-done(((bf16[64,16,128]{2,1,0:T(8,128)(2,1)}), bf16[64,16,128]{2,1,0:T(8,128)(2,1)S(1)}, u32[]{:S(2)}, u32[]{:S(2)}) %all-to-all-start.2) | async-done | bytes 262176 | tf_op jit(solution)/shard_map/all_to_all | solution.py:20
  90.2 2.2 %fusion.13 = f32[128,4096]{1,0:T(8,128)S(1)} fusion(bf16[256,4096]{1,0:T(8,128)(2,1)} %get-tuple-element.22, bf16[4,256,128]{2,1,0:T(8,128)(2,1)S(1)} %bitcast.71, s32[]{:T(128)S(6)} %select_n.76), kind=kOutput, calls=%fused_computation.37 | convolution fusion | flops 268435456 | bytes 4259844 | tf_op jit(solution)/shard_map/dot_general | solution.py:267
  92.9 1.1 copy-done.2
  94.5 1.1 copy-done.4
  96.2 0.9 pad_maximum_fusion.1
  97.1 0.9 shard_map.117
  98.0 4.3 %all-to-all-start.3 = ((f32[4,16,128]{2,1,0:T(8,128)}), f32[4,16,128]{2,1,0:T(8,128)S(1)}, u32[]{:S(2)}, u32[]{:S(2)}) async-start(f32[4,16,128]{2,1,0:T(8,128)} %shard_map.117), calls=%async_computation.3 | async-start | bytes 65536 | tf_op jit(solution)/shard_map/all_to_all | solution.py:20
  102.3 0.9 constant_dynamic-slice_fusion.4
  103.2 4.6 %all-to-all-done.3 = f32[4,16,128]{2,1,0:T(8,128)S(1)} async-done(((f32[4,16,128]{2,1,0:T(8,128)}), f32[4,16,128]{2,1,0:T(8,128)S(1)}, u32[]{:S(2)}, u32[]{:S(2)}) %all-to-all-start.3) | async-done | bytes 32800 | tf_op jit(solution)/shard_map/all_to_all | solution.py:20
  107.8 0.7 broadcast_in_dim.36
  108.5 6.6 %all-to-all-start.4 = ((bf16[64,16,128]{2,1,0:T(8,128)(2,1)}), bf16[64,16,128]{2,1,0:T(8,128)(2,1)S(1)}, u32[]{:S(2)}, u32[]{:S(2)}) async-start(bf16[64,16,128]{2,1,0:T(8,128)(2,1)} %broadcast_in_dim.36), calls=%async_computation.4 | async-start | bytes 524288 | tf_op jit(solution)/shard_map/all_to_all | solution.py:20
  115.1 1.3 maximum_add_fusion
  116.4 0.7 fusion.7
  117.4 1.1 pad_maximum_fusion.2.matrix_ref
  118.4 7.9 %all-to-all-done.4 = bf16[64,16,128]{2,1,0:T(8,128)(2,1)S(1)} async-done(((bf16[64,16,128]{2,1,0:T(8,128)(2,1)}), bf16[64,16,128]{2,1,0:T(8,128)(2,1)S(1)}, u32[]{:S(2)}, u32[]{:S(2)}) %all-to-all-start.4) | async-done | bytes 262176 | tf_op jit(solution)/shard_map/all_to_all | solution.py:20
  126.3 1.0 shard_map.118
  127.3 4.1 %all-to-all-start.5 = ((bf16[32,16,128]{2,1,0:T(8,128)(2,1)}), bf16[32,16,128]{2,1,0:T(8,128)(2,1)S(1)}, u32[]{:S(2)}, u32[]{:S(2)}) async-start(bf16[32,16,128]{2,1,0:T(8,128)(2,1)} %get-tuple-element.30), calls=%async_computation.5 | async-start | bytes 262144 | tf_op jit(solution)/shard_map/all_to_all | solution.py:20
  133.2 8.1 %all-to-all-done.5 = bf16[32,16,128]{2,1,0:T(8,128)(2,1)S(1)} async-done(((bf16[32,16,128]{2,1,0:T(8,128)(2,1)}), bf16[32,16,128]{2,1,0:T(8,128)(2,1)S(1)}, u32[]{:S(2)}, u32[]{:S(2)}) %all-to-all-start.5) | async-done | bytes 131104 | tf_op jit(solution)/shard_map/all_to_all | solution.py:20
  141.3 0.9 shard_map.119
  142.2 3.8 %all-to-all-start.6 = ((bf16[32,16,128]{2,1,0:T(8,128)(2,1)}), bf16[32,16,128]{2,1,0:T(8,128)(2,1)S(1)}, u32[]{:S(2)}, u32[]{:S(2)}) async-start(bf16[32,16,128]{2,1,0:T(8,128)(2,1)} %shard_map.119), calls=%async_computation.6 | async-start | bytes 262144 | tf_op jit(solution)/shard_map/all_to_all | solution.py:20
  146.1 1.8 %fusion.5 = f32[4096,32]{0,1:T(8,128)} fusion(f32[2,32,4096]{2,1,0:T(8,128)S(1)} %maximum_add_fusion, bf16[32,4096]{1,0:T(8,128)(2,1)} %collective-permute-done.7), kind=kLoop, calls=%fused_computation.18 | loop fusion | flops 262144 | bytes 1310720 | tf_op jit(solution)/shard_map/transpose | solution.py:276
  147.9 8.0 %all-to-all-done.6 = bf16[32,16,128]{2,1,0:T(8,128)(2,1)S(1)} async-done(((bf16[32,16,128]{2,1,0:T(8,128)(2,1)}), bf16[32,16,128]{2,1,0:T(8,128)(2,1)S(1)}, u32[]{:S(2)}, u32[]{:S(2)}) %all-to-all-start.6) | async-done | bytes 131104 | tf_op jit(solution)/shard_map/all_to_all | solution.py:20
  156.3 0.7 copy.71
  (69 shorter events, 7.6 us)
Async XLA Ops:
  2.1 22.3 %all-to-all-start = ((bf16[16,16,512]{2,1,0:T(8,128)(2,1)}), bf16[16,16,512]{2,1,0:T(8,128)(2,1)S(1)}, u32[]{:S(2)}, u32[]{:S(2)}) async-start(bf16[16,16,512]{2,1,0:T(8,128)(2,1)} %broadcast_in_dim.28), calls=%async_computation | async-start | bytes 524288 | tf_op jit(solution)/shard_map/all_to_all | solution.py:20
  11.7 3.9 %copy-start.7 = (f32[512]{0:T(512)S(1)}, f32[512]{0:T(512)}, u32[]{:S(2)}) copy-start(f32[512]{0:T(512)} %param.14) | copy-start | bytes 6148
  15.0 6.0 %copy-start.6 = (s32[4096]{0:T(1024)S(1)}, s32[4096]{0:T(1024)}, u32[]{:S(2)}) copy-start(s32[4096]{0:T(1024)} %param.17) | copy-start | bytes 49156
  15.0 47.9 %collective-permute-start.8 = (bf16[128,1024]{1,0:T(8,128)(2,1)S(1)}, bf16[128,1024]{1,0:T(8,128)(2,1)S(1)}, u32[]{:S(2)}, u32[]{:S(2)}) collective-permute-start(bf16[128,1024]{1,0:T(8,128)(2,1)S(1)} %copy.59), channel_id=1, source_target_pairs={{0,32},{1,33},{2,34},{3,35},{4,36},{5,37},{6,38},{7,39},{8,40},{9,... | collective-permute-start | bytes 786440 | tf_op jit(solution)/shard_map/ppermute | solution.py:30
  21.1 7.1 %copy-start.9 = (f32[8]{0:T(128)S(1)}, f32[8]{0:T(128)}, u32[]{:S(2)}) copy-start(f32[8]{0:T(128)} %param.13) | copy-start | bytes 100
  21.1 7.1 %copy-start.10 = (s32[16]{0:T(128)S(1)}, s32[16]{0:T(128)}, u32[]{:S(2)}) copy-start(s32[16]{0:T(128)} %param.11) | copy-start | bytes 196
  21.1 12.7 %copy-start.1 = (bf16[4096,128]{1,0:T(8,128)(2,1)S(1)}, bf16[4096,128]{1,0:T(8,128)(2,1)}, u32[]{:S(2)}) copy-start(bf16[4096,128]{1,0:T(8,128)(2,1)} %coef_ref.7) | copy-start | bytes 3145732
  24.4 9.4 %collective-permute-start = (bf16[256,512]{1,0:T(8,128)(2,1)S(1)}, bf16[256,512]{1,0:T(8,128)(2,1)S(1)}, u32[]{:S(2)}, u32[]{:S(2)}) collective-permute-start(bf16[256,512]{1,0:T(8,128)(2,1)S(1)} %bitcast.76), channel_id=1, source_target_pairs={{0,16},{1,17},{2,18},{3,19},{4,20},{5,21},{6,22},{7,23},{8,24},{9,... | collective-permute-start | bytes 786440 | tf_op jit(solution)/shard_map/ppermute | solution.py:30
  26.6 14.8 %collective-permute-start.4 = (bf16[256,512]{1,0:T(8,128)(2,1)S(1)}, bf16[256,512]{1,0:T(8,128)(2,1)S(1)}, u32[]{:S(2)}, u32[]{:S(2)}) collective-permute-start(bf16[256,512]{1,0:T(8,128)(2,1)S(1)} %bitcast.77), channel_id=1, source_target_pairs={{0,32},{1,33},{2,34},{3,35},{4,36},{5,37},{6,38},{7,39},{8,40},{9,... | collective-permute-start | bytes 786440 | tf_op jit(solution)/shard_map/ppermute | solution.py:30
  28.1 18.3 %collective-permute-start.2 = (bf16[256,512]{1,0:T(8,128)(2,1)S(1)}, bf16[256,512]{1,0:T(8,128)(2,1)S(1)}, u32[]{:S(2)}, u32[]{:S(2)}) collective-permute-start(bf16[256,512]{1,0:T(8,128)(2,1)S(1)} %bitcast.78), channel_id=1, source_target_pairs={{0,48},{1,49},{2,50},{3,51},{4,52},{5,53},{6,54},{7,55},{8,56},{9,... | collective-permute-start | bytes 786440 | tf_op jit(solution)/shard_map/ppermute | solution.py:30
  33.8 2.2 %copy-start = (bf16[4096,512]{1,0:T(8,128)(2,1)S(1)}, bf16[4096,512]{1,0:T(8,128)(2,1)}, u32[]{:S(2)}) copy-start(bf16[4096,512]{1,0:T(8,128)(2,1)} %get-tuple-element.41.centers_ref) | copy-start | bytes 12582916
  39.3 13.8 %collective-permute-start.1 = (bf16[256,128]{1,0:T(8,128)(2,1)S(1)}, bf16[256,128]{1,0:T(8,128)(2,1)S(1)}, u32[]{:S(2)}, u32[]{:S(2)}) collective-permute-start(bf16[256,128]{1,0:T(8,128)(2,1)S(1)} %get-tuple-element.18), channel_id=1, source_target_pairs={{0,16},{1,17},{2,18},{3,19},{4,20},{5,21},{6,22},{7,23},{8,24},{9,... | collective-permute-start | bytes 196616 | tf_op jit(solution)/shard_map/ppermute | solution.py:30
  44.7 8.4 %collective-permute-start.5 = (bf16[256,128]{1,0:T(8,128)(2,1)S(1)}, bf16[256,128]{1,0:T(8,128)(2,1)S(1)}, u32[]{:S(2)}, u32[]{:S(2)}) collective-permute-start(bf16[256,128]{1,0:T(8,128)(2,1)S(1)} %get-tuple-element.20), channel_id=1, source_target_pairs={{0,32},{1,33},{2,34},{3,35},{4,36},{5,37},{6,38},{7,39},{8,40},{9,... | collective-permute-start | bytes 196616 | tf_op jit(solution)/shard_map/ppermute | solution.py:30
  49.7 4.4 %collective-permute-start.3 = (bf16[256,128]{1,0:T(8,128)(2,1)S(1)}, bf16[256,128]{1,0:T(8,128)(2,1)S(1)}, u32[]{:S(2)}, u32[]{:S(2)}) collective-permute-start(bf16[256,128]{1,0:T(8,128)(2,1)S(1)} %get-tuple-element.19), channel_id=1, source_target_pairs={{0,48},{1,49},{2,50},{3,51},{4,52},{5,53},{6,54},{7,55},{8,56},{9,... | collective-permute-start | bytes 196616 | tf_op jit(solution)/shard_map/ppermute | solution.py:30
  53.1 18.9 %copy-start.8 = (f32[16,128]{1,0:T(8,128)S(1)}, f32[16,128]{1,0:T(8,128)}, u32[]{:S(2)}) copy-start(f32[16,128]{1,0:T(8,128)} %param.12) | copy-start | bytes 24580
  54.8 17.2 %all-to-all-start.1 = ((bf16[16,16,128]{2,1,0:T(8,128)(2,1)}), bf16[16,16,128]{2,1,0:T(8,128)(2,1)S(1)}, u32[]{:S(2)}, u32[]{:S(2)}) async-start(bf16[16,16,128]{2,1,0:T(8,128)(2,1)} %bitcast.2), calls=%async_computation.1 | async-start | bytes 131072 | tf_op jit(solution)/shard_map/all_to_all | solution.py:20
  72.8 17.4 %all-to-all-start.2 = ((bf16[64,16,128]{2,1,0:T(8,128)(2,1)}), bf16[64,16,128]{2,1,0:T(8,128)(2,1)S(1)}, u32[]{:S(2)}, u32[]{:S(2)}) async-start(bf16[64,16,128]{2,1,0:T(8,128)(2,1)} %broadcast_in_dim.31), calls=%async_computation.2 | async-start | bytes 524288 | tf_op jit(solution)/shard_map/all_to_all | solution.py:20
  90.2 2.2 %copy-start.3 = (bf16[256,4096]{1,0:T(8,128)(2,1)S(1)}, bf16[256,4096]{1,0:T(8,128)(2,1)}, u32[]{:S(2)}) copy-start(bf16[256,4096]{1,0:T(8,128)(2,1)} %get-tuple-element.25) | copy-start | bytes 6291460
  92.4 1.6 %copy-start.2 = (bf16[256,4096]{1,0:T(8,128)(2,1)S(1)}, bf16[256,4096]{1,0:T(8,128)(2,1)}, u32[]{:S(2)}) copy-start(bf16[256,4096]{1,0:T(8,128)(2,1)} %get-tuple-element.23) | copy-start | bytes 6291460
  94.0 1.6 %copy-start.4 = (bf16[256,4096]{1,0:T(8,128)(2,1)S(1)}, bf16[256,4096]{1,0:T(8,128)(2,1)}, u32[]{:S(2)}) copy-start(bf16[256,4096]{1,0:T(8,128)(2,1)} %get-tuple-element.24) | copy-start | bytes 6291460
  97.0 18.0 %collective-permute-start.6 = (bf16[2,32,4096]{2,1,0:T(8,128)(2,1)}, bf16[2,32,4096]{2,1,0:T(8,128)(2,1)}, u32[]{:S(2)}, u32[]{:S(2)}) collective-permute-start(bf16[2,32,4096]{2,1,0:T(8,128)(2,1)} %pad_maximum_fusion.1), channel_id=1, source_target_pairs={{0,64},{64,0},{128,192},{192,128},{1,65},{65,1},{129,193},{193,129... | collective-permute-start | bytes 1572872 | tf_op jit(solution)/shard_map/ppermute | solution.py:30
  98.0 9.7 %all-to-all-start.3 = ((f32[4,16,128]{2,1,0:T(8,128)}), f32[4,16,128]{2,1,0:T(8,128)S(1)}, u32[]{:S(2)}, u32[]{:S(2)}) async-start(f32[4,16,128]{2,1,0:T(8,128)} %shard_map.117), calls=%async_computation.3 | async-start | bytes 65536 | tf_op jit(solution)/shard_map/all_to_all | solution.py:20
  108.5 17.8 %all-to-all-start.4 = ((bf16[64,16,128]{2,1,0:T(8,128)(2,1)}), bf16[64,16,128]{2,1,0:T(8,128)(2,1)S(1)}, u32[]{:S(2)}, u32[]{:S(2)}) async-start(bf16[64,16,128]{2,1,0:T(8,128)(2,1)} %broadcast_in_dim.36), calls=%async_computation.4 | async-start | bytes 524288 | tf_op jit(solution)/shard_map/all_to_all | solution.py:20
  115.1 16.3 %copy-start.5 = (bf16[64,2048]{1,0:T(8,128)(2,1)S(1)}, bf16[64,2048]{1,0:T(8,128)(2,1)}, u32[]{:S(2)}) copy-start(bf16[64,2048]{1,0:T(8,128)(2,1)} %slice.32) | copy-start | bytes 786436
  117.2 28.9 %collective-permute-start.7 = (bf16[32,4096]{1,0:T(8,128)(2,1)}, bf16[32,4096]{1,0:T(8,128)(2,1)}, u32[]{:S(2)}, u32[]{:S(2)}) collective-permute-start(bf16[32,4096]{1,0:T(8,128)(2,1)} %fusion.7), channel_id=1, source_target_pairs={{0,128},{64,192},{128,0},{192,64},{1,129},{65,193},{129,1},{193,65... | collective-permute-start | bytes 786440 | tf_op jit(solution)/shard_map/ppermute | solution.py:30
  127.3 14.0 %all-to-all-start.5 = ((bf16[32,16,128]{2,1,0:T(8,128)(2,1)}), bf16[32,16,128]{2,1,0:T(8,128)(2,1)S(1)}, u32[]{:S(2)}, u32[]{:S(2)}) async-start(bf16[32,16,128]{2,1,0:T(8,128)(2,1)} %get-tuple-element.30), calls=%async_computation.5 | async-start | bytes 262144 | tf_op jit(solution)/shard_map/all_to_all | solution.py:20
  142.2 13.7 %all-to-all-start.6 = ((bf16[32,16,128]{2,1,0:T(8,128)(2,1)}), bf16[32,16,128]{2,1,0:T(8,128)(2,1)S(1)}, u32[]{:S(2)}, u32[]{:S(2)}) async-start(bf16[32,16,128]{2,1,0:T(8,128)(2,1)} %shard_map.119), calls=%async_computation.6 | async-start | bytes 262144 | tf_op jit(solution)/shard_map/all_to_all | solution.py:20

commit v5 on v4

--- a/solution.py
+++ b/solution.py
@@ -34,44 +34,81 @@
     return lax.dynamic_index_in_dim(x, index, 0, keepdims=False)
 
 
-def kernel_block(points_ref, centers_ref, norm_ref, coef_ref, kernel_ref, value_ref, slots, sems):
-    samples = points_ref[...]
+def scale_step(centers_ref, scale_ref, scaled_ref, norm_ref, slots, sems):
+    loads = []
+    for i in range(slots.shape[0]):
+        rows = pl.ds(i * TILE, TILE)
+        loads.append(pltpu.make_async_copy(centers_ref.at[rows, :], slots.at[i], sems.at[i]))
+        loads[-1].start()
+    for i, load in enumerate(loads):
+        rows = pl.ds(i * TILE, TILE)
+        load.wait()
+        scaled = (slots[i].astype(F32) * scale_ref[...]).astype(BF)
+        scaled_ref[rows, :] = scaled
+        wide = scaled.astype(F32)
+        norm = 0.5 * jnp.sum(wide * wide, axis=1, keepdims=True)
+        norm_ref[:, rows] = jnp.broadcast_to(norm, (TILE, LANES)).T[0:1, :]
+
+
+def scaled_and_norm(centers, scale):
+    total, depth = centers.shape
+    steps = total // TILE
+    return pl.pallas_call(
+        scale_step,
+        out_shape=(pltpu.VMEM((total, depth), BF), jax.ShapeDtypeStruct((1, total), F32)),
+        in_specs=[pl.BlockSpec(memory_space=pltpu.HBM), VMEM],
+        out_specs=[VMEM, VMEM],
+        scratch_shapes=[pltpu.VMEM((steps, TILE, depth), BF), pltpu.SemaphoreType.DMA((steps,))],
+        compiler_params=pltpu.CompilerParams(vmem_limit_bytes=24 * 1024 * 1024),
+        cost_estimate=pl.CostEstimate(
+            flops=4 * total * depth, bytes_accessed=2 * total * depth, transcendentals=0
+        ),
+    )(pltpu.with_memory_space_constraint(centers, pltpu.HBM), scale)
+
+
+def kernel_block(
+    slot_ref, points_ref, scale_ref, centers_ref, norm_ref, coef_ref, *refs
+):
+    scaled_ref, kernel_ref, value_ref = refs[-3:]
+    samples = (points_ref[...].astype(F32) * scale_ref[...]).astype(BF)
+    scaled_ref[...] = samples
     wide = samples.astype(F32)
     left = 0.5 * jnp.sum(wide * wide, axis=1, keepdims=True)
-    total = jnp.zeros(value_ref.shape, F32)
-    saves = []
+    total = jnp.zeros(value_ref.shape[1:], F32)
     for i in range(centers_ref.shape[0] // TILE):
         rows = pl.ds(i * TILE, TILE)
         products = lax.dot_general(
             samples, centers_ref[rows, :], (((1,), (1,)), ((), ())), preferred_element_type=F32
         )
         block = jnp.exp(products - left - norm_ref[:, rows]).astype(BF)
-        slots[i] = block
-        saves.append(pltpu.make_async_copy(slots.at[i], kernel_ref.at[:, rows], sems.at[i]))
-        saves[-1].start()
+        kernel_ref[:, rows] = block
         total += jnp.dot(block, coef_ref[rows, :], preferred_element_type=F32)
-    value_ref[...] = total.astype(value_ref.dtype)
-    for save in saves:
-        save.wait()
-
-
-def kernel_and_value(samples, anchors, norms, coefficients):
+    if len(refs) > 3:
+        value_ref[...] = refs[0][...]
+    value_ref[slot_ref[0]] = total.astype(value_ref.dtype)
+
+
+def kernel_and_value(slot, samples, scale, anchors, norms, coefficients, values=None):
     count, depth = samples.shape
     total, cols = coefficients.shape
-    steps = total // TILE
+    args = [samples, scale, pltpu.with_memory_space_constraint(anchors, pltpu.VMEM)]
+    args += [norms, coefficients] + ([] if values is None else [values])
     return pl.pallas_call(
         kernel_block,
-        out_shape=(pltpu.HBM((count, total), BF), jax.ShapeDtypeStruct((count, cols), BF)),
-        in_specs=[VMEM] * 4,
-        out_specs=[pl.BlockSpec(memory_space=pltpu.HBM), VMEM],
-        scratch_shapes=[pltpu.VMEM((steps, count, TILE), BF), pltpu.SemaphoreType.DMA((steps,))],
+        out_shape=(
+            jax.ShapeDtypeStruct((count, depth), BF),
+            pltpu.VMEM((count, total), BF),
+            jax.ShapeDtypeStruct((PLANES, count, cols), BF),
+        ),
+        in_specs=[pl.BlockSpec(memory_space=pltpu.SMEM)] + [VMEM] * len(args),
+        out_specs=[VMEM] * 3,
         compiler_params=pltpu.CompilerParams(vmem_limit_bytes=24 * 1024 * 1024),
         cost_estimate=pl.CostEstimate(
             flops=2 * count * total * (depth + cols),
             bytes_accessed=2 * count * total,
             transcendentals=count * total,
         ),
-    )(samples, pltpu.with_memory_space_constraint(anchors, pltpu.VMEM), norms, coefficients)
+    )(slot, *args)
 
 
 def lane_block(shape, width, index):
@@ -116,32 +153,43 @@
     sent_ref[...] = jnp.broadcast_to(total.astype(BF)[None], sent_ref.shape)
 
 
-def last_step(matrix_ref, update_ref, high_ref, out_ref):
-    strip = out_ref.shape[0]
+def last_step(panel_ref, matrix_ref, update_ref, low_ref, high_ref, out_ref):
+    strip = low_ref.shape[0]
     fold = int(round((matrix_ref.shape[0] // strip) ** 0.5))
+    width = LANES // fold
     product = jnp.dot(matrix_ref[...], update_ref[...], preferred_element_type=F32)
-    out_ref[...] = high_ref[...] - folded_sum(product, fold, strip, range(fold))
-
-
-def window_step(chosen_ref, residual_ref, pieces_ref):
-    window = lax.dot_general(
+    changed = high_ref[...] - folded_sum(product, fold, strip, range(fold))
+    solved = jnp.where(panel_ref[0] == 0, low_ref[...], changed)
+    rows = jnp.concatenate([turned(solved, -f * width) for f in range(fold)], axis=0)
+    out_ref[...] = rows.T[:width, :]
+
+
+def window_step(chosen_ref, residual_ref, window_ref):
+    window_ref[...] = lax.dot_general(
         chosen_ref[...], residual_ref[...], (((0,), (0,)), ((), ())), preferred_element_type=F32
     )
-    groups, strip, _ = pieces_ref.shape
+
+
+def fold_step(group_ref, parts_ref, sent_ref):
+    groups = parts_ref.shape[0]
+    strip = sent_ref.shape[1]
     width = LANES // groups
+    window = jnp.sum(parts_ref[...].astype(F32), axis=0)
+    result = None
     for p in range(groups):
         out = None
         for r in range(window.shape[0] // strip):
             part = turned(window[r * strip : (r + 1) * strip, :], (r - p) * width)
             out = part if out is None else jnp.where(lane_block(part.shape, width, r), part, out)
-        pieces_ref[p] = out
-
-
-def whole(body, shapes, *args):
+        result = out if result is None else jnp.where(group_ref[0] == p, out, result)
+    sent_ref[...] = jnp.broadcast_to(result.astype(BF)[None], sent_ref.shape)
+
+
+def whole(body, shapes, *args, scalars=0):
     return pl.pallas_call(
         body,
         out_shape=shapes,
-        in_specs=[VMEM] * len(args),
+        in_specs=[pl.BlockSpec(memory_space=pltpu.SMEM)] * scalars + [VMEM] * (len(args) - scalars),
         out_specs=jax.tree.map(lambda _: VMEM, shapes),
         compiler_params=pltpu.CompilerParams(vmem_limit_bytes=16 * 1024 * 1024),
     )(*args)
@@ -186,16 +234,10 @@
     plane = shard // plane_size
     plane_points = plane_size * own_points
 
-    own_scaled = (points.astype(F32) * inv_scale[None, :]).astype(BF)
-    plane_rows = exchanged(copies(own_scaled, plane_size), "ctr", PLANES)
+    plane_rows = exchanged(copies(points, plane_size), "ctr", PLANES)
     plane_rows = plane_rows.reshape(plane_points, depth)
-    chunks = [plane_rows] + [None] * (PLANES - 1)
-    for k in (2, 1, 3):
-        chunks[k] = swapped(plane_rows, "ctr", k * plane_size)
-
-    scaled_centers = (centers.astype(F32) * inv_scale[None, :]).astype(BF)
-    center_norm = half_norm(scaled_centers)
-
+    scale = inv_scale[None, :]
+    scaled_centers, center_norm = scaled_and_norm(centers, scale)
     blocks = center_index.reshape(own_rows, shards)
     order = blocks[0] // shard_rows
     here = order == shard
@@ -203,6 +245,21 @@
     choose = (local[:, None] == jnp.arange(shard_rows, dtype=jnp.int32)[None, :]).astype(BF)
     chosen = jnp.dot(choose, scaled_centers, preferred_element_type=F32).astype(BF)
     chosen_norm = half_norm(chosen)
+    plane_rows, scaled_centers, chosen, order = lax.optimization_barrier(
+        (plane_rows, scaled_centers, chosen, order)
+    )
+    chunks = [plane_rows] + [None] * (PLANES - 1)
+    for k in (2, 1, 3):
+        chunks[k] = swapped(plane_rows, "ctr", k * plane_size)
+    values = None
+    kernels = [None] * PLANES
+    for k in (0, 1, 3, 2):
+        slot = (plane ^ k).astype(jnp.int32).reshape(1)
+        chunks[k], kernels[k], values = kernel_and_value(
+            slot, chunks[k], scale, scaled_centers, center_norm, coefficients, values
+        )
+    values, panel_inverse = lax.optimization_barrier((values, panel_inverse))
+
     place = (order[:, None] == jnp.arange(shards, dtype=jnp.int32)[None, :]).astype(BF)
 
     inverse = panel_inverse.astype(BF)
@@ -210,27 +267,40 @@
     turned_inverse = jnp.einsum(
         "rhqj,js->hrsq", inverse.reshape(own_rows, count, strip, shards), place
     ).reshape(count * own_rows, shards * strip)
-    other_inverse = swapped(turned_inverse, "ctr", panel_shards)
-
-    kernels = [None] * PLANES
-    arrived = None
-    for k in (0, 1, 3, 2):
-        kernels[k], value = kernel_and_value(
-            chunks[k], scaled_centers, center_norm[None, :], coefficients
-        )
-        value = value if k == 0 else swapped(value, "ctr", k * plane_size)
-        value = value.astype(F32)
-        arrived = value if arrived is None else arrived + value
-    arrived, inverse, factor, chosen = lax.optimization_barrier(
-        (arrived, inverse, factor[:, :panel_rows].astype(BF), chosen)
-    )
 
     def folded(matrix):
         m = matrix.reshape(own_rows, panel_shards, fold, strip)
         return m.transpose(2, 0, 1, 3).reshape(fold * own_rows, panel_shards * strip)
 
-    factor_rows = folded(factor)
+    near = jnp.stack(chunks)
+    products = lax.dot_general(
+        near, chosen, (((2,), (1,)), ((), ())), preferred_element_type=F32
+    )
+    chosen_kernel = jnp.exp(products - half_norm(near)[:, :, None] - chosen_norm).astype(BF)
+    chosen_kernel = jnp.concatenate([pick(chosen_kernel, plane ^ k) for k in range(PLANES)], axis=0)
+
+    own_weight = class_lookup(point_class, class_weight)
+    shares = exchanged(values.reshape(shards, own_points, target_count), "ctr")
+    predicted = jnp.sum(shares.astype(F32), axis=0)
+    own_residual = (own_weight[:, None] * (predicted - targets)).astype(BF)
+    own_residual, factor, inverse = lax.optimization_barrier(
+        (own_residual, factor[:, :panel_rows], inverse)
+    )
+    factor_rows = folded(factor.astype(BF))
     inverse_rows = folded(inverse)
+    residual = exchanged(copies(own_residual, shards), "ctr")
+    residual = residual.reshape(shards * own_points, target_count)
+
+    index = group.astype(jnp.int32).reshape(1)
+    window = whole(
+        window_step, jax.ShapeDtypeStruct((own_rows, target_count), F32), chosen_kernel, residual
+    )
+    parts = lax.all_gather(window, "pts")
+    sent = jax.ShapeDtypeStruct((shards, strip, LANES), BF)
+    window = whole(fold_step, sent, index, parts, scalars=1)
+    window, turned_inverse = lax.optimization_barrier((window, turned_inverse))
+    other_inverse = swapped(turned_inverse, "ctr", panel_shards)
+    other_inverse, residual = lax.optimization_barrier((other_inverse, residual))
     solve_rows = jnp.concatenate(
         [
             jnp.where(panel == 0, turned_inverse, other_inverse),
@@ -238,28 +308,8 @@
         ],
         axis=0,
     )
-    near = jnp.stack(chunks)
-    products = lax.dot_general(
-        near, chosen, (((2,), (1,)), ((), ())), preferred_element_type=F32
-    )
-    chosen_kernel = jnp.exp(products - half_norm(near)[:, :, None] - chosen_norm).astype(BF)
-    chosen_kernel = jnp.concatenate([pick(chosen_kernel, plane ^ k) for k in range(PLANES)], axis=0)
-
-    own_weight = class_lookup(point_class, class_weight)
-    shares = exchanged(
-        arrived.astype(BF).reshape(plane_size, own_points, target_count), "ctr", PLANES
-    )
-    predicted = jnp.sum(shares.astype(F32), axis=0)
-    own_residual = (own_weight[:, None] * (predicted - targets)).astype(BF)
-    residual = exchanged(copies(own_residual, shards), "ctr")
-    residual = residual.reshape(shards * own_points, target_count)
-
-    pieces = whole(
-        window_step, jax.ShapeDtypeStruct((groups, strip, LANES), F32), chosen_kernel, residual
-    )
-    pieces = exchanged(pieces, "pts")
-    window = jnp.sum(pieces, axis=0).astype(BF)
-    window = exchanged(copies(window, shards), "ctr").reshape(shards * strip, LANES)
+    window = exchanged(window, "ctr")
+    window = window.reshape(shards * strip, LANES)
 
     planes = residual.reshape(PLANES, plane_points, target_count)
     backward = None
@@ -282,10 +332,17 @@
     first = exchanged(first, "ctr", HALVES).reshape(half * strip, LANES)
     update = whole(middle_step, sent, factor_rows, first)
     update = exchanged(update, "ctr", HALVES).reshape(half * strip, LANES)
-    changed = whole(last_step, packed, inverse_rows, update, high)
-    solved = jnp.where(panel == 0, low, changed)
-    solved = solved.reshape(strip, fold, target_slice).transpose(1, 0, 2)
-    return (gradient, solved.reshape(own_rows, target_slice))
+    solved = whole(
+        last_step,
+        jax.ShapeDtypeStruct((target_slice, own_rows), F32),
+        panel.astype(jnp.int32).reshape(1),
+        inverse_rows,
+        update,
+        low,
+        high,
+        scalars=1,
+    )
+    return (gradient, solved.T)
 
 
 def solution(mesh):

time: 158 us -> 154 us (0.975)
  waiting for transfers between devices: 50.2 us -> 32.5 us
  local copies, waits for them, and re-layouts: 15.3 us -> 28.1 us
  other arithmetic: 14 us -> 5.46 us
  blocking collectives: 0 us -> 6.93 us
  Pallas kernels: 16.1 us -> 19.6 us
    all_to_all x7 -> x6, waiting for transfers between devices: 45.4 us -> 31.2 us  [exchanged(): lax.all_to_all(pieces, axis, 0, 0, tiled=True, axis_index_groups=groups i...]
    unnamed x24 -> x52, local copies, waits for them, and re-layouts: 6.39 us -> 15.3 us
    all_gather x0 -> x1, blocking collectives: none -> 6.93 us  [body(): parts = lax.all_gather(window, 'pts')]
    reduce_sum x2 -> x1, other arithmetic: 5.63 us -> 1.39 us  [half_norm(): return 0.5 * jnp.sum(jnp.square(rows.astype(F32)), axis=-1)]
    pallas_call x8 -> x10, Pallas kernels: 16.1 us -> 19.6 us  [the longest x4 12 us: kernel_and_value(): pl.pallas_call(kernel_block, out_shape=(jax.ShapeDtypeStruct((count, dept...]
    ppermute x9 -> x6, waiting for transfers between devices: 4.76 us -> 1.31 us  [swapped(): lax.ppermute(x, axis, [(i, i ^ bits) for i in range(lax.axis_size(axis))])]
    optimization_barrier x1 -> x3, local copies, waits for them, and re-layouts: 0.27 us -> 3.19 us  [the longest x1 2.04 us: body(): values, panel_inverse = lax.optimization_barrier((values, panel_inverse))]
    dot_general x1, matrix products: 3.27 us -> 0.98 us  [body(): jnp.dot(choose, scaled_centers, preferred_element_type=F32).astype(BF)]
  transfers between devices with their start and end apart: 16 -> 12, of which waited for: 8 -> 7; matrix products, arithmetic and copies ran while one was open for 16% -> 14% of each run, Pallas kernels for 10% -> 10%
where the time goes in v5:
time: 154 us; the launch traced here: 152 us
  starting transfers between devices  52.2 us (34%)
  waiting for transfers between devices  32.5 us (21%)
  local copies, waits for them, and re-layouts  28.1 us (18%)
  Pallas kernels  19.6 us (13%)
  blocking collectives  6.93 us (4%)
  matrix products  6.53 us (4%)
  other arithmetic  5.46 us (4%)
    all_to_all x6, starting transfers between devices, exchanged(): lax.all_to_all(pieces, axis, 0, 0, tiled=True, axis_index_groups=groups i...  43.5 us
    all_to_all x6, waiting for transfers between devices, exchanged(): lax.all_to_all(pieces, axis, 0, 0, tiled=True, axis_index_groups=groups i...  31.2 us
    unnamed x52, local copies, waits for them, and re-layouts  15.3 us
    pallas_call x4, Pallas kernels, kernel_and_value(): pl.pallas_call(kernel_block, out_shape=(jax.ShapeDtypeStruct((count, dept...  12 us
    ppermute x6, starting transfers between devices, swapped(): lax.ppermute(x, axis, [(i, i ^ bits) for i in range(lax.axis_size(axis))])  8.7 us
    all_gather x1, blocking collectives, body(): parts = lax.all_gather(window, 'pts')  6.93 us
    pallas_call x5, Pallas kernels, whole(): pl.pallas_call(body, out_shape=shapes, in_specs=[pl.BlockSpec(memory_spac...  3.98 us
    dot_general x4, matrix products, body(): lax.dot_general(pick(planes, plane ^ k), kernels[k], (((0,), (0,)), ((),...  3.77 us
  transfers between devices with their start and end apart: 12, of which 7 were waited for; matrix products, arithmetic and copies ran while one was open for 14% of the time, Pallas kernels for 10%

profile of v5, /device:TPU:4, one launch (start us, length us, event | category | flops | bytes accessed | tf_op | source)
XLA Modules:
  0.0 152.4 jit_solution(8942261144041534106)
XLA Ops:
  0.6 1.4 broadcast_in_dim.26
  2.1 9.6 %all-to-all-start = ((bf16[16,16,512]{2,1,0:T(8,128)(2,1)}), bf16[16,16,512]{2,1,0:T(8,128)(2,1)S(1)}, u32[]{:S(2)}, u32[]{:S(2)}) async-start(bf16[16,16,512]{2,1,0:T(8,128)(2,1)} %broadcast_in_dim.26), calls=%async_computation | async-start | bytes 524288 | tf_op jit(solution)/shard_map/all_to_all | solution.py:20
  13.8 3.6 %shard_map.113 = (bf16[4096,512]{1,0:T(8,128)(2,1)S(1)}, f32[1,4096]{1,0:T(1,128)S(1)}) custom-call(bf16[4096,512]{1,0:T(8,128)(2,1)} %centers_ref.1, f32[1,512]{1,0:T(1,128)S(1)} %bitcast.97), custom_call_target="tpu_custom_call" | custom-call | flops 8388608 | bytes 4194304 | tf_op jit(solution)/shard_map/pallas_call | solution.py:56
  17.7 1.0 fusion.10
  18.7 2.0 %copy-done = bf16[4096,512]{1,0:T(8,128)(2,1)} copy-done((bf16[4096,512]{1,0:T(8,128)(2,1)}, bf16[4096,512]{1,0:T(8,128)(2,1)S(1)}, u32[]{:S(2)}) %copy-start) | copy-done | bytes 4194328
  20.6 3.1 %all-to-all-done = bf16[16,16,512]{2,1,0:T(8,128)(2,1)S(1)} async-done(((bf16[16,16,512]{2,1,0:T(8,128)(2,1)}), bf16[16,16,512]{2,1,0:T(8,128)(2,1)S(1)}, u32[]{:S(2)}, u32[]{:S(2)}) %all-to-all-start) | async-done | bytes 262176 | tf_op jit(solution)/shard_map/all_to_all | solution.py:20
  23.7 1.2 collective-permute-start
  25.0 1.1 slice.15
  26.1 1.0 copy.52
  27.1 2.9 %collective-permute-start.1 = (bf16[256,512]{1,0:T(8,128)(2,1)S(1)}, bf16[256,512]{1,0:T(8,128)(2,1)S(1)}, u32[]{:S(2)}, u32[]{:S(2)}) collective-permute-start(bf16[256,512]{1,0:T(8,128)(2,1)S(1)} %bitcast.84), channel_id=1, source_target_pairs={{0,32},{1,33},{2,34},{3,35},{4,36},{5,37},{6,38},{7,39},{8,40},{9,... | collective-permute-start | bytes 786440 | tf_op jit(solution)/shard_map/ppermute | solution.py:30
  30.0 2.2 %copy-done.1 = bf16[4096,512]{1,0:T(8,128)(2,1)S(1)} copy-done((bf16[4096,512]{1,0:T(8,128)(2,1)S(1)}, bf16[4096,512]{1,0:T(8,128)(2,1)}, u32[]{:S(2)}) %copy-start.1) | copy-done | bytes 4194328
  32.2 2.6 %shard_map.114 = (bf16[256,512]{1,0:T(8,128)(2,1)S(1)}, bf16[256,4096]{1,0:T(8,128)(2,1)S(1)}, bf16[4,256,128]{2,1,0:T(8,128)(2,1)S(1)}) custom-call(s32[1]{0:T(128)} %bitcast.1.slot_ref, bf16[256,512]{1,0:T(8,128)(2,1)S(1)} %bitcast.85, f32[1,512]{1,0:T(1,128)S(1)} %bitcast.98, bf16[4096,512]{1,0:T(8,128)(2,1)S(1)} %copy-done.1, ...), custom_call_target="tpu_custom_call" | custom-call | flops 1342177280 | bytes 2097152 | tf_op jit(solution)/shard_map/pallas_call | solution.py:96
  34.8 1.3 copy-done.3
  37.5 0.9 copy-done.9
  38.5 2.6 %shard_map.115 = (bf16[256,512]{1,0:T(8,128)(2,1)S(1)}, bf16[256,4096]{1,0:T(8,128)(2,1)S(1)}, bf16[4,256,128]{2,1,0:T(8,128)(2,1)S(1)}) custom-call(s32[1]{0:T(128)} %bitcast.5.slot_ref, bf16[256,512]{1,0:T(8,128)(2,1)S(1)} %copy-done.9, f32[1,512]{1,0:T(1,128)S(1)} %bitcast.99, bf16[4096,512]{1,0:T(8,128)(2,1)S(1)} %copy-done.1, ...), custom_call_target="tpu_custom_call" | custom-call | flops 1342177280 | bytes 2097152 | tf_op jit(solution)/shard_map/pallas_call | solution.py:96
  41.8 3.5 %shard_map.116 = (bf16[256,512]{1,0:T(8,128)(2,1)S(1)}, bf16[256,4096]{1,0:T(8,128)(2,1)S(1)}, bf16[4,256,128]{2,1,0:T(8,128)(2,1)S(1)}) custom-call(s32[1]{0:T(128)} %bitcast.8.slot_ref, bf16[256,512]{1,0:T(8,128)(2,1)} %collective-permute-done.2.points_ref, f32[1,512]{1,0:T(1,128)S(1)} %bitcast.100, bf16[4096,512]{1,0:T(8,128)(2,1)S(1)} %copy-done.1, ...), custom_call_target="tpu_custom_call" | custom-call | flops 1342177280 | bytes 2097152 | tf_op jit(solution)/shard_map/pallas_call | solution.py:96
  45.3 1.3 copy-done.5
  47.4 3.3 %shard_map.117 = (bf16[256,512]{1,0:T(8,128)(2,1)S(1)}, bf16[256,4096]{1,0:T(8,128)(2,1)S(1)}, bf16[4,256,128]{2,1,0:T(8,128)(2,1)}) custom-call(s32[1]{0:T(128)} %bitcast.7.slot_ref, bf16[256,512]{1,0:T(8,128)(2,1)S(1)} %collective-permute-done.1.points_ref, f32[1,512]{1,0:T(1,128)S(1)} %bitcast.101, bf16[4096,512]{1,0:T(8,128)(2,1)S(1)} %copy-done.1, ...), custom_call_target="tpu_custom_call" | custom-call | flops 1342177280 | bytes 2097152 | tf_op jit(solution)/shard_map/pallas_call | solution.py:96
  50.7 1.4 copy-done.6
  52.8 8.7 %all-to-all-start.1 = ((bf16[64,16,128]{2,1,0:T(8,128)(2,1)}), bf16[64,16,128]{2,1,0:T(8,128)(2,1)S(1)}, u32[]{:S(2)}, u32[]{:S(2)}) async-start(bf16[64,16,128]{2,1,0:T(8,128)(2,1)} %bitcast.16), calls=%async_computation.1 | async-start | bytes 524288 | tf_op jit(solution)/shard_map/all_to_all | solution.py:20
  61.5 2.0 %copy.40 = bf16[64,2048]{0,1:T(8,128)(2,1)} copy(f32[64,2048]{1,0:T(8,128)} %param.19) | data formatting | bytes 786432 | tf_op jit(solution)/shard_map/optimization_barrier | solution.py:261
  63.6 1.4 multiply_reduce_fusion
  65.0 6.6 %all-to-all-done.1 = bf16[64,16,128]{2,1,0:T(8,128)(2,1)S(1)} async-done(((bf16[64,16,128]{2,1,0:T(8,128)(2,1)}), bf16[64,16,128]{2,1,0:T(8,128)(2,1)S(1)}, u32[]{:S(2)}, u32[]{:S(2)}) %all-to-all-start.1) | async-done | bytes 262176 | tf_op jit(solution)/shard_map/all_to_all | solution.py:20
  72.4 6.6 %all-to-all-start.2 = ((bf16[64,16,128]{2,1,0:T(8,128)(2,1)}), bf16[64,16,128]{2,1,0:T(8,128)(2,1)S(1)}, u32[]{:S(2)}, u32[]{:S(2)}) async-start(bf16[64,16,128]{2,1,0:T(8,128)(2,1)} %broadcast_in_dim.56), calls=%async_computation.2 | async-start | bytes 524288 | tf_op jit(solution)/shard_map/all_to_all | solution.py:20
  80.1 1.3 convolution_bitcast_fusion
  82.3 6.7 %all-to-all-done.2 = bf16[64,16,128]{2,1,0:T(8,128)(2,1)S(1)} async-done(((bf16[64,16,128]{2,1,0:T(8,128)(2,1)}), bf16[64,16,128]{2,1,0:T(8,128)(2,1)S(1)}, u32[]{:S(2)}, u32[]{:S(2)}) %all-to-all-start.2) | async-done | bytes 262176 | tf_op jit(solution)/shard_map/all_to_all | solution.py:20
  89.2 6.9 %all-gather = f32[256,128]{1,0:T(8,128)S(1)} all-gather(f32[64,128]{1,0:T(8,128)S(1)} %shard_map.118), channel_id=2, replica_groups=mesh['pts'=4,'ctr'=64] {'pts'}, dimensions={0}, use_global_device_ids=true | all-gather | bytes 163840 | tf_op jit(solution)/shard_map/all_gather | solution.py:298
  96.1 0.8 shard_map.119
  97.1 1.6 %collective-permute-start.3 = (bf16[128,1024]{1,0:T(8,128)(2,1)S(1)}, bf16[128,1024]{1,0:T(8,128)(2,1)S(1)}, u32[]{:S(2)}, u32[]{:S(2)}) collective-permute-start(bf16[128,1024]{1,0:T(8,128)(2,1)S(1)} %copy.43), channel_id=1, source_target_pairs={{0,32},{1,33},{2,34},{3,35},{4,36},{5,37},{6,38},{7,39},{8,40},{9,... | collective-permute-start | bytes 786440 | tf_op jit(solution)/shard_map/ppermute | solution.py:30
  98.7 7.4 %all-to-all-start.3 = ((bf16[64,16,128]{2,1,0:T(8,128)(2,1)}), bf16[64,16,128]{2,1,0:T(8,128)(2,1)S(1)}, u32[]{:S(2)}, u32[]{:S(2)}) async-start(bf16[64,16,128]{2,1,0:T(8,128)(2,1)} %shard_map.119), calls=%async_computation.3 | async-start | bytes 524288 | tf_op jit(solution)/shard_map/all_to_all | solution.py:20
  106.0 1.3 collective-permute-done.3
  107.3 2.2 %fusion.11 = f32[128,4096]{1,0:T(8,128)S(1)} fusion(bf16[256,4096]{1,0:T(8,128)(2,1)} %copy-done.5, bf16[4,256,128]{2,1,0:T(8,128)(2,1)S(1)} %bitcast.77, s32[]{:T(128)S(6)} %select_n.70), kind=kOutput, calls=%fused_computation.30 | convolution fusion | flops 268435456 | bytes 4259844 | tf_op jit(solution)/shard_map/dot_general | solution.py:317
  110.6 1.0 copy-done.7
  112.5 0.9 constant_dynamic-slice_fusion.1
  113.4 4.2 %all-to-all-done.3 = bf16[64,16,128]{2,1,0:T(8,128)(2,1)S(1)} async-done(((bf16[64,16,128]{2,1,0:T(8,128)(2,1)}), bf16[64,16,128]{2,1,0:T(8,128)(2,1)S(1)}, u32[]{:S(2)}, u32[]{:S(2)}) %all-to-all-start.3) | async-done | bytes 262176 | tf_op jit(solution)/shard_map/all_to_all | solution.py:20
  117.6 1.0 shard_map.120
  118.6 4.1 %all-to-all-start.4 = ((bf16[32,16,128]{2,1,0:T(8,128)(2,1)}), bf16[32,16,128]{2,1,0:T(8,128)(2,1)S(1)}, u32[]{:S(2)}, u32[]{:S(2)}) async-start(bf16[32,16,128]{2,1,0:T(8,128)(2,1)} %get-tuple-element.59), calls=%async_computation.4 | async-start | bytes 262144 | tf_op jit(solution)/shard_map/all_to_all | solution.py:20
  122.8 0.8 copy-done.22
  123.5 1.3 maximum_add_fusion
  125.6 2.9 %collective-permute-start.5 = (bf16[32,4096]{1,0:T(8,128)(2,1)}, bf16[32,4096]{1,0:T(8,128)(2,1)S(1)}, u32[]{:S(2)}, u32[]{:S(2)}) collective-permute-start(bf16[32,4096]{1,0:T(8,128)(2,1)} %fusion.8), channel_id=1, source_target_pairs={{0,128},{64,192},{128,0},{192,64},{1,129},{65,193},{129,1},{193,65... | collective-permute-start | bytes 786440 | tf_op jit(solution)/shard_map/ppermute | solution.py:30
  128.5 1.1 copy.45
  129.5 1.5 reshape.100
  131.1 1.5 all-to-all-done.4
  132.6 0.9 shard_map.121
  133.6 7.1 %all-to-all-start.5 = ((bf16[32,16,128]{2,1,0:T(8,128)(2,1)}), bf16[32,16,128]{2,1,0:T(8,128)(2,1)S(1)}, u32[]{:S(2)}, u32[]{:S(2)}) async-start(bf16[32,16,128]{2,1,0:T(8,128)(2,1)} %shard_map.121), calls=%async_computation.5 | async-start | bytes 262144 | tf_op jit(solution)/shard_map/all_to_all | solution.py:20
  141.5 9.1 %all-to-all-done.5 = bf16[32,16,128]{2,1,0:T(8,128)(2,1)S(1)} async-done(((bf16[32,16,128]{2,1,0:T(8,128)(2,1)}), bf16[32,16,128]{2,1,0:T(8,128)(2,1)S(1)}, u32[]{:S(2)}, u32[]{:S(2)}) %all-to-all-start.5) | async-done | bytes 131104 | tf_op jit(solution)/shard_map/all_to_all | solution.py:20
  150.5 1.0 shard_map.122
  151.6 0.8 fusion.6
  (84 shorter events, 12.5 us)
Async XLA Ops:
  2.1 21.6 %all-to-all-start = ((bf16[16,16,512]{2,1,0:T(8,128)(2,1)}), bf16[16,16,512]{2,1,0:T(8,128)(2,1)S(1)}, u32[]{:S(2)}, u32[]{:S(2)}) async-start(bf16[16,16,512]{2,1,0:T(8,128)(2,1)} %broadcast_in_dim.26), calls=%async_computation | async-start | bytes 524288 | tf_op jit(solution)/shard_map/all_to_all | solution.py:20
  13.2 0.7 copy-start.18
  17.6 7.3 %copy-start.24 = (f32[8]{0:T(128)S(1)}, f32[8]{0:T(128)}, u32[]{:S(2)}) copy-start(f32[8]{0:T(128)} %param.13) | copy-start | bytes 100
  17.6 7.3 %copy-start.25 = (s32[16]{0:T(128)S(1)}, s32[16]{0:T(128)}, u32[]{:S(2)}) copy-start(s32[16]{0:T(128)} %param.11) | copy-start | bytes 196
  17.6 12.3 %copy-start.2 = (bf16[4096,128]{1,0:T(8,128)(2,1)S(1)}, bf16[4096,128]{1,0:T(8,128)(2,1)}, u32[]{:S(2)}) copy-start(bf16[4096,128]{1,0:T(8,128)(2,1)} %coef_ref.7) | copy-start | bytes 3145732
  17.6 12.3 %copy-start.19 = (f32[512]{0:T(512)S(1)}, f32[512]{0:T(512)}, u32[]{:S(2)}) copy-start(f32[512]{0:T(512)} %param.14) | copy-start | bytes 6148
  18.6 2.0 %copy-start = (bf16[4096,512]{1,0:T(8,128)(2,1)}, bf16[4096,512]{1,0:T(8,128)(2,1)S(1)}, u32[]{:S(2)}) copy-start(bf16[4096,512]{1,0:T(8,128)(2,1)S(1)} %get-tuple-element.34.centers_ref) | copy-start | bytes 12582916
  23.7 13.1 %collective-permute-start = (bf16[256,512]{1,0:T(8,128)(2,1)S(1)}, bf16[256,512]{1,0:T(8,128)(2,1)S(1)}, u32[]{:S(2)}, u32[]{:S(2)}) collective-permute-start(bf16[256,512]{1,0:T(8,128)(2,1)S(1)} %bitcast.82), channel_id=1, source_target_pairs={{0,16},{1,17},{2,18},{3,19},{4,20},{5,21},{6,22},{7,23},{8,24},{9,... | collective-permute-start | bytes 786440 | tf_op jit(solution)/shard_map/ppermute | solution.py:30
  24.9 16.2 %collective-permute-start.2 = (bf16[256,512]{1,0:T(8,128)(2,1)S(1)}, bf16[256,512]{1,0:T(8,128)(2,1)}, u32[]{:S(2)}, u32[]{:S(2)}) collective-permute-start(bf16[256,512]{1,0:T(8,128)(2,1)S(1)} %bitcast.83), channel_id=1, source_target_pairs={{0,48},{1,49},{2,50},{3,51},{4,52},{5,53},{6,54},{7,55},{8,56},{9,... | collective-permute-start | bytes 786440 | tf_op jit(solution)/shard_map/ppermute | solution.py:30
  27.1 19.6 %collective-permute-start.1 = (bf16[256,512]{1,0:T(8,128)(2,1)S(1)}, bf16[256,512]{1,0:T(8,128)(2,1)S(1)}, u32[]{:S(2)}, u32[]{:S(2)}) collective-permute-start(bf16[256,512]{1,0:T(8,128)(2,1)S(1)} %bitcast.84), channel_id=1, source_target_pairs={{0,32},{1,33},{2,34},{3,35},{4,36},{5,37},{6,38},{7,39},{8,40},{9,... | collective-permute-start | bytes 786440 | tf_op jit(solution)/shard_map/ppermute | solution.py:30
  30.0 2.2 %copy-start.1 = (bf16[4096,512]{1,0:T(8,128)(2,1)S(1)}, bf16[4096,512]{1,0:T(8,128)(2,1)}, u32[]{:S(2)}) copy-start(bf16[4096,512]{1,0:T(8,128)(2,1)} %copy-done) | copy-start | bytes 12582916
  34.8 1.4 copy-start.3
  36.1 0.7 copy-start.10
  36.8 0.7 copy-start.8
  37.5 0.9 copy-start.9
  41.0 0.7 copy-start.12
  45.3 1.3 copy-start.5
  46.7 0.7 copy-start.14
  47.4 16.1 %copy-start.11 = (bf16[256,512]{1,0:T(8,128)(2,1)S(1)}, bf16[256,512]{1,0:T(8,128)(2,1)}, u32[]{:S(2)}) copy-start(bf16[256,512]{1,0:T(8,128)(2,1)} %copy-done.10) | copy-start | bytes 786436
  50.7 1.4 copy-start.6
  52.1 0.7 copy-start.16
  52.8 18.8 %copy-start.23 = (f32[16,128]{1,0:T(8,128)S(1)}, f32[16,128]{1,0:T(8,128)}, u32[]{:S(2)}) copy-start(f32[16,128]{1,0:T(8,128)} %param.12) | copy-start | bytes 24580
  52.8 26.3 %copy-start.13 = (bf16[256,512]{1,0:T(8,128)(2,1)S(1)}, bf16[256,512]{1,0:T(8,128)(2,1)}, u32[]{:S(2)}) copy-start(bf16[256,512]{1,0:T(8,128)(2,1)} %copy-done.12) | copy-start | bytes 786436
  52.8 26.3 %copy-start.15 = (bf16[256,512]{1,0:T(8,128)(2,1)S(1)}, bf16[256,512]{1,0:T(8,128)(2,1)}, u32[]{:S(2)}) copy-start(bf16[256,512]{1,0:T(8,128)(2,1)} %copy-done.14) | copy-start | bytes 786436
  52.8 26.3 %copy-start.17 = (bf16[256,512]{1,0:T(8,128)(2,1)S(1)}, bf16[256,512]{1,0:T(8,128)(2,1)}, u32[]{:S(2)}) copy-start(bf16[256,512]{1,0:T(8,128)(2,1)} %copy-done.16) | copy-start | bytes 786436
  52.8 18.7 %all-to-all-start.1 = ((bf16[64,16,128]{2,1,0:T(8,128)(2,1)}), bf16[64,16,128]{2,1,0:T(8,128)(2,1)S(1)}, u32[]{:S(2)}, u32[]{:S(2)}) async-start(bf16[64,16,128]{2,1,0:T(8,128)(2,1)} %bitcast.16), calls=%async_computation.1 | async-start | bytes 524288 | tf_op jit(solution)/shard_map/all_to_all | solution.py:20
  72.4 16.5 %all-to-all-start.2 = ((bf16[64,16,128]{2,1,0:T(8,128)(2,1)}), bf16[64,16,128]{2,1,0:T(8,128)(2,1)S(1)}, u32[]{:S(2)}, u32[]{:S(2)}) async-start(bf16[64,16,128]{2,1,0:T(8,128)(2,1)} %broadcast_in_dim.56), calls=%async_computation.2 | async-start | bytes 524288 | tf_op jit(solution)/shard_map/all_to_all | solution.py:20
  97.1 10.3 %collective-permute-start.3 = (bf16[128,1024]{1,0:T(8,128)(2,1)S(1)}, bf16[128,1024]{1,0:T(8,128)(2,1)S(1)}, u32[]{:S(2)}, u32[]{:S(2)}) collective-permute-start(bf16[128,1024]{1,0:T(8,128)(2,1)S(1)} %copy.43), channel_id=1, source_target_pairs={{0,32},{1,33},{2,34},{3,35},{4,36},{5,37},{6,38},{7,39},{8,40},{9,... | collective-permute-start | bytes 786440 | tf_op jit(solution)/shard_map/ppermute | solution.py:30
  98.7 19.0 %all-to-all-start.3 = ((bf16[64,16,128]{2,1,0:T(8,128)(2,1)}), bf16[64,16,128]{2,1,0:T(8,128)(2,1)S(1)}, u32[]{:S(2)}, u32[]{:S(2)}) async-start(bf16[64,16,128]{2,1,0:T(8,128)(2,1)} %shard_map.119), calls=%async_computation.3 | async-start | bytes 524288 | tf_op jit(solution)/shard_map/all_to_all | solution.py:20
  107.3 2.2 %copy-start.4 = (bf16[256,4096]{1,0:T(8,128)(2,1)S(1)}, bf16[256,4096]{1,0:T(8,128)(2,1)}, u32[]{:S(2)}) copy-start(bf16[256,4096]{1,0:T(8,128)(2,1)} %copy-done.3) | copy-start | bytes 6291460
  110.1 1.6 %copy-start.7 = (bf16[256,4096]{1,0:T(8,128)(2,1)S(1)}, bf16[256,4096]{1,0:T(8,128)(2,1)}, u32[]{:S(2)}) copy-start(bf16[256,4096]{1,0:T(8,128)(2,1)} %copy-done.6) | copy-start | bytes 6291460
  112.3 10.4 %collective-permute-start.4 = (bf16[2,32,4096]{2,1,0:T(8,128)(2,1)S(1)}, bf16[2,32,4096]{2,1,0:T(8,128)(2,1)S(1)}, u32[]{:S(2)}, u32[]{:S(2)}) collective-permute-start(bf16[2,32,4096]{2,1,0:T(8,128)(2,1)S(1)} %pad_maximum_fusion.1), channel_id=1, source_target_pairs={{0,64},{64,0},{128,192},{192,128},{1,65},{65,1},{129,193},{193,129... | collective-permute-start | bytes 1572872 | tf_op jit(solution)/shard_map/ppermute | solution.py:30
  117.6 10.8 %copy-start.21 = (bf16[64,2048]{0,1:T(8,128)(2,1)S(1)}, bf16[64,2048]{0,1:T(8,128)(2,1)}, u32[]{:S(2)}) copy-start(bf16[64,2048]{0,1:T(8,128)(2,1)} %copy.52) | copy-start | bytes 786436
  118.6 14.0 %all-to-all-start.4 = ((bf16[32,16,128]{2,1,0:T(8,128)(2,1)}), bf16[32,16,128]{2,1,0:T(8,128)(2,1)S(1)}, u32[]{:S(2)}, u32[]{:S(2)}) async-start(bf16[32,16,128]{2,1,0:T(8,128)(2,1)} %get-tuple-element.59), calls=%async_computation.4 | async-start | bytes 262144 | tf_op jit(solution)/shard_map/all_to_all | solution.py:20
  122.8 0.8 copy-start.22
  124.8 15.9 %copy-start.20 = (bf16[64,2048]{0,1:T(8,128)(2,1)S(1)}, bf16[64,2048]{0,1:T(8,128)(2,1)}, u32[]{:S(2)}) copy-start(bf16[64,2048]{0,1:T(8,128)(2,1)} %copy.40) | copy-start | bytes 786436
  125.6 26.0 %collective-permute-start.5 = (bf16[32,4096]{1,0:T(8,128)(2,1)}, bf16[32,4096]{1,0:T(8,128)(2,1)S(1)}, u32[]{:S(2)}, u32[]{:S(2)}) collective-permute-start(bf16[32,4096]{1,0:T(8,128)(2,1)} %fusion.8), channel_id=1, source_target_pairs={{0,128},{64,192},{128,0},{192,64},{1,129},{65,193},{129,1},{193,65... | collective-permute-start | bytes 786440 | tf_op jit(solution)/shard_map/ppermute | solution.py:30
  133.6 16.9 %all-to-all-start.5 = ((bf16[32,16,128]{2,1,0:T(8,128)(2,1)}), bf16[32,16,128]{2,1,0:T(8,128)(2,1)S(1)}, u32[]{:S(2)}, u32[]{:S(2)}) async-start(bf16[32,16,128]{2,1,0:T(8,128)(2,1)} %shard_map.121), calls=%async_computation.5 | async-start | bytes 262144 | tf_op jit(solution)/shard_map/all_to_all | solution.py:20

commit v6 on v5

--- a/solution.py
+++ b/solution.py
@@ -1,3 +1,5 @@
+import functools
+
 import jax
 import jax.numpy as jnp
 from jax import lax
@@ -34,74 +36,130 @@
     return lax.dynamic_index_in_dim(x, index, 0, keepdims=False)
 
 
-def scale_step(centers_ref, scale_ref, scaled_ref, norm_ref, slots, sems):
+def scale_step(
+    centers_ref, scale_ref, local_ref, scaled_ref, norm_ref, chosen_ref, extra_ref, slots, sems, outs
+):
     loads = []
     for i in range(slots.shape[0]):
         rows = pl.ds(i * TILE, TILE)
         loads.append(pltpu.make_async_copy(centers_ref.at[rows, :], slots.at[i], sems.at[i]))
         loads[-1].start()
+    count = chosen_ref.shape[0]
+    chosen = jnp.zeros(chosen_ref.shape, F32)
+    lane = lax.broadcasted_iota(jnp.int32, (count, TILE), 1)
+    saves = []
     for i, load in enumerate(loads):
         rows = pl.ds(i * TILE, TILE)
         load.wait()
         scaled = (slots[i].astype(F32) * scale_ref[...]).astype(BF)
-        scaled_ref[rows, :] = scaled
+        slots[i] = scaled
+        saves.append(pltpu.make_async_copy(slots.at[i], scaled_ref.at[rows, :], outs.at[i]))
+        saves[-1].start()
         wide = scaled.astype(F32)
         norm = 0.5 * jnp.sum(wide * wide, axis=1, keepdims=True)
         norm_ref[:, rows] = jnp.broadcast_to(norm, (TILE, LANES)).T[0:1, :]
-
-
-def scaled_and_norm(centers, scale):
+        pick_rows = (lane + i * TILE == local_ref[...]).astype(F32).astype(BF)
+        chosen += jnp.dot(pick_rows, scaled, preferred_element_type=F32)
+    chosen_ref[...] = chosen.astype(BF)
+    norm = 0.5 * jnp.sum(chosen * chosen, axis=1, keepdims=True)
+    extra_ref[...] = jnp.broadcast_to(norm, (count, LANES)).T[0:1, :]
+    for save in saves:
+        save.wait()
+
+
+def scaled_and_norm(centers, scale, local):
     total, depth = centers.shape
+    count = local.shape[0]
     steps = total // TILE
     return pl.pallas_call(
         scale_step,
-        out_shape=(pltpu.VMEM((total, depth), BF), jax.ShapeDtypeStruct((1, total), F32)),
-        in_specs=[pl.BlockSpec(memory_space=pltpu.HBM), VMEM],
-        out_specs=[VMEM, VMEM],
-        scratch_shapes=[pltpu.VMEM((steps, TILE, depth), BF), pltpu.SemaphoreType.DMA((steps,))],
+        out_shape=(
+            pltpu.HBM((total, depth), BF),
+            jax.ShapeDtypeStruct((1, total), F32),
+            jax.ShapeDtypeStruct((count, depth), BF),
+            jax.ShapeDtypeStruct((1, count), F32),
+        ),
+        in_specs=[pl.BlockSpec(memory_space=pltpu.HBM), VMEM, VMEM],
+        out_specs=[pl.BlockSpec(memory_space=pltpu.HBM)] + [VMEM] * 3,
+        scratch_shapes=[pltpu.VMEM((steps, TILE, depth), BF)]
+        + [pltpu.SemaphoreType.DMA((steps,))] * 2,
         compiler_params=pltpu.CompilerParams(vmem_limit_bytes=24 * 1024 * 1024),
         cost_estimate=pl.CostEstimate(
             flops=4 * total * depth, bytes_accessed=2 * total * depth, transcendentals=0
         ),
-    )(pltpu.with_memory_space_constraint(centers, pltpu.HBM), scale)
+    )(pltpu.with_memory_space_constraint(centers, pltpu.HBM), scale, local)
 
 
 def kernel_block(
-    slot_ref, points_ref, scale_ref, centers_ref, norm_ref, coef_ref, *refs
+    held, slot_ref, points_ref, scale_ref, centers_ref, norm_ref, coef_ref, chosen_ref, extra_ref, *refs
 ):
-    scaled_ref, kernel_ref, value_ref = refs[-3:]
+    kernel_ref, value_ref, picked_ref, slots, sems, *stream = refs[2 * held :]
+    steps = centers_ref.shape[0] // TILE
+    loads = []
+    if stream:
+        for i in range(steps):
+            rows = pl.ds(i * TILE, TILE)
+            loads.append(
+                pltpu.make_async_copy(centers_ref.at[rows, :], stream[0].at[i], stream[1].at[i])
+            )
+            loads[-1].start()
     samples = (points_ref[...].astype(F32) * scale_ref[...]).astype(BF)
-    scaled_ref[...] = samples
     wide = samples.astype(F32)
     left = 0.5 * jnp.sum(wide * wide, axis=1, keepdims=True)
+
+    def block(anchors, norm):
+        products = lax.dot_general(
+            samples, anchors, (((1,), (1,)), ((), ())), preferred_element_type=F32
+        )
+        return jnp.exp(products - left - norm).astype(BF)
+
+    if held:
+        value_ref[...] = refs[0][...]
+        picked_ref[...] = refs[1][...]
     total = jnp.zeros(value_ref.shape[1:], F32)
-    for i in range(centers_ref.shape[0] // TILE):
+    saves = []
+    before = None
+    for i in range(steps):
         rows = pl.ds(i * TILE, TILE)
-        products = lax.dot_general(
-            samples, centers_ref[rows, :], (((1,), (1,)), ((), ())), preferred_element_type=F32
-        )
-        block = jnp.exp(products - left - norm_ref[:, rows]).astype(BF)
-        kernel_ref[:, rows] = block
-        total += jnp.dot(block, coef_ref[rows, :], preferred_element_type=F32)
-    if len(refs) > 3:
-        value_ref[...] = refs[0][...]
+        if stream:
+            loads[i].wait()
+        anchors = stream[0][i] if stream else centers_ref[rows, :]
+        current = block(anchors, norm_ref[:, rows])
+        slots[i] = current
+        saves.append(pltpu.make_async_copy(slots.at[i], kernel_ref.at[:, rows], sems.at[i]))
+        saves[-1].start()
+        if before is not None:
+            coef = coef_ref[pl.ds((i - 1) * TILE, TILE), :]
+            total += jnp.dot(before, coef, preferred_element_type=F32)
+        before = current
+    coef = coef_ref[pl.ds((steps - 1) * TILE, TILE), :]
+    total += jnp.dot(before, coef, preferred_element_type=F32)
     value_ref[slot_ref[0]] = total.astype(value_ref.dtype)
-
-
-def kernel_and_value(slot, samples, scale, anchors, norms, coefficients, values=None):
+    picked_ref[slot_ref[0]] = block(chosen_ref[...], extra_ref[...])
+    for save in saves:
+        save.wait()
+
+
+def kernel_and_value(slot, samples, scale, anchors, norms, coefficients, chosen, extra, *held):
     count, depth = samples.shape
     total, cols = coefficients.shape
-    args = [samples, scale, pltpu.with_memory_space_constraint(anchors, pltpu.VMEM)]
-    args += [norms, coefficients] + ([] if values is None else [values])
+    steps = total // TILE
+    space = VMEM if held else pl.BlockSpec(memory_space=pltpu.HBM)
+    loaded = [pltpu.VMEM((steps, TILE, depth), BF), pltpu.SemaphoreType.DMA((steps,))]
+    args = [samples, scale, anchors if held else pltpu.with_memory_space_constraint(anchors, pltpu.HBM)]
+    args += [norms, coefficients, chosen, extra, *held]
     return pl.pallas_call(
-        kernel_block,
+        functools.partial(kernel_block, bool(held)),
         out_shape=(
-            jax.ShapeDtypeStruct((count, depth), BF),
-            pltpu.VMEM((count, total), BF),
+            pltpu.HBM((count, total), BF),
             jax.ShapeDtypeStruct((PLANES, count, cols), BF),
+            jax.ShapeDtypeStruct((PLANES, count, chosen.shape[0]), BF),
         ),
-        in_specs=[pl.BlockSpec(memory_space=pltpu.SMEM)] + [VMEM] * len(args),
-        out_specs=[VMEM] * 3,
+        in_specs=[pl.BlockSpec(memory_space=pltpu.SMEM), VMEM, VMEM, space]
+        + [VMEM] * (len(args) - 3),
+        out_specs=[pl.BlockSpec(memory_space=pltpu.HBM), VMEM, VMEM],
+        scratch_shapes=[pltpu.VMEM((steps, count, TILE), BF), pltpu.SemaphoreType.DMA((steps,))]
+        + ([] if held else loaded),
         compiler_params=pltpu.CompilerParams(vmem_limit_bytes=24 * 1024 * 1024),
         cost_estimate=pl.CostEstimate(
             flops=2 * count * total * (depth + cols),
@@ -145,23 +203,51 @@
     sent_ref[...] = jnp.broadcast_to(low.astype(BF)[None], sent_ref.shape)
 
 
-def middle_step(matrix_ref, solved_ref, sent_ref):
-    strip = sent_ref.shape[1]
-    fold = int(round((matrix_ref.shape[0] // strip) ** 0.5))
-    product = jnp.dot(matrix_ref[...], solved_ref[...], preferred_element_type=F32)
-    total = folded_sum(product, fold, strip, range(fold))
-    sent_ref[...] = jnp.broadcast_to(total.astype(BF)[None], sent_ref.shape)
-
-
-def last_step(panel_ref, matrix_ref, update_ref, low_ref, high_ref, out_ref):
-    strip = low_ref.shape[0]
-    fold = int(round((matrix_ref.shape[0] // strip) ** 0.5))
+def natural_product(matrix_ref, data_ref, rows_ref):
+    parts, fold, strip, _ = rows_ref.shape
+    data = data_ref[...].astype(F32).reshape(parts * strip, LANES)
+    for f in range(fold):
+        piece = turned(data, -f * (LANES // fold)).astype(BF)
+        rows_ref[:, f] = piece.reshape(parts, strip, LANES)
+    right = rows_ref[...].reshape(parts * fold * strip, LANES)
+    return jnp.dot(matrix_ref[...].astype(BF), right, preferred_element_type=F32)
+
+
+def middle_step(matrix_ref, data_ref, sent_ref, rows_ref):
+    product = natural_product(matrix_ref, data_ref, rows_ref)
+    _, fold, strip, _ = rows_ref.shape
     width = LANES // fold
-    product = jnp.dot(matrix_ref[...], update_ref[...], preferred_element_type=F32)
-    changed = high_ref[...] - folded_sum(product, fold, strip, range(fold))
-    solved = jnp.where(panel_ref[0] == 0, low_ref[...], changed)
-    rows = jnp.concatenate([turned(solved, -f * width) for f in range(fold)], axis=0)
-    out_ref[...] = rows.T[:width, :]
+    out = None
+    for f in range(fold):
+        part = turned(product[f * strip : (f + 1) * strip, :], f * width)
+        out = part if out is None else jnp.where(lane_block(part.shape, width, f), part, out)
+    sent_ref[...] = jnp.broadcast_to(out.astype(BF)[None], sent_ref.shape)
+
+
+def last_step(panel_ref, matrix_ref, data_ref, low_ref, high_ref, out_ref, rows_ref):
+    product = natural_product(matrix_ref, data_ref, rows_ref)
+    _, fold, strip, _ = rows_ref.shape
+    width = LANES // fold
+    low = jnp.concatenate([turned(low_ref[...], -f * width) for f in range(fold)], axis=0)
+    high = jnp.concatenate([turned(high_ref[...], -f * width) for f in range(fold)], axis=0)
+    solved = jnp.where(panel_ref[0] == 0, low, high - product)
+    out_ref[...] = solved.T[:width, :]
+
+
+def panel_call(body, shape, matrix, parts, fold, data, *more, scalars=()):
+    rows, depth = matrix.shape[0], parts * data.shape[0] // parts * fold
+    strip = data.shape[0] // parts
+    return pl.pallas_call(
+        body,
+        grid=(1,),
+        out_shape=shape,
+        in_specs=[pl.BlockSpec(memory_space=pltpu.SMEM)] * len(scalars)
+        + [pl.BlockSpec((rows, depth), lambda i: (0, 0))]
+        + [VMEM] * (1 + len(more)),
+        out_specs=VMEM,
+        scratch_shapes=[pltpu.VMEM((parts, fold, strip, LANES), BF)],
+        compiler_params=pltpu.CompilerParams(vmem_limit_bytes=16 * 1024 * 1024),
+    )(*scalars, matrix, data, *more)
 
 
 def window_step(chosen_ref, residual_ref, window_ref):
@@ -236,28 +322,24 @@
 
     plane_rows = exchanged(copies(points, plane_size), "ctr", PLANES)
     plane_rows = plane_rows.reshape(plane_points, depth)
-    scale = inv_scale[None, :]
-    scaled_centers, center_norm = scaled_and_norm(centers, scale)
     blocks = center_index.reshape(own_rows, shards)
     order = blocks[0] // shard_rows
     here = order == shard
     local = jnp.sum(jnp.where(here[None, :], blocks - shard * shard_rows, 0), axis=1)
-    choose = (local[:, None] == jnp.arange(shard_rows, dtype=jnp.int32)[None, :]).astype(BF)
-    chosen = jnp.dot(choose, scaled_centers, preferred_element_type=F32).astype(BF)
-    chosen_norm = half_norm(chosen)
-    plane_rows, scaled_centers, chosen, order = lax.optimization_barrier(
-        (plane_rows, scaled_centers, chosen, order)
-    )
+    scale = inv_scale[None, :]
+    scaled_centers, center_norm, chosen, extra = scaled_and_norm(centers, scale, local[:, None])
+    plane_rows, extra = lax.optimization_barrier((plane_rows, extra))
     chunks = [plane_rows] + [None] * (PLANES - 1)
     for k in (2, 1, 3):
         chunks[k] = swapped(plane_rows, "ctr", k * plane_size)
-    values = None
+    held = ()
     kernels = [None] * PLANES
     for k in (0, 1, 3, 2):
         slot = (plane ^ k).astype(jnp.int32).reshape(1)
-        chunks[k], kernels[k], values = kernel_and_value(
-            slot, chunks[k], scale, scaled_centers, center_norm, coefficients, values
+        kernels[k], *held = kernel_and_value(
+            slot, chunks[k], scale, scaled_centers, center_norm, coefficients, chosen, extra, *held
         )
+    values, picked = held
     values, panel_inverse = lax.optimization_barrier((values, panel_inverse))
 
     place = (order[:, None] == jnp.arange(shards, dtype=jnp.int32)[None, :]).astype(BF)
@@ -268,32 +350,19 @@
         "rhqj,js->hrsq", inverse.reshape(own_rows, count, strip, shards), place
     ).reshape(count * own_rows, shards * strip)
 
-    def folded(matrix):
-        m = matrix.reshape(own_rows, panel_shards, fold, strip)
-        return m.transpose(2, 0, 1, 3).reshape(fold * own_rows, panel_shards * strip)
-
-    near = jnp.stack(chunks)
-    products = lax.dot_general(
-        near, chosen, (((2,), (1,)), ((), ())), preferred_element_type=F32
-    )
-    chosen_kernel = jnp.exp(products - half_norm(near)[:, :, None] - chosen_norm).astype(BF)
-    chosen_kernel = jnp.concatenate([pick(chosen_kernel, plane ^ k) for k in range(PLANES)], axis=0)
-
     own_weight = class_lookup(point_class, class_weight)
     shares = exchanged(values.reshape(shards, own_points, target_count), "ctr")
     predicted = jnp.sum(shares.astype(F32), axis=0)
     own_residual = (own_weight[:, None] * (predicted - targets)).astype(BF)
-    own_residual, factor, inverse = lax.optimization_barrier(
-        (own_residual, factor[:, :panel_rows], inverse)
-    )
-    factor_rows = folded(factor.astype(BF))
-    inverse_rows = folded(inverse)
     residual = exchanged(copies(own_residual, shards), "ctr")
     residual = residual.reshape(shards * own_points, target_count)
 
     index = group.astype(jnp.int32).reshape(1)
     window = whole(
-        window_step, jax.ShapeDtypeStruct((own_rows, target_count), F32), chosen_kernel, residual
+        window_step,
+        jax.ShapeDtypeStruct((own_rows, target_count), F32),
+        picked.reshape(shards * own_points, own_rows),
+        residual,
     )
     parts = lax.all_gather(window, "pts")
     sent = jax.ShapeDtypeStruct((shards, strip, LANES), BF)
@@ -330,17 +399,18 @@
     packed = jax.ShapeDtypeStruct((strip, LANES), F32)
     first, low, high = whole(first_step, (sent, packed, packed), solve_rows, window)
     first = exchanged(first, "ctr", HALVES).reshape(half * strip, LANES)
-    update = whole(middle_step, sent, factor_rows, first)
+    update = panel_call(middle_step, sent, factor, half, fold, first)
     update = exchanged(update, "ctr", HALVES).reshape(half * strip, LANES)
-    solved = whole(
+    solved = panel_call(
         last_step,
         jax.ShapeDtypeStruct((target_slice, own_rows), F32),
-        panel.astype(jnp.int32).reshape(1),
-        inverse_rows,
+        panel_inverse,
+        half,
+        fold,
         update,
         low,
         high,
-        scalars=1,
+        scalars=(panel.astype(jnp.int32).reshape(1),),
     )
     return (gradient, solved.T)
 

time: 154 us -> 140 us (0.909)
  local copies, waits for them, and re-layouts: 28.1 us -> 8.64 us
  blocking collectives: 6.93 us -> 20 us
  starting transfers between devices: 52.2 us -> 45.9 us
  Pallas kernels: 19.6 us -> 22.6 us
  matrix products: 6.53 us -> 4.35 us
    all_to_all x0 -> x1, blocking collectives: none -> 13 us  [exchanged(): lax.all_to_all(pieces, axis, 0, 0, tiled=True, axis_index_groups=groups i...]
    unnamed x52 -> x28, local copies, waits for them, and re-layouts: 15.3 us -> 3.87 us
    all_to_all x6 -> x5, starting transfers between devices: 43.5 us -> 37.3 us  [exchanged(): lax.all_to_all(pieces, axis, 0, 0, tiled=True, axis_index_groups=groups i...]
    pallas_call x5 -> x7, Pallas kernels: 15.6 us -> 20.5 us  [the longest x4 14.5 us: kernel_and_value(): pl.pallas_call(functools.partial(kernel_block, bool(held)), out_shape=(pl...]
    optimization_barrier x2 -> x0, local copies, waits for them, and re-layouts: 3.05 us -> none  [the longest x1 2.04 us: body(): values, panel_inverse = lax.optimization_barrier((values, panel_inverse))]
    pallas_call x5 -> x3, Pallas kernels: 3.98 us -> 2.04 us  [whole(): pl.pallas_call(body, out_shape=shapes, in_specs=[pl.BlockSpec(memory_spac...]
    reshape x4 -> x1, local copies, waits for them, and re-layouts: 2.07 us -> 0.51 us  [body(): inverse.reshape(own_rows, count, strip, shards)]
    all_to_all x6 -> x5, waiting for transfers between devices: 31.2 us -> 30.5 us  [exchanged(): lax.all_to_all(pieces, axis, 0, 0, tiled=True, axis_index_groups=groups i...]
  transfers between devices with their start and end apart: 12 -> 11, of which waited for: 7 -> 7; matrix products, arithmetic and copies ran while one was open for 14% -> 8% of each run, Pallas kernels for 10% -> 13%
where the time goes in v6:
time: 140 us; the launch traced here: 139 us
  starting transfers between devices  45.9 us (33%)
  waiting for transfers between devices  32 us (23%)
  Pallas kernels  22.6 us (16%)
  blocking collectives  20 us (14%)
  local copies, waits for them, and re-layouts  8.64 us (6%)
  other arithmetic  4.85 us (3%)
  matrix products  4.35 us (3%)
    all_to_all x5, starting transfers between devices, exchanged(): lax.all_to_all(pieces, axis, 0, 0, tiled=True, axis_index_groups=groups i...  37.3 us
    all_to_all x5, waiting for transfers between devices, exchanged(): lax.all_to_all(pieces, axis, 0, 0, tiled=True, axis_index_groups=groups i...  30.5 us
    pallas_call x4, Pallas kernels, kernel_and_value(): pl.pallas_call(functools.partial(kernel_block, bool(held)), out_shape=(pl...  14.5 us
    all_to_all x1, blocking collectives, exchanged(): lax.all_to_all(pieces, axis, 0, 0, tiled=True, axis_index_groups=groups i...  13 us
    ppermute x6, starting transfers between devices, swapped(): lax.ppermute(x, axis, [(i, i ^ bits) for i in range(lax.axis_size(axis))])  8.59 us
    all_gather x1, blocking collectives, body(): parts = lax.all_gather(window, 'pts')  6.93 us
    pallas_call x1, Pallas kernels, scaled_and_norm(): pl.pallas_call(scale_step, out_shape=(pltpu.HBM((total, depth), BF), jax....  4.61 us
    unnamed x28, local copies, waits for them, and re-layouts  3.87 us
  transfers between devices with their start and end apart: 11, of which 7 were waited for; matrix products, arithmetic and copies ran while one was open for 8% of the time, Pallas kernels for 13%

profile of v6, /device:TPU:4, one launch (start us, length us, event | category | flops | bytes accessed | tf_op | source)
XLA Modules:
  0.0 139.3 jit_solution(9389015117663988841)
XLA Ops:
  0.6 1.4 %broadcast_in_dim.32 = bf16[16,16,512]{2,1,0:T(8,128)(2,1)} broadcast(bf16[16,512]{1,0:T(8,128)(2,1)} %param.10), dimensions={1,2} | broadcast | bytes 278528 | tf_op jit(solution)/shard_map/broadcast_in_dim | solution.py:28
  2.1 9.6 %all-to-all-start = ((bf16[16,16,512]{2,1,0:T(8,128)(2,1)}), bf16[16,16,512]{2,1,0:T(8,128)(2,1)S(1)}, u32[]{:S(2)}, u32[]{:S(2)}) async-start(bf16[16,16,512]{2,1,0:T(8,128)(2,1)} %broadcast_in_dim.32), calls=%async_computation | async-start | bytes 524288 | tf_op jit(solution)/shard_map/all_to_all | solution.py:22
  11.7 0.7 broadcast_subtract_fusion
  12.5 0.7 broadcast_compare_fusion
  13.4 0.7 copy-done.4
  14.1 4.6 %shard_map.113 = (bf16[4096,512]{1,0:T(8,128)(2,1)}, f32[1,4096]{1,0:T(1,128)S(1)}, bf16[64,512]{1,0:T(8,128)(2,1)S(1)}, f32[1,64]{1,0:T(1,128)S(1)}) custom-call(bf16[4096,512]{1,0:T(8,128)(2,1)} %centers_ref.1, f32[1,512]{1,0:T(1,128)S(1)} %bitcast.68, s32[64,1]{1,0:T(8,128)S(1)} %copy.21.local_ref), custom_call_target="tpu_custom_call" | custom-call | flops 8388608 | bytes 4194304 | tf_op jit(solution)/shard_map/pallas_call | solution.py:74
  18.7 5.0 %all-to-all-done = bf16[16,16,512]{2,1,0:T(8,128)(2,1)S(1)} async-done(((bf16[16,16,512]{2,1,0:T(8,128)(2,1)}), bf16[16,16,512]{2,1,0:T(8,128)(2,1)S(1)}, u32[]{:S(2)}, u32[]{:S(2)}) %all-to-all-start) | async-done | bytes 262176 | tf_op jit(solution)/shard_map/all_to_all | solution.py:22
  23.7 1.2 collective-permute-start.2
  24.9 2.9 %collective-permute-start = (bf16[256,512]{1,0:T(8,128)(2,1)S(1)}, bf16[256,512]{1,0:T(8,128)(2,1)S(1)}, u32[]{:S(2)}, u32[]{:S(2)}) collective-permute-start(bf16[256,512]{1,0:T(8,128)(2,1)S(1)} %bitcast.61), channel_id=1, source_target_pairs={{0,32},{1,33},{2,34},{3,35},{4,36},{5,37},{6,38},{7,39},{8,40},{9,... | collective-permute-start | bytes 786440 | tf_op jit(solution)/shard_map/ppermute | solution.py:32
  27.8 5.5 %shard_map.114 = (bf16[256,4096]{1,0:T(8,128)(2,1)}, bf16[4,256,128]{2,1,0:T(8,128)(2,1)S(1)}, bf16[4,256,64]{2,1,0:T(8,128)(2,1)S(1)}) custom-call(s32[1]{0:T(128)} %bitcast.7.slot_ref, bf16[256,512]{1,0:T(8,128)(2,1)S(1)} %bitcast.62, f32[1,512]{1,0:T(1,128)S(1)} %bitcast.69, bf16[4096,512]{1,0:T(8,128)(2,1)} %get-tuple-element.31.centers_ref, ...), custom_call_target="tpu_custom_call" | custom-call | flops 1342177280 | bytes 2097152 | tf_op jit(solution)/shard_map/pallas_call | solution.py:151
  33.3 2.8 %shard_map.115 = (bf16[256,4096]{1,0:T(8,128)(2,1)}, bf16[4,256,128]{2,1,0:T(8,128)(2,1)S(1)}, bf16[4,256,64]{2,1,0:T(8,128)(2,1)S(1)}) custom-call(s32[1]{0:T(128)} %bitcast.6.slot_ref, bf16[256,512]{1,0:T(8,128)(2,1)S(1)} %collective-permute-done.2.points_ref, f32[1,512]{1,0:T(1,128)S(1)} %bitcast.70, bf16[4096,512]{1,0:T(8,128)(2,1)S(1)} %copy-done, ...), custom_call_target="tpu_custom_call" | custom-call | flops 1342177280 | bytes 2097152 | tf_op jit(solution)/shard_map/pallas_call | solution.py:151
  36.1 0.4 collective-permute-done.1.points_ref
  36.5 2.8 %shard_map.116 = (bf16[256,4096]{1,0:T(8,128)(2,1)}, bf16[4,256,128]{2,1,0:T(8,128)(2,1)S(1)}, bf16[4,256,64]{2,1,0:T(8,128)(2,1)S(1)}) custom-call(s32[1]{0:T(128)} %bitcast.5.slot_ref, bf16[256,512]{1,0:T(8,128)(2,1)S(1)} %collective-permute-done.1.points_ref, f32[1,512]{1,0:T(1,128)S(1)} %bitcast.71, bf16[4096,512]{1,0:T(8,128)(2,1)S(1)} %copy-done, ...), custom_call_target="tpu_custom_call" | custom-call | flops 1342177280 | bytes 2097152 | tf_op jit(solution)/shard_map/pallas_call | solution.py:151
  39.3 3.5 %shard_map.117 = (bf16[256,4096]{1,0:T(8,128)(2,1)}, bf16[4,256,128]{2,1,0:T(8,128)(2,1)}, bf16[4,256,64]{2,1,0:T(8,128)(2,1)S(1)}) custom-call(s32[1]{0:T(128)} %bitcast.1.slot_ref, bf16[256,512]{1,0:T(8,128)(2,1)S(1)} %collective-permute-done.points_ref, f32[1,512]{1,0:T(1,128)S(1)} %bitcast.72, bf16[4096,512]{1,0:T(8,128)(2,1)S(1)} %copy-done, ...), custom_call_target="tpu_custom_call" | custom-call | flops 1342177280 | bytes 2097152 | tf_op jit(solution)/shard_map/pallas_call | solution.py:151
  42.8 8.6 %all-to-all-start.1 = ((bf16[64,16,128]{2,1,0:T(8,128)(2,1)}), bf16[64,16,128]{2,1,0:T(8,128)(2,1)S(1)}, u32[]{:S(2)}, u32[]{:S(2)}) async-start(bf16[64,16,128]{2,1,0:T(8,128)(2,1)} %bitcast.9), calls=%async_computation.1 | async-start | bytes 524288 | tf_op jit(solution)/shard_map/all_to_all | solution.py:22
  51.4 9.8 %all-to-all-done.1 = bf16[64,16,128]{2,1,0:T(8,128)(2,1)S(1)} async-done(((bf16[64,16,128]{2,1,0:T(8,128)(2,1)}), bf16[64,16,128]{2,1,0:T(8,128)(2,1)S(1)}, u32[]{:S(2)}, u32[]{:S(2)}) %all-to-all-start.1) | async-done | bytes 262176 | tf_op jit(solution)/shard_map/all_to_all | solution.py:22
  61.4 0.7 broadcast_in_dim.56
  62.1 6.7 %all-to-all-start.2 = ((bf16[64,16,128]{2,1,0:T(8,128)(2,1)}), bf16[64,16,128]{2,1,0:T(8,128)(2,1)S(1)}, u32[]{:S(2)}, u32[]{:S(2)}) async-start(bf16[64,16,128]{2,1,0:T(8,128)(2,1)} %broadcast_in_dim.56), calls=%async_computation.2 | async-start | bytes 524288 | tf_op jit(solution)/shard_map/all_to_all | solution.py:22
  69.0 0.5 reshape.77
  69.5 0.6 convolution_bitcast_fusion
  70.1 0.5 copy.23
  70.7 0.2 reshape.78
  70.9 7.9 %all-to-all-done.2 = bf16[64,16,128]{2,1,0:T(8,128)(2,1)S(1)} async-done(((bf16[64,16,128]{2,1,0:T(8,128)(2,1)}), bf16[64,16,128]{2,1,0:T(8,128)(2,1)S(1)}, u32[]{:S(2)}, u32[]{:S(2)}) %all-to-all-start.2) | async-done | bytes 262176 | tf_op jit(solution)/shard_map/all_to_all | solution.py:22
  78.8 0.2 shard_map.118
  79.0 6.9 %all-gather = f32[256,128]{1,0:T(8,128)S(1)} all-gather(f32[64,128]{1,0:T(8,128)S(1)} %shard_map.118), channel_id=2, replica_groups=mesh['pts'=4,'ctr'=64] {'pts'}, dimensions={0}, use_global_device_ids=true | all-gather | bytes 163840 | tf_op jit(solution)/shard_map/all_gather | solution.py:367
  86.0 0.8 shard_map.119
  86.9 1.6 %collective-permute-start.3 = (bf16[128,1024]{1,0:T(8,128)(2,1)S(1)}, bf16[128,1024]{1,0:T(8,128)(2,1)S(1)}, u32[]{:S(2)}, u32[]{:S(2)}) collective-permute-start(bf16[128,1024]{1,0:T(8,128)(2,1)S(1)} %copy.24), channel_id=1, source_target_pairs={{0,32},{1,33},{2,34},{3,35},{4,36},{5,37},{6,38},{7,39},{8,40},{9,... | collective-permute-start | bytes 786440 | tf_op jit(solution)/shard_map/ppermute | solution.py:32
  88.5 7.5 %all-to-all-start.3 = ((bf16[64,16,128]{2,1,0:T(8,128)(2,1)}), bf16[64,16,128]{2,1,0:T(8,128)(2,1)S(1)}, u32[]{:S(2)}, u32[]{:S(2)}) async-start(bf16[64,16,128]{2,1,0:T(8,128)(2,1)} %shard_map.119), calls=%async_computation.3 | async-start | bytes 524288 | tf_op jit(solution)/shard_map/all_to_all | solution.py:22
  96.0 1.1 collective-permute-done.3
  97.2 2.2 %fusion.5 = f32[128,4096]{1,0:T(8,128)S(1)} fusion(bf16[256,4096]{1,0:T(8,128)(2,1)} %get-tuple-element.50, bf16[4,256,128]{2,1,0:T(8,128)(2,1)S(1)} %bitcast.55, s32[]{:T(128)S(6)} %select_n.66), kind=kOutput, calls=%fused_computation.18 | convolution fusion | flops 268435456 | bytes 4259844 | tf_op jit(solution)/shard_map/dot_general | solution.py:386
  99.4 0.5 fusion.9
  99.9 1.1 copy-done.8
  101.0 0.5 convolution_add_fusion.1
  101.5 1.1 copy-done.10
  102.6 0.5 fusion
  103.2 0.9 pad_maximum_fusion
  104.1 0.9 constant_dynamic-slice_fusion.1
  105.0 2.6 %all-to-all-done.3 = bf16[64,16,128]{2,1,0:T(8,128)(2,1)S(1)} async-done(((bf16[64,16,128]{2,1,0:T(8,128)(2,1)}), bf16[64,16,128]{2,1,0:T(8,128)(2,1)S(1)}, u32[]{:S(2)}, u32[]{:S(2)}) %all-to-all-start.3) | async-done | bytes 262176 | tf_op jit(solution)/shard_map/all_to_all | solution.py:22
  107.6 1.0 shard_map.120
  108.6 5.0 %all-to-all-start.4 = ((bf16[32,16,128]{2,1,0:T(8,128)(2,1)}), bf16[32,16,128]{2,1,0:T(8,128)(2,1)S(1)}, u32[]{:S(2)}, u32[]{:S(2)}) async-start(bf16[32,16,128]{2,1,0:T(8,128)(2,1)} %get-tuple-element.53), calls=%async_computation.4 | async-start | bytes 262144 | tf_op jit(solution)/shard_map/all_to_all | solution.py:22
  113.6 1.3 maximum_add_fusion
  114.9 0.9 copy-done.6
  115.9 2.9 %collective-permute-start.5 = (bf16[32,4096]{1,0:T(8,128)(2,1)S(1)}, bf16[32,4096]{1,0:T(8,128)(2,1)S(1)}, u32[]{:S(2)}, u32[]{:S(2)}) collective-permute-start(bf16[32,4096]{1,0:T(8,128)(2,1)S(1)} %fusion.4), channel_id=1, source_target_pairs={{0,128},{64,192},{128,0},{192,64},{1,129},{65,193},{129,1},{193,65... | collective-permute-start | bytes 786440 | tf_op jit(solution)/shard_map/ppermute | solution.py:32
  118.8 5.2 %all-to-all-done.4 = bf16[32,16,128]{2,1,0:T(8,128)(2,1)S(1)} async-done(((bf16[32,16,128]{2,1,0:T(8,128)(2,1)}), bf16[32,16,128]{2,1,0:T(8,128)(2,1)S(1)}, u32[]{:S(2)}, u32[]{:S(2)}) %all-to-all-start.4) | async-done | bytes 131104 | tf_op jit(solution)/shard_map/all_to_all | solution.py:22
  124.0 0.4 shard_map.121
  124.4 13.0 %all_to_all.30 = bf16[32,16,128]{2,1,0:T(8,128)(2,1)S(1)} all-to-all(bf16[32,16,128]{2,1,0:T(8,128)(2,1)S(1)} %shard_map.121), channel_id=1, replica_groups={{0,1,2,3,4,5,6,7,8,9,10,11,12,13,14,15,16,17,18,19,20,21,22,23,24,25,26..., dimensions={0} | all-to-all | bytes 262144 | tf_op jit(solution)/shard_map/all_to_all | solution.py:22
  137.4 1.0 shard_map.122
  138.5 0.8 fusion.2
  (42 shorter events, 0.9 us)
Async XLA Ops:
  2.1 21.6 %all-to-all-start = ((bf16[16,16,512]{2,1,0:T(8,128)(2,1)}), bf16[16,16,512]{2,1,0:T(8,128)(2,1)S(1)}, u32[]{:S(2)}, u32[]{:S(2)}) async-start(bf16[16,16,512]{2,1,0:T(8,128)(2,1)} %broadcast_in_dim.32), calls=%async_computation | async-start | bytes 524288 | tf_op jit(solution)/shard_map/all_to_all | solution.py:22
  13.4 0.7 copy-start.4
  14.1 13.7 %copy-start.1 = (bf16[4096,128]{1,0:T(8,128)(2,1)S(1)}, bf16[4096,128]{1,0:T(8,128)(2,1)}, u32[]{:S(2)}) copy-start(bf16[4096,128]{1,0:T(8,128)(2,1)} %coef_ref.7) | copy-start | bytes 3145732
  14.1 13.7 %copy-start.5 = (f32[512]{0:T(512)S(1)}, f32[512]{0:T(512)}, u32[]{:S(2)}) copy-start(f32[512]{0:T(512)} %param.14) | copy-start | bytes 6148
  23.7 9.6 %collective-permute-start.2 = (bf16[256,512]{1,0:T(8,128)(2,1)S(1)}, bf16[256,512]{1,0:T(8,128)(2,1)S(1)}, u32[]{:S(2)}, u32[]{:S(2)}) collective-permute-start(bf16[256,512]{1,0:T(8,128)(2,1)S(1)} %bitcast.59), channel_id=1, source_target_pairs={{0,16},{1,17},{2,18},{3,19},{4,20},{5,21},{6,22},{7,23},{8,24},{9,... | collective-permute-start | bytes 786440 | tf_op jit(solution)/shard_map/ppermute | solution.py:32
  24.9 11.6 %collective-permute-start.1 = (bf16[256,512]{1,0:T(8,128)(2,1)S(1)}, bf16[256,512]{1,0:T(8,128)(2,1)S(1)}, u32[]{:S(2)}, u32[]{:S(2)}) collective-permute-start(bf16[256,512]{1,0:T(8,128)(2,1)S(1)} %bitcast.60), channel_id=1, source_target_pairs={{0,48},{1,49},{2,50},{3,51},{4,52},{5,53},{6,54},{7,55},{8,56},{9,... | collective-permute-start | bytes 786440 | tf_op jit(solution)/shard_map/ppermute | solution.py:32
  24.9 14.3 %collective-permute-start = (bf16[256,512]{1,0:T(8,128)(2,1)S(1)}, bf16[256,512]{1,0:T(8,128)(2,1)S(1)}, u32[]{:S(2)}, u32[]{:S(2)}) collective-permute-start(bf16[256,512]{1,0:T(8,128)(2,1)S(1)} %bitcast.61), channel_id=1, source_target_pairs={{0,32},{1,33},{2,34},{3,35},{4,36},{5,37},{6,38},{7,39},{8,40},{9,... | collective-permute-start | bytes 786440 | tf_op jit(solution)/shard_map/ppermute | solution.py:32
  27.8 5.5 %copy-start = (bf16[4096,512]{1,0:T(8,128)(2,1)S(1)}, bf16[4096,512]{1,0:T(8,128)(2,1)}, u32[]{:S(2)}) copy-start(bf16[4096,512]{1,0:T(8,128)(2,1)} %get-tuple-element.31.centers_ref) | copy-start | bytes 12582916
  39.3 12.1 %copy-start.12 = (f32[8]{0:T(128)S(1)}, f32[8]{0:T(128)}, u32[]{:S(2)}) copy-start(f32[8]{0:T(128)} %param.13) | copy-start | bytes 100
  39.3 12.1 %copy-start.13 = (s32[16]{0:T(128)S(1)}, s32[16]{0:T(128)}, u32[]{:S(2)}) copy-start(s32[16]{0:T(128)} %param.11) | copy-start | bytes 196
  39.3 22.0 %copy-start.11 = (f32[16,128]{1,0:T(8,128)S(1)}, f32[16,128]{1,0:T(8,128)}, u32[]{:S(2)}) copy-start(f32[16,128]{1,0:T(8,128)} %param.12) | copy-start | bytes 24580
  39.3 29.6 %copy-start.2 = (f32[64,2048]{1,0:T(8,128)S(1)}, f32[64,2048]{1,0:T(8,128)}, u32[]{:S(2)}) copy-start(f32[64,2048]{1,0:T(8,128)} %matrix_ref.2) | copy-start | bytes 1572868
  42.8 18.5 %all-to-all-start.1 = ((bf16[64,16,128]{2,1,0:T(8,128)(2,1)}), bf16[64,16,128]{2,1,0:T(8,128)(2,1)S(1)}, u32[]{:S(2)}, u32[]{:S(2)}) async-start(bf16[64,16,128]{2,1,0:T(8,128)(2,1)} %bitcast.9), calls=%async_computation.1 | async-start | bytes 524288 | tf_op jit(solution)/shard_map/all_to_all | solution.py:22
  62.1 16.6 %all-to-all-start.2 = ((bf16[64,16,128]{2,1,0:T(8,128)(2,1)}), bf16[64,16,128]{2,1,0:T(8,128)(2,1)S(1)}, u32[]{:S(2)}, u32[]{:S(2)}) async-start(bf16[64,16,128]{2,1,0:T(8,128)(2,1)} %broadcast_in_dim.56), calls=%async_computation.2 | async-start | bytes 524288 | tf_op jit(solution)/shard_map/all_to_all | solution.py:22
  86.9 10.2 %collective-permute-start.3 = (bf16[128,1024]{1,0:T(8,128)(2,1)S(1)}, bf16[128,1024]{1,0:T(8,128)(2,1)S(1)}, u32[]{:S(2)}, u32[]{:S(2)}) collective-permute-start(bf16[128,1024]{1,0:T(8,128)(2,1)S(1)} %copy.24), channel_id=1, source_target_pairs={{0,32},{1,33},{2,34},{3,35},{4,36},{5,37},{6,38},{7,39},{8,40},{9,... | collective-permute-start | bytes 786440 | tf_op jit(solution)/shard_map/ppermute | solution.py:32
  88.5 19.1 %all-to-all-start.3 = ((bf16[64,16,128]{2,1,0:T(8,128)(2,1)}), bf16[64,16,128]{2,1,0:T(8,128)(2,1)S(1)}, u32[]{:S(2)}, u32[]{:S(2)}) async-start(bf16[64,16,128]{2,1,0:T(8,128)(2,1)} %shard_map.119), calls=%async_computation.3 | async-start | bytes 524288 | tf_op jit(solution)/shard_map/all_to_all | solution.py:22
  97.2 2.2 %copy-start.9 = (bf16[256,4096]{1,0:T(8,128)(2,1)S(1)}, bf16[256,4096]{1,0:T(8,128)(2,1)}, u32[]{:S(2)}) copy-start(bf16[256,4096]{1,0:T(8,128)(2,1)} %get-tuple-element.47) | copy-start | bytes 6291460
  99.4 1.6 %copy-start.8 = (bf16[256,4096]{1,0:T(8,128)(2,1)S(1)}, bf16[256,4096]{1,0:T(8,128)(2,1)}, u32[]{:S(2)}) copy-start(bf16[256,4096]{1,0:T(8,128)(2,1)} %get-tuple-element.48) | copy-start | bytes 6291460
  101.0 1.6 %copy-start.10 = (bf16[256,4096]{1,0:T(8,128)(2,1)S(1)}, bf16[256,4096]{1,0:T(8,128)(2,1)}, u32[]{:S(2)}) copy-start(bf16[256,4096]{1,0:T(8,128)(2,1)} %get-tuple-element.49) | copy-start | bytes 6291460
  104.0 9.5 %collective-permute-start.4 = (bf16[2,32,4096]{2,1,0:T(8,128)(2,1)}, bf16[2,32,4096]{2,1,0:T(8,128)(2,1)}, u32[]{:S(2)}, u32[]{:S(2)}) collective-permute-start(bf16[2,32,4096]{2,1,0:T(8,128)(2,1)} %pad_maximum_fusion), channel_id=1, source_target_pairs={{0,64},{64,0},{128,192},{192,128},{1,65},{65,1},{129,193},{193,129... | collective-permute-start | bytes 1572872 | tf_op jit(solution)/shard_map/ppermute | solution.py:32
  107.6 16.4 %copy-start.3 = (f32[64,4096]{1,0:T(8,128)S(1)}, f32[64,4096]{1,0:T(8,128)}, u32[]{:S(2)}) copy-start(f32[64,4096]{1,0:T(8,128)} %matrix_ref.1) | copy-start | bytes 3145732
  108.6 15.4 %all-to-all-start.4 = ((bf16[32,16,128]{2,1,0:T(8,128)(2,1)}), bf16[32,16,128]{2,1,0:T(8,128)(2,1)S(1)}, u32[]{:S(2)}, u32[]{:S(2)}) async-start(bf16[32,16,128]{2,1,0:T(8,128)(2,1)} %get-tuple-element.53), calls=%async_computation.4 | async-start | bytes 262144 | tf_op jit(solution)/shard_map/all_to_all | solution.py:22
  114.9 1.0 copy-start.6
  115.9 22.6 %collective-permute-start.5 = (bf16[32,4096]{1,0:T(8,128)(2,1)S(1)}, bf16[32,4096]{1,0:T(8,128)(2,1)S(1)}, u32[]{:S(2)}, u32[]{:S(2)}) collective-permute-start(bf16[32,4096]{1,0:T(8,128)(2,1)S(1)} %fusion.4), channel_id=1, source_target_pairs={{0,128},{64,192},{128,0},{192,64},{1,129},{65,193},{129,1},{193,65... | collective-permute-start | bytes 786440 | tf_op jit(solution)/shard_map/ppermute | solution.py:32
  124.0 14.5 %copy-start.7 = (f32[2,32,4096]{2,1,0:T(8,128)S(1)}, f32[2,32,4096]{2,1,0:T(8,128)}, u32[]{:S(2)}) copy-start(f32[2,32,4096]{2,1,0:T(8,128)} %copy-done.6) | copy-start | bytes 3145732

commit v7 on v6

--- a/solution.py
+++ b/solution.py
@@ -93,14 +93,16 @@
 def kernel_block(
     held, slot_ref, points_ref, scale_ref, centers_ref, norm_ref, coef_ref, chosen_ref, extra_ref, *refs
 ):
-    kernel_ref, value_ref, picked_ref, slots, sems, *stream = refs[2 * held :]
+    kernel_ref, value_ref, picked_ref, *rest = refs[2 * held :]
+    stream = [] if held else [rest[0], rest[-1]]
+    slots, sems = rest[-2:] if held else rest[1:3]
     steps = centers_ref.shape[0] // TILE
     loads = []
     if stream:
         for i in range(steps):
             rows = pl.ds(i * TILE, TILE)
             loads.append(
-                pltpu.make_async_copy(centers_ref.at[rows, :], stream[0].at[i], stream[1].at[i])
+                pltpu.make_async_copy(centers_ref.at[rows, :], stream[0].at[rows, :], stream[1].at[i])
             )
             loads[-1].start()
     samples = (points_ref[...].astype(F32) * scale_ref[...]).astype(BF)
@@ -123,7 +125,7 @@
         rows = pl.ds(i * TILE, TILE)
         if stream:
             loads[i].wait()
-        anchors = stream[0][i] if stream else centers_ref[rows, :]
+        anchors = stream[0][rows, :] if stream else centers_ref[rows, :]
         current = block(anchors, norm_ref[:, rows])
         slots[i] = current
         saves.append(pltpu.make_async_copy(slots.at[i], kernel_ref.at[:, rows], sems.at[i]))
@@ -145,7 +147,6 @@
     total, cols = coefficients.shape
     steps = total // TILE
     space = VMEM if held else pl.BlockSpec(memory_space=pltpu.HBM)
-    loaded = [pltpu.VMEM((steps, TILE, depth), BF), pltpu.SemaphoreType.DMA((steps,))]
     args = [samples, scale, anchors if held else pltpu.with_memory_space_constraint(anchors, pltpu.HBM)]
     args += [norms, coefficients, chosen, extra, *held]
     return pl.pallas_call(
@@ -154,12 +155,13 @@
             pltpu.HBM((count, total), BF),
             jax.ShapeDtypeStruct((PLANES, count, cols), BF),
             jax.ShapeDtypeStruct((PLANES, count, chosen.shape[0]), BF),
-        ),
+        )
+        + (() if held else (pltpu.VMEM((total, depth), BF),)),
         in_specs=[pl.BlockSpec(memory_space=pltpu.SMEM), VMEM, VMEM, space]
         + [VMEM] * (len(args) - 3),
-        out_specs=[pl.BlockSpec(memory_space=pltpu.HBM), VMEM, VMEM],
-        scratch_shapes=[pltpu.VMEM((steps, count, TILE), BF), pltpu.SemaphoreType.DMA((steps,))]
-        + ([] if held else loaded),
+        out_specs=[pl.BlockSpec(memory_space=pltpu.HBM)] + [VMEM] * (2 if held else 3),
+        scratch_shapes=[pltpu.VMEM((steps, count, TILE), BF)]
+        + [pltpu.SemaphoreType.DMA((steps,))] * (1 if held else 2),
         compiler_params=pltpu.CompilerParams(vmem_limit_bytes=24 * 1024 * 1024),
         cost_estimate=pl.CostEstimate(
             flops=2 * count * total * (depth + cols),
@@ -250,6 +252,12 @@
     )(*scalars, matrix, data, *more)
 
 
+def residual_step(shares_ref, targets_ref, weight_ref, sent_ref):
+    predicted = jnp.sum(shares_ref[...].astype(F32), axis=0)
+    residual = (weight_ref[...] * (predicted - targets_ref[...])).astype(BF)
+    sent_ref[...] = jnp.broadcast_to(residual[None], sent_ref.shape)
+
+
 def window_step(chosen_ref, residual_ref, window_ref):
     window_ref[...] = lax.dot_general(
         chosen_ref[...], residual_ref[...], (((0,), (0,)), ((), ())), preferred_element_type=F32
@@ -279,10 +287,6 @@
         out_specs=jax.tree.map(lambda _: VMEM, shapes),
         compiler_params=pltpu.CompilerParams(vmem_limit_bytes=16 * 1024 * 1024),
     )(*args)
-
-
-def half_norm(rows):
-    return 0.5 * jnp.sum(jnp.square(rows.astype(F32)), axis=-1)
 
 
 def class_lookup(labels, table):
@@ -328,7 +332,17 @@
     local = jnp.sum(jnp.where(here[None, :], blocks - shard * shard_rows, 0), axis=1)
     scale = inv_scale[None, :]
     scaled_centers, center_norm, chosen, extra = scaled_and_norm(centers, scale, local[:, None])
-    plane_rows, extra = lax.optimization_barrier((plane_rows, extra))
+    place = (order[:, None] == jnp.arange(shards, dtype=jnp.int32)[None, :]).astype(BF)
+
+    inverse = panel_inverse.astype(BF)
+    count = panel_rows // (strip * shards)
+    turned_inverse = jnp.einsum(
+        "rhqj,js->hrsq", inverse.reshape(own_rows, count, strip, shards), place
+    ).reshape(count * own_rows, shards * strip)
+    weight = class_lookup(point_class, class_weight)[:, None]
+    plane_rows, extra, turned_inverse, weight = lax.optimization_barrier(
+        (plane_rows, extra, turned_inverse, weight)
+    )
     chunks = [plane_rows] + [None] * (PLANES - 1)
     for k in (2, 1, 3):
         chunks[k] = swapped(plane_rows, "ctr", k * plane_size)
@@ -339,23 +353,19 @@
         kernels[k], *held = kernel_and_value(
             slot, chunks[k], scale, scaled_centers, center_norm, coefficients, chosen, extra, *held
         )
+        if k == 0:
+            scaled_centers = held.pop()
     values, picked = held
-    values, panel_inverse = lax.optimization_barrier((values, panel_inverse))
-
-    place = (order[:, None] == jnp.arange(shards, dtype=jnp.int32)[None, :]).astype(BF)
-
-    inverse = panel_inverse.astype(BF)
-    count = panel_rows // (strip * shards)
-    turned_inverse = jnp.einsum(
-        "rhqj,js->hrsq", inverse.reshape(own_rows, count, strip, shards), place
-    ).reshape(count * own_rows, shards * strip)
-
-    own_weight = class_lookup(point_class, class_weight)
+
     shares = exchanged(values.reshape(shards, own_points, target_count), "ctr")
-    predicted = jnp.sum(shares.astype(F32), axis=0)
-    own_residual = (own_weight[:, None] * (predicted - targets)).astype(BF)
-    residual = exchanged(copies(own_residual, shards), "ctr")
-    residual = residual.reshape(shards * own_points, target_count)
+    residual = whole(
+        residual_step,
+        jax.ShapeDtypeStruct((shards, own_points, target_count), BF),
+        shares,
+        targets,
+        weight,
+    )
+    residual = exchanged(residual, "ctr").reshape(shards * own_points, target_count)
 
     index = group.astype(jnp.int32).reshape(1)
     window = whole(

time: 140 us -> 142 us (1.014)
  starting transfers between devices: 45.9 us -> 48.4 us
  local copies, waits for them, and re-layouts: 8.64 us -> 6.55 us
    all_to_all x5, starting transfers between devices: 37.3 us -> 39.6 us  [exchanged(): lax.all_to_all(pieces, axis, 0, 0, tiled=True, axis_index_groups=groups i...]
    unnamed x28 -> x20, local copies, waits for them, and re-layouts: 3.87 us -> 2.23 us
where the time goes in v7:
time: 142 us; the launch traced here: 141 us
  starting transfers between devices  48.4 us (34%)
  waiting for transfers between devices  33.1 us (23%)
  Pallas kernels  23.2 us (16%)
  blocking collectives  19.7 us (14%)
  local copies, waits for them, and re-layouts  6.55 us (5%)
  other arithmetic  5.01 us (4%)
  matrix products  4.36 us (3%)
    all_to_all x5, starting transfers between devices, exchanged(): lax.all_to_all(pieces, axis, 0, 0, tiled=True, axis_index_groups=groups i...  39.6 us
    all_to_all x5, waiting for transfers between devices, exchanged(): lax.all_to_all(pieces, axis, 0, 0, tiled=True, axis_index_groups=groups i...  31.6 us
    pallas_call x4, Pallas kernels, kernel_and_value(): pl.pallas_call(functools.partial(kernel_block, bool(held)), out_shape=(pl...  14.3 us
    all_to_all x1, blocking collectives, exchanged(): lax.all_to_all(pieces, axis, 0, 0, tiled=True, axis_index_groups=groups i...  12.8 us
    ppermute x6, starting transfers between devices, swapped(): lax.ppermute(x, axis, [(i, i ^ bits) for i in range(lax.axis_size(axis))])  8.77 us
    all_gather x1, blocking collectives, body(): parts = lax.all_gather(window, 'pts')  6.93 us
    pallas_call x1, Pallas kernels, scaled_and_norm(): pl.pallas_call(scale_step, out_shape=(pltpu.HBM((total, depth), BF), jax....  4.63 us
    dot_general x4, matrix products, body(): lax.dot_general(pick(planes, plane ^ k), kernels[k], (((0,), (0,)), ((),...  3.72 us
  transfers between devices with their start and end apart: 11, of which 7 were waited for; matrix products, arithmetic and copies ran while one was open for 8% of the time, Pallas kernels for 13%

profile of v7, /device:TPU:4, one launch (start us, length us, event | category | flops | bytes accessed | tf_op | source)
XLA Modules:
  0.0 141.3 jit_solution(1496184946084117850)
XLA Ops:
  0.6 1.4 %broadcast_in_dim.45 = bf16[16,16,512]{2,1,0:T(8,128)(2,1)} broadcast(bf16[16,512]{1,0:T(8,128)(2,1)} %param.10), dimensions={1,2} | broadcast | bytes 278528 | tf_op jit(solution)/shard_map/broadcast_in_dim | solution.py:28
  2.1 9.6 %all-to-all-start = ((bf16[16,16,512]{2,1,0:T(8,128)(2,1)}), bf16[16,16,512]{2,1,0:T(8,128)(2,1)S(1)}, u32[]{:S(2)}, u32[]{:S(2)}) async-start(bf16[16,16,512]{2,1,0:T(8,128)(2,1)} %broadcast_in_dim.45), calls=%async_computation | async-start | bytes 524288 | tf_op jit(solution)/shard_map/all_to_all | solution.py:22
  11.7 0.7 broadcast_subtract_fusion
  12.4 0.7 broadcast_compare_fusion
  13.2 0.1 select_reduce_fusion
  13.4 1.1 convert_element_type.15
  14.5 0.5 reshape.69
  15.0 0.6 convolution_bitcast_fusion
  15.6 0.5 copy.25
  16.2 0.3 reshape.70
  16.5 4.6 %shard_map.113 = (bf16[4096,512]{1,0:T(8,128)(2,1)}, f32[1,4096]{1,0:T(1,128)S(1)}, bf16[64,512]{1,0:T(8,128)(2,1)S(1)}, f32[1,64]{1,0:T(1,128)S(1)}) custom-call(bf16[4096,512]{1,0:T(8,128)(2,1)} %centers_ref.1, f32[1,512]{1,0:T(1,128)S(1)} %bitcast.69, s32[64,1]{1,0:T(8,128)S(1)} %copy.23.local_ref), custom_call_target="tpu_custom_call" | custom-call | flops 8388608 | bytes 4194304 | tf_op jit(solution)/shard_map/pallas_call | solution.py:74
  21.2 2.5 %all-to-all-done = bf16[16,16,512]{2,1,0:T(8,128)(2,1)S(1)} async-done(((bf16[16,16,512]{2,1,0:T(8,128)(2,1)}), bf16[16,16,512]{2,1,0:T(8,128)(2,1)S(1)}, u32[]{:S(2)}, u32[]{:S(2)}) %all-to-all-start) | async-done | bytes 262176 | tf_op jit(solution)/shard_map/all_to_all | solution.py:22
  23.7 1.2 collective-permute-start.2
  24.9 2.9 %collective-permute-start = (bf16[256,512]{1,0:T(8,128)(2,1)S(1)}, bf16[256,512]{1,0:T(8,128)(2,1)S(1)}, u32[]{:S(2)}, u32[]{:S(2)}) collective-permute-start(bf16[256,512]{1,0:T(8,128)(2,1)S(1)} %bitcast.62), channel_id=1, source_target_pairs={{0,32},{1,33},{2,34},{3,35},{4,36},{5,37},{6,38},{7,39},{8,40},{9,... | collective-permute-start | bytes 786440 | tf_op jit(solution)/shard_map/ppermute | solution.py:32
  27.8 5.3 %shard_map.114 = (bf16[256,4096]{1,0:T(8,128)(2,1)}, bf16[4,256,128]{2,1,0:T(8,128)(2,1)S(1)}, bf16[4,256,64]{2,1,0:T(8,128)(2,1)S(1)}, bf16[4096,512]{1,0:T(8,128)(2,1)S(1)}) custom-call(s32[1]{0:T(128)} %bitcast.9.slot_ref, bf16[256,512]{1,0:T(8,128)(2,1)S(1)} %bitcast.63, f32[1,512]{1,0:T(1,128)S(1)} %bitcast.70, ...), custom_call_target="tpu_custom_call" | custom-call | flops 1342177280 | bytes 2097152 | tf_op jit(solution)/shard_map/pallas_call | solution.py:152
  33.1 2.8 %shard_map.115 = (bf16[256,4096]{1,0:T(8,128)(2,1)}, bf16[4,256,128]{2,1,0:T(8,128)(2,1)S(1)}, bf16[4,256,64]{2,1,0:T(8,128)(2,1)S(1)}) custom-call(s32[1]{0:T(128)} %bitcast.11.slot_ref, bf16[256,512]{1,0:T(8,128)(2,1)S(1)} %collective-permute-done.2.points_ref, f32[1,512]{1,0:T(1,128)S(1)} %bitcast.71, ...), custom_call_target="tpu_custom_call" | custom-call | flops 1342177280 | bytes 2097152 | tf_op jit(solution)/shard_map/pallas_call | solution.py:152
  35.9 0.6 collective-permute-done.1.points_ref
  36.5 2.8 %shard_map.116 = (bf16[256,4096]{1,0:T(8,128)(2,1)}, bf16[4,256,128]{2,1,0:T(8,128)(2,1)S(1)}, bf16[4,256,64]{2,1,0:T(8,128)(2,1)S(1)}) custom-call(s32[1]{0:T(128)} %bitcast.10.slot_ref, bf16[256,512]{1,0:T(8,128)(2,1)S(1)} %collective-permute-done.1.points_ref, f32[1,512]{1,0:T(1,128)S(1)} %bitcast.72, ...), custom_call_target="tpu_custom_call" | custom-call | flops 1342177280 | bytes 2097152 | tf_op jit(solution)/shard_map/pallas_call | solution.py:152
  39.3 3.5 %shard_map.117 = (bf16[256,4096]{1,0:T(8,128)(2,1)}, bf16[4,256,128]{2,1,0:T(8,128)(2,1)}, bf16[4,256,64]{2,1,0:T(8,128)(2,1)S(1)}) custom-call(s32[1]{0:T(128)} %bitcast.1.slot_ref, bf16[256,512]{1,0:T(8,128)(2,1)S(1)} %collective-permute-done.points_ref, f32[1,512]{1,0:T(1,128)S(1)} %bitcast.73, bf16[4096,512]{1,0:T(8,128)(2,1)S(1)} %get-tuple-element.36.centers_ref, ...), custom_call_target="tpu_custom_call" | custom-call | flops 1342177280 | bytes 2097152 | tf_op jit(solution)/shard_map/pallas_call | solution.py:152
  42.7 11.1 %all-to-all-start.1 = ((bf16[64,16,128]{2,1,0:T(8,128)(2,1)}), bf16[64,16,128]{2,1,0:T(8,128)(2,1)S(1)}, u32[]{:S(2)}, u32[]{:S(2)}) async-start(bf16[64,16,128]{2,1,0:T(8,128)(2,1)} %bitcast.13), calls=%async_computation.1 | async-start | bytes 524288 | tf_op jit(solution)/shard_map/all_to_all | solution.py:22
  53.9 9.8 %all-to-all-done.1.shares_ref = bf16[64,16,128]{2,1,0:T(8,128)(2,1)S(1)} async-done(((bf16[64,16,128]{2,1,0:T(8,128)(2,1)}), bf16[64,16,128]{2,1,0:T(8,128)(2,1)S(1)}, u32[]{:S(2)}, u32[]{:S(2)}) %all-to-all-start.1) | async-done | bytes 262176 | tf_op jit(solution)/shard_map/all_to_all | solution.py:22
  63.7 0.8 shard_map.118
  64.5 6.7 %all-to-all-start.2 = ((bf16[64,16,128]{2,1,0:T(8,128)(2,1)}), bf16[64,16,128]{2,1,0:T(8,128)(2,1)S(1)}, u32[]{:S(2)}, u32[]{:S(2)}) async-start(bf16[64,16,128]{2,1,0:T(8,128)(2,1)} %shard_map.118), calls=%async_computation.2 | async-start | bytes 524288 | tf_op jit(solution)/shard_map/all_to_all | solution.py:22
  71.3 9.9 %all-to-all-done.2 = bf16[64,16,128]{2,1,0:T(8,128)(2,1)S(1)} async-done(((bf16[64,16,128]{2,1,0:T(8,128)(2,1)}), bf16[64,16,128]{2,1,0:T(8,128)(2,1)S(1)}, u32[]{:S(2)}, u32[]{:S(2)}) %all-to-all-start.2) | async-done | bytes 262176 | tf_op jit(solution)/shard_map/all_to_all | solution.py:22
  81.2 0.2 shard_map.119
  81.4 6.9 %all-gather = f32[256,128]{1,0:T(8,128)S(1)} all-gather(f32[64,128]{1,0:T(8,128)S(1)} %shard_map.119), channel_id=2, replica_groups=mesh['pts'=4,'ctr'=64] {'pts'}, dimensions={0}, use_global_device_ids=true | all-gather | bytes 163840 | tf_op jit(solution)/shard_map/all_gather | solution.py:377
  88.3 0.8 shard_map.120
  89.2 0.1 copy.27
  89.3 1.6 %collective-permute-start.3 = (bf16[128,1024]{1,0:T(8,128)(2,1)S(1)}, bf16[128,1024]{1,0:T(8,128)(2,1)S(1)}, u32[]{:S(2)}, u32[]{:S(2)}) collective-permute-start(bf16[128,1024]{1,0:T(8,128)(2,1)S(1)} %copy.27), channel_id=1, source_target_pairs={{0,32},{1,33},{2,34},{3,35},{4,36},{5,37},{6,38},{7,39},{8,40},{9,... | collective-permute-start | bytes 786440 | tf_op jit(solution)/shard_map/ppermute | solution.py:32
  90.9 7.7 %all-to-all-start.3 = ((bf16[64,16,128]{2,1,0:T(8,128)(2,1)}), bf16[64,16,128]{2,1,0:T(8,128)(2,1)S(1)}, u32[]{:S(2)}, u32[]{:S(2)}) async-start(bf16[64,16,128]{2,1,0:T(8,128)(2,1)} %shard_map.120), calls=%async_computation.3 | async-start | bytes 524288 | tf_op jit(solution)/shard_map/all_to_all | solution.py:22
  98.6 0.9 collective-permute-done.3
  99.5 2.2 %fusion.5 = f32[128,4096]{1,0:T(8,128)S(1)} fusion(bf16[256,4096]{1,0:T(8,128)(2,1)} %get-tuple-element.52, bf16[4,256,128]{2,1,0:T(8,128)(2,1)S(1)} %bitcast.56, s32[]{:T(128)S(6)} %select_n.66), kind=kOutput, calls=%fused_computation.17 | convolution fusion | flops 268435456 | bytes 4259844 | tf_op jit(solution)/shard_map/dot_general | solution.py:396
  101.7 0.5 fusion.9
  102.2 1.1 copy-done.5
  103.3 0.5 convolution_add_fusion.1
  103.8 1.1 copy-done.7
  104.9 0.5 fusion
  105.8 1.1 constant_dynamic-slice_fusion.1
  106.9 3.3 %all-to-all-done.3 = bf16[64,16,128]{2,1,0:T(8,128)(2,1)S(1)} async-done(((bf16[64,16,128]{2,1,0:T(8,128)(2,1)}), bf16[64,16,128]{2,1,0:T(8,128)(2,1)S(1)}, u32[]{:S(2)}, u32[]{:S(2)}) %all-to-all-start.3) | async-done | bytes 262176 | tf_op jit(solution)/shard_map/all_to_all | solution.py:22
  110.2 1.0 shard_map.121
  111.2 4.5 %all-to-all-start.4 = ((bf16[32,16,128]{2,1,0:T(8,128)(2,1)}), bf16[32,16,128]{2,1,0:T(8,128)(2,1)S(1)}, u32[]{:S(2)}, u32[]{:S(2)}) async-start(bf16[32,16,128]{2,1,0:T(8,128)(2,1)} %get-tuple-element.55), calls=%async_computation.4 | async-start | bytes 262144 | tf_op jit(solution)/shard_map/all_to_all | solution.py:22
  115.7 1.3 maximum_add_fusion
  117.1 3.0 %collective-permute-start.5 = (bf16[32,4096]{1,0:T(8,128)(2,1)S(1)}, bf16[32,4096]{1,0:T(8,128)(2,1)S(1)}, u32[]{:S(2)}, u32[]{:S(2)}) collective-permute-start(bf16[32,4096]{1,0:T(8,128)(2,1)S(1)} %fusion.4), channel_id=1, source_target_pairs={{0,128},{64,192},{128,0},{192,64},{1,129},{65,193},{129,1},{193,65... | collective-permute-start | bytes 786440 | tf_op jit(solution)/shard_map/ppermute | solution.py:32
  120.1 6.1 %all-to-all-done.4 = bf16[32,16,128]{2,1,0:T(8,128)(2,1)S(1)} async-done(((bf16[32,16,128]{2,1,0:T(8,128)(2,1)}), bf16[32,16,128]{2,1,0:T(8,128)(2,1)S(1)}, u32[]{:S(2)}, u32[]{:S(2)}) %all-to-all-start.4) | async-done | bytes 131104 | tf_op jit(solution)/shard_map/all_to_all | solution.py:22
  126.1 0.4 shard_map.122
  126.6 12.8 %all_to_all.30 = bf16[32,16,128]{2,1,0:T(8,128)(2,1)S(1)} all-to-all(bf16[32,16,128]{2,1,0:T(8,128)(2,1)S(1)} %shard_map.122), channel_id=1, replica_groups={{0,1,2,3,4,5,6,7,8,9,10,11,12,13,14,15,16,17,18,19,20,21,22,23,24,25,26..., dimensions={0} | all-to-all | bytes 262144 | tf_op jit(solution)/shard_map/all_to_all | solution.py:22
  139.4 1.0 shard_map.123
  140.4 0.8 fusion.2
  (33 shorter events, 0.7 us)
Async XLA Ops:
  2.1 21.6 %all-to-all-start = ((bf16[16,16,512]{2,1,0:T(8,128)(2,1)}), bf16[16,16,512]{2,1,0:T(8,128)(2,1)S(1)}, u32[]{:S(2)}, u32[]{:S(2)}) async-start(bf16[16,16,512]{2,1,0:T(8,128)(2,1)} %broadcast_in_dim.45), calls=%async_computation | async-start | bytes 524288 | tf_op jit(solution)/shard_map/all_to_all | solution.py:22
  13.4 3.1 %copy-start.3 = (f32[512]{0:T(512)S(1)}, f32[512]{0:T(512)}, u32[]{:S(2)}) copy-start(f32[512]{0:T(512)} %param.14) | copy-start | bytes 6148
  16.4 4.7 %copy-start.8 = (f32[8]{0:T(128)S(1)}, f32[8]{0:T(128)}, u32[]{:S(2)}) copy-start(f32[8]{0:T(128)} %param.13) | copy-start | bytes 100
  16.5 4.7 %copy-start.9 = (s32[16]{0:T(128)S(1)}, s32[16]{0:T(128)}, u32[]{:S(2)}) copy-start(s32[16]{0:T(128)} %param.11) | copy-start | bytes 196
  16.5 11.3 %copy-start = (bf16[4096,128]{1,0:T(8,128)(2,1)S(1)}, bf16[4096,128]{1,0:T(8,128)(2,1)}, u32[]{:S(2)}) copy-start(bf16[4096,128]{1,0:T(8,128)(2,1)} %coef_ref.7) | copy-start | bytes 3145732
  23.7 9.4 %collective-permute-start.2 = (bf16[256,512]{1,0:T(8,128)(2,1)S(1)}, bf16[256,512]{1,0:T(8,128)(2,1)S(1)}, u32[]{:S(2)}, u32[]{:S(2)}) collective-permute-start(bf16[256,512]{1,0:T(8,128)(2,1)S(1)} %bitcast.60), channel_id=1, source_target_pairs={{0,16},{1,17},{2,18},{3,19},{4,20},{5,21},{6,22},{7,23},{8,24},{9,... | collective-permute-start | bytes 786440 | tf_op jit(solution)/shard_map/ppermute | solution.py:32
  24.9 11.6 %collective-permute-start.1 = (bf16[256,512]{1,0:T(8,128)(2,1)S(1)}, bf16[256,512]{1,0:T(8,128)(2,1)S(1)}, u32[]{:S(2)}, u32[]{:S(2)}) collective-permute-start(bf16[256,512]{1,0:T(8,128)(2,1)S(1)} %bitcast.61), channel_id=1, source_target_pairs={{0,48},{1,49},{2,50},{3,51},{4,52},{5,53},{6,54},{7,55},{8,56},{9,... | collective-permute-start | bytes 786440 | tf_op jit(solution)/shard_map/ppermute | solution.py:32
  24.9 14.3 %collective-permute-start = (bf16[256,512]{1,0:T(8,128)(2,1)S(1)}, bf16[256,512]{1,0:T(8,128)(2,1)S(1)}, u32[]{:S(2)}, u32[]{:S(2)}) collective-permute-start(bf16[256,512]{1,0:T(8,128)(2,1)S(1)} %bitcast.62), channel_id=1, source_target_pairs={{0,32},{1,33},{2,34},{3,35},{4,36},{5,37},{6,38},{7,39},{8,40},{9,... | collective-permute-start | bytes 786440 | tf_op jit(solution)/shard_map/ppermute | solution.py:32
  39.2 24.5 %copy-start.4 = (f32[16,128]{1,0:T(8,128)S(1)}, f32[16,128]{1,0:T(8,128)}, u32[]{:S(2)}) copy-start(f32[16,128]{1,0:T(8,128)} %targets_ref.1) | copy-start | bytes 24580
  42.7 21.0 %all-to-all-start.1 = ((bf16[64,16,128]{2,1,0:T(8,128)(2,1)}), bf16[64,16,128]{2,1,0:T(8,128)(2,1)S(1)}, u32[]{:S(2)}, u32[]{:S(2)}) async-start(bf16[64,16,128]{2,1,0:T(8,128)(2,1)} %bitcast.13), calls=%async_computation.1 | async-start | bytes 524288 | tf_op jit(solution)/shard_map/all_to_all | solution.py:22
  64.5 16.6 %all-to-all-start.2 = ((bf16[64,16,128]{2,1,0:T(8,128)(2,1)}), bf16[64,16,128]{2,1,0:T(8,128)(2,1)S(1)}, u32[]{:S(2)}, u32[]{:S(2)}) async-start(bf16[64,16,128]{2,1,0:T(8,128)(2,1)} %shard_map.118), calls=%async_computation.2 | async-start | bytes 524288 | tf_op jit(solution)/shard_map/all_to_all | solution.py:22
  89.3 10.2 %collective-permute-start.3 = (bf16[128,1024]{1,0:T(8,128)(2,1)S(1)}, bf16[128,1024]{1,0:T(8,128)(2,1)S(1)}, u32[]{:S(2)}, u32[]{:S(2)}) collective-permute-start(bf16[128,1024]{1,0:T(8,128)(2,1)S(1)} %copy.27), channel_id=1, source_target_pairs={{0,32},{1,33},{2,34},{3,35},{4,36},{5,37},{6,38},{7,39},{8,40},{9,... | collective-permute-start | bytes 786440 | tf_op jit(solution)/shard_map/ppermute | solution.py:32
  90.9 19.3 %all-to-all-start.3 = ((bf16[64,16,128]{2,1,0:T(8,128)(2,1)}), bf16[64,16,128]{2,1,0:T(8,128)(2,1)S(1)}, u32[]{:S(2)}, u32[]{:S(2)}) async-start(bf16[64,16,128]{2,1,0:T(8,128)(2,1)} %shard_map.120), calls=%async_computation.3 | async-start | bytes 524288 | tf_op jit(solution)/shard_map/all_to_all | solution.py:22
  99.5 2.2 %copy-start.6 = (bf16[256,4096]{1,0:T(8,128)(2,1)S(1)}, bf16[256,4096]{1,0:T(8,128)(2,1)}, u32[]{:S(2)}) copy-start(bf16[256,4096]{1,0:T(8,128)(2,1)} %get-tuple-element.49) | copy-start | bytes 6291460
  101.7 1.6 %copy-start.5 = (bf16[256,4096]{1,0:T(8,128)(2,1)S(1)}, bf16[256,4096]{1,0:T(8,128)(2,1)}, u32[]{:S(2)}) copy-start(bf16[256,4096]{1,0:T(8,128)(2,1)} %get-tuple-element.50) | copy-start | bytes 6291460
  103.3 1.6 %copy-start.7 = (bf16[256,4096]{1,0:T(8,128)(2,1)S(1)}, bf16[256,4096]{1,0:T(8,128)(2,1)}, u32[]{:S(2)}) copy-start(bf16[256,4096]{1,0:T(8,128)(2,1)} %get-tuple-element.51) | copy-start | bytes 6291460
  105.6 10.1 %collective-permute-start.4 = (bf16[2,32,4096]{2,1,0:T(8,128)(2,1)S(1)}, bf16[2,32,4096]{2,1,0:T(8,128)(2,1)S(1)}, u32[]{:S(2)}, u32[]{:S(2)}) collective-permute-start(bf16[2,32,4096]{2,1,0:T(8,128)(2,1)S(1)} %pad_maximum_fusion), channel_id=1, source_target_pairs={{0,64},{64,0},{128,192},{192,128},{1,65},{65,1},{129,193},{193,129... | collective-permute-start | bytes 1572872 | tf_op jit(solution)/shard_map/ppermute | solution.py:32
  110.2 15.9 %copy-start.2 = (f32[64,4096]{1,0:T(8,128)S(1)}, f32[64,4096]{1,0:T(8,128)}, u32[]{:S(2)}) copy-start(f32[64,4096]{1,0:T(8,128)} %matrix_ref.2) | copy-start | bytes 3145732
  111.2 15.0 %all-to-all-start.4 = ((bf16[32,16,128]{2,1,0:T(8,128)(2,1)}), bf16[32,16,128]{2,1,0:T(8,128)(2,1)S(1)}, u32[]{:S(2)}, u32[]{:S(2)}) async-start(bf16[32,16,128]{2,1,0:T(8,128)(2,1)} %get-tuple-element.55), calls=%async_computation.4 | async-start | bytes 262144 | tf_op jit(solution)/shard_map/all_to_all | solution.py:22
  115.7 23.7 %copy-start.1 = (f32[64,2048]{1,0:T(8,128)S(1)}, f32[64,2048]{1,0:T(8,128)}, u32[]{:S(2)}) copy-start(f32[64,2048]{1,0:T(8,128)} %matrix_ref.3) | copy-start | bytes 1572868
  117.1 23.3 %collective-permute-start.5 = (bf16[32,4096]{1,0:T(8,128)(2,1)S(1)}, bf16[32,4096]{1,0:T(8,128)(2,1)S(1)}, u32[]{:S(2)}, u32[]{:S(2)}) collective-permute-start(bf16[32,4096]{1,0:T(8,128)(2,1)S(1)} %fusion.4), channel_id=1, source_target_pairs={{0,128},{64,192},{128,0},{192,64},{1,129},{65,193},{129,1},{193,65... | collective-permute-start | bytes 786440 | tf_op jit(solution)/shard_map/ppermute | solution.py:32

commit v8 on v7

--- a/solution.py
+++ b/solution.py
@@ -13,6 +13,7 @@
 PLANES = 4
 HALVES = 2
 TILE = 512
+EARLY = 2
 VMEM = pl.BlockSpec(memory_space=pltpu.VMEM)
 
 
@@ -30,10 +31,6 @@
 
 def swapped(x, axis, bits):
     return lax.ppermute(x, axis, [(i, i ^ bits) for i in range(lax.axis_size(axis))])
-
-
-def pick(x, index):
-    return lax.dynamic_index_in_dim(x, index, 0, keepdims=False)
 
 
 def scale_step(
@@ -123,8 +120,9 @@
     before = None
     for i in range(steps):
         rows = pl.ds(i * TILE, TILE)
-        if stream:
-            loads[i].wait()
+        if stream and i in (0, EARLY):
+            for load in loads[i : EARLY if i == 0 else steps]:
+                load.wait()
         anchors = stream[0][rows, :] if stream else centers_ref[rows, :]
         current = block(anchors, norm_ref[:, rows])
         slots[i] = current
@@ -277,6 +275,61 @@
             out = part if out is None else jnp.where(lane_block(part.shape, width, r), part, out)
         result = out if result is None else jnp.where(group_ref[0] == p, out, result)
     sent_ref[...] = jnp.broadcast_to(result.astype(BF)[None], sent_ref.shape)
+
+
+def gradient_step(index_ref, residual_ref, token_ref, *refs):
+    blocks, (*parts, turned_ref, stage_ref) = refs[:PLANES], refs[PLANES:]
+    count = residual_ref.shape[1]
+    plane, group = index_ref[0], index_ref[1]
+
+    @pl.when(pl.program_id(0) == 0)
+    def _():
+        for k in range(PLANES):
+            piece = residual_ref[plane ^ k].astype(F32)
+            turned_ref[:, k * count : (k + 1) * count] = piece.T.astype(BF)
+
+    total = None
+    for k in range(PLANES):
+        left = turned_ref[:, k * count : (k + 1) * count]
+        part = jnp.dot(left, blocks[k][...], preferred_element_type=F32)
+        total = part if total is None else total + part
+    stage_ref[...] = total.reshape(stage_ref.shape)
+    for k, part_ref in enumerate(parts):
+        part_ref[...] = stage_ref[group ^ k].astype(part_ref.dtype)
+
+
+def gradient_parts(plane, group, residual, token, kernels, groups):
+    _, count, cols = residual.shape
+    total = kernels[0].shape[1]
+    shape = (cols // groups, total)
+    part = pl.BlockSpec((cols // groups, TILE), lambda i: (0, i))
+    return pl.pallas_call(
+        gradient_step,
+        grid=(total // TILE,),
+        out_shape=tuple(jax.ShapeDtypeStruct(shape, t) for t in (F32, BF, F32, BF)),
+        in_specs=[
+            pl.BlockSpec(memory_space=pltpu.SMEM),
+            pl.BlockSpec(residual.shape, lambda i: (0, 0, 0)),
+            pl.BlockSpec(token.shape, lambda i: (0, 0)),
+        ]
+        + [pl.BlockSpec((count, TILE), lambda i: (0, i))] * PLANES,
+        out_specs=[part] * groups,
+        scratch_shapes=[
+            pltpu.VMEM((cols, PLANES * count), BF),
+            pltpu.VMEM((groups, cols // groups, TILE), F32),
+        ],
+        compiler_params=pltpu.CompilerParams(vmem_limit_bytes=16 * 1024 * 1024),
+        cost_estimate=pl.CostEstimate(
+            flops=2 * PLANES * count * cols * total,
+            bytes_accessed=2 * PLANES * count * total,
+            transcendentals=0,
+        ),
+    )(
+        jnp.stack([plane, group]).astype(jnp.int32),
+        residual,
+        token,
+        *[pltpu.with_memory_space_constraint(kernel, pltpu.HBM) for kernel in kernels],
+    )
 
 
 def whole(body, shapes, *args, scalars=0):
@@ -365,7 +418,10 @@
         targets,
         weight,
     )
+    residual, turned_inverse = lax.optimization_barrier((residual, turned_inverse))
+    other_inverse = swapped(turned_inverse, "ctr", panel_shards)
     residual = exchanged(residual, "ctr").reshape(shards * own_points, target_count)
+    residual, other_inverse = lax.optimization_barrier((residual, other_inverse))
 
     index = group.astype(jnp.int32).reshape(1)
     window = whole(
@@ -377,9 +433,7 @@
     parts = lax.all_gather(window, "pts")
     sent = jax.ShapeDtypeStruct((shards, strip, LANES), BF)
     window = whole(fold_step, sent, index, parts, scalars=1)
-    window, turned_inverse = lax.optimization_barrier((window, turned_inverse))
-    other_inverse = swapped(turned_inverse, "ctr", panel_shards)
-    other_inverse, residual = lax.optimization_barrier((other_inverse, residual))
+    token = window[0]
     solve_rows = jnp.concatenate(
         [
             jnp.where(panel == 0, turned_inverse, other_inverse),
@@ -391,24 +445,18 @@
     window = window.reshape(shards * strip, LANES)
 
     planes = residual.reshape(PLANES, plane_points, target_count)
-    backward = None
-    for k in range(PLANES):
-        part = lax.dot_general(
-            pick(planes, plane ^ k), kernels[k], (((0,), (0,)), ((), ())), preferred_element_type=F32
-        )
-        backward = part if backward is None else backward + part
-    backward = backward.reshape(groups, target_slice, shard_rows)
-    near_pair = jnp.stack([pick(backward, group), pick(backward, group ^ 2)])
-    far_pair = jnp.stack([pick(backward, group ^ 1), pick(backward, group ^ 3)]).astype(BF)
-    near_pair = near_pair + swapped(far_pair, "pts", 1).astype(F32)
-    gradient = near_pair[0] + swapped(near_pair[1].astype(BF), "pts", 2).astype(F32)
-    gradient = gradient.T
+    near, far, near_other, far_other = gradient_parts(plane, group, planes, token, kernels, groups)
+    far_other = swapped(far_other, "pts", 1)
+    far = swapped(far, "pts", 1)
 
     half = shards // HALVES
     sent = jax.ShapeDtypeStruct((half, strip, LANES), BF)
     packed = jax.ShapeDtypeStruct((strip, LANES), F32)
     first, low, high = whole(first_step, (sent, packed, packed), solve_rows, window)
     first = exchanged(first, "ctr", HALVES).reshape(half * strip, LANES)
+    first, near_other = lax.optimization_barrier((first, near_other))
+    other = swapped((near_other + far_other.astype(F32)).astype(BF), "pts", 2)
+    gradient = (near + far.astype(F32) + other.astype(F32)).T
     update = panel_call(middle_step, sent, factor, half, fold, first)
     update = exchanged(update, "ctr", HALVES).reshape(half * strip, LANES)
     solved = panel_call(

time: 142 us -> 148 us (1.042)
  Pallas kernels: 23.2 us -> 30.8 us
  matrix products: 4.36 us -> 0.64 us
  starting transfers between devices: 48.4 us -> 51 us
  waiting for transfers between devices: 33.1 us -> 35.1 us
  local copies, waits for them, and re-layouts: 6.55 us -> 4.61 us
    pallas_call x0 -> x1, Pallas kernels: none -> 7.86 us  [gradient_parts(): pl.pallas_call(gradient_step, grid=(total // TILE,), out_shape=tuple((jax...]
    ppermute x6 -> x7, waiting for transfers between devices: 1.49 us -> 9.17 us  [swapped(): lax.ppermute(x, axis, [(i, i ^ bits) for i in range(lax.axis_size(axis))])]
    all_to_all x5, waiting for transfers between devices: 31.6 us -> 26 us  [exchanged(): lax.all_to_all(pieces, axis, 0, 0, tiled=True, axis_index_groups=groups i...]
    dot_general x4 -> x0, matrix products: 3.72 us -> none  [body(): lax.dot_general(pick(planes, plane ^ k), kernels[k], (((0,), (0,)), ((),...]
    all_to_all x5, starting transfers between devices: 39.6 us -> 43.1 us  [exchanged(): lax.all_to_all(pieces, axis, 0, 0, tiled=True, axis_index_groups=groups i...]
    unnamed x20 -> x16, local copies, waits for them, and re-layouts: 2.23 us -> 0.75 us
    ppermute x6 -> x7, starting transfers between devices: 8.77 us -> 7.84 us  [swapped(): lax.ppermute(x, axis, [(i, i ^ bits) for i in range(lax.axis_size(axis))])]
  transfers between devices with their start and end apart: 11 -> 12, of which waited for: 7 -> 8; matrix products, arithmetic and copies ran while one was open for 8% -> 5% of each run, Pallas kernels for 13% -> 17%
where the time goes in v8:
time: 148 us
  starting transfers between devices  51 us (34%)
  waiting for transfers between devices  35.1 us (24%)
  Pallas kernels  30.8 us (21%)
  blocking collectives  19.8 us (13%)
  other arithmetic  4.71 us (3%)
  local copies, waits for them, and re-layouts  4.61 us (3%)
    all_to_all x5, starting transfers between devices, exchanged(): lax.all_to_all(pieces, axis, 0, 0, tiled=True, axis_index_groups=groups i...  43.1 us
    all_to_all x5, waiting for transfers between devices, exchanged(): lax.all_to_all(pieces, axis, 0, 0, tiled=True, axis_index_groups=groups i...  26 us
    pallas_call x4, Pallas kernels, kernel_and_value(): pl.pallas_call(functools.partial(kernel_block, bool(held)), out_shape=(pl...  14.1 us
    all_to_all x1, blocking collectives, exchanged(): lax.all_to_all(pieces, axis, 0, 0, tiled=True, axis_index_groups=groups i...  12.8 us
    ppermute x7, waiting for transfers between devices, swapped(): lax.ppermute(x, axis, [(i, i ^ bits) for i in range(lax.axis_size(axis))])  9.17 us
    pallas_call x1, Pallas kernels, gradient_parts(): pl.pallas_call(gradient_step, grid=(total // TILE,), out_shape=tuple((jax...  7.86 us
    ppermute x7, starting transfers between devices, swapped(): lax.ppermute(x, axis, [(i, i ^ bits) for i in range(lax.axis_size(axis))])  7.84 us
    all_gather x1, blocking collectives, body(): parts = lax.all_gather(window, 'pts')  6.93 us
  transfers between devices with their start and end apart: 12, of which 8 were waited for; matrix products, arithmetic and copies ran while one was open for 5% of the time, Pallas kernels for 17%

profile of v8, /device:TPU:4, one launch (start us, length us, event | category | flops | bytes accessed | tf_op | source)
XLA Modules:
  0.0 147.6 jit_solution(3137959743601079268)
XLA Ops:
  0.6 1.4 broadcast_in_dim.45
  2.1 9.6 %all-to-all-start = ((bf16[16,16,512]{2,1,0:T(8,128)(2,1)}), bf16[16,16,512]{2,1,0:T(8,128)(2,1)S(1)}, u32[]{:S(2)}, u32[]{:S(2)}) async-start(bf16[16,16,512]{2,1,0:T(8,128)(2,1)} %broadcast_in_dim.45), calls=%async_computation | async-start | bytes 524288 | tf_op jit(solution)/shard_map/all_to_all | solution.py:23
  11.7 0.7 broadcast_subtract_fusion
  12.4 0.7 broadcast_compare_fusion
  13.2 0.1 select_reduce_fusion
  13.3 0.1 copy.23.local_ref
  13.4 1.1 convert_element_type.16
  14.5 0.5 reshape.60
  15.0 0.6 convolution_bitcast_fusion
  15.6 0.5 copy.25
  16.2 0.2 reshape.61
  16.5 4.6 %shard_map.113 = (bf16[4096,512]{1,0:T(8,128)(2,1)}, f32[1,4096]{1,0:T(1,128)S(1)}, bf16[64,512]{1,0:T(8,128)(2,1)S(1)}, f32[1,64]{1,0:T(1,128)S(1)}) custom-call(bf16[4096,512]{1,0:T(8,128)(2,1)} %centers_ref.1, f32[1,512]{1,0:T(1,128)S(1)} %bitcast.43, s32[64,1]{1,0:T(8,128)S(1)} %copy.23.local_ref), custom_call_target="tpu_custom_call" | custom-call | flops 8388608 | bytes 4194304 | tf_op jit(solution)/shard_map/pallas_call | solution.py:71
  21.1 0.1 select_reduce_fusion.1
  21.2 2.5 %all-to-all-done = bf16[16,16,512]{2,1,0:T(8,128)(2,1)S(1)} async-done(((bf16[16,16,512]{2,1,0:T(8,128)(2,1)}), bf16[16,16,512]{2,1,0:T(8,128)(2,1)S(1)}, u32[]{:S(2)}, u32[]{:S(2)}) %all-to-all-start) | async-done | bytes 262176 | tf_op jit(solution)/shard_map/all_to_all | solution.py:23
  23.7 1.2 collective-permute-start.2
  24.9 2.9 %collective-permute-start = (bf16[256,512]{1,0:T(8,128)(2,1)S(1)}, bf16[256,512]{1,0:T(8,128)(2,1)S(1)}, u32[]{:S(2)}, u32[]{:S(2)}) collective-permute-start(bf16[256,512]{1,0:T(8,128)(2,1)S(1)} %bitcast.36), channel_id=1, source_target_pairs={{0,32},{1,33},{2,34},{3,35},{4,36},{5,37},{6,38},{7,39},{8,40},{9,... | collective-permute-start | bytes 786440 | tf_op jit(solution)/shard_map/ppermute | solution.py:33
  27.8 4.7 %shard_map.114 = (bf16[256,4096]{1,0:T(8,128)(2,1)}, bf16[4,256,128]{2,1,0:T(8,128)(2,1)S(1)}, bf16[4,256,64]{2,1,0:T(8,128)(2,1)S(1)}, bf16[4096,512]{1,0:T(8,128)(2,1)S(1)}) custom-call(s32[1]{0:T(128)} %bitcast.slot_ref, bf16[256,512]{1,0:T(8,128)(2,1)S(1)} %bitcast.37, f32[1,512]{1,0:T(1,128)S(1)} %bitcast.44, ...), custom_call_target="tpu_custom_call" | custom-call | flops 1342177280 | bytes 2097152 | tf_op jit(solution)/shard_map/pallas_call | solution.py:150
  32.5 0.3 collective-permute-done.2.points_ref
  32.7 2.9 %shard_map.115 = (bf16[256,4096]{1,0:T(8,128)(2,1)}, bf16[4,256,128]{2,1,0:T(8,128)(2,1)S(1)}, bf16[4,256,64]{2,1,0:T(8,128)(2,1)S(1)}) custom-call(s32[1]{0:T(128)} %bitcast.11.slot_ref, bf16[256,512]{1,0:T(8,128)(2,1)S(1)} %collective-permute-done.2.points_ref, f32[1,512]{1,0:T(1,128)S(1)} %bitcast.45, ...), custom_call_target="tpu_custom_call" | custom-call | flops 1342177280 | bytes 2097152 | tf_op jit(solution)/shard_map/pallas_call | solution.py:150
  35.6 0.8 collective-permute-done.1.points_ref
  36.5 2.9 %shard_map.116 = (bf16[256,4096]{1,0:T(8,128)(2,1)}, bf16[4,256,128]{2,1,0:T(8,128)(2,1)S(1)}, bf16[4,256,64]{2,1,0:T(8,128)(2,1)S(1)}) custom-call(s32[1]{0:T(128)} %bitcast.10.slot_ref, bf16[256,512]{1,0:T(8,128)(2,1)S(1)} %collective-permute-done.1.points_ref, f32[1,512]{1,0:T(1,128)S(1)} %bitcast.46, ...), custom_call_target="tpu_custom_call" | custom-call | flops 1342177280 | bytes 2097152 | tf_op jit(solution)/shard_map/pallas_call | solution.py:150
  39.4 3.6 %shard_map.117 = (bf16[256,4096]{1,0:T(8,128)(2,1)}, bf16[4,256,128]{2,1,0:T(8,128)(2,1)}, bf16[4,256,64]{2,1,0:T(8,128)(2,1)S(1)}) custom-call(s32[1]{0:T(128)} %bitcast.2.slot_ref, bf16[256,512]{1,0:T(8,128)(2,1)S(1)} %collective-permute-done.points_ref, f32[1,512]{1,0:T(1,128)S(1)} %bitcast.47, bf16[4096,512]{1,0:T(8,128)(2,1)S(1)} %get-tuple-element.42.centers_ref, ...), custom_call_target="tpu_custom_call" | custom-call | flops 1342177280 | bytes 2097152 | tf_op jit(solution)/shard_map/pallas_call | solution.py:150
  43.0 11.1 %all-to-all-start.1 = ((bf16[64,16,128]{2,1,0:T(8,128)(2,1)}), bf16[64,16,128]{2,1,0:T(8,128)(2,1)S(1)}, u32[]{:S(2)}, u32[]{:S(2)}) async-start(bf16[64,16,128]{2,1,0:T(8,128)(2,1)} %bitcast.12), calls=%async_computation.1 | async-start | bytes 524288 | tf_op jit(solution)/shard_map/all_to_all | solution.py:23
  54.2 9.8 %all-to-all-done.1.shares_ref = bf16[64,16,128]{2,1,0:T(8,128)(2,1)S(1)} async-done(((bf16[64,16,128]{2,1,0:T(8,128)(2,1)}), bf16[64,16,128]{2,1,0:T(8,128)(2,1)S(1)}, u32[]{:S(2)}, u32[]{:S(2)}) %all-to-all-start.1) | async-done | bytes 262176 | tf_op jit(solution)/shard_map/all_to_all | solution.py:23
  64.0 0.8 shard_map.118
  64.8 6.7 %all-to-all-start.2 = ((bf16[64,16,128]{2,1,0:T(8,128)(2,1)}), bf16[64,16,128]{2,1,0:T(8,128)(2,1)S(1)}, u32[]{:S(2)}, u32[]{:S(2)}) async-start(bf16[64,16,128]{2,1,0:T(8,128)(2,1)} %shard_map.118), calls=%async_computation.2 | async-start | bytes 524288 | tf_op jit(solution)/shard_map/all_to_all | solution.py:23
  71.5 0.1 copy.27
  71.7 0.4 collective-permute-start.3
  72.2 8.1 %collective-permute-done.3 = bf16[128,1024]{1,0:T(8,128)(2,1)S(1)} collective-permute-done((bf16[128,1024]{1,0:T(8,128)(2,1)S(1)}, bf16[128,1024]{1,0:T(8,128)(2,1)S(1)}, u32[]{:S(2)}, u32[]{:S(2)}) %collective-permute-start.3) | collective-permute-done | bytes 262176 | tf_op jit(solution)/shard_map/ppermute | solution.py:33
  80.3 1.2 all-to-all-done.2
  81.4 0.2 shard_map.119
  81.7 6.9 %all-gather = f32[256,128]{1,0:T(8,128)S(1)} all-gather(f32[64,128]{1,0:T(8,128)S(1)} %shard_map.119), channel_id=2, replica_groups=mesh['pts'=4,'ctr'=64] {'pts'}, dimensions={0}, use_global_device_ids=true | all-gather | bytes 163840 | tf_op jit(solution)/shard_map/all_gather | solution.py:433
  88.6 0.8 shard_map.120
  89.4 9.5 %all-to-all-start.3 = ((bf16[64,16,128]{2,1,0:T(8,128)(2,1)}), bf16[64,16,128]{2,1,0:T(8,128)(2,1)S(1)}, u32[]{:S(2)}, u32[]{:S(2)}) async-start(bf16[64,16,128]{2,1,0:T(8,128)(2,1)} %shard_map.120), calls=%async_computation.3 | async-start | bytes 524288 | tf_op jit(solution)/shard_map/all_to_all | solution.py:23
  98.9 0.7 slice_bitcast_fusion.token_ref
  99.6 7.9 %shard_map.121 = (f32[32,4096]{1,0:T(8,128)S(1)}, bf16[32,4096]{1,0:T(8,128)(2,1)S(1)}, f32[32,4096]{1,0:T(8,128)S(1)}, bf16[32,4096]{1,0:T(8,128)(2,1)}) custom-call(s32[2]{0:T(128)S(1)} %pad_add_fusion.index_ref, bf16[4,256,128]{2,1,0:T(8,128)(2,1)S(1)} %bitcast.33, bf16[16,128]{1,0:T(8,128)(2,1)S(1)} %slice_bitcast_fusion.token_ref, ...), custom_call_target="tpu_custom_call" | custom-call | flops 1073741824 | bytes 8388608 | tf_op jit(solution)/shard_map/pallas_call | solution.py:306
  107.5 0.7 copy-done.5
  108.3 2.4 %all-to-all-done.3 = bf16[64,16,128]{2,1,0:T(8,128)(2,1)S(1)} async-done(((bf16[64,16,128]{2,1,0:T(8,128)(2,1)}), bf16[64,16,128]{2,1,0:T(8,128)(2,1)S(1)}, u32[]{:S(2)}, u32[]{:S(2)}) %all-to-all-start.3) | async-done | bytes 262176 | tf_op jit(solution)/shard_map/all_to_all | solution.py:23
  110.7 1.0 shard_map.122
  111.7 6.3 %all-to-all-start.4 = ((bf16[32,16,128]{2,1,0:T(8,128)(2,1)}), bf16[32,16,128]{2,1,0:T(8,128)(2,1)S(1)}, u32[]{:S(2)}, u32[]{:S(2)}) async-start(bf16[32,16,128]{2,1,0:T(8,128)(2,1)} %get-tuple-element.63), calls=%async_computation.4 | async-start | bytes 262144 | tf_op jit(solution)/shard_map/all_to_all | solution.py:23
  118.0 0.3 collective-permute-start.4
  118.3 10.1 %all-to-all-done.4 = bf16[32,16,128]{2,1,0:T(8,128)(2,1)S(1)} async-done(((bf16[32,16,128]{2,1,0:T(8,128)(2,1)}), bf16[32,16,128]{2,1,0:T(8,128)(2,1)S(1)}, u32[]{:S(2)}, u32[]{:S(2)}) %all-to-all-start.4) | async-done | bytes 131104 | tf_op jit(solution)/shard_map/all_to_all | solution.py:23
  128.4 1.0 add_convert_fusion
  129.3 3.0 %collective-permute-start.6 = (bf16[32,4096]{1,0:T(8,128)(2,1)S(1)}, bf16[32,4096]{1,0:T(8,128)(2,1)S(1)}, u32[]{:S(2)}, u32[]{:S(2)}) collective-permute-start(bf16[32,4096]{1,0:T(8,128)(2,1)S(1)} %add_convert_fusion), channel_id=1, source_target_pairs={{0,128},{64,192},{128,0},{192,64},{1,129},{65,193},{129,1},{193,65... | collective-permute-start | bytes 786440 | tf_op jit(solution)/shard_map/ppermute | solution.py:33
  132.3 0.4 shard_map.123
  132.8 12.8 %all_to_all.30 = bf16[32,16,128]{2,1,0:T(8,128)(2,1)S(1)} all-to-all(bf16[32,16,128]{2,1,0:T(8,128)(2,1)S(1)} %shard_map.123), channel_id=1, replica_groups={{0,1,2,3,4,5,6,7,8,9,10,11,12,13,14,15,16,17,18,19,20,21,22,23,24,25,26..., dimensions={0} | all-to-all | bytes 262144 | tf_op jit(solution)/shard_map/all_to_all | solution.py:23
  145.6 1.0 shard_map.124
  146.7 0.9 add_bitcast_fusion
  (26 shorter events, 0.4 us)
Async XLA Ops:
  2.1 21.6 %all-to-all-start = ((bf16[16,16,512]{2,1,0:T(8,128)(2,1)}), bf16[16,16,512]{2,1,0:T(8,128)(2,1)S(1)}, u32[]{:S(2)}, u32[]{:S(2)}) async-start(bf16[16,16,512]{2,1,0:T(8,128)(2,1)} %broadcast_in_dim.45), calls=%async_computation | async-start | bytes 524288 | tf_op jit(solution)/shard_map/all_to_all | solution.py:23
  13.4 3.1 %copy-start.3 = (f32[512]{0:T(512)S(1)}, f32[512]{0:T(512)}, u32[]{:S(2)}) copy-start(f32[512]{0:T(512)} %param.14) | copy-start | bytes 6148
  16.4 4.7 %copy-start.6 = (f32[8]{0:T(128)S(1)}, f32[8]{0:T(128)}, u32[]{:S(2)}) copy-start(f32[8]{0:T(128)} %param.13) | copy-start | bytes 100
  16.5 4.7 %copy-start.7 = (s32[16]{0:T(128)S(1)}, s32[16]{0:T(128)}, u32[]{:S(2)}) copy-start(s32[16]{0:T(128)} %param.11) | copy-start | bytes 196
  16.5 11.3 %copy-start = (bf16[4096,128]{1,0:T(8,128)(2,1)S(1)}, bf16[4096,128]{1,0:T(8,128)(2,1)}, u32[]{:S(2)}) copy-start(bf16[4096,128]{1,0:T(8,128)(2,1)} %coef_ref.7) | copy-start | bytes 3145732
  23.7 9.0 %collective-permute-start.2 = (bf16[256,512]{1,0:T(8,128)(2,1)S(1)}, bf16[256,512]{1,0:T(8,128)(2,1)S(1)}, u32[]{:S(2)}, u32[]{:S(2)}) collective-permute-start(bf16[256,512]{1,0:T(8,128)(2,1)S(1)} %bitcast.34), channel_id=1, source_target_pairs={{0,16},{1,17},{2,18},{3,19},{4,20},{5,21},{6,22},{7,23},{8,24},{9,... | collective-permute-start | bytes 786440 | tf_op jit(solution)/shard_map/ppermute | solution.py:33
  24.9 11.6 %collective-permute-start.1 = (bf16[256,512]{1,0:T(8,128)(2,1)S(1)}, bf16[256,512]{1,0:T(8,128)(2,1)S(1)}, u32[]{:S(2)}, u32[]{:S(2)}) collective-permute-start(bf16[256,512]{1,0:T(8,128)(2,1)S(1)} %bitcast.35), channel_id=1, source_target_pairs={{0,48},{1,49},{2,50},{3,51},{4,52},{5,53},{6,54},{7,55},{8,56},{9,... | collective-permute-start | bytes 786440 | tf_op jit(solution)/shard_map/ppermute | solution.py:33
  24.9 14.5 %collective-permute-start = (bf16[256,512]{1,0:T(8,128)(2,1)S(1)}, bf16[256,512]{1,0:T(8,128)(2,1)S(1)}, u32[]{:S(2)}, u32[]{:S(2)}) collective-permute-start(bf16[256,512]{1,0:T(8,128)(2,1)S(1)} %bitcast.36), channel_id=1, source_target_pairs={{0,32},{1,33},{2,34},{3,35},{4,36},{5,37},{6,38},{7,39},{8,40},{9,... | collective-permute-start | bytes 786440 | tf_op jit(solution)/shard_map/ppermute | solution.py:33
  39.4 24.6 %copy-start.4 = (f32[16,128]{1,0:T(8,128)S(1)}, f32[16,128]{1,0:T(8,128)}, u32[]{:S(2)}) copy-start(f32[16,128]{1,0:T(8,128)} %targets_ref.1) | copy-start | bytes 24580
  43.0 21.0 %all-to-all-start.1 = ((bf16[64,16,128]{2,1,0:T(8,128)(2,1)}), bf16[64,16,128]{2,1,0:T(8,128)(2,1)S(1)}, u32[]{:S(2)}, u32[]{:S(2)}) async-start(bf16[64,16,128]{2,1,0:T(8,128)(2,1)} %bitcast.12), calls=%async_computation.1 | async-start | bytes 524288 | tf_op jit(solution)/shard_map/all_to_all | solution.py:23
  64.8 16.6 %all-to-all-start.2 = ((bf16[64,16,128]{2,1,0:T(8,128)(2,1)}), bf16[64,16,128]{2,1,0:T(8,128)(2,1)S(1)}, u32[]{:S(2)}, u32[]{:S(2)}) async-start(bf16[64,16,128]{2,1,0:T(8,128)(2,1)} %shard_map.118), calls=%async_computation.2 | async-start | bytes 524288 | tf_op jit(solution)/shard_map/all_to_all | solution.py:23
  71.7 8.6 %collective-permute-start.3 = (bf16[128,1024]{1,0:T(8,128)(2,1)S(1)}, bf16[128,1024]{1,0:T(8,128)(2,1)S(1)}, u32[]{:S(2)}, u32[]{:S(2)}) collective-permute-start(bf16[128,1024]{1,0:T(8,128)(2,1)S(1)} %copy.27), channel_id=1, source_target_pairs={{0,32},{1,33},{2,34},{3,35},{4,36},{5,37},{6,38},{7,39},{8,40},{9,... | collective-permute-start | bytes 786440 | tf_op jit(solution)/shard_map/ppermute | solution.py:33
  89.4 21.3 %all-to-all-start.3 = ((bf16[64,16,128]{2,1,0:T(8,128)(2,1)}), bf16[64,16,128]{2,1,0:T(8,128)(2,1)S(1)}, u32[]{:S(2)}, u32[]{:S(2)}) async-start(bf16[64,16,128]{2,1,0:T(8,128)(2,1)} %shard_map.120), calls=%async_computation.3 | async-start | bytes 524288 | tf_op jit(solution)/shard_map/all_to_all | solution.py:23
  107.5 0.7 copy-start.5
  108.2 24.2 %copy-start.2 = (f32[64,4096]{1,0:T(8,128)S(1)}, f32[64,4096]{1,0:T(8,128)}, u32[]{:S(2)}) copy-start(f32[64,4096]{1,0:T(8,128)} %matrix_ref.2) | copy-start | bytes 3145732
  108.2 20.2 %collective-permute-start.5 = (bf16[32,4096]{1,0:T(8,128)(2,1)}, bf16[32,4096]{1,0:T(8,128)(2,1)}, u32[]{:S(2)}, u32[]{:S(2)}) collective-permute-start(bf16[32,4096]{1,0:T(8,128)(2,1)} %get-tuple-element.66), channel_id=1, source_target_pairs={{0,64},{64,0},{128,192},{192,128},{1,65},{65,1},{129,193},{193,129... | collective-permute-start | bytes 786440 | tf_op jit(solution)/shard_map/ppermute | solution.py:33
  108.3 37.4 %copy-start.1 = (f32[64,2048]{1,0:T(8,128)S(1)}, f32[64,2048]{1,0:T(8,128)}, u32[]{:S(2)}) copy-start(f32[64,2048]{1,0:T(8,128)} %matrix_ref.3) | copy-start | bytes 1572868
  111.7 16.7 %all-to-all-start.4 = ((bf16[32,16,128]{2,1,0:T(8,128)(2,1)}), bf16[32,16,128]{2,1,0:T(8,128)(2,1)S(1)}, u32[]{:S(2)}, u32[]{:S(2)}) async-start(bf16[32,16,128]{2,1,0:T(8,128)(2,1)} %get-tuple-element.63), calls=%async_computation.4 | async-start | bytes 262144 | tf_op jit(solution)/shard_map/all_to_all | solution.py:23
  118.0 28.7 %collective-permute-start.4 = (bf16[32,4096]{1,0:T(8,128)(2,1)}, bf16[32,4096]{1,0:T(8,128)(2,1)S(1)}, u32[]{:S(2)}, u32[]{:S(2)}) collective-permute-start(bf16[32,4096]{1,0:T(8,128)(2,1)} %copy-done.5), channel_id=1, source_target_pairs={{0,64},{64,0},{128,192},{192,128},{1,65},{65,1},{129,193},{193,129... | collective-permute-start | bytes 786440 | tf_op jit(solution)/shard_map/ppermute | solution.py:33
  129.3 17.3 %collective-permute-start.6 = (bf16[32,4096]{1,0:T(8,128)(2,1)S(1)}, bf16[32,4096]{1,0:T(8,128)(2,1)S(1)}, u32[]{:S(2)}, u32[]{:S(2)}) collective-permute-start(bf16[32,4096]{1,0:T(8,128)(2,1)S(1)} %add_convert_fusion), channel_id=1, source_target_pairs={{0,128},{64,192},{128,0},{192,64},{1,129},{65,193},{129,1},{193,65... | collective-permute-start | bytes 786440 | tf_op jit(solution)/shard_map/ppermute | solution.py:33

commit v9 on v6

--- a/solution.py
+++ b/solution.py
@@ -13,6 +13,7 @@
 PLANES = 4
 HALVES = 2
 TILE = 512
+EARLY = 2
 VMEM = pl.BlockSpec(memory_space=pltpu.VMEM)
 
 
@@ -121,8 +122,9 @@
     before = None
     for i in range(steps):
         rows = pl.ds(i * TILE, TILE)
-        if stream:
-            loads[i].wait()
+        if stream and i in (0, EARLY):
+            for load in loads[i : EARLY if i == 0 else steps]:
+                load.wait()
         anchors = stream[0][i] if stream else centers_ref[rows, :]
         current = block(anchors, norm_ref[:, rows])
         slots[i] = current
@@ -248,6 +250,12 @@
         scratch_shapes=[pltpu.VMEM((parts, fold, strip, LANES), BF)],
         compiler_params=pltpu.CompilerParams(vmem_limit_bytes=16 * 1024 * 1024),
     )(*scalars, matrix, data, *more)
+
+
+def residual_step(shares_ref, targets_ref, weight_ref, sent_ref):
+    predicted = jnp.sum(shares_ref[...].astype(F32), axis=0)
+    residual = (weight_ref[...] * (predicted - targets_ref[...])).astype(BF)
+    sent_ref[...] = jnp.broadcast_to(residual[None], sent_ref.shape)
 
 
 def window_step(chosen_ref, residual_ref, window_ref):
@@ -350,12 +358,16 @@
         "rhqj,js->hrsq", inverse.reshape(own_rows, count, strip, shards), place
     ).reshape(count * own_rows, shards * strip)
 
-    own_weight = class_lookup(point_class, class_weight)
+    weight = class_lookup(point_class, class_weight)[:, None]
     shares = exchanged(values.reshape(shards, own_points, target_count), "ctr")
-    predicted = jnp.sum(shares.astype(F32), axis=0)
-    own_residual = (own_weight[:, None] * (predicted - targets)).astype(BF)
-    residual = exchanged(copies(own_residual, shards), "ctr")
-    residual = residual.reshape(shards * own_points, target_count)
+    residual = whole(
+        residual_step,
+        jax.ShapeDtypeStruct((shards, own_points, target_count), BF),
+        shares,
+        targets,
+        weight,
+    )
+    residual = exchanged(residual, "ctr").reshape(shards * own_points, target_count)
 
     index = group.astype(jnp.int32).reshape(1)
     window = whole(

time: 140 us -> 140 us (level)
    pallas_call x3 -> x4, Pallas kernels: 2.04 us -> 2.84 us  [whole(): pl.pallas_call(body, out_shape=shapes, in_specs=[pl.BlockSpec(memory_spac...]
  transfers between devices with their start and end apart: 11 -> 11, of which waited for: 7 -> 8; matrix products, arithmetic and copies ran while one was open for 8% -> 8% of each run, Pallas kernels for 13% -> 12%
where the time goes in v9:
time: 140 us; the launch traced here: 139 us
  starting transfers between devices  45.9 us (33%)
  waiting for transfers between devices  32.6 us (23%)
  Pallas kernels  22.7 us (16%)
  blocking collectives  20 us (14%)
  local copies, waits for them, and re-layouts  7.99 us (6%)
  other arithmetic  4.69 us (3%)
  matrix products  4.35 us (3%)
    all_to_all x5, starting transfers between devices, exchanged(): lax.all_to_all(pieces, axis, 0, 0, tiled=True, axis_index_groups=groups i...  37.3 us
    all_to_all x5, waiting for transfers between devices, exchanged(): lax.all_to_all(pieces, axis, 0, 0, tiled=True, axis_index_groups=groups i...  30.4 us
    pallas_call x4, Pallas kernels, kernel_and_value(): pl.pallas_call(functools.partial(kernel_block, bool(held)), out_shape=(pl...  13.8 us
    all_to_all x1, blocking collectives, exchanged(): lax.all_to_all(pieces, axis, 0, 0, tiled=True, axis_index_groups=groups i...  13 us
    ppermute x6, starting transfers between devices, swapped(): lax.ppermute(x, axis, [(i, i ^ bits) for i in range(lax.axis_size(axis))])  8.6 us
    all_gather x1, blocking collectives, body(): parts = lax.all_gather(window, 'pts')  6.93 us
    pallas_call x1, Pallas kernels, scaled_and_norm(): pl.pallas_call(scale_step, out_shape=(pltpu.HBM((total, depth), BF), jax....  4.61 us
    unnamed x28, local copies, waits for them, and re-layouts  3.87 us
  transfers between devices with their start and end apart: 11, of which 8 were waited for; matrix products, arithmetic and copies ran while one was open for 8% of the time, Pallas kernels for 12%

profile of v9, /device:TPU:4, one launch (start us, length us, event | category | flops | bytes accessed | tf_op | source)
XLA Modules:
  0.0 139.2 jit_solution(6567944680267806952)
XLA Ops:
  0.6 1.4 %broadcast_in_dim.45 = bf16[16,16,512]{2,1,0:T(8,128)(2,1)} broadcast(bf16[16,512]{1,0:T(8,128)(2,1)} %param.10), dimensions={1,2} | broadcast | bytes 278528 | tf_op jit(solution)/shard_map/broadcast_in_dim | solution.py:29
  2.1 9.6 %all-to-all-start = ((bf16[16,16,512]{2,1,0:T(8,128)(2,1)}), bf16[16,16,512]{2,1,0:T(8,128)(2,1)S(1)}, u32[]{:S(2)}, u32[]{:S(2)}) async-start(bf16[16,16,512]{2,1,0:T(8,128)(2,1)} %broadcast_in_dim.45), calls=%async_computation | async-start | bytes 524288 | tf_op jit(solution)/shard_map/all_to_all | solution.py:23
  11.7 0.7 broadcast_subtract_fusion
  12.5 0.7 broadcast_compare_fusion
  13.4 0.7 copy-done.4
  14.1 4.6 %shard_map.113 = (bf16[4096,512]{1,0:T(8,128)(2,1)}, f32[1,4096]{1,0:T(1,128)S(1)}, bf16[64,512]{1,0:T(8,128)(2,1)S(1)}, f32[1,64]{1,0:T(1,128)S(1)}) custom-call(bf16[4096,512]{1,0:T(8,128)(2,1)} %centers_ref.1, f32[1,512]{1,0:T(1,128)S(1)} %bitcast.69, s32[64,1]{1,0:T(8,128)S(1)} %copy.23.local_ref), custom_call_target="tpu_custom_call" | custom-call | flops 8388608 | bytes 4194304 | tf_op jit(solution)/shard_map/pallas_call | solution.py:75
  18.7 5.0 %all-to-all-done = bf16[16,16,512]{2,1,0:T(8,128)(2,1)S(1)} async-done(((bf16[16,16,512]{2,1,0:T(8,128)(2,1)}), bf16[16,16,512]{2,1,0:T(8,128)(2,1)S(1)}, u32[]{:S(2)}, u32[]{:S(2)}) %all-to-all-start) | async-done | bytes 262176 | tf_op jit(solution)/shard_map/all_to_all | solution.py:23
  23.7 1.2 collective-permute-start.2
  24.9 2.9 %collective-permute-start = (bf16[256,512]{1,0:T(8,128)(2,1)S(1)}, bf16[256,512]{1,0:T(8,128)(2,1)S(1)}, u32[]{:S(2)}, u32[]{:S(2)}) collective-permute-start(bf16[256,512]{1,0:T(8,128)(2,1)S(1)} %bitcast.62), channel_id=1, source_target_pairs={{0,32},{1,33},{2,34},{3,35},{4,36},{5,37},{6,38},{7,39},{8,40},{9,... | collective-permute-start | bytes 786440 | tf_op jit(solution)/shard_map/ppermute | solution.py:33
  27.8 4.8 %shard_map.114 = (bf16[256,4096]{1,0:T(8,128)(2,1)}, bf16[4,256,128]{2,1,0:T(8,128)(2,1)S(1)}, bf16[4,256,64]{2,1,0:T(8,128)(2,1)S(1)}) custom-call(s32[1]{0:T(128)} %bitcast.7.slot_ref, bf16[256,512]{1,0:T(8,128)(2,1)S(1)} %bitcast.63, f32[1,512]{1,0:T(1,128)S(1)} %bitcast.70, bf16[4096,512]{1,0:T(8,128)(2,1)} %get-tuple-element.31.centers_ref, ...), custom_call_target="tpu_custom_call" | custom-call | flops 1342177280 | bytes 2097152 | tf_op jit(solution)/shard_map/pallas_call | solution.py:153
  32.7 2.8 %shard_map.115 = (bf16[256,4096]{1,0:T(8,128)(2,1)}, bf16[4,256,128]{2,1,0:T(8,128)(2,1)S(1)}, bf16[4,256,64]{2,1,0:T(8,128)(2,1)S(1)}) custom-call(s32[1]{0:T(128)} %bitcast.6.slot_ref, bf16[256,512]{1,0:T(8,128)(2,1)S(1)} %collective-permute-done.2.points_ref, f32[1,512]{1,0:T(1,128)S(1)} %bitcast.71, bf16[4096,512]{1,0:T(8,128)(2,1)S(1)} %copy-done, ...), custom_call_target="tpu_custom_call" | custom-call | flops 1342177280 | bytes 2097152 | tf_op jit(solution)/shard_map/pallas_call | solution.py:153
  35.5 1.0 collective-permute-done.1.points_ref
  36.5 2.7 %shard_map.116 = (bf16[256,4096]{1,0:T(8,128)(2,1)}, bf16[4,256,128]{2,1,0:T(8,128)(2,1)S(1)}, bf16[4,256,64]{2,1,0:T(8,128)(2,1)S(1)}) custom-call(s32[1]{0:T(128)} %bitcast.5.slot_ref, bf16[256,512]{1,0:T(8,128)(2,1)S(1)} %collective-permute-done.1.points_ref, f32[1,512]{1,0:T(1,128)S(1)} %bitcast.72, bf16[4096,512]{1,0:T(8,128)(2,1)S(1)} %copy-done, ...), custom_call_target="tpu_custom_call" | custom-call | flops 1342177280 | bytes 2097152 | tf_op jit(solution)/shard_map/pallas_call | solution.py:153
  39.3 3.5 %shard_map.117 = (bf16[256,4096]{1,0:T(8,128)(2,1)}, bf16[4,256,128]{2,1,0:T(8,128)(2,1)}, bf16[4,256,64]{2,1,0:T(8,128)(2,1)S(1)}) custom-call(s32[1]{0:T(128)} %bitcast.1.slot_ref, bf16[256,512]{1,0:T(8,128)(2,1)S(1)} %collective-permute-done.points_ref, f32[1,512]{1,0:T(1,128)S(1)} %bitcast.73, bf16[4096,512]{1,0:T(8,128)(2,1)S(1)} %copy-done, ...), custom_call_target="tpu_custom_call" | custom-call | flops 1342177280 | bytes 2097152 | tf_op jit(solution)/shard_map/pallas_call | solution.py:153
  42.7 8.6 %all-to-all-start.1 = ((bf16[64,16,128]{2,1,0:T(8,128)(2,1)}), bf16[64,16,128]{2,1,0:T(8,128)(2,1)S(1)}, u32[]{:S(2)}, u32[]{:S(2)}) async-start(bf16[64,16,128]{2,1,0:T(8,128)(2,1)} %bitcast.9), calls=%async_computation.1 | async-start | bytes 524288 | tf_op jit(solution)/shard_map/all_to_all | solution.py:23
  51.5 9.7 %all-to-all-done.1.shares_ref = bf16[64,16,128]{2,1,0:T(8,128)(2,1)S(1)} async-done(((bf16[64,16,128]{2,1,0:T(8,128)(2,1)}), bf16[64,16,128]{2,1,0:T(8,128)(2,1)S(1)}, u32[]{:S(2)}, u32[]{:S(2)}) %all-to-all-start.1) | async-done | bytes 262176 | tf_op jit(solution)/shard_map/all_to_all | solution.py:23
  61.2 0.8 shard_map.118
  62.0 6.7 %all-to-all-start.2 = ((bf16[64,16,128]{2,1,0:T(8,128)(2,1)}), bf16[64,16,128]{2,1,0:T(8,128)(2,1)S(1)}, u32[]{:S(2)}, u32[]{:S(2)}) async-start(bf16[64,16,128]{2,1,0:T(8,128)(2,1)} %shard_map.118), calls=%async_computation.2 | async-start | bytes 524288 | tf_op jit(solution)/shard_map/all_to_all | solution.py:23
  68.8 0.5 reshape.75
  69.3 0.6 convolution_bitcast_fusion
  70.0 0.5 copy.26
  70.5 0.2 reshape.76
  70.8 7.9 %all-to-all-done.2 = bf16[64,16,128]{2,1,0:T(8,128)(2,1)S(1)} async-done(((bf16[64,16,128]{2,1,0:T(8,128)(2,1)}), bf16[64,16,128]{2,1,0:T(8,128)(2,1)S(1)}, u32[]{:S(2)}, u32[]{:S(2)}) %all-to-all-start.2) | async-done | bytes 262176 | tf_op jit(solution)/shard_map/all_to_all | solution.py:23
  78.6 0.2 shard_map.119
  78.9 6.9 %all-gather = f32[256,128]{1,0:T(8,128)S(1)} all-gather(f32[64,128]{1,0:T(8,128)S(1)} %shard_map.119), channel_id=2, replica_groups=mesh['pts'=4,'ctr'=64] {'pts'}, dimensions={0}, use_global_device_ids=true | all-gather | bytes 163840 | tf_op jit(solution)/shard_map/all_gather | solution.py:379
  85.8 0.8 shard_map.120
  86.8 1.6 %collective-permute-start.3 = (bf16[128,1024]{1,0:T(8,128)(2,1)S(1)}, bf16[128,1024]{1,0:T(8,128)(2,1)S(1)}, u32[]{:S(2)}, u32[]{:S(2)}) collective-permute-start(bf16[128,1024]{1,0:T(8,128)(2,1)S(1)} %copy.27), channel_id=1, source_target_pairs={{0,32},{1,33},{2,34},{3,35},{4,36},{5,37},{6,38},{7,39},{8,40},{9,... | collective-permute-start | bytes 786440 | tf_op jit(solution)/shard_map/ppermute | solution.py:33
  88.4 7.5 %all-to-all-start.3 = ((bf16[64,16,128]{2,1,0:T(8,128)(2,1)}), bf16[64,16,128]{2,1,0:T(8,128)(2,1)S(1)}, u32[]{:S(2)}, u32[]{:S(2)}) async-start(bf16[64,16,128]{2,1,0:T(8,128)(2,1)} %shard_map.120), calls=%async_computation.3 | async-start | bytes 524288 | tf_op jit(solution)/shard_map/all_to_all | solution.py:23
  95.8 1.1 collective-permute-done.3
  97.0 2.2 %fusion.5 = f32[128,4096]{1,0:T(8,128)S(1)} fusion(bf16[256,4096]{1,0:T(8,128)(2,1)} %get-tuple-element.50, bf16[4,256,128]{2,1,0:T(8,128)(2,1)S(1)} %bitcast.56, s32[]{:T(128)S(6)} %select_n.66), kind=kOutput, calls=%fused_computation.17 | convolution fusion | flops 268435456 | bytes 4259844 | tf_op jit(solution)/shard_map/dot_general | solution.py:398
  99.2 0.5 fusion.9
  99.7 1.1 copy-done.9
  100.8 0.5 convolution_add_fusion.1
  101.3 1.1 copy-done.11
  102.4 0.5 fusion
  103.0 0.8 pad_maximum_fusion
  103.9 0.9 constant_dynamic-slice_fusion.1
  104.8 2.6 %all-to-all-done.3 = bf16[64,16,128]{2,1,0:T(8,128)(2,1)S(1)} async-done(((bf16[64,16,128]{2,1,0:T(8,128)(2,1)}), bf16[64,16,128]{2,1,0:T(8,128)(2,1)S(1)}, u32[]{:S(2)}, u32[]{:S(2)}) %all-to-all-start.3) | async-done | bytes 262176 | tf_op jit(solution)/shard_map/all_to_all | solution.py:23
  107.4 1.0 shard_map.121
  108.4 5.0 %all-to-all-start.4 = ((bf16[32,16,128]{2,1,0:T(8,128)(2,1)}), bf16[32,16,128]{2,1,0:T(8,128)(2,1)S(1)}, u32[]{:S(2)}, u32[]{:S(2)}) async-start(bf16[32,16,128]{2,1,0:T(8,128)(2,1)} %get-tuple-element.53), calls=%async_computation.4 | async-start | bytes 262144 | tf_op jit(solution)/shard_map/all_to_all | solution.py:23
  113.4 1.3 maximum_add_fusion
  114.8 0.9 copy-done.7
  115.7 2.9 %collective-permute-start.5 = (bf16[32,4096]{1,0:T(8,128)(2,1)S(1)}, bf16[32,4096]{1,0:T(8,128)(2,1)S(1)}, u32[]{:S(2)}, u32[]{:S(2)}) collective-permute-start(bf16[32,4096]{1,0:T(8,128)(2,1)S(1)} %fusion.4), channel_id=1, source_target_pairs={{0,128},{64,192},{128,0},{192,64},{1,129},{65,193},{129,1},{193,65... | collective-permute-start | bytes 786440 | tf_op jit(solution)/shard_map/ppermute | solution.py:33
  118.6 5.2 %all-to-all-done.4 = bf16[32,16,128]{2,1,0:T(8,128)(2,1)S(1)} async-done(((bf16[32,16,128]{2,1,0:T(8,128)(2,1)}), bf16[32,16,128]{2,1,0:T(8,128)(2,1)S(1)}, u32[]{:S(2)}, u32[]{:S(2)}) %all-to-all-start.4) | async-done | bytes 131104 | tf_op jit(solution)/shard_map/all_to_all | solution.py:23
  123.8 0.4 shard_map.122
  124.2 13.0 %all_to_all.30 = bf16[32,16,128]{2,1,0:T(8,128)(2,1)S(1)} all-to-all(bf16[32,16,128]{2,1,0:T(8,128)(2,1)S(1)} %shard_map.122), channel_id=1, replica_groups={{0,1,2,3,4,5,6,7,8,9,10,11,12,13,14,15,16,17,18,19,20,21,22,23,24,25,26..., dimensions={0} | all-to-all | bytes 262144 | tf_op jit(solution)/shard_map/all_to_all | solution.py:23
  137.3 1.0 shard_map.123
  138.3 0.8 fusion.2
  (41 shorter events, 1.0 us)
Async XLA Ops:
  2.1 21.6 %all-to-all-start = ((bf16[16,16,512]{2,1,0:T(8,128)(2,1)}), bf16[16,16,512]{2,1,0:T(8,128)(2,1)S(1)}, u32[]{:S(2)}, u32[]{:S(2)}) async-start(bf16[16,16,512]{2,1,0:T(8,128)(2,1)} %broadcast_in_dim.45), calls=%async_computation | async-start | bytes 524288 | tf_op jit(solution)/shard_map/all_to_all | solution.py:23
  13.4 0.7 copy-start.4
  14.1 13.7 %copy-start.1 = (bf16[4096,128]{1,0:T(8,128)(2,1)S(1)}, bf16[4096,128]{1,0:T(8,128)(2,1)}, u32[]{:S(2)}) copy-start(bf16[4096,128]{1,0:T(8,128)(2,1)} %coef_ref.7) | copy-start | bytes 3145732
  14.1 13.7 %copy-start.5 = (f32[512]{0:T(512)S(1)}, f32[512]{0:T(512)}, u32[]{:S(2)}) copy-start(f32[512]{0:T(512)} %param.14) | copy-start | bytes 6148
  23.7 9.0 %collective-permute-start.2 = (bf16[256,512]{1,0:T(8,128)(2,1)S(1)}, bf16[256,512]{1,0:T(8,128)(2,1)S(1)}, u32[]{:S(2)}, u32[]{:S(2)}) collective-permute-start(bf16[256,512]{1,0:T(8,128)(2,1)S(1)} %bitcast.60), channel_id=1, source_target_pairs={{0,16},{1,17},{2,18},{3,19},{4,20},{5,21},{6,22},{7,23},{8,24},{9,... | collective-permute-start | bytes 786440 | tf_op jit(solution)/shard_map/ppermute | solution.py:33
  24.9 11.6 %collective-permute-start.1 = (bf16[256,512]{1,0:T(8,128)(2,1)S(1)}, bf16[256,512]{1,0:T(8,128)(2,1)S(1)}, u32[]{:S(2)}, u32[]{:S(2)}) collective-permute-start(bf16[256,512]{1,0:T(8,128)(2,1)S(1)} %bitcast.61), channel_id=1, source_target_pairs={{0,48},{1,49},{2,50},{3,51},{4,52},{5,53},{6,54},{7,55},{8,56},{9,... | collective-permute-start | bytes 786440 | tf_op jit(solution)/shard_map/ppermute | solution.py:33
  24.9 14.3 %collective-permute-start = (bf16[256,512]{1,0:T(8,128)(2,1)S(1)}, bf16[256,512]{1,0:T(8,128)(2,1)S(1)}, u32[]{:S(2)}, u32[]{:S(2)}) collective-permute-start(bf16[256,512]{1,0:T(8,128)(2,1)S(1)} %bitcast.62), channel_id=1, source_target_pairs={{0,32},{1,33},{2,34},{3,35},{4,36},{5,37},{6,38},{7,39},{8,40},{9,... | collective-permute-start | bytes 786440 | tf_op jit(solution)/shard_map/ppermute | solution.py:33
  27.8 4.9 %copy-start = (bf16[4096,512]{1,0:T(8,128)(2,1)S(1)}, bf16[4096,512]{1,0:T(8,128)(2,1)}, u32[]{:S(2)}) copy-start(bf16[4096,512]{1,0:T(8,128)(2,1)} %get-tuple-element.31.centers_ref) | copy-start | bytes 12582916
  39.2 12.1 %copy-start.12 = (f32[8]{0:T(128)S(1)}, f32[8]{0:T(128)}, u32[]{:S(2)}) copy-start(f32[8]{0:T(128)} %param.13) | copy-start | bytes 100
  39.2 12.1 %copy-start.13 = (s32[16]{0:T(128)S(1)}, s32[16]{0:T(128)}, u32[]{:S(2)}) copy-start(s32[16]{0:T(128)} %param.11) | copy-start | bytes 196
  39.3 21.9 %copy-start.6 = (f32[16,128]{1,0:T(8,128)S(1)}, f32[16,128]{1,0:T(8,128)}, u32[]{:S(2)}) copy-start(f32[16,128]{1,0:T(8,128)} %targets_ref.1) | copy-start | bytes 24580
  39.3 29.5 %copy-start.2 = (f32[64,2048]{1,0:T(8,128)S(1)}, f32[64,2048]{1,0:T(8,128)}, u32[]{:S(2)}) copy-start(f32[64,2048]{1,0:T(8,128)} %matrix_ref.2) | copy-start | bytes 1572868
  42.7 18.5 %all-to-all-start.1 = ((bf16[64,16,128]{2,1,0:T(8,128)(2,1)}), bf16[64,16,128]{2,1,0:T(8,128)(2,1)S(1)}, u32[]{:S(2)}, u32[]{:S(2)}) async-start(bf16[64,16,128]{2,1,0:T(8,128)(2,1)} %bitcast.9), calls=%async_computation.1 | async-start | bytes 524288 | tf_op jit(solution)/shard_map/all_to_all | solution.py:23
  62.0 16.6 %all-to-all-start.2 = ((bf16[64,16,128]{2,1,0:T(8,128)(2,1)}), bf16[64,16,128]{2,1,0:T(8,128)(2,1)S(1)}, u32[]{:S(2)}, u32[]{:S(2)}) async-start(bf16[64,16,128]{2,1,0:T(8,128)(2,1)} %shard_map.118), calls=%async_computation.2 | async-start | bytes 524288 | tf_op jit(solution)/shard_map/all_to_all | solution.py:23
  86.8 10.2 %collective-permute-start.3 = (bf16[128,1024]{1,0:T(8,128)(2,1)S(1)}, bf16[128,1024]{1,0:T(8,128)(2,1)S(1)}, u32[]{:S(2)}, u32[]{:S(2)}) collective-permute-start(bf16[128,1024]{1,0:T(8,128)(2,1)S(1)} %copy.27), channel_id=1, source_target_pairs={{0,32},{1,33},{2,34},{3,35},{4,36},{5,37},{6,38},{7,39},{8,40},{9,... | collective-permute-start | bytes 786440 | tf_op jit(solution)/shard_map/ppermute | solution.py:33
  88.4 19.1 %all-to-all-start.3 = ((bf16[64,16,128]{2,1,0:T(8,128)(2,1)}), bf16[64,16,128]{2,1,0:T(8,128)(2,1)S(1)}, u32[]{:S(2)}, u32[]{:S(2)}) async-start(bf16[64,16,128]{2,1,0:T(8,128)(2,1)} %shard_map.120), calls=%async_computation.3 | async-start | bytes 524288 | tf_op jit(solution)/shard_map/all_to_all | solution.py:23
  97.0 2.2 %copy-start.10 = (bf16[256,4096]{1,0:T(8,128)(2,1)S(1)}, bf16[256,4096]{1,0:T(8,128)(2,1)}, u32[]{:S(2)}) copy-start(bf16[256,4096]{1,0:T(8,128)(2,1)} %get-tuple-element.47) | copy-start | bytes 6291460
  99.2 1.6 %copy-start.9 = (bf16[256,4096]{1,0:T(8,128)(2,1)S(1)}, bf16[256,4096]{1,0:T(8,128)(2,1)}, u32[]{:S(2)}) copy-start(bf16[256,4096]{1,0:T(8,128)(2,1)} %get-tuple-element.48) | copy-start | bytes 6291460
  100.8 1.6 %copy-start.11 = (bf16[256,4096]{1,0:T(8,128)(2,1)S(1)}, bf16[256,4096]{1,0:T(8,128)(2,1)}, u32[]{:S(2)}) copy-start(bf16[256,4096]{1,0:T(8,128)(2,1)} %get-tuple-element.49) | copy-start | bytes 6291460
  103.9 9.6 %collective-permute-start.4 = (bf16[2,32,4096]{2,1,0:T(8,128)(2,1)}, bf16[2,32,4096]{2,1,0:T(8,128)(2,1)}, u32[]{:S(2)}, u32[]{:S(2)}) collective-permute-start(bf16[2,32,4096]{2,1,0:T(8,128)(2,1)} %pad_maximum_fusion), channel_id=1, source_target_pairs={{0,64},{64,0},{128,192},{192,128},{1,65},{65,1},{129,193},{193,129... | collective-permute-start | bytes 1572872 | tf_op jit(solution)/shard_map/ppermute | solution.py:33
  107.4 16.4 %copy-start.3 = (f32[64,4096]{1,0:T(8,128)S(1)}, f32[64,4096]{1,0:T(8,128)}, u32[]{:S(2)}) copy-start(f32[64,4096]{1,0:T(8,128)} %matrix_ref.1) | copy-start | bytes 3145732
  108.4 15.4 %all-to-all-start.4 = ((bf16[32,16,128]{2,1,0:T(8,128)(2,1)}), bf16[32,16,128]{2,1,0:T(8,128)(2,1)S(1)}, u32[]{:S(2)}, u32[]{:S(2)}) async-start(bf16[32,16,128]{2,1,0:T(8,128)(2,1)} %get-tuple-element.53), calls=%async_computation.4 | async-start | bytes 262144 | tf_op jit(solution)/shard_map/all_to_all | solution.py:23
  114.7 1.0 copy-start.7
  115.7 22.6 %collective-permute-start.5 = (bf16[32,4096]{1,0:T(8,128)(2,1)S(1)}, bf16[32,4096]{1,0:T(8,128)(2,1)S(1)}, u32[]{:S(2)}, u32[]{:S(2)}) collective-permute-start(bf16[32,4096]{1,0:T(8,128)(2,1)S(1)} %fusion.4), channel_id=1, source_target_pairs={{0,128},{64,192},{128,0},{192,64},{1,129},{65,193},{129,1},{193,65... | collective-permute-start | bytes 786440 | tf_op jit(solution)/shard_map/ppermute | solution.py:33
  123.8 14.5 %copy-start.8 = (f32[2,32,4096]{2,1,0:T(8,128)S(1)}, f32[2,32,4096]{2,1,0:T(8,128)}, u32[]{:S(2)}) copy-start(f32[2,32,4096]{2,1,0:T(8,128)} %copy-done.7) | copy-start | bytes 3145732

commit v10 on v9

--- a/solution.py
+++ b/solution.py
@@ -259,9 +259,10 @@
 
 
 def window_step(chosen_ref, residual_ref, window_ref):
-    window_ref[...] = lax.dot_general(
+    window = lax.dot_general(
         chosen_ref[...], residual_ref[...], (((0,), (0,)), ((), ())), preferred_element_type=F32
     )
+    window_ref[...] = window.astype(window_ref.dtype)
 
 
 def fold_step(group_ref, parts_ref, sent_ref):
@@ -372,7 +373,7 @@
     index = group.astype(jnp.int32).reshape(1)
     window = whole(
         window_step,
-        jax.ShapeDtypeStruct((own_rows, target_count), F32),
+        jax.ShapeDtypeStruct((own_rows, target_count), BF),
         picked.reshape(shards * own_points, own_rows),
         residual,
     )

time: 140 us -> 140 us (level)
  transfers between devices with their start and end apart: 11 -> 11, of which waited for: 8 -> 8; matrix products, arithmetic and copies ran while one was open for 8% -> 8% of each run, Pallas kernels for 12% -> 13%
where the time goes in v10:
time: 140 us; the launch traced here: 139 us
  starting transfers between devices  45.9 us (33%)
  waiting for transfers between devices  32.6 us (23%)
  Pallas kernels  22.7 us (16%)
  blocking collectives  19.8 us (14%)
  local copies, waits for them, and re-layouts  7.98 us (6%)
  other arithmetic  4.69 us (3%)
  matrix products  4.36 us (3%)
    all_to_all x5, starting transfers between devices, exchanged(): lax.all_to_all(pieces, axis, 0, 0, tiled=True, axis_index_groups=groups i...  37.3 us
    all_to_all x5, waiting for transfers between devices, exchanged(): lax.all_to_all(pieces, axis, 0, 0, tiled=True, axis_index_groups=groups i...  30.4 us
    pallas_call x4, Pallas kernels, kernel_and_value(): pl.pallas_call(functools.partial(kernel_block, bool(held)), out_shape=(pl...  13.8 us
    all_to_all x1, blocking collectives, exchanged(): lax.all_to_all(pieces, axis, 0, 0, tiled=True, axis_index_groups=groups i...  13 us
    ppermute x6, starting transfers between devices, swapped(): lax.ppermute(x, axis, [(i, i ^ bits) for i in range(lax.axis_size(axis))])  8.6 us
    all_gather x1, blocking collectives, body(): parts = lax.all_gather(window, 'pts')  6.75 us
    pallas_call x1, Pallas kernels, scaled_and_norm(): pl.pallas_call(scale_step, out_shape=(pltpu.HBM((total, depth), BF), jax....  4.61 us
    unnamed x28, local copies, waits for them, and re-layouts  3.87 us
  transfers between devices with their start and end apart: 11, of which 8 were waited for; matrix products, arithmetic and copies ran while one was open for 8% of the time, Pallas kernels for 13%

profile of v10, /device:TPU:4, one launch (start us, length us, event | category | flops | bytes accessed | tf_op | source)
XLA Modules:
  0.0 139.0 jit_solution(5402269343242781636)
XLA Ops:
  0.6 1.4 %broadcast_in_dim.45 = bf16[16,16,512]{2,1,0:T(8,128)(2,1)} broadcast(bf16[16,512]{1,0:T(8,128)(2,1)} %param.10), dimensions={1,2} | broadcast | bytes 278528 | tf_op jit(solution)/shard_map/broadcast_in_dim | solution.py:29
  2.1 9.6 %all-to-all-start = ((bf16[16,16,512]{2,1,0:T(8,128)(2,1)}), bf16[16,16,512]{2,1,0:T(8,128)(2,1)S(1)}, u32[]{:S(2)}, u32[]{:S(2)}) async-start(bf16[16,16,512]{2,1,0:T(8,128)(2,1)} %broadcast_in_dim.45), calls=%async_computation | async-start | bytes 524288 | tf_op jit(solution)/shard_map/all_to_all | solution.py:23
  11.7 0.7 broadcast_subtract_fusion
  12.5 0.7 broadcast_compare_fusion
  13.4 0.7 copy-done.4
  14.1 4.6 %shard_map.113 = (bf16[4096,512]{1,0:T(8,128)(2,1)}, f32[1,4096]{1,0:T(1,128)S(1)}, bf16[64,512]{1,0:T(8,128)(2,1)S(1)}, f32[1,64]{1,0:T(1,128)S(1)}) custom-call(bf16[4096,512]{1,0:T(8,128)(2,1)} %centers_ref.1, f32[1,512]{1,0:T(1,128)S(1)} %bitcast.69, s32[64,1]{1,0:T(8,128)S(1)} %copy.23.local_ref), custom_call_target="tpu_custom_call" | custom-call | flops 8388608 | bytes 4194304 | tf_op jit(solution)/shard_map/pallas_call | solution.py:75
  18.7 5.0 %all-to-all-done = bf16[16,16,512]{2,1,0:T(8,128)(2,1)S(1)} async-done(((bf16[16,16,512]{2,1,0:T(8,128)(2,1)}), bf16[16,16,512]{2,1,0:T(8,128)(2,1)S(1)}, u32[]{:S(2)}, u32[]{:S(2)}) %all-to-all-start) | async-done | bytes 262176 | tf_op jit(solution)/shard_map/all_to_all | solution.py:23
  23.7 1.2 collective-permute-start.2
  24.9 2.9 %collective-permute-start = (bf16[256,512]{1,0:T(8,128)(2,1)S(1)}, bf16[256,512]{1,0:T(8,128)(2,1)S(1)}, u32[]{:S(2)}, u32[]{:S(2)}) collective-permute-start(bf16[256,512]{1,0:T(8,128)(2,1)S(1)} %bitcast.62), channel_id=1, source_target_pairs={{0,32},{1,33},{2,34},{3,35},{4,36},{5,37},{6,38},{7,39},{8,40},{9,... | collective-permute-start | bytes 786440 | tf_op jit(solution)/shard_map/ppermute | solution.py:33
  27.8 4.8 %shard_map.114 = (bf16[256,4096]{1,0:T(8,128)(2,1)}, bf16[4,256,128]{2,1,0:T(8,128)(2,1)S(1)}, bf16[4,256,64]{2,1,0:T(8,128)(2,1)S(1)}) custom-call(s32[1]{0:T(128)} %bitcast.7.slot_ref, bf16[256,512]{1,0:T(8,128)(2,1)S(1)} %bitcast.63, f32[1,512]{1,0:T(1,128)S(1)} %bitcast.70, bf16[4096,512]{1,0:T(8,128)(2,1)} %get-tuple-element.31.centers_ref, ...), custom_call_target="tpu_custom_call" | custom-call | flops 1342177280 | bytes 2097152 | tf_op jit(solution)/shard_map/pallas_call | solution.py:153
  32.7 2.8 %shard_map.115 = (bf16[256,4096]{1,0:T(8,128)(2,1)}, bf16[4,256,128]{2,1,0:T(8,128)(2,1)S(1)}, bf16[4,256,64]{2,1,0:T(8,128)(2,1)S(1)}) custom-call(s32[1]{0:T(128)} %bitcast.6.slot_ref, bf16[256,512]{1,0:T(8,128)(2,1)S(1)} %collective-permute-done.2.points_ref, f32[1,512]{1,0:T(1,128)S(1)} %bitcast.71, bf16[4096,512]{1,0:T(8,128)(2,1)S(1)} %copy-done, ...), custom_call_target="tpu_custom_call" | custom-call | flops 1342177280 | bytes 2097152 | tf_op jit(solution)/shard_map/pallas_call | solution.py:153
  35.5 1.0 collective-permute-done.1.points_ref
  36.5 2.7 %shard_map.116 = (bf16[256,4096]{1,0:T(8,128)(2,1)}, bf16[4,256,128]{2,1,0:T(8,128)(2,1)S(1)}, bf16[4,256,64]{2,1,0:T(8,128)(2,1)S(1)}) custom-call(s32[1]{0:T(128)} %bitcast.5.slot_ref, bf16[256,512]{1,0:T(8,128)(2,1)S(1)} %collective-permute-done.1.points_ref, f32[1,512]{1,0:T(1,128)S(1)} %bitcast.72, bf16[4096,512]{1,0:T(8,128)(2,1)S(1)} %copy-done, ...), custom_call_target="tpu_custom_call" | custom-call | flops 1342177280 | bytes 2097152 | tf_op jit(solution)/shard_map/pallas_call | solution.py:153
  39.3 3.5 %shard_map.117 = (bf16[256,4096]{1,0:T(8,128)(2,1)}, bf16[4,256,128]{2,1,0:T(8,128)(2,1)}, bf16[4,256,64]{2,1,0:T(8,128)(2,1)S(1)}) custom-call(s32[1]{0:T(128)} %bitcast.1.slot_ref, bf16[256,512]{1,0:T(8,128)(2,1)S(1)} %collective-permute-done.points_ref, f32[1,512]{1,0:T(1,128)S(1)} %bitcast.73, bf16[4096,512]{1,0:T(8,128)(2,1)S(1)} %copy-done, ...), custom_call_target="tpu_custom_call" | custom-call | flops 1342177280 | bytes 2097152 | tf_op jit(solution)/shard_map/pallas_call | solution.py:153
  42.7 8.6 %all-to-all-start.1 = ((bf16[64,16,128]{2,1,0:T(8,128)(2,1)}), bf16[64,16,128]{2,1,0:T(8,128)(2,1)S(1)}, u32[]{:S(2)}, u32[]{:S(2)}) async-start(bf16[64,16,128]{2,1,0:T(8,128)(2,1)} %bitcast.9), calls=%async_computation.1 | async-start | bytes 524288 | tf_op jit(solution)/shard_map/all_to_all | solution.py:23
  51.5 9.7 %all-to-all-done.1.shares_ref = bf16[64,16,128]{2,1,0:T(8,128)(2,1)S(1)} async-done(((bf16[64,16,128]{2,1,0:T(8,128)(2,1)}), bf16[64,16,128]{2,1,0:T(8,128)(2,1)S(1)}, u32[]{:S(2)}, u32[]{:S(2)}) %all-to-all-start.1) | async-done | bytes 262176 | tf_op jit(solution)/shard_map/all_to_all | solution.py:23
  61.2 0.8 shard_map.118
  62.0 6.7 %all-to-all-start.2 = ((bf16[64,16,128]{2,1,0:T(8,128)(2,1)}), bf16[64,16,128]{2,1,0:T(8,128)(2,1)S(1)}, u32[]{:S(2)}, u32[]{:S(2)}) async-start(bf16[64,16,128]{2,1,0:T(8,128)(2,1)} %shard_map.118), calls=%async_computation.2 | async-start | bytes 524288 | tf_op jit(solution)/shard_map/all_to_all | solution.py:23
  68.8 0.5 reshape.75
  69.3 0.6 convolution_bitcast_fusion
  70.0 0.5 copy.26
  70.5 0.2 reshape.76
  70.8 7.9 %all-to-all-done.2 = bf16[64,16,128]{2,1,0:T(8,128)(2,1)S(1)} async-done(((bf16[64,16,128]{2,1,0:T(8,128)(2,1)}), bf16[64,16,128]{2,1,0:T(8,128)(2,1)S(1)}, u32[]{:S(2)}, u32[]{:S(2)}) %all-to-all-start.2) | async-done | bytes 262176 | tf_op jit(solution)/shard_map/all_to_all | solution.py:23
  78.6 0.2 shard_map.119
  78.9 6.8 %all-gather = bf16[256,128]{1,0:T(8,128)(2,1)S(1)} all-gather(bf16[64,128]{1,0:T(8,128)(2,1)S(1)} %shard_map.119), channel_id=2, replica_groups=mesh['pts'=4,'ctr'=64] {'pts'}, dimensions={0}, use_global_device_ids=true | all-gather | bytes 81920 | tf_op jit(solution)/shard_map/all_gather | solution.py:380
  85.6 0.8 shard_map.120
  86.6 1.6 %collective-permute-start.3 = (bf16[128,1024]{1,0:T(8,128)(2,1)S(1)}, bf16[128,1024]{1,0:T(8,128)(2,1)S(1)}, u32[]{:S(2)}, u32[]{:S(2)}) collective-permute-start(bf16[128,1024]{1,0:T(8,128)(2,1)S(1)} %copy.27), channel_id=1, source_target_pairs={{0,32},{1,33},{2,34},{3,35},{4,36},{5,37},{6,38},{7,39},{8,40},{9,... | collective-permute-start | bytes 786440 | tf_op jit(solution)/shard_map/ppermute | solution.py:33
  88.2 7.5 %all-to-all-start.3 = ((bf16[64,16,128]{2,1,0:T(8,128)(2,1)}), bf16[64,16,128]{2,1,0:T(8,128)(2,1)S(1)}, u32[]{:S(2)}, u32[]{:S(2)}) async-start(bf16[64,16,128]{2,1,0:T(8,128)(2,1)} %shard_map.120), calls=%async_computation.3 | async-start | bytes 524288 | tf_op jit(solution)/shard_map/all_to_all | solution.py:23
  95.7 1.1 collective-permute-done.3
  96.8 2.2 %fusion.5 = f32[128,4096]{1,0:T(8,128)S(1)} fusion(bf16[256,4096]{1,0:T(8,128)(2,1)} %get-tuple-element.50, bf16[4,256,128]{2,1,0:T(8,128)(2,1)S(1)} %bitcast.56, s32[]{:T(128)S(6)} %select_n.66), kind=kOutput, calls=%fused_computation.17 | convolution fusion | flops 268435456 | bytes 4259844 | tf_op jit(solution)/shard_map/dot_general | solution.py:399
  99.0 0.5 fusion.9
  99.5 1.1 copy-done.9
  100.6 0.5 convolution_add_fusion.1
  101.1 1.1 copy-done.11
  102.2 0.5 fusion
  102.8 0.8 pad_maximum_fusion
  103.8 0.9 constant_dynamic-slice_fusion.1
  104.6 2.6 %all-to-all-done.3 = bf16[64,16,128]{2,1,0:T(8,128)(2,1)S(1)} async-done(((bf16[64,16,128]{2,1,0:T(8,128)(2,1)}), bf16[64,16,128]{2,1,0:T(8,128)(2,1)S(1)}, u32[]{:S(2)}, u32[]{:S(2)}) %all-to-all-start.3) | async-done | bytes 262176 | tf_op jit(solution)/shard_map/all_to_all | solution.py:23
  107.2 1.0 shard_map.121
  108.2 5.0 %all-to-all-start.4 = ((bf16[32,16,128]{2,1,0:T(8,128)(2,1)}), bf16[32,16,128]{2,1,0:T(8,128)(2,1)S(1)}, u32[]{:S(2)}, u32[]{:S(2)}) async-start(bf16[32,16,128]{2,1,0:T(8,128)(2,1)} %get-tuple-element.53), calls=%async_computation.4 | async-start | bytes 262144 | tf_op jit(solution)/shard_map/all_to_all | solution.py:23
  113.3 1.3 maximum_add_fusion
  114.6 0.9 copy-done.7
  115.5 2.9 %collective-permute-start.5 = (bf16[32,4096]{1,0:T(8,128)(2,1)S(1)}, bf16[32,4096]{1,0:T(8,128)(2,1)S(1)}, u32[]{:S(2)}, u32[]{:S(2)}) collective-permute-start(bf16[32,4096]{1,0:T(8,128)(2,1)S(1)} %fusion.4), channel_id=1, source_target_pairs={{0,128},{64,192},{128,0},{192,64},{1,129},{65,193},{129,1},{193,65... | collective-permute-start | bytes 786440 | tf_op jit(solution)/shard_map/ppermute | solution.py:33
  118.4 5.2 %all-to-all-done.4 = bf16[32,16,128]{2,1,0:T(8,128)(2,1)S(1)} async-done(((bf16[32,16,128]{2,1,0:T(8,128)(2,1)}), bf16[32,16,128]{2,1,0:T(8,128)(2,1)S(1)}, u32[]{:S(2)}, u32[]{:S(2)}) %all-to-all-start.4) | async-done | bytes 131104 | tf_op jit(solution)/shard_map/all_to_all | solution.py:23
  123.6 0.4 shard_map.122
  124.1 13.0 %all_to_all.30 = bf16[32,16,128]{2,1,0:T(8,128)(2,1)S(1)} all-to-all(bf16[32,16,128]{2,1,0:T(8,128)(2,1)S(1)} %shard_map.122), channel_id=1, replica_groups={{0,1,2,3,4,5,6,7,8,9,10,11,12,13,14,15,16,17,18,19,20,21,22,23,24,25,26..., dimensions={0} | all-to-all | bytes 262144 | tf_op jit(solution)/shard_map/all_to_all | solution.py:23
  137.1 1.0 shard_map.123
  138.2 0.8 fusion.2
  (41 shorter events, 1.0 us)
Async XLA Ops:
  2.1 21.6 %all-to-all-start = ((bf16[16,16,512]{2,1,0:T(8,128)(2,1)}), bf16[16,16,512]{2,1,0:T(8,128)(2,1)S(1)}, u32[]{:S(2)}, u32[]{:S(2)}) async-start(bf16[16,16,512]{2,1,0:T(8,128)(2,1)} %broadcast_in_dim.45), calls=%async_computation | async-start | bytes 524288 | tf_op jit(solution)/shard_map/all_to_all | solution.py:23
  13.4 0.7 copy-start.4
  14.1 13.7 %copy-start.1 = (bf16[4096,128]{1,0:T(8,128)(2,1)S(1)}, bf16[4096,128]{1,0:T(8,128)(2,1)}, u32[]{:S(2)}) copy-start(bf16[4096,128]{1,0:T(8,128)(2,1)} %coef_ref.7) | copy-start | bytes 3145732
  14.1 13.7 %copy-start.5 = (f32[512]{0:T(512)S(1)}, f32[512]{0:T(512)}, u32[]{:S(2)}) copy-start(f32[512]{0:T(512)} %param.14) | copy-start | bytes 6148
  23.7 9.0 %collective-permute-start.2 = (bf16[256,512]{1,0:T(8,128)(2,1)S(1)}, bf16[256,512]{1,0:T(8,128)(2,1)S(1)}, u32[]{:S(2)}, u32[]{:S(2)}) collective-permute-start(bf16[256,512]{1,0:T(8,128)(2,1)S(1)} %bitcast.60), channel_id=1, source_target_pairs={{0,16},{1,17},{2,18},{3,19},{4,20},{5,21},{6,22},{7,23},{8,24},{9,... | collective-permute-start | bytes 786440 | tf_op jit(solution)/shard_map/ppermute | solution.py:33
  24.9 11.6 %collective-permute-start.1 = (bf16[256,512]{1,0:T(8,128)(2,1)S(1)}, bf16[256,512]{1,0:T(8,128)(2,1)S(1)}, u32[]{:S(2)}, u32[]{:S(2)}) collective-permute-start(bf16[256,512]{1,0:T(8,128)(2,1)S(1)} %bitcast.61), channel_id=1, source_target_pairs={{0,48},{1,49},{2,50},{3,51},{4,52},{5,53},{6,54},{7,55},{8,56},{9,... | collective-permute-start | bytes 786440 | tf_op jit(solution)/shard_map/ppermute | solution.py:33
  24.9 14.3 %collective-permute-start = (bf16[256,512]{1,0:T(8,128)(2,1)S(1)}, bf16[256,512]{1,0:T(8,128)(2,1)S(1)}, u32[]{:S(2)}, u32[]{:S(2)}) collective-permute-start(bf16[256,512]{1,0:T(8,128)(2,1)S(1)} %bitcast.62), channel_id=1, source_target_pairs={{0,32},{1,33},{2,34},{3,35},{4,36},{5,37},{6,38},{7,39},{8,40},{9,... | collective-permute-start | bytes 786440 | tf_op jit(solution)/shard_map/ppermute | solution.py:33
  27.8 4.9 %copy-start = (bf16[4096,512]{1,0:T(8,128)(2,1)S(1)}, bf16[4096,512]{1,0:T(8,128)(2,1)}, u32[]{:S(2)}) copy-start(bf16[4096,512]{1,0:T(8,128)(2,1)} %get-tuple-element.31.centers_ref) | copy-start | bytes 12582916
  39.2 12.1 %copy-start.12 = (f32[8]{0:T(128)S(1)}, f32[8]{0:T(128)}, u32[]{:S(2)}) copy-start(f32[8]{0:T(128)} %param.13) | copy-start | bytes 100
  39.2 12.1 %copy-start.13 = (s32[16]{0:T(128)S(1)}, s32[16]{0:T(128)}, u32[]{:S(2)}) copy-start(s32[16]{0:T(128)} %param.11) | copy-start | bytes 196
  39.3 21.9 %copy-start.6 = (f32[16,128]{1,0:T(8,128)S(1)}, f32[16,128]{1,0:T(8,128)}, u32[]{:S(2)}) copy-start(f32[16,128]{1,0:T(8,128)} %targets_ref.1) | copy-start | bytes 24580
  39.3 29.5 %copy-start.2 = (f32[64,2048]{1,0:T(8,128)S(1)}, f32[64,2048]{1,0:T(8,128)}, u32[]{:S(2)}) copy-start(f32[64,2048]{1,0:T(8,128)} %matrix_ref.2) | copy-start | bytes 1572868
  42.7 18.5 %all-to-all-start.1 = ((bf16[64,16,128]{2,1,0:T(8,128)(2,1)}), bf16[64,16,128]{2,1,0:T(8,128)(2,1)S(1)}, u32[]{:S(2)}, u32[]{:S(2)}) async-start(bf16[64,16,128]{2,1,0:T(8,128)(2,1)} %bitcast.9), calls=%async_computation.1 | async-start | bytes 524288 | tf_op jit(solution)/shard_map/all_to_all | solution.py:23
  62.0 16.6 %all-to-all-start.2 = ((bf16[64,16,128]{2,1,0:T(8,128)(2,1)}), bf16[64,16,128]{2,1,0:T(8,128)(2,1)S(1)}, u32[]{:S(2)}, u32[]{:S(2)}) async-start(bf16[64,16,128]{2,1,0:T(8,128)(2,1)} %shard_map.118), calls=%async_computation.2 | async-start | bytes 524288 | tf_op jit(solution)/shard_map/all_to_all | solution.py:23
  86.6 10.2 %collective-permute-start.3 = (bf16[128,1024]{1,0:T(8,128)(2,1)S(1)}, bf16[128,1024]{1,0:T(8,128)(2,1)S(1)}, u32[]{:S(2)}, u32[]{:S(2)}) collective-permute-start(bf16[128,1024]{1,0:T(8,128)(2,1)S(1)} %copy.27), channel_id=1, source_target_pairs={{0,32},{1,33},{2,34},{3,35},{4,36},{5,37},{6,38},{7,39},{8,40},{9,... | collective-permute-start | bytes 786440 | tf_op jit(solution)/shard_map/ppermute | solution.py:33
  88.2 19.0 %all-to-all-start.3 = ((bf16[64,16,128]{2,1,0:T(8,128)(2,1)}), bf16[64,16,128]{2,1,0:T(8,128)(2,1)S(1)}, u32[]{:S(2)}, u32[]{:S(2)}) async-start(bf16[64,16,128]{2,1,0:T(8,128)(2,1)} %shard_map.120), calls=%async_computation.3 | async-start | bytes 524288 | tf_op jit(solution)/shard_map/all_to_all | solution.py:23
  96.8 2.2 %copy-start.10 = (bf16[256,4096]{1,0:T(8,128)(2,1)S(1)}, bf16[256,4096]{1,0:T(8,128)(2,1)}, u32[]{:S(2)}) copy-start(bf16[256,4096]{1,0:T(8,128)(2,1)} %get-tuple-element.47) | copy-start | bytes 6291460
  99.0 1.6 %copy-start.9 = (bf16[256,4096]{1,0:T(8,128)(2,1)S(1)}, bf16[256,4096]{1,0:T(8,128)(2,1)}, u32[]{:S(2)}) copy-start(bf16[256,4096]{1,0:T(8,128)(2,1)} %get-tuple-element.48) | copy-start | bytes 6291460
  100.6 1.6 %copy-start.11 = (bf16[256,4096]{1,0:T(8,128)(2,1)S(1)}, bf16[256,4096]{1,0:T(8,128)(2,1)}, u32[]{:S(2)}) copy-start(bf16[256,4096]{1,0:T(8,128)(2,1)} %get-tuple-element.49) | copy-start | bytes 6291460
  103.7 9.6 %collective-permute-start.4 = (bf16[2,32,4096]{2,1,0:T(8,128)(2,1)}, bf16[2,32,4096]{2,1,0:T(8,128)(2,1)}, u32[]{:S(2)}, u32[]{:S(2)}) collective-permute-start(bf16[2,32,4096]{2,1,0:T(8,128)(2,1)} %pad_maximum_fusion), channel_id=1, source_target_pairs={{0,64},{64,0},{128,192},{192,128},{1,65},{65,1},{129,193},{193,129... | collective-permute-start | bytes 1572872 | tf_op jit(solution)/shard_map/ppermute | solution.py:33
  107.2 16.4 %copy-start.3 = (f32[64,4096]{1,0:T(8,128)S(1)}, f32[64,4096]{1,0:T(8,128)}, u32[]{:S(2)}) copy-start(f32[64,4096]{1,0:T(8,128)} %matrix_ref.1) | copy-start | bytes 3145732
  108.2 15.4 %all-to-all-start.4 = ((bf16[32,16,128]{2,1,0:T(8,128)(2,1)}), bf16[32,16,128]{2,1,0:T(8,128)(2,1)S(1)}, u32[]{:S(2)}, u32[]{:S(2)}) async-start(bf16[32,16,128]{2,1,0:T(8,128)(2,1)} %get-tuple-element.53), calls=%async_computation.4 | async-start | bytes 262144 | tf_op jit(solution)/shard_map/all_to_all | solution.py:23
  114.6 1.0 copy-start.7
  115.5 22.6 %collective-permute-start.5 = (bf16[32,4096]{1,0:T(8,128)(2,1)S(1)}, bf16[32,4096]{1,0:T(8,128)(2,1)S(1)}, u32[]{:S(2)}, u32[]{:S(2)}) collective-permute-start(bf16[32,4096]{1,0:T(8,128)(2,1)S(1)} %fusion.4), channel_id=1, source_target_pairs={{0,128},{64,192},{128,0},{192,64},{1,129},{65,193},{129,1},{193,65... | collective-permute-start | bytes 786440 | tf_op jit(solution)/shard_map/ppermute | solution.py:33
  123.6 14.5 %copy-start.8 = (f32[2,32,4096]{2,1,0:T(8,128)S(1)}, f32[2,32,4096]{2,1,0:T(8,128)}, u32[]{:S(2)}) copy-start(f32[2,32,4096]{2,1,0:T(8,128)} %copy-done.7) | copy-start | bytes 3145732

commit v11 on v10

--- a/solution.py
+++ b/solution.py
@@ -368,7 +368,10 @@
         targets,
         weight,
     )
+    residual, turned_inverse = lax.optimization_barrier((residual, turned_inverse))
+    other_inverse = swapped(turned_inverse, "ctr", panel_shards)
     residual = exchanged(residual, "ctr").reshape(shards * own_points, target_count)
+    residual, other_inverse = lax.optimization_barrier((residual, other_inverse))
 
     index = group.astype(jnp.int32).reshape(1)
     window = whole(
@@ -380,8 +383,8 @@
     parts = lax.all_gather(window, "pts")
     sent = jax.ShapeDtypeStruct((shards, strip, LANES), BF)
     window = whole(fold_step, sent, index, parts, scalars=1)
-    window, turned_inverse = lax.optimization_barrier((window, turned_inverse))
-    other_inverse = swapped(turned_inverse, "ctr", panel_shards)
+    window, other_inverse = lax.optimization_barrier((window, other_inverse))
+    other_inverse = swapped(other_inverse, "pts", 1)
     other_inverse, residual = lax.optimization_barrier((other_inverse, residual))
     solve_rows = jnp.concatenate(
         [

time: 140 us -> 140 us (level)
    all_to_all x5, waiting for transfers between devices: 30.4 us -> 22.9 us  [exchanged(): lax.all_to_all(pieces, axis, 0, 0, tiled=True, axis_index_groups=groups i...]
    ppermute x6 -> x7, waiting for transfers between devices: 2.2 us -> 9.23 us  [swapped(): lax.ppermute(x, axis, [(i, i ^ bits) for i in range(lax.axis_size(axis))])]
    all_to_all x5, starting transfers between devices: 37.3 us -> 39.2 us  [exchanged(): lax.all_to_all(pieces, axis, 0, 0, tiled=True, axis_index_groups=groups i...]
    ppermute x6 -> x7, starting transfers between devices: 8.6 us -> 7.77 us  [swapped(): lax.ppermute(x, axis, [(i, i ^ bits) for i in range(lax.axis_size(axis))])]
  transfers between devices with their start and end apart: 11 -> 12, of which waited for: 8 -> 8; matrix products, arithmetic and copies ran while one was open for 8% -> 8% of each run, Pallas kernels for 13% -> 12%
where the time goes in v11:
time: 140 us
  starting transfers between devices  47 us (34%)
  waiting for transfers between devices  32.2 us (23%)
  Pallas kernels  22.7 us (16%)
  blocking collectives  19.8 us (14%)
  local copies, waits for them, and re-layouts  7.98 us (6%)
  other arithmetic  4.68 us (3%)
  matrix products  4.35 us (3%)
    all_to_all x5, starting transfers between devices, exchanged(): lax.all_to_all(pieces, axis, 0, 0, tiled=True, axis_index_groups=groups i...  39.2 us
    all_to_all x5, waiting for transfers between devices, exchanged(): lax.all_to_all(pieces, axis, 0, 0, tiled=True, axis_index_groups=groups i...  22.9 us
    pallas_call x4, Pallas kernels, kernel_and_value(): pl.pallas_call(functools.partial(kernel_block, bool(held)), out_shape=(pl...  13.8 us
    all_to_all x1, blocking collectives, exchanged(): lax.all_to_all(pieces, axis, 0, 0, tiled=True, axis_index_groups=groups i...  13 us
    ppermute x7, waiting for transfers between devices, swapped(): lax.ppermute(x, axis, [(i, i ^ bits) for i in range(lax.axis_size(axis))])  9.23 us
    ppermute x7, starting transfers between devices, swapped(): lax.ppermute(x, axis, [(i, i ^ bits) for i in range(lax.axis_size(axis))])  7.77 us
    all_gather x1, blocking collectives, body(): parts = lax.all_gather(window, 'pts')  6.75 us
    pallas_call x1, Pallas kernels, scaled_and_norm(): pl.pallas_call(scale_step, out_shape=(pltpu.HBM((total, depth), BF), jax....  4.62 us
  transfers between devices with their start and end apart: 12, of which 8 were waited for; matrix products, arithmetic and copies ran while one was open for 8% of the time, Pallas kernels for 12%

profile of v11, /device:TPU:4, one launch (start us, length us, event | category | flops | bytes accessed | tf_op | source)
XLA Modules:
  0.0 139.6 jit_solution(15398971817616564668)
XLA Ops:
  0.6 1.4 %broadcast_in_dim.45 = bf16[16,16,512]{2,1,0:T(8,128)(2,1)} broadcast(bf16[16,512]{1,0:T(8,128)(2,1)} %param.10), dimensions={1,2} | broadcast | bytes 278528 | tf_op jit(solution)/shard_map/broadcast_in_dim | solution.py:29
  2.1 9.6 %all-to-all-start = ((bf16[16,16,512]{2,1,0:T(8,128)(2,1)}), bf16[16,16,512]{2,1,0:T(8,128)(2,1)S(1)}, u32[]{:S(2)}, u32[]{:S(2)}) async-start(bf16[16,16,512]{2,1,0:T(8,128)(2,1)} %broadcast_in_dim.45), calls=%async_computation | async-start | bytes 524288 | tf_op jit(solution)/shard_map/all_to_all | solution.py:23
  11.7 0.7 broadcast_subtract_fusion
  12.5 0.7 broadcast_compare_fusion
  13.4 0.7 copy-done.4
  14.1 4.6 %shard_map.113 = (bf16[4096,512]{1,0:T(8,128)(2,1)}, f32[1,4096]{1,0:T(1,128)S(1)}, bf16[64,512]{1,0:T(8,128)(2,1)S(1)}, f32[1,64]{1,0:T(1,128)S(1)}) custom-call(bf16[4096,512]{1,0:T(8,128)(2,1)} %centers_ref.1, f32[1,512]{1,0:T(1,128)S(1)} %bitcast.69, s32[64,1]{1,0:T(8,128)S(1)} %copy.23.local_ref), custom_call_target="tpu_custom_call" | custom-call | flops 8388608 | bytes 4194304 | tf_op jit(solution)/shard_map/pallas_call | solution.py:75
  18.7 5.0 %all-to-all-done = bf16[16,16,512]{2,1,0:T(8,128)(2,1)S(1)} async-done(((bf16[16,16,512]{2,1,0:T(8,128)(2,1)}), bf16[16,16,512]{2,1,0:T(8,128)(2,1)S(1)}, u32[]{:S(2)}, u32[]{:S(2)}) %all-to-all-start) | async-done | bytes 262176 | tf_op jit(solution)/shard_map/all_to_all | solution.py:23
  23.7 1.2 collective-permute-start.2
  24.9 2.9 %collective-permute-start = (bf16[256,512]{1,0:T(8,128)(2,1)S(1)}, bf16[256,512]{1,0:T(8,128)(2,1)S(1)}, u32[]{:S(2)}, u32[]{:S(2)}) collective-permute-start(bf16[256,512]{1,0:T(8,128)(2,1)S(1)} %bitcast.62), channel_id=1, source_target_pairs={{0,32},{1,33},{2,34},{3,35},{4,36},{5,37},{6,38},{7,39},{8,40},{9,... | collective-permute-start | bytes 786440 | tf_op jit(solution)/shard_map/ppermute | solution.py:33
  27.8 4.8 %shard_map.114 = (bf16[256,4096]{1,0:T(8,128)(2,1)}, bf16[4,256,128]{2,1,0:T(8,128)(2,1)S(1)}, bf16[4,256,64]{2,1,0:T(8,128)(2,1)S(1)}) custom-call(s32[1]{0:T(128)} %bitcast.7.slot_ref, bf16[256,512]{1,0:T(8,128)(2,1)S(1)} %bitcast.63, f32[1,512]{1,0:T(1,128)S(1)} %bitcast.70, bf16[4096,512]{1,0:T(8,128)(2,1)} %get-tuple-element.35.centers_ref, ...), custom_call_target="tpu_custom_call" | custom-call | flops 1342177280 | bytes 2097152 | tf_op jit(solution)/shard_map/pallas_call | solution.py:153
  32.7 2.8 %shard_map.115 = (bf16[256,4096]{1,0:T(8,128)(2,1)}, bf16[4,256,128]{2,1,0:T(8,128)(2,1)S(1)}, bf16[4,256,64]{2,1,0:T(8,128)(2,1)S(1)}) custom-call(s32[1]{0:T(128)} %bitcast.6.slot_ref, bf16[256,512]{1,0:T(8,128)(2,1)S(1)} %collective-permute-done.2.points_ref, f32[1,512]{1,0:T(1,128)S(1)} %bitcast.71, bf16[4096,512]{1,0:T(8,128)(2,1)S(1)} %copy-done, ...), custom_call_target="tpu_custom_call" | custom-call | flops 1342177280 | bytes 2097152 | tf_op jit(solution)/shard_map/pallas_call | solution.py:153
  35.5 1.0 collective-permute-done.1.points_ref
  36.5 2.8 %shard_map.116 = (bf16[256,4096]{1,0:T(8,128)(2,1)}, bf16[4,256,128]{2,1,0:T(8,128)(2,1)S(1)}, bf16[4,256,64]{2,1,0:T(8,128)(2,1)S(1)}) custom-call(s32[1]{0:T(128)} %bitcast.5.slot_ref, bf16[256,512]{1,0:T(8,128)(2,1)S(1)} %collective-permute-done.1.points_ref, f32[1,512]{1,0:T(1,128)S(1)} %bitcast.72, bf16[4096,512]{1,0:T(8,128)(2,1)S(1)} %copy-done, ...), custom_call_target="tpu_custom_call" | custom-call | flops 1342177280 | bytes 2097152 | tf_op jit(solution)/shard_map/pallas_call | solution.py:153
  39.3 3.4 %shard_map.117 = (bf16[256,4096]{1,0:T(8,128)(2,1)}, bf16[4,256,128]{2,1,0:T(8,128)(2,1)}, bf16[4,256,64]{2,1,0:T(8,128)(2,1)S(1)}) custom-call(s32[1]{0:T(128)} %bitcast.1.slot_ref, bf16[256,512]{1,0:T(8,128)(2,1)S(1)} %collective-permute-done.points_ref, f32[1,512]{1,0:T(1,128)S(1)} %bitcast.73, bf16[4096,512]{1,0:T(8,128)(2,1)S(1)} %copy-done, ...), custom_call_target="tpu_custom_call" | custom-call | flops 1342177280 | bytes 2097152 | tf_op jit(solution)/shard_map/pallas_call | solution.py:153
  42.7 8.6 %all-to-all-start.1 = ((bf16[64,16,128]{2,1,0:T(8,128)(2,1)}), bf16[64,16,128]{2,1,0:T(8,128)(2,1)S(1)}, u32[]{:S(2)}, u32[]{:S(2)}) async-start(bf16[64,16,128]{2,1,0:T(8,128)(2,1)} %bitcast.9), calls=%async_computation.1 | async-start | bytes 524288 | tf_op jit(solution)/shard_map/all_to_all | solution.py:23
  51.6 0.5 reshape.74
  52.1 0.6 convolution_bitcast_fusion
  52.7 0.5 copy.26
  53.3 0.2 reshape.75
  53.5 7.7 %all-to-all-done.1.shares_ref = bf16[64,16,128]{2,1,0:T(8,128)(2,1)S(1)} async-done(((bf16[64,16,128]{2,1,0:T(8,128)(2,1)}), bf16[64,16,128]{2,1,0:T(8,128)(2,1)S(1)}, u32[]{:S(2)}, u32[]{:S(2)}) %all-to-all-start.1) | async-done | bytes 262176 | tf_op jit(solution)/shard_map/all_to_all | solution.py:23
  61.2 0.8 shard_map.118
  62.0 6.7 %all-to-all-start.2 = ((bf16[64,16,128]{2,1,0:T(8,128)(2,1)}), bf16[64,16,128]{2,1,0:T(8,128)(2,1)S(1)}, u32[]{:S(2)}, u32[]{:S(2)}) async-start(bf16[64,16,128]{2,1,0:T(8,128)(2,1)} %shard_map.118), calls=%async_computation.2 | async-start | bytes 524288 | tf_op jit(solution)/shard_map/all_to_all | solution.py:23
  68.9 0.4 collective-permute-start.3
  69.4 8.1 %collective-permute-done.3 = bf16[128,1024]{1,0:T(8,128)(2,1)S(1)} collective-permute-done((bf16[128,1024]{1,0:T(8,128)(2,1)S(1)}, bf16[128,1024]{1,0:T(8,128)(2,1)S(1)}, u32[]{:S(2)}, u32[]{:S(2)}) %collective-permute-start.3) | collective-permute-done | bytes 262176 | tf_op jit(solution)/shard_map/ppermute | solution.py:33
  77.5 1.2 all-to-all-done.2
  78.9 6.8 %all-gather = bf16[256,128]{1,0:T(8,128)(2,1)S(1)} all-gather(bf16[64,128]{1,0:T(8,128)(2,1)S(1)} %shard_map.119), channel_id=2, replica_groups=mesh['pts'=4,'ctr'=64] {'pts'}, dimensions={0}, use_global_device_ids=true | all-gather | bytes 81920 | tf_op jit(solution)/shard_map/all_gather | solution.py:383
  85.7 0.8 shard_map.120
  86.5 0.3 collective-permute-start.4
  86.8 9.5 %all-to-all-start.3 = ((bf16[64,16,128]{2,1,0:T(8,128)(2,1)}), bf16[64,16,128]{2,1,0:T(8,128)(2,1)S(1)}, u32[]{:S(2)}, u32[]{:S(2)}) async-start(bf16[64,16,128]{2,1,0:T(8,128)(2,1)} %shard_map.120), calls=%async_computation.3 | async-start | bytes 524288 | tf_op jit(solution)/shard_map/all_to_all | solution.py:23
  96.3 2.2 %fusion.5 = f32[128,4096]{1,0:T(8,128)S(1)} fusion(bf16[256,4096]{1,0:T(8,128)(2,1)} %get-tuple-element.58, bf16[4,256,128]{2,1,0:T(8,128)(2,1)S(1)} %bitcast.56, s32[]{:T(128)S(6)} %select_n.66), kind=kOutput, calls=%fused_computation.17 | convolution fusion | flops 268435456 | bytes 4259844 | tf_op jit(solution)/shard_map/dot_general | solution.py:402
  98.5 0.5 fusion.9
  99.0 1.1 copy-done.9
  100.1 0.5 convolution_add_fusion.1
  100.6 1.1 copy-done.11
  101.7 0.5 fusion
  102.3 0.8 pad_maximum_fusion
  103.2 0.9 constant_dynamic-slice_fusion.1
  104.1 3.9 %all-to-all-done.3 = bf16[64,16,128]{2,1,0:T(8,128)(2,1)S(1)} async-done(((bf16[64,16,128]{2,1,0:T(8,128)(2,1)}), bf16[64,16,128]{2,1,0:T(8,128)(2,1)S(1)}, u32[]{:S(2)}, u32[]{:S(2)}) %all-to-all-start.3) | async-done | bytes 262176 | tf_op jit(solution)/shard_map/all_to_all | solution.py:23
  108.0 1.0 shard_map.121
  109.0 4.9 %all-to-all-start.4 = ((bf16[32,16,128]{2,1,0:T(8,128)(2,1)}), bf16[32,16,128]{2,1,0:T(8,128)(2,1)S(1)}, u32[]{:S(2)}, u32[]{:S(2)}) async-start(bf16[32,16,128]{2,1,0:T(8,128)(2,1)} %get-tuple-element.61), calls=%async_computation.4 | async-start | bytes 262144 | tf_op jit(solution)/shard_map/all_to_all | solution.py:23
  113.8 1.3 maximum_add_fusion
  115.2 0.9 copy-done.7
  116.1 2.9 %collective-permute-start.6 = (bf16[32,4096]{1,0:T(8,128)(2,1)S(1)}, bf16[32,4096]{1,0:T(8,128)(2,1)S(1)}, u32[]{:S(2)}, u32[]{:S(2)}) collective-permute-start(bf16[32,4096]{1,0:T(8,128)(2,1)S(1)} %fusion.4), channel_id=1, source_target_pairs={{0,128},{64,192},{128,0},{192,64},{1,129},{65,193},{129,1},{193,65... | collective-permute-start | bytes 786440 | tf_op jit(solution)/shard_map/ppermute | solution.py:33
  119.0 5.2 %all-to-all-done.4 = bf16[32,16,128]{2,1,0:T(8,128)(2,1)S(1)} async-done(((bf16[32,16,128]{2,1,0:T(8,128)(2,1)}), bf16[32,16,128]{2,1,0:T(8,128)(2,1)S(1)}, u32[]{:S(2)}, u32[]{:S(2)}) %all-to-all-start.4) | async-done | bytes 131104 | tf_op jit(solution)/shard_map/all_to_all | solution.py:23
  124.2 0.4 shard_map.122
  124.7 13.0 %all_to_all.30 = bf16[32,16,128]{2,1,0:T(8,128)(2,1)S(1)} all-to-all(bf16[32,16,128]{2,1,0:T(8,128)(2,1)S(1)} %shard_map.122), channel_id=1, replica_groups={{0,1,2,3,4,5,6,7,8,9,10,11,12,13,14,15,16,17,18,19,20,21,22,23,24,25,26..., dimensions={0} | all-to-all | bytes 262144 | tf_op jit(solution)/shard_map/all_to_all | solution.py:23
  137.7 1.0 shard_map.123
  138.7 0.8 fusion.2
  (43 shorter events, 1.2 us)
Async XLA Ops:
  2.1 21.6 %all-to-all-start = ((bf16[16,16,512]{2,1,0:T(8,128)(2,1)}), bf16[16,16,512]{2,1,0:T(8,128)(2,1)S(1)}, u32[]{:S(2)}, u32[]{:S(2)}) async-start(bf16[16,16,512]{2,1,0:T(8,128)(2,1)} %broadcast_in_dim.45), calls=%async_computation | async-start | bytes 524288 | tf_op jit(solution)/shard_map/all_to_all | solution.py:23
  13.4 0.7 copy-start.4
  14.1 13.7 %copy-start.1 = (bf16[4096,128]{1,0:T(8,128)(2,1)S(1)}, bf16[4096,128]{1,0:T(8,128)(2,1)}, u32[]{:S(2)}) copy-start(bf16[4096,128]{1,0:T(8,128)(2,1)} %coef_ref.7) | copy-start | bytes 3145732
  14.1 13.7 %copy-start.5 = (f32[512]{0:T(512)S(1)}, f32[512]{0:T(512)}, u32[]{:S(2)}) copy-start(f32[512]{0:T(512)} %param.14) | copy-start | bytes 6148
  23.7 9.0 %collective-permute-start.2 = (bf16[256,512]{1,0:T(8,128)(2,1)S(1)}, bf16[256,512]{1,0:T(8,128)(2,1)S(1)}, u32[]{:S(2)}, u32[]{:S(2)}) collective-permute-start(bf16[256,512]{1,0:T(8,128)(2,1)S(1)} %bitcast.60), channel_id=1, source_target_pairs={{0,16},{1,17},{2,18},{3,19},{4,20},{5,21},{6,22},{7,23},{8,24},{9,... | collective-permute-start | bytes 786440 | tf_op jit(solution)/shard_map/ppermute | solution.py:33
  24.9 11.6 %collective-permute-start.1 = (bf16[256,512]{1,0:T(8,128)(2,1)S(1)}, bf16[256,512]{1,0:T(8,128)(2,1)S(1)}, u32[]{:S(2)}, u32[]{:S(2)}) collective-permute-start(bf16[256,512]{1,0:T(8,128)(2,1)S(1)} %bitcast.61), channel_id=1, source_target_pairs={{0,48},{1,49},{2,50},{3,51},{4,52},{5,53},{6,54},{7,55},{8,56},{9,... | collective-permute-start | bytes 786440 | tf_op jit(solution)/shard_map/ppermute | solution.py:33
  24.9 14.3 %collective-permute-start = (bf16[256,512]{1,0:T(8,128)(2,1)S(1)}, bf16[256,512]{1,0:T(8,128)(2,1)S(1)}, u32[]{:S(2)}, u32[]{:S(2)}) collective-permute-start(bf16[256,512]{1,0:T(8,128)(2,1)S(1)} %bitcast.62), channel_id=1, source_target_pairs={{0,32},{1,33},{2,34},{3,35},{4,36},{5,37},{6,38},{7,39},{8,40},{9,... | collective-permute-start | bytes 786440 | tf_op jit(solution)/shard_map/ppermute | solution.py:33
  27.8 4.9 %copy-start = (bf16[4096,512]{1,0:T(8,128)(2,1)S(1)}, bf16[4096,512]{1,0:T(8,128)(2,1)}, u32[]{:S(2)}) copy-start(bf16[4096,512]{1,0:T(8,128)(2,1)} %get-tuple-element.35.centers_ref) | copy-start | bytes 12582916
  39.3 12.1 %copy-start.12 = (f32[8]{0:T(128)S(1)}, f32[8]{0:T(128)}, u32[]{:S(2)}) copy-start(f32[8]{0:T(128)} %param.13) | copy-start | bytes 100
  39.3 12.1 %copy-start.13 = (s32[16]{0:T(128)S(1)}, s32[16]{0:T(128)}, u32[]{:S(2)}) copy-start(s32[16]{0:T(128)} %param.11) | copy-start | bytes 196
  39.3 12.2 %copy-start.2 = (f32[64,2048]{1,0:T(8,128)S(1)}, f32[64,2048]{1,0:T(8,128)}, u32[]{:S(2)}) copy-start(f32[64,2048]{1,0:T(8,128)} %matrix_ref.2) | copy-start | bytes 1572868
  42.7 18.5 %all-to-all-start.1 = ((bf16[64,16,128]{2,1,0:T(8,128)(2,1)}), bf16[64,16,128]{2,1,0:T(8,128)(2,1)S(1)}, u32[]{:S(2)}, u32[]{:S(2)}) async-start(bf16[64,16,128]{2,1,0:T(8,128)(2,1)} %bitcast.9), calls=%async_computation.1 | async-start | bytes 524288 | tf_op jit(solution)/shard_map/all_to_all | solution.py:23
  51.5 9.7 %copy-start.6 = (f32[16,128]{1,0:T(8,128)S(1)}, f32[16,128]{1,0:T(8,128)}, u32[]{:S(2)}) copy-start(f32[16,128]{1,0:T(8,128)} %targets_ref.1) | copy-start | bytes 24580
  62.0 16.6 %all-to-all-start.2 = ((bf16[64,16,128]{2,1,0:T(8,128)(2,1)}), bf16[64,16,128]{2,1,0:T(8,128)(2,1)S(1)}, u32[]{:S(2)}, u32[]{:S(2)}) async-start(bf16[64,16,128]{2,1,0:T(8,128)(2,1)} %shard_map.118), calls=%async_computation.2 | async-start | bytes 524288 | tf_op jit(solution)/shard_map/all_to_all | solution.py:23
  68.9 8.6 %collective-permute-start.3 = (bf16[128,1024]{1,0:T(8,128)(2,1)S(1)}, bf16[128,1024]{1,0:T(8,128)(2,1)S(1)}, u32[]{:S(2)}, u32[]{:S(2)}) collective-permute-start(bf16[128,1024]{1,0:T(8,128)(2,1)S(1)} %copy.27), channel_id=1, source_target_pairs={{0,32},{1,33},{2,34},{3,35},{4,36},{5,37},{6,38},{7,39},{8,40},{9,... | collective-permute-start | bytes 786440 | tf_op jit(solution)/shard_map/ppermute | solution.py:33
  86.5 9.8 %collective-permute-start.4 = (bf16[128,1024]{1,0:T(8,128)(2,1)S(1)}, bf16[128,1024]{1,0:T(8,128)(2,1)S(1)}, u32[]{:S(2)}, u32[]{:S(2)}) collective-permute-start(bf16[128,1024]{1,0:T(8,128)(2,1)S(1)} %collective-permute-done.3), channel_id=1, source_target_pairs={{0,64},{64,0},{128,192},{192,128},{1,65},{65,1},{129,193},{193,129... | collective-permute-start | bytes 786440 | tf_op jit(solution)/shard_map/ppermute | solution.py:33
  86.8 21.2 %all-to-all-start.3 = ((bf16[64,16,128]{2,1,0:T(8,128)(2,1)}), bf16[64,16,128]{2,1,0:T(8,128)(2,1)S(1)}, u32[]{:S(2)}, u32[]{:S(2)}) async-start(bf16[64,16,128]{2,1,0:T(8,128)(2,1)} %shard_map.120), calls=%async_computation.3 | async-start | bytes 524288 | tf_op jit(solution)/shard_map/all_to_all | solution.py:23
  96.3 2.2 %copy-start.10 = (bf16[256,4096]{1,0:T(8,128)(2,1)S(1)}, bf16[256,4096]{1,0:T(8,128)(2,1)}, u32[]{:S(2)}) copy-start(bf16[256,4096]{1,0:T(8,128)(2,1)} %get-tuple-element.55) | copy-start | bytes 6291460
  98.5 1.6 %copy-start.9 = (bf16[256,4096]{1,0:T(8,128)(2,1)S(1)}, bf16[256,4096]{1,0:T(8,128)(2,1)}, u32[]{:S(2)}) copy-start(bf16[256,4096]{1,0:T(8,128)(2,1)} %get-tuple-element.56) | copy-start | bytes 6291460
  100.1 1.6 %copy-start.11 = (bf16[256,4096]{1,0:T(8,128)(2,1)S(1)}, bf16[256,4096]{1,0:T(8,128)(2,1)}, u32[]{:S(2)}) copy-start(bf16[256,4096]{1,0:T(8,128)(2,1)} %get-tuple-element.57) | copy-start | bytes 6291460
  103.2 10.7 %collective-permute-start.5 = (bf16[2,32,4096]{2,1,0:T(8,128)(2,1)}, bf16[2,32,4096]{2,1,0:T(8,128)(2,1)}, u32[]{:S(2)}, u32[]{:S(2)}) collective-permute-start(bf16[2,32,4096]{2,1,0:T(8,128)(2,1)} %pad_maximum_fusion), channel_id=1, source_target_pairs={{0,64},{64,0},{128,192},{192,128},{1,65},{65,1},{129,193},{193,129... | collective-permute-start | bytes 1572872 | tf_op jit(solution)/shard_map/ppermute | solution.py:33
  108.0 16.2 %copy-start.3 = (f32[64,4096]{1,0:T(8,128)S(1)}, f32[64,4096]{1,0:T(8,128)}, u32[]{:S(2)}) copy-start(f32[64,4096]{1,0:T(8,128)} %matrix_ref.1) | copy-start | bytes 3145732
  109.0 15.2 %all-to-all-start.4 = ((bf16[32,16,128]{2,1,0:T(8,128)(2,1)}), bf16[32,16,128]{2,1,0:T(8,128)(2,1)S(1)}, u32[]{:S(2)}, u32[]{:S(2)}) async-start(bf16[32,16,128]{2,1,0:T(8,128)(2,1)} %get-tuple-element.61), calls=%async_computation.4 | async-start | bytes 262144 | tf_op jit(solution)/shard_map/all_to_all | solution.py:23
  115.1 1.0 copy-start.7
  116.1 22.6 %collective-permute-start.6 = (bf16[32,4096]{1,0:T(8,128)(2,1)S(1)}, bf16[32,4096]{1,0:T(8,128)(2,1)S(1)}, u32[]{:S(2)}, u32[]{:S(2)}) collective-permute-start(bf16[32,4096]{1,0:T(8,128)(2,1)S(1)} %fusion.4), channel_id=1, source_target_pairs={{0,128},{64,192},{128,0},{192,64},{1,129},{65,193},{129,1},{193,65... | collective-permute-start | bytes 786440 | tf_op jit(solution)/shard_map/ppermute | solution.py:33
  124.2 14.5 %copy-start.8 = (f32[2,32,4096]{2,1,0:T(8,128)S(1)}, f32[2,32,4096]{2,1,0:T(8,128)}, u32[]{:S(2)}) copy-start(f32[2,32,4096]{2,1,0:T(8,128)} %copy-done.7) | copy-start | bytes 3145732

commit v12 on v10

--- a/solution.py
+++ b/solution.py
@@ -343,7 +343,7 @@
         chunks[k] = swapped(plane_rows, "ctr", k * plane_size)
     held = ()
     kernels = [None] * PLANES
-    for k in (0, 1, 3, 2):
+    for k in (0, 1, 2, 3):
         slot = (plane ^ k).astype(jnp.int32).reshape(1)
         kernels[k], *held = kernel_and_value(
             slot, chunks[k], scale, scaled_centers, center_norm, coefficients, chosen, extra, *held

time: 140 us -> 138 us (0.986)
  no operation moved by 1% of the time
where the time goes in v12:
time: 138 us
  starting transfers between devices  44.7 us (32%)
  waiting for transfers between devices  32.4 us (23%)
  Pallas kernels  22.7 us (16%)
  blocking collectives  19.8 us (14%)
  local copies, waits for them, and re-layouts  7.98 us (6%)
  other arithmetic  4.69 us (3%)
  matrix products  4.36 us (3%)
    all_to_all x5, starting transfers between devices, exchanged(): lax.all_to_all(pieces, axis, 0, 0, tiled=True, axis_index_groups=groups i...  36.6 us
    all_to_all x5, waiting for transfers between devices, exchanged(): lax.all_to_all(pieces, axis, 0, 0, tiled=True, axis_index_groups=groups i...  30.3 us
    pallas_call x4, Pallas kernels, kernel_and_value(): pl.pallas_call(functools.partial(kernel_block, bool(held)), out_shape=(pl...  13.8 us
    all_to_all x1, blocking collectives, exchanged(): lax.all_to_all(pieces, axis, 0, 0, tiled=True, axis_index_groups=groups i...  13 us
    ppermute x6, starting transfers between devices, swapped(): lax.ppermute(x, axis, [(i, i ^ bits) for i in range(lax.axis_size(axis))])  8.03 us
    all_gather x1, blocking collectives, body(): parts = lax.all_gather(window, 'pts')  6.75 us
    pallas_call x1, Pallas kernels, scaled_and_norm(): pl.pallas_call(scale_step, out_shape=(pltpu.HBM((total, depth), BF), jax....  4.61 us
    unnamed x28, local copies, waits for them, and re-layouts  3.87 us
  transfers between devices with their start and end apart: 11, of which 8 were waited for; matrix products, arithmetic and copies ran while one was open for 8% of the time, Pallas kernels for 13%

profile of v12, /device:TPU:4, one launch (start us, length us, event | category | flops | bytes accessed | tf_op | source)
XLA Modules:
  0.0 137.5 jit_solution(10286307002011254834)
XLA Ops:
  0.6 1.4 %broadcast_in_dim.45 = bf16[16,16,512]{2,1,0:T(8,128)(2,1)} broadcast(bf16[16,512]{1,0:T(8,128)(2,1)} %param.10), dimensions={1,2} | broadcast | bytes 278528 | tf_op jit(solution)/shard_map/broadcast_in_dim | solution.py:29
  2.1 9.6 %all-to-all-start = ((bf16[16,16,512]{2,1,0:T(8,128)(2,1)}), bf16[16,16,512]{2,1,0:T(8,128)(2,1)S(1)}, u32[]{:S(2)}, u32[]{:S(2)}) async-start(bf16[16,16,512]{2,1,0:T(8,128)(2,1)} %broadcast_in_dim.45), calls=%async_computation | async-start | bytes 524288 | tf_op jit(solution)/shard_map/all_to_all | solution.py:23
  11.7 0.7 broadcast_subtract_fusion
  12.5 0.7 broadcast_compare_fusion
  13.4 0.7 copy-done.4
  14.1 4.6 %shard_map.113 = (bf16[4096,512]{1,0:T(8,128)(2,1)}, f32[1,4096]{1,0:T(1,128)S(1)}, bf16[64,512]{1,0:T(8,128)(2,1)S(1)}, f32[1,64]{1,0:T(1,128)S(1)}) custom-call(bf16[4096,512]{1,0:T(8,128)(2,1)} %centers_ref.1, f32[1,512]{1,0:T(1,128)S(1)} %bitcast.69, s32[64,1]{1,0:T(8,128)S(1)} %copy.23.local_ref), custom_call_target="tpu_custom_call" | custom-call | flops 8388608 | bytes 4194304 | tf_op jit(solution)/shard_map/pallas_call | solution.py:75
  18.7 5.0 %all-to-all-done = bf16[16,16,512]{2,1,0:T(8,128)(2,1)S(1)} async-done(((bf16[16,16,512]{2,1,0:T(8,128)(2,1)}), bf16[16,16,512]{2,1,0:T(8,128)(2,1)S(1)}, u32[]{:S(2)}, u32[]{:S(2)}) %all-to-all-start) | async-done | bytes 262176 | tf_op jit(solution)/shard_map/all_to_all | solution.py:23
  23.7 1.2 collective-permute-start.2
  24.9 0.8 collective-permute-start.1
  25.7 1.5 %collective-permute-start = (bf16[256,512]{1,0:T(8,128)(2,1)S(1)}, bf16[256,512]{1,0:T(8,128)(2,1)S(1)}, u32[]{:S(2)}, u32[]{:S(2)}) collective-permute-start(bf16[256,512]{1,0:T(8,128)(2,1)S(1)} %bitcast.62), channel_id=1, source_target_pairs={{0,48},{1,49},{2,50},{3,51},{4,52},{5,53},{6,54},{7,55},{8,56},{9,... | collective-permute-start | bytes 786440 | tf_op jit(solution)/shard_map/ppermute | solution.py:33
  27.2 4.8 %shard_map.114 = (bf16[256,4096]{1,0:T(8,128)(2,1)}, bf16[4,256,128]{2,1,0:T(8,128)(2,1)S(1)}, bf16[4,256,64]{2,1,0:T(8,128)(2,1)S(1)}) custom-call(s32[1]{0:T(128)} %bitcast.7.slot_ref, bf16[256,512]{1,0:T(8,128)(2,1)S(1)} %bitcast.63, f32[1,512]{1,0:T(1,128)S(1)} %bitcast.70, bf16[4096,512]{1,0:T(8,128)(2,1)} %get-tuple-element.31.centers_ref, ...), custom_call_target="tpu_custom_call" | custom-call | flops 1342177280 | bytes 2097152 | tf_op jit(solution)/shard_map/pallas_call | solution.py:153
  32.0 0.7 collective-permute-done.2.points_ref
  32.7 2.8 %shard_map.115 = (bf16[256,4096]{1,0:T(8,128)(2,1)}, bf16[4,256,128]{2,1,0:T(8,128)(2,1)S(1)}, bf16[4,256,64]{2,1,0:T(8,128)(2,1)S(1)}) custom-call(s32[1]{0:T(128)} %bitcast.6.slot_ref, bf16[256,512]{1,0:T(8,128)(2,1)S(1)} %collective-permute-done.2.points_ref, f32[1,512]{1,0:T(1,128)S(1)} %bitcast.71, bf16[4096,512]{1,0:T(8,128)(2,1)S(1)} %copy-done, ...), custom_call_target="tpu_custom_call" | custom-call | flops 1342177280 | bytes 2097152 | tf_op jit(solution)/shard_map/pallas_call | solution.py:153
  35.6 2.7 %shard_map.116 = (bf16[256,4096]{1,0:T(8,128)(2,1)}, bf16[4,256,128]{2,1,0:T(8,128)(2,1)S(1)}, bf16[4,256,64]{2,1,0:T(8,128)(2,1)S(1)}) custom-call(s32[1]{0:T(128)} %bitcast.5.slot_ref, bf16[256,512]{1,0:T(8,128)(2,1)S(1)} %collective-permute-done.1.points_ref, f32[1,512]{1,0:T(1,128)S(1)} %bitcast.72, bf16[4096,512]{1,0:T(8,128)(2,1)S(1)} %copy-done, ...), custom_call_target="tpu_custom_call" | custom-call | flops 1342177280 | bytes 2097152 | tf_op jit(solution)/shard_map/pallas_call | solution.py:153
  38.4 3.4 %shard_map.117 = (bf16[256,4096]{1,0:T(8,128)(2,1)}, bf16[4,256,128]{2,1,0:T(8,128)(2,1)}, bf16[4,256,64]{2,1,0:T(8,128)(2,1)S(1)}) custom-call(s32[1]{0:T(128)} %bitcast.1.slot_ref, bf16[256,512]{1,0:T(8,128)(2,1)S(1)} %collective-permute-done.points_ref, f32[1,512]{1,0:T(1,128)S(1)} %bitcast.73, bf16[4096,512]{1,0:T(8,128)(2,1)S(1)} %copy-done, ...), custom_call_target="tpu_custom_call" | custom-call | flops 1342177280 | bytes 2097152 | tf_op jit(solution)/shard_map/pallas_call | solution.py:153
  41.8 8.0 %all-to-all-start.1 = ((bf16[64,16,128]{2,1,0:T(8,128)(2,1)}), bf16[64,16,128]{2,1,0:T(8,128)(2,1)S(1)}, u32[]{:S(2)}, u32[]{:S(2)}) async-start(bf16[64,16,128]{2,1,0:T(8,128)(2,1)} %bitcast.9), calls=%async_computation.1 | async-start | bytes 524288 | tf_op jit(solution)/shard_map/all_to_all | solution.py:23
  50.1 9.8 %all-to-all-done.1.shares_ref = bf16[64,16,128]{2,1,0:T(8,128)(2,1)S(1)} async-done(((bf16[64,16,128]{2,1,0:T(8,128)(2,1)}), bf16[64,16,128]{2,1,0:T(8,128)(2,1)S(1)}, u32[]{:S(2)}, u32[]{:S(2)}) %all-to-all-start.1) | async-done | bytes 262176 | tf_op jit(solution)/shard_map/all_to_all | solution.py:23
  59.8 0.8 shard_map.118
  60.6 6.7 %all-to-all-start.2 = ((bf16[64,16,128]{2,1,0:T(8,128)(2,1)}), bf16[64,16,128]{2,1,0:T(8,128)(2,1)S(1)}, u32[]{:S(2)}, u32[]{:S(2)}) async-start(bf16[64,16,128]{2,1,0:T(8,128)(2,1)} %shard_map.118), calls=%async_computation.2 | async-start | bytes 524288 | tf_op jit(solution)/shard_map/all_to_all | solution.py:23
  67.4 0.5 reshape.75
  67.9 0.6 convolution_bitcast_fusion
  68.6 0.5 copy.26
  69.1 0.2 reshape.76
  69.4 7.9 %all-to-all-done.2 = bf16[64,16,128]{2,1,0:T(8,128)(2,1)S(1)} async-done(((bf16[64,16,128]{2,1,0:T(8,128)(2,1)}), bf16[64,16,128]{2,1,0:T(8,128)(2,1)S(1)}, u32[]{:S(2)}, u32[]{:S(2)}) %all-to-all-start.2) | async-done | bytes 262176 | tf_op jit(solution)/shard_map/all_to_all | solution.py:23
  77.5 6.8 %all-gather = bf16[256,128]{1,0:T(8,128)(2,1)S(1)} all-gather(bf16[64,128]{1,0:T(8,128)(2,1)S(1)} %shard_map.119), channel_id=2, replica_groups=mesh['pts'=4,'ctr'=64] {'pts'}, dimensions={0}, use_global_device_ids=true | all-gather | bytes 81920 | tf_op jit(solution)/shard_map/all_gather | solution.py:380
  84.3 0.8 shard_map.120
  85.2 1.6 %collective-permute-start.3 = (bf16[128,1024]{1,0:T(8,128)(2,1)S(1)}, bf16[128,1024]{1,0:T(8,128)(2,1)S(1)}, u32[]{:S(2)}, u32[]{:S(2)}) collective-permute-start(bf16[128,1024]{1,0:T(8,128)(2,1)S(1)} %copy.27), channel_id=1, source_target_pairs={{0,32},{1,33},{2,34},{3,35},{4,36},{5,37},{6,38},{7,39},{8,40},{9,... | collective-permute-start | bytes 786440 | tf_op jit(solution)/shard_map/ppermute | solution.py:33
  86.9 7.3 %all-to-all-start.3 = ((bf16[64,16,128]{2,1,0:T(8,128)(2,1)}), bf16[64,16,128]{2,1,0:T(8,128)(2,1)S(1)}, u32[]{:S(2)}, u32[]{:S(2)}) async-start(bf16[64,16,128]{2,1,0:T(8,128)(2,1)} %shard_map.120), calls=%async_computation.3 | async-start | bytes 524288 | tf_op jit(solution)/shard_map/all_to_all | solution.py:23
  94.2 1.3 collective-permute-done.3
  95.5 2.2 %fusion.9 = f32[128,4096]{1,0:T(8,128)S(1)} fusion(bf16[256,4096]{1,0:T(8,128)(2,1)} %get-tuple-element.47, bf16[4,256,128]{2,1,0:T(8,128)(2,1)S(1)} %bitcast.56, s32[]{:T(128)S(6)} %select_n.63), kind=kOutput, calls=%fused_computation.21 | convolution fusion | flops 268435456 | bytes 4259844 | tf_op jit(solution)/shard_map/dot_general | solution.py:399
  97.7 0.5 fusion.5
  98.2 1.1 copy-done.9
  99.3 0.5 convolution_add_fusion.1
  99.8 1.1 copy-done.11
  100.9 0.5 fusion
  101.5 0.8 pad_maximum_fusion
  102.5 0.9 constant_dynamic-slice_fusion.1
  103.3 2.4 %all-to-all-done.3 = bf16[64,16,128]{2,1,0:T(8,128)(2,1)S(1)} async-done(((bf16[64,16,128]{2,1,0:T(8,128)(2,1)}), bf16[64,16,128]{2,1,0:T(8,128)(2,1)S(1)}, u32[]{:S(2)}, u32[]{:S(2)}) %all-to-all-start.3) | async-done | bytes 262176 | tf_op jit(solution)/shard_map/all_to_all | solution.py:23
  105.8 1.0 shard_map.121
  106.8 5.0 %all-to-all-start.4 = ((bf16[32,16,128]{2,1,0:T(8,128)(2,1)}), bf16[32,16,128]{2,1,0:T(8,128)(2,1)S(1)}, u32[]{:S(2)}, u32[]{:S(2)}) async-start(bf16[32,16,128]{2,1,0:T(8,128)(2,1)} %get-tuple-element.53), calls=%async_computation.4 | async-start | bytes 262144 | tf_op jit(solution)/shard_map/all_to_all | solution.py:23
  111.8 1.3 maximum_add_fusion
  113.1 0.9 copy-done.7
  114.0 2.9 %collective-permute-start.5 = (bf16[32,4096]{1,0:T(8,128)(2,1)S(1)}, bf16[32,4096]{1,0:T(8,128)(2,1)S(1)}, u32[]{:S(2)}, u32[]{:S(2)}) collective-permute-start(bf16[32,4096]{1,0:T(8,128)(2,1)S(1)} %fusion.4), channel_id=1, source_target_pairs={{0,128},{64,192},{128,0},{192,64},{1,129},{65,193},{129,1},{193,65... | collective-permute-start | bytes 786440 | tf_op jit(solution)/shard_map/ppermute | solution.py:33
  116.9 5.2 %all-to-all-done.4 = bf16[32,16,128]{2,1,0:T(8,128)(2,1)S(1)} async-done(((bf16[32,16,128]{2,1,0:T(8,128)(2,1)}), bf16[32,16,128]{2,1,0:T(8,128)(2,1)S(1)}, u32[]{:S(2)}, u32[]{:S(2)}) %all-to-all-start.4) | async-done | bytes 131104 | tf_op jit(solution)/shard_map/all_to_all | solution.py:23
  122.1 0.4 shard_map.122
  122.6 13.0 %all_to_all.30 = bf16[32,16,128]{2,1,0:T(8,128)(2,1)S(1)} all-to-all(bf16[32,16,128]{2,1,0:T(8,128)(2,1)S(1)} %shard_map.122), channel_id=1, replica_groups={{0,1,2,3,4,5,6,7,8,9,10,11,12,13,14,15,16,17,18,19,20,21,22,23,24,25,26..., dimensions={0} | all-to-all | bytes 262144 | tf_op jit(solution)/shard_map/all_to_all | solution.py:23
  135.6 1.0 shard_map.123
  136.7 0.8 fusion.2
  (41 shorter events, 1.2 us)
Async XLA Ops:
  2.1 21.6 %all-to-all-start = ((bf16[16,16,512]{2,1,0:T(8,128)(2,1)}), bf16[16,16,512]{2,1,0:T(8,128)(2,1)S(1)}, u32[]{:S(2)}, u32[]{:S(2)}) async-start(bf16[16,16,512]{2,1,0:T(8,128)(2,1)} %broadcast_in_dim.45), calls=%async_computation | async-start | bytes 524288 | tf_op jit(solution)/shard_map/all_to_all | solution.py:23
  13.4 0.7 copy-start.4
  14.1 13.1 %copy-start.1 = (bf16[4096,128]{1,0:T(8,128)(2,1)S(1)}, bf16[4096,128]{1,0:T(8,128)(2,1)}, u32[]{:S(2)}) copy-start(bf16[4096,128]{1,0:T(8,128)(2,1)} %coef_ref.7) | copy-start | bytes 3145732
  14.1 13.1 %copy-start.5 = (f32[512]{0:T(512)S(1)}, f32[512]{0:T(512)}, u32[]{:S(2)}) copy-start(f32[512]{0:T(512)} %param.14) | copy-start | bytes 6148
  23.7 9.0 %collective-permute-start.2 = (bf16[256,512]{1,0:T(8,128)(2,1)S(1)}, bf16[256,512]{1,0:T(8,128)(2,1)S(1)}, u32[]{:S(2)}, u32[]{:S(2)}) collective-permute-start(bf16[256,512]{1,0:T(8,128)(2,1)S(1)} %bitcast.60), channel_id=1, source_target_pairs={{0,16},{1,17},{2,18},{3,19},{4,20},{5,21},{6,22},{7,23},{8,24},{9,... | collective-permute-start | bytes 786440 | tf_op jit(solution)/shard_map/ppermute | solution.py:33
  24.9 10.7 %collective-permute-start.1 = (bf16[256,512]{1,0:T(8,128)(2,1)S(1)}, bf16[256,512]{1,0:T(8,128)(2,1)S(1)}, u32[]{:S(2)}, u32[]{:S(2)}) collective-permute-start(bf16[256,512]{1,0:T(8,128)(2,1)S(1)} %bitcast.61), channel_id=1, source_target_pairs={{0,32},{1,33},{2,34},{3,35},{4,36},{5,37},{6,38},{7,39},{8,40},{9,... | collective-permute-start | bytes 786440 | tf_op jit(solution)/shard_map/ppermute | solution.py:33
  25.7 12.6 %collective-permute-start = (bf16[256,512]{1,0:T(8,128)(2,1)S(1)}, bf16[256,512]{1,0:T(8,128)(2,1)S(1)}, u32[]{:S(2)}, u32[]{:S(2)}) collective-permute-start(bf16[256,512]{1,0:T(8,128)(2,1)S(1)} %bitcast.62), channel_id=1, source_target_pairs={{0,48},{1,49},{2,50},{3,51},{4,52},{5,53},{6,54},{7,55},{8,56},{9,... | collective-permute-start | bytes 786440 | tf_op jit(solution)/shard_map/ppermute | solution.py:33
  27.2 5.5 %copy-start = (bf16[4096,512]{1,0:T(8,128)(2,1)S(1)}, bf16[4096,512]{1,0:T(8,128)(2,1)}, u32[]{:S(2)}) copy-start(bf16[4096,512]{1,0:T(8,128)(2,1)} %get-tuple-element.31.centers_ref) | copy-start | bytes 12582916
  38.3 11.5 %copy-start.12 = (f32[8]{0:T(128)S(1)}, f32[8]{0:T(128)}, u32[]{:S(2)}) copy-start(f32[8]{0:T(128)} %param.13) | copy-start | bytes 100
  38.3 11.5 %copy-start.13 = (s32[16]{0:T(128)S(1)}, s32[16]{0:T(128)}, u32[]{:S(2)}) copy-start(s32[16]{0:T(128)} %param.11) | copy-start | bytes 196
  38.4 21.5 %copy-start.6 = (f32[16,128]{1,0:T(8,128)S(1)}, f32[16,128]{1,0:T(8,128)}, u32[]{:S(2)}) copy-start(f32[16,128]{1,0:T(8,128)} %targets_ref.1) | copy-start | bytes 24580
  38.4 29.0 %copy-start.2 = (f32[64,2048]{1,0:T(8,128)S(1)}, f32[64,2048]{1,0:T(8,128)}, u32[]{:S(2)}) copy-start(f32[64,2048]{1,0:T(8,128)} %matrix_ref.2) | copy-start | bytes 1572868
  41.8 18.0 %all-to-all-start.1 = ((bf16[64,16,128]{2,1,0:T(8,128)(2,1)}), bf16[64,16,128]{2,1,0:T(8,128)(2,1)S(1)}, u32[]{:S(2)}, u32[]{:S(2)}) async-start(bf16[64,16,128]{2,1,0:T(8,128)(2,1)} %bitcast.9), calls=%async_computation.1 | async-start | bytes 524288 | tf_op jit(solution)/shard_map/all_to_all | solution.py:23
  60.6 16.6 %all-to-all-start.2 = ((bf16[64,16,128]{2,1,0:T(8,128)(2,1)}), bf16[64,16,128]{2,1,0:T(8,128)(2,1)S(1)}, u32[]{:S(2)}, u32[]{:S(2)}) async-start(bf16[64,16,128]{2,1,0:T(8,128)(2,1)} %shard_map.118), calls=%async_computation.2 | async-start | bytes 524288 | tf_op jit(solution)/shard_map/all_to_all | solution.py:23
  85.2 10.3 %collective-permute-start.3 = (bf16[128,1024]{1,0:T(8,128)(2,1)S(1)}, bf16[128,1024]{1,0:T(8,128)(2,1)S(1)}, u32[]{:S(2)}, u32[]{:S(2)}) collective-permute-start(bf16[128,1024]{1,0:T(8,128)(2,1)S(1)} %copy.27), channel_id=1, source_target_pairs={{0,32},{1,33},{2,34},{3,35},{4,36},{5,37},{6,38},{7,39},{8,40},{9,... | collective-permute-start | bytes 786440 | tf_op jit(solution)/shard_map/ppermute | solution.py:33
  86.9 18.9 %all-to-all-start.3 = ((bf16[64,16,128]{2,1,0:T(8,128)(2,1)}), bf16[64,16,128]{2,1,0:T(8,128)(2,1)S(1)}, u32[]{:S(2)}, u32[]{:S(2)}) async-start(bf16[64,16,128]{2,1,0:T(8,128)(2,1)} %shard_map.120), calls=%async_computation.3 | async-start | bytes 524288 | tf_op jit(solution)/shard_map/all_to_all | solution.py:23
  95.5 2.2 %copy-start.10 = (bf16[256,4096]{1,0:T(8,128)(2,1)S(1)}, bf16[256,4096]{1,0:T(8,128)(2,1)}, u32[]{:S(2)}) copy-start(bf16[256,4096]{1,0:T(8,128)(2,1)} %get-tuple-element.50) | copy-start | bytes 6291460
  97.7 1.6 %copy-start.9 = (bf16[256,4096]{1,0:T(8,128)(2,1)S(1)}, bf16[256,4096]{1,0:T(8,128)(2,1)}, u32[]{:S(2)}) copy-start(bf16[256,4096]{1,0:T(8,128)(2,1)} %get-tuple-element.48) | copy-start | bytes 6291460
  99.3 1.6 %copy-start.11 = (bf16[256,4096]{1,0:T(8,128)(2,1)S(1)}, bf16[256,4096]{1,0:T(8,128)(2,1)}, u32[]{:S(2)}) copy-start(bf16[256,4096]{1,0:T(8,128)(2,1)} %get-tuple-element.49) | copy-start | bytes 6291460
  102.4 9.4 %collective-permute-start.4 = (bf16[2,32,4096]{2,1,0:T(8,128)(2,1)}, bf16[2,32,4096]{2,1,0:T(8,128)(2,1)}, u32[]{:S(2)}, u32[]{:S(2)}) collective-permute-start(bf16[2,32,4096]{2,1,0:T(8,128)(2,1)} %pad_maximum_fusion), channel_id=1, source_target_pairs={{0,64},{64,0},{128,192},{192,128},{1,65},{65,1},{129,193},{193,129... | collective-permute-start | bytes 1572872 | tf_op jit(solution)/shard_map/ppermute | solution.py:33
  105.8 16.4 %copy-start.3 = (f32[64,4096]{1,0:T(8,128)S(1)}, f32[64,4096]{1,0:T(8,128)}, u32[]{:S(2)}) copy-start(f32[64,4096]{1,0:T(8,128)} %matrix_ref.1) | copy-start | bytes 3145732
  106.8 15.4 %all-to-all-start.4 = ((bf16[32,16,128]{2,1,0:T(8,128)(2,1)}), bf16[32,16,128]{2,1,0:T(8,128)(2,1)S(1)}, u32[]{:S(2)}, u32[]{:S(2)}) async-start(bf16[32,16,128]{2,1,0:T(8,128)(2,1)} %get-tuple-element.53), calls=%async_computation.4 | async-start | bytes 262144 | tf_op jit(solution)/shard_map/all_to_all | solution.py:23
  113.1 1.0 copy-start.7
  114.0 22.6 %collective-permute-start.5 = (bf16[32,4096]{1,0:T(8,128)(2,1)S(1)}, bf16[32,4096]{1,0:T(8,128)(2,1)S(1)}, u32[]{:S(2)}, u32[]{:S(2)}) collective-permute-start(bf16[32,4096]{1,0:T(8,128)(2,1)S(1)} %fusion.4), channel_id=1, source_target_pairs={{0,128},{64,192},{128,0},{192,64},{1,129},{65,193},{129,1},{193,65... | collective-permute-start | bytes 786440 | tf_op jit(solution)/shard_map/ppermute | solution.py:33
  122.1 14.5 %copy-start.8 = (f32[2,32,4096]{2,1,0:T(8,128)S(1)}, f32[2,32,4096]{2,1,0:T(8,128)}, u32[]{:S(2)}) copy-start(f32[2,32,4096]{2,1,0:T(8,128)} %copy-done.7) | copy-start | bytes 3145732

commit v13 on v12

--- a/solution.py
+++ b/solution.py
@@ -343,7 +343,7 @@
         chunks[k] = swapped(plane_rows, "ctr", k * plane_size)
     held = ()
     kernels = [None] * PLANES
-    for k in (0, 1, 2, 3):
+    for k in (0, 2, 1, 3):
         slot = (plane ^ k).astype(jnp.int32).reshape(1)
         kernels[k], *held = kernel_and_value(
             slot, chunks[k], scale, scaled_centers, center_norm, coefficients, chosen, extra, *held

time: 138 us -> 139 us (level)
  transfers between devices with their start and end apart: 11 -> 11, of which waited for: 8 -> 7; matrix products, arithmetic and copies ran while one was open for 8% -> 8% of each run, Pallas kernels for 13% -> 13%
where the time goes in v13:
time: 139 us; the launch traced here: 138 us
  starting transfers between devices  44.3 us (32%)
  waiting for transfers between devices  33.3 us (24%)
  Pallas kernels  22.7 us (16%)
  blocking collectives  19.8 us (14%)
  local copies, waits for them, and re-layouts  7.99 us (6%)
  other arithmetic  4.69 us (3%)
  matrix products  4.35 us (3%)
    all_to_all x5, starting transfers between devices, exchanged(): lax.all_to_all(pieces, axis, 0, 0, tiled=True, axis_index_groups=groups i...  35.8 us
    all_to_all x5, waiting for transfers between devices, exchanged(): lax.all_to_all(pieces, axis, 0, 0, tiled=True, axis_index_groups=groups i...  30.4 us
    pallas_call x4, Pallas kernels, kernel_and_value(): pl.pallas_call(functools.partial(kernel_block, bool(held)), out_shape=(pl...  13.8 us
    all_to_all x1, blocking collectives, exchanged(): lax.all_to_all(pieces, axis, 0, 0, tiled=True, axis_index_groups=groups i...  13 us
    ppermute x6, starting transfers between devices, swapped(): lax.ppermute(x, axis, [(i, i ^ bits) for i in range(lax.axis_size(axis))])  8.51 us
    all_gather x1, blocking collectives, body(): parts = lax.all_gather(window, 'pts')  6.75 us
    pallas_call x1, Pallas kernels, scaled_and_norm(): pl.pallas_call(scale_step, out_shape=(pltpu.HBM((total, depth), BF), jax....  4.61 us
    unnamed x28, local copies, waits for them, and re-layouts  3.87 us
  transfers between devices with their start and end apart: 11, of which 7 were waited for; matrix products, arithmetic and copies ran while one was open for 8% of the time, Pallas kernels for 13%

profile of v13, /device:TPU:4, one launch (start us, length us, event | category | flops | bytes accessed | tf_op | source)
XLA Modules:
  0.0 138.0 jit_solution(5000663050755693928)
XLA Ops:
  0.6 1.4 %broadcast_in_dim.45 = bf16[16,16,512]{2,1,0:T(8,128)(2,1)} broadcast(bf16[16,512]{1,0:T(8,128)(2,1)} %param.10), dimensions={1,2} | broadcast | bytes 278528 | tf_op jit(solution)/shard_map/broadcast_in_dim | solution.py:29
  2.1 9.6 %all-to-all-start = ((bf16[16,16,512]{2,1,0:T(8,128)(2,1)}), bf16[16,16,512]{2,1,0:T(8,128)(2,1)S(1)}, u32[]{:S(2)}, u32[]{:S(2)}) async-start(bf16[16,16,512]{2,1,0:T(8,128)(2,1)} %broadcast_in_dim.45), calls=%async_computation | async-start | bytes 524288 | tf_op jit(solution)/shard_map/all_to_all | solution.py:23
  11.7 0.7 broadcast_subtract_fusion
  12.5 0.7 broadcast_compare_fusion
  13.4 0.7 copy-done.4
  14.1 4.6 %shard_map.113 = (bf16[4096,512]{1,0:T(8,128)(2,1)}, f32[1,4096]{1,0:T(1,128)S(1)}, bf16[64,512]{1,0:T(8,128)(2,1)S(1)}, f32[1,64]{1,0:T(1,128)S(1)}) custom-call(bf16[4096,512]{1,0:T(8,128)(2,1)} %centers_ref.1, f32[1,512]{1,0:T(1,128)S(1)} %bitcast.69, s32[64,1]{1,0:T(8,128)S(1)} %copy.23.local_ref), custom_call_target="tpu_custom_call" | custom-call | flops 8388608 | bytes 4194304 | tf_op jit(solution)/shard_map/pallas_call | solution.py:75
  18.7 5.0 %all-to-all-done = bf16[16,16,512]{2,1,0:T(8,128)(2,1)S(1)} async-done(((bf16[16,16,512]{2,1,0:T(8,128)(2,1)}), bf16[16,16,512]{2,1,0:T(8,128)(2,1)S(1)}, u32[]{:S(2)}, u32[]{:S(2)}) %all-to-all-start) | async-done | bytes 262176 | tf_op jit(solution)/shard_map/all_to_all | solution.py:23
  23.7 0.5 collective-permute-start.2
  24.2 2.1 %collective-permute-start.1 = (bf16[256,512]{1,0:T(8,128)(2,1)S(1)}, bf16[256,512]{1,0:T(8,128)(2,1)S(1)}, u32[]{:S(2)}, u32[]{:S(2)}) collective-permute-start(bf16[256,512]{1,0:T(8,128)(2,1)S(1)} %bitcast.61), channel_id=1, source_target_pairs={{0,16},{1,17},{2,18},{3,19},{4,20},{5,21},{6,22},{7,23},{8,24},{9,... | collective-permute-start | bytes 786440 | tf_op jit(solution)/shard_map/ppermute | solution.py:33
  26.3 1.5 %collective-permute-start = (bf16[256,512]{1,0:T(8,128)(2,1)S(1)}, bf16[256,512]{1,0:T(8,128)(2,1)S(1)}, u32[]{:S(2)}, u32[]{:S(2)}) collective-permute-start(bf16[256,512]{1,0:T(8,128)(2,1)S(1)} %bitcast.62), channel_id=1, source_target_pairs={{0,48},{1,49},{2,50},{3,51},{4,52},{5,53},{6,54},{7,55},{8,56},{9,... | collective-permute-start | bytes 786440 | tf_op jit(solution)/shard_map/ppermute | solution.py:33
  27.8 4.8 %shard_map.114 = (bf16[256,4096]{1,0:T(8,128)(2,1)}, bf16[4,256,128]{2,1,0:T(8,128)(2,1)S(1)}, bf16[4,256,64]{2,1,0:T(8,128)(2,1)S(1)}) custom-call(s32[1]{0:T(128)} %bitcast.7.slot_ref, bf16[256,512]{1,0:T(8,128)(2,1)S(1)} %bitcast.63, f32[1,512]{1,0:T(1,128)S(1)} %bitcast.70, bf16[4096,512]{1,0:T(8,128)(2,1)} %get-tuple-element.31.centers_ref, ...), custom_call_target="tpu_custom_call" | custom-call | flops 1342177280 | bytes 2097152 | tf_op jit(solution)/shard_map/pallas_call | solution.py:153
  32.6 1.7 %collective-permute-done.2.points_ref = bf16[256,512]{1,0:T(8,128)(2,1)S(1)} collective-permute-done((bf16[256,512]{1,0:T(8,128)(2,1)S(1)}, bf16[256,512]{1,0:T(8,128)(2,1)S(1)}, u32[]{:S(2)}, u32[]{:S(2)}) %collective-permute-start.2) | collective-permute-done | bytes 262176 | tf_op jit(solution)/shard_map/ppermute | solution.py:33
  34.3 2.8 %shard_map.115 = (bf16[256,4096]{1,0:T(8,128)(2,1)}, bf16[4,256,128]{2,1,0:T(8,128)(2,1)S(1)}, bf16[4,256,64]{2,1,0:T(8,128)(2,1)S(1)}) custom-call(s32[1]{0:T(128)} %bitcast.6.slot_ref, bf16[256,512]{1,0:T(8,128)(2,1)S(1)} %collective-permute-done.2.points_ref, f32[1,512]{1,0:T(1,128)S(1)} %bitcast.71, bf16[4096,512]{1,0:T(8,128)(2,1)S(1)} %copy-done, ...), custom_call_target="tpu_custom_call" | custom-call | flops 1342177280 | bytes 2097152 | tf_op jit(solution)/shard_map/pallas_call | solution.py:153
  37.1 2.7 %shard_map.116 = (bf16[256,4096]{1,0:T(8,128)(2,1)}, bf16[4,256,128]{2,1,0:T(8,128)(2,1)S(1)}, bf16[4,256,64]{2,1,0:T(8,128)(2,1)S(1)}) custom-call(s32[1]{0:T(128)} %bitcast.5.slot_ref, bf16[256,512]{1,0:T(8,128)(2,1)S(1)} %collective-permute-done.1.points_ref, f32[1,512]{1,0:T(1,128)S(1)} %bitcast.72, bf16[4096,512]{1,0:T(8,128)(2,1)S(1)} %copy-done, ...), custom_call_target="tpu_custom_call" | custom-call | flops 1342177280 | bytes 2097152 | tf_op jit(solution)/shard_map/pallas_call | solution.py:153
  39.9 3.4 %shard_map.117 = (bf16[256,4096]{1,0:T(8,128)(2,1)}, bf16[4,256,128]{2,1,0:T(8,128)(2,1)}, bf16[4,256,64]{2,1,0:T(8,128)(2,1)S(1)}) custom-call(s32[1]{0:T(128)} %bitcast.1.slot_ref, bf16[256,512]{1,0:T(8,128)(2,1)S(1)} %collective-permute-done.points_ref, f32[1,512]{1,0:T(1,128)S(1)} %bitcast.73, bf16[4096,512]{1,0:T(8,128)(2,1)S(1)} %copy-done, ...), custom_call_target="tpu_custom_call" | custom-call | flops 1342177280 | bytes 2097152 | tf_op jit(solution)/shard_map/pallas_call | solution.py:153
  43.3 7.1 %all-to-all-start.1 = ((bf16[64,16,128]{2,1,0:T(8,128)(2,1)}), bf16[64,16,128]{2,1,0:T(8,128)(2,1)S(1)}, u32[]{:S(2)}, u32[]{:S(2)}) async-start(bf16[64,16,128]{2,1,0:T(8,128)(2,1)} %bitcast.9), calls=%async_computation.1 | async-start | bytes 524288 | tf_op jit(solution)/shard_map/all_to_all | solution.py:23
  50.6 9.8 %all-to-all-done.1.shares_ref = bf16[64,16,128]{2,1,0:T(8,128)(2,1)S(1)} async-done(((bf16[64,16,128]{2,1,0:T(8,128)(2,1)}), bf16[64,16,128]{2,1,0:T(8,128)(2,1)S(1)}, u32[]{:S(2)}, u32[]{:S(2)}) %all-to-all-start.1) | async-done | bytes 262176 | tf_op jit(solution)/shard_map/all_to_all | solution.py:23
  60.4 0.8 shard_map.118
  61.2 6.6 %all-to-all-start.2 = ((bf16[64,16,128]{2,1,0:T(8,128)(2,1)}), bf16[64,16,128]{2,1,0:T(8,128)(2,1)S(1)}, u32[]{:S(2)}, u32[]{:S(2)}) async-start(bf16[64,16,128]{2,1,0:T(8,128)(2,1)} %shard_map.118), calls=%async_computation.2 | async-start | bytes 524288 | tf_op jit(solution)/shard_map/all_to_all | solution.py:23
  67.9 0.5 reshape.75
  68.5 0.6 convolution_bitcast_fusion
  69.1 0.5 copy.26
  69.6 0.2 reshape.76
  69.9 7.9 %all-to-all-done.2 = bf16[64,16,128]{2,1,0:T(8,128)(2,1)S(1)} async-done(((bf16[64,16,128]{2,1,0:T(8,128)(2,1)}), bf16[64,16,128]{2,1,0:T(8,128)(2,1)S(1)}, u32[]{:S(2)}, u32[]{:S(2)}) %all-to-all-start.2) | async-done | bytes 262176 | tf_op jit(solution)/shard_map/all_to_all | solution.py:23
  78.0 6.8 %all-gather = bf16[256,128]{1,0:T(8,128)(2,1)S(1)} all-gather(bf16[64,128]{1,0:T(8,128)(2,1)S(1)} %shard_map.119), channel_id=2, replica_groups=mesh['pts'=4,'ctr'=64] {'pts'}, dimensions={0}, use_global_device_ids=true | all-gather | bytes 81920 | tf_op jit(solution)/shard_map/all_gather | solution.py:380
  84.8 0.8 shard_map.120
  85.7 1.5 %collective-permute-start.3 = (bf16[128,1024]{1,0:T(8,128)(2,1)S(1)}, bf16[128,1024]{1,0:T(8,128)(2,1)S(1)}, u32[]{:S(2)}, u32[]{:S(2)}) collective-permute-start(bf16[128,1024]{1,0:T(8,128)(2,1)S(1)} %copy.27), channel_id=1, source_target_pairs={{0,32},{1,33},{2,34},{3,35},{4,36},{5,37},{6,38},{7,39},{8,40},{9,... | collective-permute-start | bytes 786440 | tf_op jit(solution)/shard_map/ppermute | solution.py:33
  87.2 7.5 %all-to-all-start.3 = ((bf16[64,16,128]{2,1,0:T(8,128)(2,1)}), bf16[64,16,128]{2,1,0:T(8,128)(2,1)S(1)}, u32[]{:S(2)}, u32[]{:S(2)}) async-start(bf16[64,16,128]{2,1,0:T(8,128)(2,1)} %shard_map.120), calls=%async_computation.3 | async-start | bytes 524288 | tf_op jit(solution)/shard_map/all_to_all | solution.py:23
  94.7 1.2 collective-permute-done.3
  96.0 2.2 %fusion.9 = f32[128,4096]{1,0:T(8,128)S(1)} fusion(bf16[256,4096]{1,0:T(8,128)(2,1)} %get-tuple-element.47, bf16[4,256,128]{2,1,0:T(8,128)(2,1)S(1)} %bitcast.56, s32[]{:T(128)S(6)} %select_n.63), kind=kOutput, calls=%fused_computation.21 | convolution fusion | flops 268435456 | bytes 4259844 | tf_op jit(solution)/shard_map/dot_general | solution.py:399
  98.2 0.5 fusion.5
  98.7 1.1 copy-done.9
  99.8 0.5 convolution_add_fusion.1
  100.3 1.1 copy-done.11
  101.4 0.5 fusion
  102.0 0.8 pad_maximum_fusion
  102.9 0.9 constant_dynamic-slice_fusion.1
  103.8 2.5 %all-to-all-done.3 = bf16[64,16,128]{2,1,0:T(8,128)(2,1)S(1)} async-done(((bf16[64,16,128]{2,1,0:T(8,128)(2,1)}), bf16[64,16,128]{2,1,0:T(8,128)(2,1)S(1)}, u32[]{:S(2)}, u32[]{:S(2)}) %all-to-all-start.3) | async-done | bytes 262176 | tf_op jit(solution)/shard_map/all_to_all | solution.py:23
  106.3 1.0 shard_map.121
  107.3 5.0 %all-to-all-start.4 = ((bf16[32,16,128]{2,1,0:T(8,128)(2,1)}), bf16[32,16,128]{2,1,0:T(8,128)(2,1)S(1)}, u32[]{:S(2)}, u32[]{:S(2)}) async-start(bf16[32,16,128]{2,1,0:T(8,128)(2,1)} %get-tuple-element.53), calls=%async_computation.4 | async-start | bytes 262144 | tf_op jit(solution)/shard_map/all_to_all | solution.py:23
  112.3 1.3 maximum_add_fusion
  113.7 0.9 copy-done.7
  114.6 2.9 %collective-permute-start.5 = (bf16[32,4096]{1,0:T(8,128)(2,1)S(1)}, bf16[32,4096]{1,0:T(8,128)(2,1)S(1)}, u32[]{:S(2)}, u32[]{:S(2)}) collective-permute-start(bf16[32,4096]{1,0:T(8,128)(2,1)S(1)} %fusion.4), channel_id=1, source_target_pairs={{0,128},{64,192},{128,0},{192,64},{1,129},{65,193},{129,1},{193,65... | collective-permute-start | bytes 786440 | tf_op jit(solution)/shard_map/ppermute | solution.py:33
  117.5 5.2 %all-to-all-done.4 = bf16[32,16,128]{2,1,0:T(8,128)(2,1)S(1)} async-done(((bf16[32,16,128]{2,1,0:T(8,128)(2,1)}), bf16[32,16,128]{2,1,0:T(8,128)(2,1)S(1)}, u32[]{:S(2)}, u32[]{:S(2)}) %all-to-all-start.4) | async-done | bytes 131104 | tf_op jit(solution)/shard_map/all_to_all | solution.py:23
  122.7 0.4 shard_map.122
  123.1 13.0 %all_to_all.30 = bf16[32,16,128]{2,1,0:T(8,128)(2,1)S(1)} all-to-all(bf16[32,16,128]{2,1,0:T(8,128)(2,1)S(1)} %shard_map.122), channel_id=1, replica_groups={{0,1,2,3,4,5,6,7,8,9,10,11,12,13,14,15,16,17,18,19,20,21,22,23,24,25,26..., dimensions={0} | all-to-all | bytes 262144 | tf_op jit(solution)/shard_map/all_to_all | solution.py:23
  136.2 1.0 shard_map.123
  137.2 0.8 fusion.2
  (41 shorter events, 1.1 us)
Async XLA Ops:
  2.1 21.6 %all-to-all-start = ((bf16[16,16,512]{2,1,0:T(8,128)(2,1)}), bf16[16,16,512]{2,1,0:T(8,128)(2,1)S(1)}, u32[]{:S(2)}, u32[]{:S(2)}) async-start(bf16[16,16,512]{2,1,0:T(8,128)(2,1)} %broadcast_in_dim.45), calls=%async_computation | async-start | bytes 524288 | tf_op jit(solution)/shard_map/all_to_all | solution.py:23
  13.4 0.7 copy-start.4
  14.1 13.7 %copy-start.1 = (bf16[4096,128]{1,0:T(8,128)(2,1)S(1)}, bf16[4096,128]{1,0:T(8,128)(2,1)}, u32[]{:S(2)}) copy-start(bf16[4096,128]{1,0:T(8,128)(2,1)} %coef_ref.7) | copy-start | bytes 3145732
  14.1 13.7 %copy-start.5 = (f32[512]{0:T(512)S(1)}, f32[512]{0:T(512)}, u32[]{:S(2)}) copy-start(f32[512]{0:T(512)} %param.14) | copy-start | bytes 6148
  23.7 10.6 %collective-permute-start.2 = (bf16[256,512]{1,0:T(8,128)(2,1)S(1)}, bf16[256,512]{1,0:T(8,128)(2,1)S(1)}, u32[]{:S(2)}, u32[]{:S(2)}) collective-permute-start(bf16[256,512]{1,0:T(8,128)(2,1)S(1)} %bitcast.60), channel_id=1, source_target_pairs={{0,32},{1,33},{2,34},{3,35},{4,36},{5,37},{6,38},{7,39},{8,40},{9,... | collective-permute-start | bytes 786440 | tf_op jit(solution)/shard_map/ppermute | solution.py:33
  24.2 12.9 %collective-permute-start.1 = (bf16[256,512]{1,0:T(8,128)(2,1)S(1)}, bf16[256,512]{1,0:T(8,128)(2,1)S(1)}, u32[]{:S(2)}, u32[]{:S(2)}) collective-permute-start(bf16[256,512]{1,0:T(8,128)(2,1)S(1)} %bitcast.61), channel_id=1, source_target_pairs={{0,16},{1,17},{2,18},{3,19},{4,20},{5,21},{6,22},{7,23},{8,24},{9,... | collective-permute-start | bytes 786440 | tf_op jit(solution)/shard_map/ppermute | solution.py:33
  26.3 13.5 %collective-permute-start = (bf16[256,512]{1,0:T(8,128)(2,1)S(1)}, bf16[256,512]{1,0:T(8,128)(2,1)S(1)}, u32[]{:S(2)}, u32[]{:S(2)}) collective-permute-start(bf16[256,512]{1,0:T(8,128)(2,1)S(1)} %bitcast.62), channel_id=1, source_target_pairs={{0,48},{1,49},{2,50},{3,51},{4,52},{5,53},{6,54},{7,55},{8,56},{9,... | collective-permute-start | bytes 786440 | tf_op jit(solution)/shard_map/ppermute | solution.py:33
  27.8 6.5 %copy-start = (bf16[4096,512]{1,0:T(8,128)(2,1)S(1)}, bf16[4096,512]{1,0:T(8,128)(2,1)}, u32[]{:S(2)}) copy-start(bf16[4096,512]{1,0:T(8,128)(2,1)} %get-tuple-element.31.centers_ref) | copy-start | bytes 12582916
  39.8 10.6 %copy-start.12 = (f32[8]{0:T(128)S(1)}, f32[8]{0:T(128)}, u32[]{:S(2)}) copy-start(f32[8]{0:T(128)} %param.13) | copy-start | bytes 100
  39.9 10.6 %copy-start.13 = (s32[16]{0:T(128)S(1)}, s32[16]{0:T(128)}, u32[]{:S(2)}) copy-start(s32[16]{0:T(128)} %param.11) | copy-start | bytes 196
  39.9 20.6 %copy-start.6 = (f32[16,128]{1,0:T(8,128)S(1)}, f32[16,128]{1,0:T(8,128)}, u32[]{:S(2)}) copy-start(f32[16,128]{1,0:T(8,128)} %targets_ref.1) | copy-start | bytes 24580
  39.9 28.0 %copy-start.2 = (f32[64,2048]{1,0:T(8,128)S(1)}, f32[64,2048]{1,0:T(8,128)}, u32[]{:S(2)}) copy-start(f32[64,2048]{1,0:T(8,128)} %matrix_ref.2) | copy-start | bytes 1572868
  43.3 17.1 %all-to-all-start.1 = ((bf16[64,16,128]{2,1,0:T(8,128)(2,1)}), bf16[64,16,128]{2,1,0:T(8,128)(2,1)S(1)}, u32[]{:S(2)}, u32[]{:S(2)}) async-start(bf16[64,16,128]{2,1,0:T(8,128)(2,1)} %bitcast.9), calls=%async_computation.1 | async-start | bytes 524288 | tf_op jit(solution)/shard_map/all_to_all | solution.py:23
  61.2 16.5 %all-to-all-start.2 = ((bf16[64,16,128]{2,1,0:T(8,128)(2,1)}), bf16[64,16,128]{2,1,0:T(8,128)(2,1)S(1)}, u32[]{:S(2)}, u32[]{:S(2)}) async-start(bf16[64,16,128]{2,1,0:T(8,128)(2,1)} %shard_map.118), calls=%async_computation.2 | async-start | bytes 524288 | tf_op jit(solution)/shard_map/all_to_all | solution.py:23
  85.7 10.2 %collective-permute-start.3 = (bf16[128,1024]{1,0:T(8,128)(2,1)S(1)}, bf16[128,1024]{1,0:T(8,128)(2,1)S(1)}, u32[]{:S(2)}, u32[]{:S(2)}) collective-permute-start(bf16[128,1024]{1,0:T(8,128)(2,1)S(1)} %copy.27), channel_id=1, source_target_pairs={{0,32},{1,33},{2,34},{3,35},{4,36},{5,37},{6,38},{7,39},{8,40},{9,... | collective-permute-start | bytes 786440 | tf_op jit(solution)/shard_map/ppermute | solution.py:33
  87.2 19.1 %all-to-all-start.3 = ((bf16[64,16,128]{2,1,0:T(8,128)(2,1)}), bf16[64,16,128]{2,1,0:T(8,128)(2,1)S(1)}, u32[]{:S(2)}, u32[]{:S(2)}) async-start(bf16[64,16,128]{2,1,0:T(8,128)(2,1)} %shard_map.120), calls=%async_computation.3 | async-start | bytes 524288 | tf_op jit(solution)/shard_map/all_to_all | solution.py:23
  96.0 2.2 %copy-start.10 = (bf16[256,4096]{1,0:T(8,128)(2,1)S(1)}, bf16[256,4096]{1,0:T(8,128)(2,1)}, u32[]{:S(2)}) copy-start(bf16[256,4096]{1,0:T(8,128)(2,1)} %get-tuple-element.50) | copy-start | bytes 6291460
  98.2 1.6 %copy-start.9 = (bf16[256,4096]{1,0:T(8,128)(2,1)S(1)}, bf16[256,4096]{1,0:T(8,128)(2,1)}, u32[]{:S(2)}) copy-start(bf16[256,4096]{1,0:T(8,128)(2,1)} %get-tuple-element.48) | copy-start | bytes 6291460
  99.8 1.6 %copy-start.11 = (bf16[256,4096]{1,0:T(8,128)(2,1)S(1)}, bf16[256,4096]{1,0:T(8,128)(2,1)}, u32[]{:S(2)}) copy-start(bf16[256,4096]{1,0:T(8,128)(2,1)} %get-tuple-element.49) | copy-start | bytes 6291460
  102.8 9.5 %collective-permute-start.4 = (bf16[2,32,4096]{2,1,0:T(8,128)(2,1)}, bf16[2,32,4096]{2,1,0:T(8,128)(2,1)}, u32[]{:S(2)}, u32[]{:S(2)}) collective-permute-start(bf16[2,32,4096]{2,1,0:T(8,128)(2,1)} %pad_maximum_fusion), channel_id=1, source_target_pairs={{0,64},{64,0},{128,192},{192,128},{1,65},{65,1},{129,193},{193,129... | collective-permute-start | bytes 1572872 | tf_op jit(solution)/shard_map/ppermute | solution.py:33
  106.3 16.4 %copy-start.3 = (f32[64,4096]{1,0:T(8,128)S(1)}, f32[64,4096]{1,0:T(8,128)}, u32[]{:S(2)}) copy-start(f32[64,4096]{1,0:T(8,128)} %matrix_ref.1) | copy-start | bytes 3145732
  107.3 15.4 %all-to-all-start.4 = ((bf16[32,16,128]{2,1,0:T(8,128)(2,1)}), bf16[32,16,128]{2,1,0:T(8,128)(2,1)S(1)}, u32[]{:S(2)}, u32[]{:S(2)}) async-start(bf16[32,16,128]{2,1,0:T(8,128)(2,1)} %get-tuple-element.53), calls=%async_computation.4 | async-start | bytes 262144 | tf_op jit(solution)/shard_map/all_to_all | solution.py:23
  113.6 1.0 copy-start.7
  114.6 22.6 %collective-permute-start.5 = (bf16[32,4096]{1,0:T(8,128)(2,1)S(1)}, bf16[32,4096]{1,0:T(8,128)(2,1)S(1)}, u32[]{:S(2)}, u32[]{:S(2)}) collective-permute-start(bf16[32,4096]{1,0:T(8,128)(2,1)S(1)} %fusion.4), channel_id=1, source_target_pairs={{0,128},{64,192},{128,0},{192,64},{1,129},{65,193},{129,1},{193,65... | collective-permute-start | bytes 786440 | tf_op jit(solution)/shard_map/ppermute | solution.py:33
  122.7 14.5 %copy-start.8 = (f32[2,32,4096]{2,1,0:T(8,128)S(1)}, f32[2,32,4096]{2,1,0:T(8,128)}, u32[]{:S(2)}) copy-start(f32[2,32,4096]{2,1,0:T(8,128)} %copy-done.7) | copy-start | bytes 3145732
